TPU v7x, 32 devices: a whole 2x2x4 slice. The times are simulated.
32 devices in a mesh: fsdp: 2 (over core), context: 4 (over y, x), tensor: 4 (over z).
Axes of the slice: x: 2, y: 2, z: 4, core: 2. Of those that a mesh axis runs over, the one named last changes fastest.
Arguments:
- inputs: bfloat16 [2, 2, 1280, 2048], P(None, 'fsdp', ('context', 'tensor')), may hold values from -6 to 6
- segments: int32 [2, 2, 1280], P(None, 'fsdp'), may hold values from 0 to 7, never falling along the last dimension, each value on 1 to 640 neighbouring positions
- norm_gain: float32 [2048], replicated, may hold values from 0.5 to 1.5
- branch_weight: bfloat16 [2048, 2560], P(('fsdp', 'context'), 'tensor'), may hold values from -0.125 to 0.125
- inner_weight: bfloat16 [2048, 2560], P(('fsdp', 'context'), 'tensor'), may hold values from -0.125 to 0.125
- conv_weight: float32 [4, 2560], P(None, 'tensor'), may hold values from -3 to 3
- conv_bias: float32 [2560], P('tensor'), may hold values from -3 to 3
- rate_weight: bfloat16 [16, 160, 160], P('tensor'), may hold values from -0.5 to 0.5
- rate_bias: float32 [2560], P('tensor'), may hold values from -4 to 4
- input_weight: bfloat16 [16, 160, 160], P('tensor'), may hold values from -0.5 to 0.5
- input_bias: float32 [2560], P('tensor'), may hold values from -4 to 4
- decay_param: float32 [2560], P('tensor'), may hold values from 4 to 11
- out_weight: bfloat16 [2560, 2048], P('tensor', ('fsdp', 'context')), may hold values from -0.5 to 0.5
- mlp_gain: float32 [2048], replicated, may hold values from 0.5 to 1.5
- gate_weight: bfloat16 [2048, 6144], P(('fsdp', 'context'), 'tensor'), may hold values from -0.125 to 0.125
- up_weight: bfloat16 [2048, 6144], P(('fsdp', 'context'), 'tensor'), may hold values from -0.125 to 0.125
- down_weight: bfloat16 [6144, 2048], P('tensor', ('fsdp', 'context')), may hold values from -0.15625 to 0.15625
- cotangent: bfloat16 [2, 2, 1280, 2048], P(None, 'fsdp', ('context', 'tensor')), may hold values from -6 to 6
Outputs:
- block_out: bfloat16 [2, 2, 1280, 2048], P(None, 'fsdp', ('context', 'tensor'))
- input_grad: float32 [2, 2, 1280, 2048], P(None, 'fsdp', ('context', 'tensor'))
- norm_gain_grad: float32 [2048], replicated
- branch_weight_grad: float32 [2048, 2560], P(('fsdp', 'context'), 'tensor')
- inner_weight_grad: float32 [2048, 2560], P(('fsdp', 'context'), 'tensor')
- conv_weight_grad: float32 [4, 2560], P(None, 'tensor')
- conv_bias_grad: float32 [2560], P('tensor')
- rate_weight_grad: float32 [16, 160, 160], P('tensor')
- rate_bias_grad: float32 [2560], P('tensor')
- input_weight_grad: float32 [16, 160, 160], P('tensor')
- input_bias_grad: float32 [2560], P('tensor')
- decay_param_grad: float32 [2560], P('tensor')
- out_weight_grad: float32 [2560, 2048], P('tensor', ('fsdp', 'context'))
- mlp_gain_grad: float32 [2048], replicated
- gate_weight_grad: float32 [2048, 6144], P(('fsdp', 'context'), 'tensor')
- up_weight_grad: float32 [2048, 6144], P(('fsdp', 'context'), 'tensor')
- down_weight_grad: float32 [6144, 2048], P('tensor', ('fsdp', 'context'))
Inputs may be any that keep to these rules, and one draw needn't show every extreme that they name: `segments`: along each sequence the numbers never fall; each document is one run of 1 to 640 positions, every number of 0 to 7 is used in each sequence, and one document of each sequence has exactly 640 positions.
All inputs are finite; a program needn't handle non-finite values.
Results may differ from a plain program's by a relative error of at most 0.014.
Values may be sent and summed in bfloat16 or wider, within the bound.
No kernel may reach another device: no remote copies, remote signals or barrier semaphores. Data moves between devices by JAX's collectives and lax.ppermute only.
A program may use at most 256 MiB of HBM per device.

v0:
```python
from functools import partial

import jax
import jax.numpy as jnp
from jax import lax
from jax.sharding import PartitionSpec as P

CONV = 4
CPOW = 8


EPS = 1e-06


def from_behind(value, axis, by):
    length = lax.axis_size(axis)
    pairs = [(i, i + by) for i in range(length) if 0 <= i + by < length]
    return lax.ppermute(value, axis, pairs)


def rms_norm(values, gain_vec):
    return values * lax.rsqrt(jnp.mean(values * values, axis=-1, keepdims=True) + EPS) * gain_vec


def round_low(values):
    return lax.optimization_barrier(values.astype(jnp.bfloat16)).astype(jnp.float32)


def combine(earlier, following):
    return (earlier[0] * following[0], following[0] * earlier[1] + following[1])


def local_scan(coeffs, offsets):
    return lax.associative_scan(combine, (coeffs, offsets), axis=1)


def gate_terms(rate_pre, input_pre, conv_vals, decay_param, starts):
    log_rate = -CPOW * jax.nn.softplus(-decay_param) * jax.nn.sigmoid(rate_pre)
    decays = jnp.where(starts, 0.0, jnp.exp(log_rate))
    input_scale = jnp.where(starts, 1.0, jnp.sqrt(-jnp.expm1(2.0 * log_rate)))
    return (decays, input_scale * jax.nn.sigmoid(input_pre) * conv_vals)


def gated_unit(gate_pre, up_pre):
    return jax.nn.gelu(gate_pre) * up_pre


def conv_mix(extended, conv_w, conv_b, same_masks):
    length_rows = extended.shape[1] - (CONV - 1)
    total = conv_b + conv_w[0] * extended[:, CONV - 1 :]
    for offset in range(1, CONV):
        total = (
            total
            + conv_w[offset]
            * extended[:, CONV - 1 - offset : CONV - 1 - offset + length_rows]
            * same_masks[offset - 1]
        )
    return total


def project(rows_in, weight):
    return jnp.einsum("sla,ab->slb", rows_in, weight, preferred_element_type=jnp.float32)


def project_back(grad_vals, weight):
    return jnp.einsum("slb,ab->sla", grad_vals, weight, preferred_element_type=jnp.float32)


def outer_sum(rows_in, grad_vals):
    return jnp.einsum("sla,slb->ab", rows_in, grad_vals, preferred_element_type=jnp.float32)


def split_blocks(values, weight):
    return values.reshape(values.shape[0], values.shape[1], weight.shape[0], weight.shape[1])


def block_mix(values, weight):
    return jnp.einsum(
        "slnb,nbc->slnc", split_blocks(values, weight), weight, preferred_element_type=jnp.float32
    ).reshape(values.shape)


def block_back(grad_vals, weight):
    return jnp.einsum(
        "slnc,nbc->slnb",
        split_blocks(grad_vals, weight),
        weight,
        preferred_element_type=jnp.float32,
    ).reshape(grad_vals.shape)


def block_outer(values, grad_vals, weight):
    return jnp.einsum(
        "slnb,slnc->nbc",
        split_blocks(values, weight),
        split_blocks(grad_vals, weight),
        preferred_element_type=jnp.float32,
    )


def fetch_weights(branch_w, inner_w, gate_w, up_w, out_w, down_w):
    return (
        lax.all_gather(branch_w, ("fsdp", "context"), axis=0, tiled=True),
        lax.all_gather(inner_w, ("fsdp", "context"), axis=0, tiled=True),
        lax.all_gather(gate_w, ("fsdp", "context"), axis=0, tiled=True),
        lax.all_gather(up_w, ("fsdp", "context"), axis=0, tiled=True),
        lax.all_gather(out_w, ("fsdp", "context"), axis=1, tiled=True),
        lax.all_gather(down_w, ("fsdp", "context"), axis=1, tiled=True),
    )


def widen_rows(values):
    return lax.all_gather(values, "tensor", axis=1, tiled=True)


def narrow_rows(partial_vals):
    return lax.psum_scatter(partial_vals, "tensor", scatter_dimension=1, tiled=True)


def widen_grads(values):
    return lax.all_gather(values, "tensor", axis=1, tiled=True)


def narrow_grads(partial_vals):
    return lax.psum_scatter(partial_vals, "tensor", scatter_dimension=1, tiled=True)


def carry_state(coeffs, offsets, reverse):
    incoming = jnp.zeros_like(offsets)
    direction = -1 if reverse else 1
    for relay_turn in range(lax.axis_size("context") - 1):
        incoming = from_behind(coeffs * incoming + offsets, "context", direction)
    return incoming


def per_device(
    inputs,
    segments,
    norm_gain,
    branch_weight,
    inner_weight,
    conv_weight,
    conv_bias,
    rate_weight,
    rate_bias,
    input_weight,
    input_bias,
    decay_param,
    out_weight,
    mlp_gain,
    gate_weight,
    up_weight,
    down_weight,
    cotangent,
):
    seq_count = inputs.shape[1]
    span_rows = inputs.shape[2] * lax.axis_size("tensor")
    context_pos = lax.axis_index("context")
    halo_rows = CONV - 1
    lead_pad = jnp.full((seq_count, halo_rows), -1, jnp.int32)
    totals = None
    block_outs = []
    input_grads = []
    for micro_idx in range(inputs.shape[0]):
        gathered = fetch_weights(
            branch_weight, inner_weight, gate_weight, up_weight, out_weight, down_weight
        )
        full_branch, full_inner, full_gate, full_up, full_out, full_down = gathered
        seg_ext = lax.dynamic_slice_in_dim(
            jnp.concatenate([lead_pad, segments[micro_idx]], axis=1),
            context_pos * span_rows,
            span_rows + halo_rows,
            axis=1,
        )
        current = seg_ext[:, halo_rows:]
        same_masks = [
            (seg_ext[:, halo_rows - offset : halo_rows - offset + span_rows] == current).astype(
                jnp.float32
            )[:, :, None]
            for offset in range(1, CONV)
        ]
        starts = (seg_ext[:, halo_rows - 1 : halo_rows - 1 + span_rows] != current)[:, :, None]
        x_rows = inputs[micro_idx].astype(jnp.float32)
        normed_one, norm_one_back = jax.vjp(rms_norm, x_rows, norm_gain)
        wide_one = widen_rows(normed_one.astype(jnp.bfloat16))
        branch_pre = project(wide_one, full_branch)
        inner_low = project(wide_one, full_inner).astype(jnp.bfloat16)
        edge_rows = from_behind(inner_low[:, span_rows - halo_rows :], "context", 1)
        extended = jnp.concatenate([edge_rows, inner_low], axis=1).astype(jnp.float32)
        conv_out, conv_back = jax.vjp(
            partial(conv_mix, same_masks=same_masks), extended, conv_weight, conv_bias
        )
        conv_low = conv_out.astype(jnp.bfloat16)
        rate_pre = block_mix(conv_low, rate_weight) + rate_bias
        input_pre = block_mix(conv_low, input_weight) + input_bias
        (decays, drives), gate_back = jax.vjp(
            partial(gate_terms, starts=starts),
            rate_pre,
            input_pre,
            conv_low.astype(jnp.float32),
            decay_param,
        )
        prod_loc, state_loc = local_scan(decays, drives)
        state_in = carry_state(prod_loc[:, -1], state_loc[:, -1], False)
        states = state_loc + prod_loc * state_in[:, None]
        gelu_branch, gelu_back = jax.vjp(jax.nn.gelu, branch_pre)
        mixed_low = (states * gelu_branch).astype(jnp.bfloat16)
        residual = x_rows + narrow_rows(project(mixed_low, full_out))
        normed_two, norm_two_back = jax.vjp(rms_norm, residual, mlp_gain)
        wide_two = widen_rows(normed_two.astype(jnp.bfloat16))
        gate_pre = project(wide_two, full_gate)
        up_pre = project(wide_two, full_up)
        hidden_val, hidden_back = jax.vjp(gated_unit, gate_pre, up_pre)
        hidden_low = hidden_val.astype(jnp.bfloat16)
        block_outs.append(
            (residual + narrow_rows(project(hidden_low, full_down))).astype(jnp.bfloat16)
        )
        out_grad = cotangent[micro_idx].astype(jnp.float32)
        wide_grad = widen_grads(cotangent[micro_idx])
        down_term = outer_sum(hidden_low, wide_grad)
        gate_grad, up_grad = hidden_back(project_back(wide_grad, full_down))
        gate_low = gate_grad.astype(jnp.bfloat16)
        up_low = up_grad.astype(jnp.bfloat16)
        gate_term = outer_sum(wide_two, gate_low)
        up_term = outer_sum(wide_two, up_low)
        normed_two_grad = round_low(
            narrow_grads(project_back(gate_low, full_gate) + project_back(up_low, full_up))
        )
        resid_norm_grad, gain_two_term = norm_two_back(normed_two_grad)
        resid_grad = out_grad + resid_norm_grad
        wide_resid = widen_grads(resid_grad.astype(jnp.bfloat16))
        out_term = outer_sum(mixed_low, wide_resid)
        mixed_grad = project_back(wide_resid, full_out)
        (branch_grad,) = gelu_back(mixed_grad * states)
        branch_low = branch_grad.astype(jnp.bfloat16)
        state_grad = mixed_grad * gelu_branch
        next_decays = jnp.concatenate([decays[:, 1:], jnp.ones_like(decays[:, :1])], axis=1)
        rev_prod, rev_grad = local_scan(jnp.flip(next_decays, 1), jnp.flip(state_grad, 1))
        rev_prod = jnp.flip(rev_prod, 1)
        rev_grad = jnp.flip(rev_grad, 1)
        grad_in = carry_state(decays[:, 0] * rev_prod[:, 0], decays[:, 0] * rev_grad[:, 0], True)
        drive_grad = rev_grad + rev_prod * grad_in[:, None]
        prev_states = jnp.concatenate([state_in[:, None], states[:, :-1]], axis=1)
        rate_grad, input_pre_grad, conv_part, decay_term = gate_back(
            (drive_grad * prev_states, drive_grad)
        )
        rate_low = rate_grad.astype(jnp.bfloat16)
        input_low = input_pre_grad.astype(jnp.bfloat16)
        rate_w_term = block_outer(conv_low, rate_low, rate_weight)
        rate_b_term = jnp.sum(rate_low.astype(jnp.float32), axis=(0, 1))
        input_w_term = block_outer(conv_low, input_low, input_weight)
        input_b_term = jnp.sum(input_low.astype(jnp.float32), axis=(0, 1))
        conv_grad = (
            conv_part + block_back(rate_low, rate_weight) + block_back(input_low, input_weight)
        )
        ext_grad, conv_w_term, conv_b_term = conv_back(conv_grad)
        edge_grad = from_behind(ext_grad[:, :halo_rows], "context", -1)
        inner_grad = ext_grad[:, halo_rows:] + jnp.concatenate(
            [jnp.zeros_like(ext_grad[:, 2 * halo_rows :]), edge_grad], axis=1
        )
        inner_low_grad = inner_grad.astype(jnp.bfloat16)
        inner_term = outer_sum(wide_one, inner_low_grad)
        branch_term = outer_sum(wide_one, branch_low)
        normed_one_grad = round_low(
            narrow_grads(
                project_back(inner_low_grad, full_inner) + project_back(branch_low, full_branch)
            )
        )
        x_norm_grad, gain_one_term = norm_one_back(normed_one_grad)
        input_grads.append(resid_grad + x_norm_grad)
        terms = (
            gain_one_term,
            branch_term,
            inner_term,
            conv_w_term,
            conv_b_term,
            rate_w_term,
            rate_b_term,
            input_w_term,
            input_b_term,
            decay_term,
            out_term,
            gain_two_term,
            gate_term,
            up_term,
            down_term,
        )
        totals = terms if totals is None else jax.tree.map(jnp.add, totals, terms)
    big_grads = (
        lax.psum_scatter(
            totals[1].astype(jnp.bfloat16), ("fsdp", "context"), scatter_dimension=0, tiled=True
        ).astype(jnp.float32),
        lax.psum_scatter(
            totals[2].astype(jnp.bfloat16), ("fsdp", "context"), scatter_dimension=0, tiled=True
        ).astype(jnp.float32),
        lax.psum_scatter(
            totals[12].astype(jnp.bfloat16), ("fsdp", "context"), scatter_dimension=0, tiled=True
        ).astype(jnp.float32),
        lax.psum_scatter(
            totals[13].astype(jnp.bfloat16), ("fsdp", "context"), scatter_dimension=0, tiled=True
        ).astype(jnp.float32),
        lax.psum_scatter(
            totals[10].astype(jnp.bfloat16), ("fsdp", "context"), scatter_dimension=1, tiled=True
        ).astype(jnp.float32),
        lax.psum_scatter(
            totals[14].astype(jnp.bfloat16), ("fsdp", "context"), scatter_dimension=1, tiled=True
        ).astype(jnp.float32),
    )
    small_grads = (
        lax.psum(totals[3].astype(jnp.bfloat16), ("fsdp", "context")).astype(jnp.float32),
        lax.psum(totals[4].astype(jnp.bfloat16), ("fsdp", "context")).astype(jnp.float32),
        lax.psum(totals[5].astype(jnp.bfloat16), ("fsdp", "context")).astype(jnp.float32),
        lax.psum(totals[6].astype(jnp.bfloat16), ("fsdp", "context")).astype(jnp.float32),
        lax.psum(totals[7].astype(jnp.bfloat16), ("fsdp", "context")).astype(jnp.float32),
        lax.psum(totals[8].astype(jnp.bfloat16), ("fsdp", "context")).astype(jnp.float32),
        lax.psum(totals[9].astype(jnp.bfloat16), ("fsdp", "context")).astype(jnp.float32),
    )
    gain_grads = lax.psum((totals[0], totals[11]), ("fsdp", "context", "tensor"))
    return (
        jnp.stack(block_outs),
        jnp.stack(input_grads),
        gain_grads[0],
        big_grads[0],
        big_grads[1],
        small_grads[0],
        small_grads[1],
        small_grads[2],
        small_grads[3],
        small_grads[4],
        small_grads[5],
        small_grads[6],
        big_grads[4],
        gain_grads[1],
        big_grads[2],
        big_grads[3],
        big_grads[5],
    )


def solution(mesh):
    placed = (
        P(None, "fsdp", ("context", "tensor"), None),
        P(None, "fsdp", None),
        P(),
        P(("fsdp", "context"), "tensor"),
        P(("fsdp", "context"), "tensor"),
        P(None, "tensor"),
        P("tensor"),
        P("tensor", None, None),
        P("tensor"),
        P("tensor", None, None),
        P("tensor"),
        P("tensor"),
        P("tensor", ("fsdp", "context")),
        P(),
        P(("fsdp", "context"), "tensor"),
        P(("fsdp", "context"), "tensor"),
        P("tensor", ("fsdp", "context")),
        P(None, "fsdp", ("context", "tensor"), None),
    )
    return jax.shard_map(
        per_device,
        mesh=mesh,
        in_specs=placed,
        out_specs=(
            P(None, "fsdp", ("context", "tensor"), None),
            P(None, "fsdp", ("context", "tensor"), None),
            P(),
            P(("fsdp", "context"), "tensor"),
            P(("fsdp", "context"), "tensor"),
            P(None, "tensor"),
            P("tensor"),
            P("tensor", None, None),
            P("tensor"),
            P("tensor", None, None),
            P("tensor"),
            P("tensor"),
            P("tensor", ("fsdp", "context")),
            P(),
            P(("fsdp", "context"), "tensor"),
            P(("fsdp", "context"), "tensor"),
            P("tensor", ("fsdp", "context")),
        ),
        check_vma=False,
    )
```

profile of v0, /device:TPU:0, one launch (start us, length us, event | category | flops | bytes accessed | tf_op | source)
XLA Modules:
  0.0 2164.5 jit_solution(8397309703831230440)
XLA Ops:
  14.8 32.1 %all-gather.17.cloned.1.call-done = bf16[1,320,2048]{2,1,0:T(8,128)(2,1)} async-done(((bf16[1,80,2048]{2,1,0:T(8,128)(2,1)}), bf16[1,320,2048]{2,1,0:T(8,128)(2,1)}) %all-gather.17.cloned.1.call-update) | async-done | bytes 1310736 | tf_op jit(solution)/shard_map/all_gather | solution.py:113
  46.9 31.0 %all-gather.19.cloned.1.call-done = bf16[2048,640]{1,0:T(8,128)(2,1)} async-done(((bf16[256,640]{1,0:T(8,128)(2,1)}), bf16[2048,640]{1,0:T(8,128)(2,1)}) %all-gather.19.cloned.1.call-update) | async-done | bytes 2621456 | tf_op jit(solution)/shard_map/all_gather | solution.py:104
  84.8 28.0 %all-gather.33.cloned.1.call-done = bf16[1,320,2048]{2,1,0:T(8,128)(2,1)} async-done(((bf16[1,80,2048]{2,1,0:T(8,128)(2,1)}), bf16[1,320,2048]{2,1,0:T(8,128)(2,1)}) %all-gather.33.cloned.1.call-update) | async-done | bytes 1310736 | tf_op jit(solution)/shard_map/all_gather | solution.py:113
  119.6 24.2 %all-gather.21.cloned.1.call-done = bf16[2048,640]{1,0:T(8,128)(2,1)} async-done(((bf16[256,640]{1,0:T(8,128)(2,1)}), bf16[2048,640]{1,0:T(8,128)(2,1)}) %all-gather.21.cloned.1.call-update) | async-done | bytes 2621456 | tf_op jit(solution)/shard_map/all_gather | solution.py:103
  161.3 4.7 exponential_select_fusion
  405.0 4.6 convolution_bitcast_fusion.3
  479.0 51.8 %reduce-scatter.19.cloned.1.call-done = f32[1,80,2048]{2,1,0:T(8,128)} async-done(((f32[1,320,2048]{2,1,0:T(8,128)}), f32[1,80,2048]{2,1,0:T(8,128)}) %reduce-scatter.19.cloned.1.call-update) | async-done | bytes 655376 | tf_op jit(solution)/shard_map/reduce_scatter | solution.py:117
  537.1 40.8 %all-gather.27.cloned.1.call-done = bf16[2048,1536]{1,0:T(8,128)(2,1)} async-done(((bf16[256,1536]{1,0:T(8,128)(2,1)}), bf16[2048,1536]{1,0:T(8,128)(2,1)}) %all-gather.27.cloned.1.call-update) | async-done | bytes 6291472 | tf_op jit(solution)/shard_map/all_gather | solution.py:105
  577.9 34.9 %all-gather.25.cloned.1.call-done = bf16[1,320,2048]{2,1,0:T(8,128)(2,1)} async-done(((bf16[1,80,2048]{2,1,0:T(8,128)(2,1)}), bf16[1,320,2048]{2,1,0:T(8,128)(2,1)}) %all-gather.25.cloned.1.call-update) | async-done | bytes 1310736 | tf_op jit(solution)/shard_map/all_gather | solution.py:113
  612.8 6.7 fusion.51
  619.5 39.6 %all-gather.29.cloned.1.call-done = bf16[2048,1536]{1,0:T(8,128)(2,1)} async-done(((bf16[256,1536]{1,0:T(8,128)(2,1)}), bf16[2048,1536]{1,0:T(8,128)(2,1)}) %all-gather.29.cloned.1.call-update) | async-done | bytes 6291472 | tf_op jit(solution)/shard_map/all_gather | solution.py:106
  659.1 6.7 fusion.49
  665.7 28.2 %all-gather.41.cloned.1.call-done = bf16[1,1,320,2048]{3,2,1,0:T(8,128)(2,1)} async-done(((bf16[1,1,80,2048]{3,2,1,0:T(8,128)(2,1)}), bf16[1,1,320,2048]{3,2,1,0:T(8,128)(2,1)}) %all-gather.41.cloned.1.call-update) | async-done | bytes 1310736 | tf_op jit(solution)/shard_map/all_gather | solution.py:121
  693.9 47.4 %all-gather.31.cloned.1.call-done = bf16[1536,2048]{1,0:T(8,128)(2,1)} async-done(((bf16[1536,256]{1,0:T(8,128)(2,1)}), bf16[1536,2048]{1,0:T(8,128)(2,1)}) %all-gather.31.cloned.1.call-update) | async-done | bytes 6291472 | tf_op jit(solution)/shard_map/all_gather | solution.py:108
  741.4 9.0 multiply_convert_fusion.1
  750.3 5.8 fusion.252
  760.4 51.8 %reduce-scatter.23.cloned.1.call-done = f32[1,80,2048]{2,1,0:T(8,128)} async-done(((f32[1,320,2048]{2,1,0:T(8,128)}), f32[1,80,2048]{2,1,0:T(8,128)}) %reduce-scatter.23.cloned.1.call-update) | async-done | bytes 655376 | tf_op jit(solution)/shard_map/reduce_scatter | solution.py:125
  817.5 31.9 %all-gather.35.cloned.1.call-done = bf16[1,320,2048]{2,1,0:T(8,128)(2,1)} async-done(((bf16[1,80,2048]{2,1,0:T(8,128)(2,1)}), bf16[1,320,2048]{2,1,0:T(8,128)(2,1)}) %all-gather.35.cloned.1.call-update) | async-done | bytes 1310736 | tf_op jit(solution)/shard_map/all_gather | solution.py:113
  849.4 6.8 fusion.36
  856.1 6.5 fusion.34
  862.7 20.4 all-gather.43.cloned.1.call-done
  883.1 8.9 multiply_convert_fusion
  891.9 5.7 fusion.253
  897.7 6.5 fusion.2
  904.3 6.9 convolution_bitcast_fusion
  911.2 44.2 %reduce-scatter.27.cloned.1.call-done = f32[1,80,2048]{2,1,0:T(8,128)} async-done(((f32[1,320,2048]{2,1,0:T(8,128)}), f32[1,80,2048]{2,1,0:T(8,128)}) %reduce-scatter.27.cloned.1.call-update) | async-done | bytes 655376 | tf_op jit(solution)/shard_map/reduce_scatter | solution.py:125
  959.2 50.2 %reduce-scatter.21.cloned.1.call-done = f32[1,80,2048]{2,1,0:T(8,128)} async-done(((f32[1,320,2048]{2,1,0:T(8,128)}), f32[1,80,2048]{2,1,0:T(8,128)}) %reduce-scatter.21.cloned.1.call-update) | async-done | bytes 655376 | tf_op jit(solution)/shard_map/reduce_scatter | solution.py:117
  1036.0 5.7 slice.1250
  1041.7 5.6 slice.1259
  1047.3 5.6 slice.1252
  1052.9 5.7 slice.1334
  1058.7 5.6 slice.1343
  1064.3 5.6 slice.1336
  1070.0 5.0 fusion.81
  1082.5 5.6 slice.1256
  1088.1 5.6 slice.1254
  1173.8 5.0 fusion.89
  1186.2 5.6 slice.1340
  1191.8 5.6 slice.1338
  1343.3 5.7 slice.1311
  1443.0 5.7 slice.1395
  1489.7 9.6 fusion.47
  1503.9 8.2 rev.17
  1512.1 8.1 rev.18
  1520.2 8.2 rev.19
  1528.4 8.1 rev.20
  1536.6 4.8 multiply_reduce_fusion.1
  1557.4 11.4 add_convert_fusion.2
  1568.9 5.2 fusion.45
  1574.2 5.6 add_convert_fusion.1
  1580.0 5.2 fusion.28
  1585.3 5.6 add_convert_fusion
  1623.7 4.8 multiply_reduce_fusion.5
  1659.6 6.6 convolution_bitcast_fusion.1
  1667.1 28.4 %all-reduce.153 = (bf16[4,640]{1,0:T(4,128)(2,1)S(1)}, bf16[640]{0:T(1024)(128)(2,1)S(1)}, bf16[640]{0:T(1024)(128)(2,1)S(1)}, bf16[640]{0:T(1024)(128)(2,1)S(1)}, bf16[640]{0:T(1024)(128)(2,1)S(1)}) all-reduce(bf16[4,640]{1,0:T(4,128)(2,1)S(1)} %add_convert_fusion.10, ...), channel_id=1, replica_groups=mesh['fsdp'=2,'context'=4,'tensor'=4] {'fsdp','context'}, use_global_device_ids=true, to_apply=%region_29.31 | all-reduce | flops 5120 | bytes 20480 | tf_op jit(solution)/shard_map/psum | solution.py:310
  1704.7 40.2 %reduce-scatter.39.cloned.1.call-done = bf16[256,1536]{1,0:T(8,128)(2,1)} async-done(((bf16[2048,1536]{1,0:T(8,128)(2,1)}), bf16[256,1536]{1,0:T(8,128)(2,1)}) %reduce-scatter.39.cloned.1.call-update) | async-done | bytes 786448 | tf_op jit(solution)/shard_map/reduce_scatter | solution.py:299
  1747.4 63.1 %reduce-scatter.41.cloned.1.call-done = bf16[1536,256]{1,0:T(8,128)(2,1)} async-done(((bf16[1536,2048]{1,0:T(8,128)(2,1)}), bf16[1536,256]{1,0:T(8,128)(2,1)}) %reduce-scatter.41.cloned.1.call-update) | async-done | bytes 786448 | tf_op jit(solution)/shard_map/reduce_scatter | solution.py:305
  1812.8 44.5 %reduce-scatter.31.cloned.1.call-done = bf16[256,640]{1,0:T(8,128)(2,1)} async-done(((bf16[2048,640]{1,0:T(8,128)(2,1)}), bf16[256,640]{1,0:T(8,128)(2,1)}) %reduce-scatter.31.cloned.1.call-update) | async-done | bytes 327696 | tf_op jit(solution)/shard_map/reduce_scatter | solution.py:290
  1859.2 45.1 %reduce-scatter.35.cloned.1.call-done = bf16[640,256]{1,0:T(8,128)(2,1)} async-done(((bf16[640,2048]{1,0:T(8,128)(2,1)}), bf16[640,256]{1,0:T(8,128)(2,1)}) %reduce-scatter.35.cloned.1.call-update) | async-done | bytes 327696 | tf_op jit(solution)/shard_map/reduce_scatter | solution.py:302
  1906.2 45.0 %reduce-scatter.33.cloned.1.call-done = bf16[256,640]{1,0:T(8,128)(2,1)} async-done(((bf16[2048,640]{1,0:T(8,128)(2,1)}), bf16[256,640]{1,0:T(8,128)(2,1)}) %reduce-scatter.33.cloned.1.call-update) | async-done | bytes 327696 | tf_op jit(solution)/shard_map/reduce_scatter | solution.py:293
  1953.0 52.4 %reduce-scatter.25.cloned.1.call-done = f32[1,80,2048]{2,1,0:T(8,128)} async-done(((f32[1,320,2048]{2,1,0:T(8,128)}), f32[1,80,2048]{2,1,0:T(8,128)}) %reduce-scatter.25.cloned.1.call-update) | async-done | bytes 655376 | tf_op jit(solution)/shard_map/reduce_scatter | solution.py:125
  2007.3 52.3 %reduce-scatter.29.cloned.1.call-done = f32[1,80,2048]{2,1,0:T(8,128)} async-done(((f32[1,320,2048]{2,1,0:T(8,128)}), f32[1,80,2048]{2,1,0:T(8,128)}) %reduce-scatter.29.cloned.1.call-update) | async-done | bytes 655376 | tf_op jit(solution)/shard_map/reduce_scatter | solution.py:125
  2064.7 49.0 %reduce-scatter.17.cloned.1.call-done = f32[1,80,2048]{2,1,0:T(8,128)} async-done(((f32[1,320,2048]{2,1,0:T(8,128)}), f32[1,80,2048]{2,1,0:T(8,128)}) %reduce-scatter.17.cloned.1.call-update) | async-done | bytes 655376 | tf_op jit(solution)/shard_map/reduce_scatter | solution.py:117
  2117.5 40.0 %all-reduce.152 = (f32[2048]{0:T(1024)}, f32[2048]{0:T(1024)}) all-reduce(f32[2048]{0:T(1024)S(1)} %add.1474, f32[2048]{0:T(1024)S(1)} %add.1485), channel_id=1, replica_groups=mesh['fsdp'=2,'context'=4,'tensor'=4] {'fsdp','context','tensor'}, use_global_device_ids=true, to_apply=%region_18.20 | all-reduce | flops 4096 | bytes 32768 | tf_op jit(solution)/shard_map/psum | solution.py:318
  (1183 shorter events, 882.3 us)
Async XLA Ops:
  7.2 143.8 %copy-start = (bf16[4,160,160]{2,1,0:T(8,128)(2,1)S(1)}, bf16[4,160,160]{2,1,0:T(8,128)(2,1)}, u32[]{:S(2)}) copy-start(bf16[4,160,160]{2,1,0:T(8,128)(2,1)} %param.28) | copy-start | bytes 614404
  7.2 39.7 %all-gather.17.cloned.1.call-start = ((), (), s32[]{:S(2)}) async-start(), calls=%async_computation.14 | async-start | bytes 1638400 | tf_op jit(solution)/shard_map/all_gather | solution.py:113
  11.4 66.6 %all-gather.19.cloned.1.call-start = ((), (), s32[]{:S(2)}) async-start(), calls=%async_computation.15 | async-start | bytes 2949120 | tf_op jit(solution)/shard_map/all_gather | solution.py:104
  12.1 100.7 %all-gather.33.cloned.1.call-start = ((), (), s32[]{:S(2)}) async-start(), calls=%async_computation.24 | async-start | bytes 1638400 | tf_op jit(solution)/shard_map/all_gather | solution.py:113
  12.9 130.8 %all-gather.21.cloned.1.call-start = ((), (), s32[]{:S(2)}) async-start(), calls=%async_computation.16 | async-start | bytes 2949120 | tf_op jit(solution)/shard_map/all_gather | solution.py:103
  13.5 391.6 %all-gather.23.cloned.1.call-start = ((), (), s32[]{:S(2)}) async-start(), calls=%async_computation.17 | async-start | bytes 2949120 | tf_op jit(solution)/shard_map/all_gather | solution.py:107
  14.0 464.9 %reduce-scatter.15.cloned.1.call-start = ((), (), s32[]{:S(2)}) async-start(), calls=%async_computation.18 | async-start | bytes 3276800 | tf_op jit(solution)/shard_map/reduce_scatter | solution.py:117
  14.2 147.0 %copy-start.163 = (pred[320]{0:T(512)(128)(4,1)}, pred[320]{0:T(512)(128)(4,1)S(1)}, u32[]{:S(2)}) copy-start(pred[320]{0:T(512)(128)(4,1)S(1)} %compare_reduce_fusion) | copy-start | bytes 964
  14.4 133.4 %copy-start.120 = (f32[320]{0:T(512)}, f32[320]{0:T(512)S(1)}, u32[]{:S(2)}) copy-start(f32[320]{0:T(512)S(1)} %get-tuple-element.50) | copy-start | bytes 3844
  14.4 133.4 %copy-start.122 = (f32[320]{0:T(512)}, f32[320]{0:T(512)S(1)}, u32[]{:S(2)}) copy-start(f32[320]{0:T(512)S(1)} %get-tuple-element.51) | copy-start | bytes 3844
  14.4 133.4 %copy-start.124 = (f32[320]{0:T(512)}, f32[320]{0:T(512)S(1)}, u32[]{:S(2)}) copy-start(f32[320]{0:T(512)S(1)} %get-tuple-element.52) | copy-start | bytes 3844
  14.7 146.6 %copy-start.160 = (pred[320]{0:T(512)(128)(4,1)}, pred[320]{0:T(512)(128)(4,1)S(1)}, u32[]{:S(2)}) copy-start(pred[320]{0:T(512)(128)(4,1)S(1)} %compare_reduce_fusion.1) | copy-start | bytes 964
  81.3 66.2 %collective-permute-start = (bf16[1,3,640]{2,1,0:T(4,128)(2,1)S(1)}, bf16[1,3,640]{2,1,0:T(4,128)(2,1)S(1)}, u32[]{:S(2)}, u32[]{:S(2)}) collective-permute-start(bf16[1,3,640]{2,1,0:T(4,128)(2,1)S(1)} %slice.1414), channel_id=1, source_target_pairs={{0,4},{4,8},{8,12},{1,5},{5,9},{9,13},{2,6},{6,10},{10,14},{3,7},{... | collective-permute-start | bytes 11528 | tf_op jit(solution)/shard_map/ppermute | solution.py:18
  116.2 31.5 %collective-permute-start.4 = (bf16[1,3,640]{2,1,0:T(4,128)(2,1)S(1)}, bf16[1,3,640]{2,1,0:T(4,128)(2,1)S(1)}, u32[]{:S(2)}, u32[]{:S(2)}) collective-permute-start(bf16[1,3,640]{2,1,0:T(4,128)(2,1)S(1)} %slice.1465), channel_id=1, source_target_pairs={{0,4},{4,8},{8,12},{1,5},{5,9},{9,13},{2,6},{6,10},{10,14},{3,7},{... | collective-permute-start | bytes 11528 | tf_op jit(solution)/shard_map/ppermute | solution.py:18
  156.9 1384.5 %copy-start.5 = (f32[1,320,640]{2,1,0:T(8,128)}, f32[1,320,640]{2,1,0:T(8,128)S(1)}, u32[]{:S(2)}) copy-start(f32[1,320,640]{2,1,0:T(8,128)S(1)} %copy.70) | copy-start | bytes 2457604
  340.4 8.8 collective-permute-start.1
  350.6 10.0 collective-permute-start.2
  361.9 39.6 %collective-permute-start.3 = (f32[1,640]{1,0:T(1,128)}, f32[1,640]{1,0:T(1,128)S(1)}, u32[]{:S(2)}, u32[]{:S(2)}) collective-permute-start(f32[1,640]{1,0:T(1,128)} %multiply_add_fusion.45), channel_id=1, source_target_pairs={{0,4},{4,8},{8,12},{1,5},{5,9},{9,13},{2,6},{6,10},{10,14},{3,7},{... | collective-permute-start | bytes 7688 | tf_op jit(solution)/shard_map/ppermute | solution.py:18
  409.9 120.9 %reduce-scatter.19.cloned.1.call-start = ((), (), s32[]{:S(2)}) async-start(), calls=%async_computation.25 | async-start | bytes 3276800 | tf_op jit(solution)/shard_map/reduce_scatter | solution.py:117
  452.2 3.2 collective-permute-start.5
  456.2 5.5 collective-permute-start.6
  462.5 8.6 collective-permute-start.7
  478.2 99.7 %all-gather.27.cloned.1.call-start = ((), (), s32[]{:S(2)}) async-start(), calls=%async_computation.20 | async-start | bytes 7077888 | tf_op jit(solution)/shard_map/all_gather | solution.py:105
  478.9 133.9 %all-gather.25.cloned.1.call-start = ((), (), s32[]{:S(2)}) async-start(), calls=%async_computation.19 | async-start | bytes 1638400 | tf_op jit(solution)/shard_map/all_gather | solution.py:113
  533.2 476.2 %copy-start.206 = (f32[80]{0:T(128)}, f32[80]{0:T(128)S(1)}, u32[]{:S(2)}) copy-start(f32[80]{0:T(128)S(1)} %fusion.194) | copy-start | bytes 964
  534.9 124.2 %all-gather.29.cloned.1.call-start = ((), (), s32[]{:S(2)}) async-start(), calls=%async_computation.21 | async-start | bytes 7077888 | tf_op jit(solution)/shard_map/all_gather | solution.py:106
  535.5 158.4 %all-gather.41.cloned.1.call-start = ((), (), s32[]{:S(2)}) async-start(), calls=%async_computation.40 | async-start | bytes 1638400 | tf_op jit(solution)/shard_map/all_gather | solution.py:121
  536.5 204.9 %all-gather.31.cloned.1.call-start = ((), (), s32[]{:S(2)}) async-start(), calls=%async_computation.22 | async-start | bytes 7077888 | tf_op jit(solution)/shard_map/all_gather | solution.py:108
  537.0 275.2 %reduce-scatter.23.cloned.1.call-start = ((), (), s32[]{:S(2)}) async-start(), calls=%async_computation.28 | async-start | bytes 3276800 | tf_op jit(solution)/shard_map/reduce_scatter | solution.py:125
  760.0 89.4 %all-gather.35.cloned.1.call-start = ((), (), s32[]{:S(2)}) async-start(), calls=%async_computation.26 | async-start | bytes 1638400 | tf_op jit(solution)/shard_map/all_gather | solution.py:113
  760.4 249.0 %copy-start.208 = (f32[80]{0:T(128)}, f32[80]{0:T(128)S(1)}, u32[]{:S(2)}) copy-start(f32[80]{0:T(128)S(1)} %fusion.196) | copy-start | bytes 964
  816.8 66.2 %all-gather.43.cloned.1.call-start = ((), (), s32[]{:S(2)}) async-start(), calls=%async_computation.41 | async-start | bytes 1638400 | tf_op jit(solution)/shard_map/all_gather | solution.py:121
  817.4 138.0 %reduce-scatter.27.cloned.1.call-start = ((), (), s32[]{:S(2)}) async-start(), calls=%async_computation.31 | async-start | bytes 3276800 | tf_op jit(solution)/shard_map/reduce_scatter | solution.py:125
  904.2 105.2 %reduce-scatter.21.cloned.1.call-start = ((), (), s32[]{:S(2)}) async-start(), calls=%async_computation.27 | async-start | bytes 3276800 | tf_op jit(solution)/shard_map/reduce_scatter | solution.py:117
  911.2 158.8 %all-gather.37.cloned.1.call-start = ((), (), s32[]{:S(2)}) async-start(), calls=%async_computation.29 | async-start | bytes 1638400 | tf_op jit(solution)/shard_map/all_gather | solution.py:121
  1012.5 161.3 %all-gather.39.cloned.1.call-start = ((), (), s32[]{:S(2)}) async-start(), calls=%async_computation.32 | async-start | bytes 1638400 | tf_op jit(solution)/shard_map/all_gather | solution.py:121
  1069.9 628.6 %all-reduce.157.cloned.1.call-start = ((), (), s32[]{:S(2)}) async-start(), calls=%async_computation.42 | async-start | bytes 1310720 | tf_op jit(solution)/shard_map/psum | solution.py:312
  1376.5 100.5 %collective-permute-start.8 = (f32[1,640]{1,0:T(1,128)}, f32[1,640]{1,0:T(1,128)}, u32[]{:S(2)}, u32[]{:S(2)}) collective-permute-start(f32[1,640]{1,0:T(1,128)} %get-tuple-element.78), channel_id=1, source_target_pairs={{4,0},{8,4},{12,8},{5,1},{9,5},{13,9},{6,2},{10,6},{14,10},{7,3},{... | collective-permute-start | bytes 7688 | tf_op jit(solution)/shard_map/ppermute | solution.py:18
  1475.7 6.1 collective-permute-start.12
  1477.7 6.7 collective-permute-start.9
  1481.9 6.4 collective-permute-start.13
  1484.5 52.0 %collective-permute-start.10 = (f32[1,640]{1,0:T(1,128)S(1)}, f32[1,640]{1,0:T(1,128)S(1)}, u32[]{:S(2)}, u32[]{:S(2)}) collective-permute-start(f32[1,640]{1,0:T(1,128)S(1)} %multiply_add_fusion.39), channel_id=1, source_target_pairs={{4,0},{8,4},{12,8},{5,1},{9,5},{13,9},{6,2},{10,6},{14,10},{7,3},{... | collective-permute-start | bytes 7688 | tf_op jit(solution)/shard_map/ppermute | solution.py:18
  1488.2 48.3 %collective-permute-start.14 = (f32[1,640]{1,0:T(1,128)S(1)}, f32[1,640]{1,0:T(1,128)S(1)}, u32[]{:S(2)}, u32[]{:S(2)}) collective-permute-start(f32[1,640]{1,0:T(1,128)S(1)} %multiply_add_fusion.36), channel_id=1, source_target_pairs={{4,0},{8,4},{12,8},{5,1},{9,5},{13,9},{6,2},{10,6},{14,10},{7,3},{... | collective-permute-start | bytes 7688 | tf_op jit(solution)/shard_map/ppermute | solution.py:18
  1557.0 145.2 %reduce-scatter.37.cloned.1.call-start = ((), (), s32[]{:S(2)}) async-start(), calls=%async_computation.37 | async-start | bytes 7077888 | tf_op jit(solution)/shard_map/reduce_scatter | solution.py:296
  1568.9 176.0 %reduce-scatter.39.cloned.1.call-start = ((), (), s32[]{:S(2)}) async-start(), calls=%async_computation.38 | async-start | bytes 7077888 | tf_op jit(solution)/shard_map/reduce_scatter | solution.py:299
  1579.8 230.7 %reduce-scatter.41.cloned.1.call-start = ((), (), s32[]{:S(2)}) async-start(), calls=%async_computation.39 | async-start | bytes 7077888 | tf_op jit(solution)/shard_map/reduce_scatter | solution.py:305
  1590.9 266.5 %reduce-scatter.31.cloned.1.call-start = ((), (), s32[]{:S(2)}) async-start(), calls=%async_computation.34 | async-start | bytes 2949120 | tf_op jit(solution)/shard_map/reduce_scatter | solution.py:290
  1598.4 305.9 %reduce-scatter.35.cloned.1.call-start = ((), (), s32[]{:S(2)}) async-start(), calls=%async_computation.36 | async-start | bytes 2949120 | tf_op jit(solution)/shard_map/reduce_scatter | solution.py:302
  1605.5 345.6 %reduce-scatter.33.cloned.1.call-start = ((), (), s32[]{:S(2)}) async-start(), calls=%async_computation.35 | async-start | bytes 2949120 | tf_op jit(solution)/shard_map/reduce_scatter | solution.py:293
  1631.3 7.3 collective-permute-start.15
  1633.1 8.2 collective-permute-start.11
  1644.6 360.8 %reduce-scatter.25.cloned.1.call-start = ((), (), s32[]{:S(2)}) async-start(), calls=%async_computation.30 | async-start | bytes 3276800 | tf_op jit(solution)/shard_map/reduce_scatter | solution.py:125
  1651.5 408.1 %reduce-scatter.29.cloned.1.call-start = ((), (), s32[]{:S(2)}) async-start(), calls=%async_computation.33 | async-start | bytes 3276800 | tf_op jit(solution)/shard_map/reduce_scatter | solution.py:125
  1658.4 455.3 %reduce-scatter.17.cloned.1.call-start = ((), (), s32[]{:S(2)}) async-start(), calls=%async_computation.23 | async-start | bytes 3276800 | tf_op jit(solution)/shard_map/reduce_scatter | solution.py:117
  1859.2 201.5 %copy-start.8 = (bf16[2,1,80,2048]{3,2,1,0:T(8,128)(2,1)S(1)}, bf16[2,1,80,2048]{3,2,1,0:T(8,128)(2,1)}, u32[]{:S(2)}) copy-start(bf16[2,1,80,2048]{3,2,1,0:T(8,128)(2,1)} %param.19) | copy-start | bytes 1966084
  1859.2 201.5 %copy-start.105 = (f32[2048]{0:T(1024)S(1)}, f32[2048]{0:T(1024)}, u32[]{:S(2)}) copy-start(f32[2048]{0:T(1024)} %param.21) | copy-start | bytes 24580
  1859.2 201.5 %copy-start.211 = (f32[80]{0:T(128)S(1)}, f32[80]{0:T(128)}, u32[]{:S(2)}) copy-start(f32[80]{0:T(128)} %copy-done.210) | copy-start | bytes 964
  1859.2 201.5 %copy-start.213 = (f32[80]{0:T(128)S(1)}, f32[80]{0:T(128)}, u32[]{:S(2)}) copy-start(f32[80]{0:T(128)} %copy-done.212) | copy-start | bytes 964
  1906.2 156.2 %copy-start.216 = (f32[80]{0:T(128)S(1)}, f32[80]{0:T(128)}, u32[]{:S(2)}) copy-start(f32[80]{0:T(128)} %copy-done.215) | copy-start | bytes 964
  1906.2 156.2 %copy-start.218 = (f32[80]{0:T(128)S(1)}, f32[80]{0:T(128)}, u32[]{:S(2)}) copy-start(f32[80]{0:T(128)} %copy-done.217) | copy-start | bytes 964
  1906.2 156.2 %copy-start.11 = (f32[1,80,2048]{2,1,0:T(8,128)S(1)}, f32[1,80,2048]{2,1,0:T(8,128)}, u32[]{:S(2)}) copy-start(f32[1,80,2048]{2,1,0:T(8,128)} %get-tuple-element.128) | copy-start | bytes 1966084
  1906.2 156.2 %copy-start.32 = (bf16[2,1,80,2048]{3,2,1,0:T(8,128)(2,1)S(1)}, bf16[2,1,80,2048]{3,2,1,0:T(8,128)(2,1)}, u32[]{:S(2)}) copy-start(bf16[2,1,80,2048]{3,2,1,0:T(8,128)(2,1)} %param.36) | copy-start | bytes 1966084
  1906.2 156.2 %copy-start.209 = (f32[80]{0:T(128)S(1)}, f32[80]{0:T(128)}, u32[]{:S(2)}) copy-start(f32[80]{0:T(128)} %copy-done.208) | copy-start | bytes 964
  1906.2 156.2 %copy-start.222 = (f32[80]{0:T(128)S(1)}, f32[80]{0:T(128)}, u32[]{:S(2)}) copy-start(f32[80]{0:T(128)} %copy-done.221) | copy-start | bytes 964
  (206 other events, 2934.6 us)
Sparse Core Ops, SparseCore 0:
  11.5 35.3 all-gather.16
  48.8 29.0 all-gather.18
  80.1 32.6 all-gather.32
  114.6 29.0 all-gather.20
  145.4 30.4 all-gather.22
  410.0 51.1 reduce-scatter.14
  478.3 52.4 reduce-scatter.18
  532.7 45.1 all-gather.26
  580.1 32.6 all-gather.24
  614.5 44.5 all-gather.28
  661.2 32.6 all-gather.40
  695.7 45.6 all-gather.30
  760.1 52.1 reduce-scatter.22
  817.0 32.3 all-gather.34
  851.3 31.6 all-gather.42
  904.3 51.0 reduce-scatter.26
  957.6 51.7 reduce-scatter.20
  1012.6 32.3 all-gather.36
  1070.1 32.3 all-gather.38
  1557.1 57.4 all-reduce.156
  1618.3 61.1 reduce-scatter.36
  1683.0 61.9 reduce-scatter.38
  1748.7 61.7 reduce-scatter.40
  1813.6 43.6 reduce-scatter.30
  1860.7 43.6 reduce-scatter.34
  1907.5 43.6 reduce-scatter.32
  1953.3 52.0 reduce-scatter.24
  2007.7 51.7 reduce-scatter.28
  2061.9 51.7 reduce-scatter.16
where the time goes:
time: 2200 us; the launch traced here: 2160 us
  waiting for transfers between devices  967 us (44%)
  local copies, waits for them, and re-layouts  614 us (28%)
  other arithmetic  256 us (12%)
  matrix products  200 us (9%)
  blocking collectives  68.4 us (3%)
  starting transfers between devices  40.2 us (2%)
    slice x234, local copies, waits for them, and re-layouts, local_scan(): return lax.associative_scan(combine, (coeffs, offsets), axis=1)  388 us
    reduce_scatter x4, waiting for transfers between devices, narrow_grads(): lax.psum_scatter(partial_vals, 'tensor', scatter_dimension=1, tiled=True)  201 us
    reduce_scatter x4, waiting for transfers between devices, narrow_rows(): lax.psum_scatter(partial_vals, 'tensor', scatter_dimension=1, tiled=True)  151 us
    pad x112, local copies, waits for them, and re-layouts, local_scan(): return lax.associative_scan(combine, (coeffs, offsets), axis=1)  149 us
    all_gather x4, waiting for transfers between devices, widen_rows(): return lax.all_gather(values, 'tensor', axis=1, tiled=True)  127 us
    mul x56, other arithmetic, combine(): return (earlier[0] * following[0], following[0] * earlier[1] + following[1])  76.4 us
    reduce_scatter x1, waiting for transfers between devices, per_device(): lax.psum_scatter(totals[14].astype(jnp.bfloat16), ('fsdp', 'context'), sc...  63.1 us
    dot_general x12, matrix products, project(): jnp.einsum('sla,ab->slb', rows_in, weight, preferred_element_type=jnp.flo...  62.1 us
  transfers between devices with their start and end apart: 45, of which 30 were waited for; matrix products, arithmetic and copies ran while one was open for 36% of the time, Pallas kernels for 0%

commit v1 on v0

v1 whole, which is shorter than its diff:
```python
from functools import partial

import jax
import jax.numpy as jnp
from jax import lax
from jax.experimental import pallas as pl
from jax.experimental.pallas import tpu as pltpu
from jax.sharding import PartitionSpec as P

CONV = 4
CPOW = 8
EPS = 1e-06
TILE = 8
F32 = jnp.float32
BF16 = jnp.bfloat16
GELU_A = 0.7978845608028654
GELU_B = 0.044715


def shift(value, axis, by):
    size = lax.axis_size(axis)
    return lax.ppermute(value, axis, [(i, (i + by) % size) for i in range(size)])


def step_by(value, axis, by):
    size = lax.axis_size(axis)
    return lax.ppermute(value, axis, [(i, i + by) for i in range(size) if 0 <= i + by < size])


def widen(block):
    size = lax.axis_size("tensor")
    return jnp.concatenate([block] + [shift(block, "tensor", k) for k in range(1, size)], axis=0)


def narrow(partial_low):
    size = lax.axis_size("tensor")
    rows = partial_low.shape[0] // size
    total = partial_low[:rows].astype(F32)
    for k in range(1, size):
        total = total + shift(partial_low[k * rows : (k + 1) * rows], "tensor", -k).astype(F32)
    return total


def sum_over(value, axis):
    size = lax.axis_size(axis)
    parts = [value] + [shift(value, axis, k) for k in range(1, size)]
    total = parts[0].astype(F32)
    for part in parts[1:]:
        total = total + part.astype(F32)
    return total


def matmul(left, right):
    return jnp.dot(left, right, preferred_element_type=F32)


def matmul_nt(left, right):
    return lax.dot_general(left, right, (((1,), (1,)), ((), ())), preferred_element_type=F32)


def matmul_tn(left, right):
    return lax.dot_general(left, right, (((0,), (0,)), ((), ())), preferred_element_type=F32)


def gelu_parts(v):
    th = jnp.tanh(GELU_A * (v + GELU_B * (v * v * v)))
    half = 0.5 * (1.0 + th)
    slope = half + 0.5 * v * (1.0 - th * th) * (GELU_A * (1.0 + 3.0 * GELU_B * (v * v)))
    return v * half, slope


def neg_expm1(z):
    series = 1.0 + z * (1.0 / 10.0)
    for n in (9.0, 8.0, 7.0, 6.0, 5.0, 4.0, 3.0, 2.0):
        series = 1.0 + z * (1.0 / n) * series
    return jnp.where(z > -0.5, -z * series, 1.0 - jnp.exp(z))


def sigmoid(v):
    return 1.0 / (1.0 + jnp.exp(-v))


def tile_scan(coeffs, offsets, reverse):
    rows, width = coeffs.shape
    a = coeffs.reshape(rows // TILE, TILE, width)
    b = offsets.reshape(rows // TILE, TILE, width)
    place = lax.broadcasted_iota(jnp.int32, a.shape, 1)
    for s in (1, 2, 4):
        if reverse:
            inside, turn = place < TILE - s, TILE - s
        else:
            inside, turn = place >= s, s
        a_far = pltpu.roll(a, turn, 1)
        b_far = pltpu.roll(b, turn, 1)
        b = jnp.where(inside, b + a * b_far, b)
        a = jnp.where(inside, a * a_far, a)
    return a, b


def forward_kernel(
    pos_ref, inner_ref, halo_ref, mask_ref, par_ref, wg_ref,
    conv_ref, pre_ref, decay_ref, prod_ref, state_ref, last_ref, ext, run,
):
    rows = inner_ref.shape[0]
    step = pl.program_id(0)

    @pl.when(step == 0)
    def _():
        ext[0:TILE] = halo_ref[...].astype(F32)
        run[0:1] = jnp.ones_like(run[0:1])
        run[1:2] = jnp.zeros_like(run[1:2])

    inner = inner_ref[...].astype(BF16).astype(F32)
    ext[TILE : TILE + rows] = inner
    mask = mask_ref[...]
    conv = par_ref[CONV : CONV + 1] + par_ref[0:1] * inner
    for k in range(1, CONV):
        conv = conv + par_ref[k : k + 1] * ext[TILE - k : TILE - k + rows] * mask[:, k - 1 : k]
    ext[0:TILE] = inner[rows - TILE :]
    conv_low = conv.astype(BF16)
    conv_ref[...] = conv_low
    pre = jnp.dot(conv_low, wg_ref[...], preferred_element_type=F32)
    width = inner.shape[1]
    rate_pre = pre[:, :width] + par_ref[CONV + 2 : CONV + 3]
    input_pre = pre[:, width:] + par_ref[CONV + 3 : CONV + 4]
    pre_ref[:, :width] = rate_pre
    pre_ref[:, width:] = input_pre
    log_rate = par_ref[CONV + 1 : CONV + 2] * sigmoid(rate_pre)
    starts = mask[:, CONV - 1 : CONV] > 0.5
    decays = jnp.where(starts, 0.0, jnp.exp(log_rate))
    scale = jnp.where(starts, 1.0, jnp.sqrt(neg_expm1(2.0 * log_rate)))
    drives = scale * sigmoid(input_pre) * conv_low.astype(F32)
    decay_ref[...] = decays
    a, b = tile_scan(decays, drives, False)
    prod, state = run[0:1], run[1:2]
    for i in range(rows // TILE):
        prods = a[i] * prod
        states = b[i] + a[i] * state
        prod_ref[i * TILE : (i + 1) * TILE] = prods
        state_ref[i * TILE : (i + 1) * TILE] = states
        prod, state = prods[TILE - 1 :], states[TILE - 1 :]
    run[0:1] = prod
    run[1:2] = state
    last_ref[0:1] = prod
    last_ref[1:2] = state


def reverse_kernel(
    pos_ref, mixed_ref, branch_ref, states_ref, decay_ref,
    low_ref, prod_ref, grad_ref, first_ref, ext, run,
):
    rows = mixed_ref.shape[0]
    step = pl.program_id(0)

    @pl.when(step == 0)
    def _():
        ext[rows : rows + TILE] = jnp.ones_like(ext[rows : rows + TILE])
        run[0:1] = jnp.ones_like(run[0:1])
        run[1:2] = jnp.zeros_like(run[1:2])

    mixed = mixed_ref[...]
    value, slope = gelu_parts(branch_ref[...])
    low_ref[...] = (mixed * states_ref[...] * slope).astype(BF16)
    decays = decay_ref[...]
    ext[0:rows] = decays
    following = ext[1 : rows + 1]
    ext[rows : rows + TILE] = decays[0:TILE]
    a, b = tile_scan(following, mixed * value, True)
    prod, grad = run[0:1], run[1:2]
    for i in reversed(range(rows // TILE)):
        prods = a[i] * prod
        grads = b[i] + a[i] * grad
        prod_ref[i * TILE : (i + 1) * TILE] = prods
        grad_ref[i * TILE : (i + 1) * TILE] = grads
        prod, grad = prods[0:1], grads[0:1]
    run[0:1] = prod
    run[1:2] = grad
    first_ref[0:1] = decays[0:1] * prod
    first_ref[1:2] = decays[0:1] * grad


def gates_kernel(
    pos_ref, prod_ref, grad_ref, in_ref, prev_ref, state_in_ref, states_ref, decay_ref, pre_ref, conv_ref,
    inner_ref, inner_prev_ref, halo_ref, mask_ref, par_ref, wg_ref,
    low_ref, inner_grad_ref, edge_ref, sums_ref, ext, later,
):
    rows, width = prod_ref.shape
    step = pl.program_id(0)
    at_start = step == pl.num_programs(0) - 1

    @pl.when(step == 0)
    def _():
        sums_ref[...] = jnp.zeros_like(sums_ref)
        later[...] = jnp.zeros_like(later)

    mask = mask_ref[...]
    starts = mask[:, CONV - 1 : CONV] > 0.5
    drive_grad = grad_ref[...] + prod_ref[...] * in_ref[...]
    ext[TILE : TILE + rows] = states_ref[...]
    ext[TILE - 1 : TILE] = jnp.where(at_start, state_in_ref[...], prev_ref[TILE - 1 : TILE])
    prev_states = ext[TILE - 1 : TILE - 1 + rows]
    rate = sigmoid(pre_ref[:, :width])
    gate = sigmoid(pre_ref[:, width:])
    conv = conv_ref[...].astype(F32)
    slope = par_ref[CONV + 1 : CONV + 2]
    log_rate = slope * rate
    decays = decay_ref[...]
    raw = jnp.sqrt(neg_expm1(2.0 * log_rate))
    scale = jnp.where(starts, 1.0, raw)
    scale_grad = drive_grad * gate * conv
    log_grad = jnp.where(
        starts, 0.0, drive_grad * prev_states * decays - scale_grad * (decays * decays) / raw
    )
    rate_low = (log_grad * slope * rate * (1.0 - rate)).astype(BF16)
    input_low = (drive_grad * scale * conv * gate * (1.0 - gate)).astype(BF16)
    low_ref[:, :width] = rate_low
    low_ref[:, width:] = input_low
    both = jnp.concatenate([rate_low, input_low], axis=1)
    conv_grad = drive_grad * scale * gate + lax.dot_general(
        both, wg_ref[...], (((1,), (1,)), ((), ())), preferred_element_type=F32
    )
    inner = inner_ref[...].astype(BF16).astype(F32)
    before = jnp.where(at_start, halo_ref[...].astype(F32), inner_prev_ref[...].astype(BF16).astype(F32))
    ext[0:TILE] = before
    ext[TILE : TILE + rows] = inner

    def total(values):
        return jnp.sum(values, axis=0, keepdims=True)

    sums_ref[0:1] += total(conv_grad * inner)
    sums_ref[CONV : CONV + 1] += total(conv_grad)
    sums_ref[CONV + 1 : CONV + 2] += total(log_grad * rate)
    sums_ref[CONV + 2 : CONV + 3] += total(rate_low.astype(F32))
    sums_ref[CONV + 3 : CONV + 4] += total(input_low.astype(F32))
    inner_grad = par_ref[0:1] * conv_grad
    heads = []
    for k in range(1, CONV):
        masked = conv_grad * mask[:, k - 1 : k]
        sums_ref[k : k + 1] += total(masked * ext[TILE - k : TILE - k + rows])
        heads.append(masked[0:TILE] * par_ref[k : k + 1])
    for k in range(1, CONV):
        masked = par_ref[k : k + 1] * (conv_grad * mask[:, k - 1 : k])
        ext[0:rows] = masked
        ext[rows : rows + TILE] = later[k - 1]
        inner_grad = inner_grad + ext[k : k + rows]
        later[k - 1] = heads[k - 1]
    inner_grad_ref[...] = inner_grad.astype(inner_grad_ref.dtype)

    @pl.when(at_start)
    def _():
        edge_ref[...] = jnp.zeros_like(edge_ref)
        for back in range(1, CONV):
            row = heads[back - 1][0:1]
            for k in range(back + 1, CONV):
                row = row + heads[k - 1][k - back : k - back + 1]
            edge_ref[TILE - back : TILE - back + 1] = row


def rows_spec(rows, width, parts, column=0, reverse=False):
    def where(step, pos):
        place = parts - 1 - step if reverse else step
        return (lax.rem(pos[0] - place + parts, parts), column)

    return pl.BlockSpec((rows, width), where)


def ordered_spec(rows, width, parts, reverse=False):
    return pl.BlockSpec((rows, width), lambda step, pos: ((parts - 1 - step if reverse else step), 0))


def before_spec(rows, width, parts, column=0):
    tiles = rows // TILE

    def where(step, pos):
        place = jnp.maximum(parts - 2 - step, 0)
        return (lax.rem(pos[0] - place + parts, parts) * tiles + tiles - 1, column)

    return pl.BlockSpec((TILE, width), where)


def whole_spec(shape):
    return pl.BlockSpec(shape, lambda step, pos: (0,) * len(shape))


def call(kernel, parts, in_specs, out_specs, out_shape, scratch, flops, moved):
    return pl.pallas_call(
        kernel,
        out_shape=out_shape,
        grid_spec=pltpu.PrefetchScalarGridSpec(
            num_scalar_prefetch=1, grid=(parts,), in_specs=in_specs, out_specs=out_specs, scratch_shapes=scratch
        ),
        cost_estimate=pl.CostEstimate(flops=flops, bytes_accessed=moved, transcendentals=flops // 100),
    )


def forward_scan(pos, both_pre, halo, mask, params, gate_w, parts):
    total, width = both_pre.shape[0], params.shape[1]
    rows = total // parts
    spec = partial(rows_spec, rows, width, parts)
    shape = jax.ShapeDtypeStruct
    return call(
        forward_kernel, parts,
        [spec(column=1), whole_spec(halo.shape), ordered_spec(rows, mask.shape[1], parts),
         whole_spec(params.shape), whole_spec(gate_w.shape)],
        [spec(), rows_spec(rows, 2 * width, parts), spec(), spec(), spec(), whole_spec((2, width))],
        [shape((total, width), BF16), shape((total, 2 * width), F32), shape((total, width), F32),
         shape((total, width), F32), shape((total, width), F32), shape((2, width), F32)],
        [pltpu.VMEM((rows + TILE, width), F32), pltpu.VMEM((TILE, width), F32)],
        4 * total * width * width + 400 * total * width, 30 * total * width + 4 * width * width,
    )(pos, both_pre, halo, mask, params, gate_w)


def reverse_scan(pos, mixed_grad, both_pre, states, decays, parts):
    total, width = states.shape
    rows = total // parts
    spec = rows_spec(rows, width, parts, reverse=True)
    shape = jax.ShapeDtypeStruct
    return call(
        reverse_kernel, parts,
        [spec, spec, spec, spec],
        [spec, spec, spec, whole_spec((2, width))],
        [shape((total, width), BF16), shape((total, width), F32), shape((total, width), F32),
         shape((2, width), F32)],
        [pltpu.VMEM((rows + TILE, width), F32), pltpu.VMEM((TILE, width), F32)],
        400 * total * width, 26 * total * width,
    )(pos, mixed_grad, both_pre, states, decays)


def gates_back(pos, prods, grads, grad_in, states, state_in, decays, pre, conv_low, both_pre, halo, mask,
               params, gate_w, parts):
    total, width = states.shape
    rows = total // parts
    spec = partial(rows_spec, rows, width, parts, reverse=True)
    shape = jax.ShapeDtypeStruct
    return call(
        gates_kernel, parts,
        [spec(), spec(), whole_spec((1, width)), before_spec(rows, width, parts), whole_spec((1, width)),
         spec(), spec(), rows_spec(rows, 2 * width, parts, reverse=True), spec(), spec(column=1),
         before_spec(rows, width, parts, column=1), whole_spec(halo.shape),
         ordered_spec(rows, mask.shape[1], parts, reverse=True), whole_spec(params.shape),
         whole_spec(gate_w.shape)],
        [rows_spec(rows, 2 * width, parts, reverse=True), spec(), whole_spec((TILE, width)),
         whole_spec((TILE, width))],
        [shape((total, 2 * width), BF16), shape((total, width), F32), shape((TILE, width), F32),
         shape((TILE, width), F32)],
        [pltpu.VMEM((rows + TILE, width), F32), pltpu.VMEM((CONV - 1, TILE, width), F32)],
        4 * total * width * width + 800 * total * width, 40 * total * width + 4 * width * width,
    )(pos, prods, grads, grad_in, states, state_in, states, decays, pre, conv_low, both_pre, both_pre, halo, mask,
      params, gate_w)


def carry_over(ends, direction):
    size = lax.axis_size("context")
    incoming = jnp.zeros_like(ends[1:2])
    parts = [step_by(ends, "context", direction * k) for k in range(1, size)]
    for part in reversed(parts):
        incoming = part[1:2] + part[0:1] * incoming
    return incoming


def block_diagonal(weight):
    count, rows, cols = weight.shape
    return jnp.concatenate(
        [jnp.pad(weight[i], ((0, 0), (i * cols, (count - 1 - i) * cols))) for i in range(count)], axis=0
    )


def diagonal_blocks(dense, count):
    rows, cols = dense.shape[0] // count, dense.shape[1] // count
    return jnp.stack([dense[i * rows : (i + 1) * rows, i * cols : (i + 1) * cols] for i in range(count)])


def per_device(
    inputs, segments, norm_gain, branch_weight, inner_weight, conv_weight, conv_bias, rate_weight, rate_bias,
    input_weight, input_bias, decay_param, out_weight, mlp_gain, gate_weight, up_weight, down_weight, cotangent,
):
    micro, seqs, rows, model = inputs.shape
    parts = lax.axis_size("tensor")
    span = rows * parts
    width = conv_bias.shape[0]
    blocks = rate_weight.shape[0]
    units = gate_weight.shape[1]
    chains = [(m, s) for m in range(micro) for s in range(seqs)]
    context_pos = lax.axis_index("context")
    tensor_pos = lax.axis_index("tensor")
    pos = tensor_pos.reshape(1).astype(jnp.int32)
    owners = ("fsdp", "context")

    both_w = lax.all_gather(jnp.concatenate([branch_weight, inner_weight], 1), owners, axis=0, tiled=True)
    out_w = lax.all_gather(out_weight, owners, axis=1, tiled=True)
    pair_w = lax.all_gather(jnp.concatenate([gate_weight, up_weight], 1), owners, axis=0, tiled=True)
    down_w = lax.all_gather(down_weight, owners, axis=1, tiled=True)
    gate_w = jnp.concatenate([block_diagonal(rate_weight), block_diagonal(input_weight)], axis=1)
    slope = -CPOW * jax.nn.softplus(-decay_param)
    params = jnp.concatenate(
        [conv_weight, conv_bias[None], slope[None], rate_bias[None], input_bias[None]], axis=0
    )

    def unit_rows(values):
        return values * lax.rsqrt(jnp.mean(values * values, axis=-1, keepdims=True) + EPS)

    def norm_back(values, grad, gain):
        inv = lax.rsqrt(jnp.mean(values * values, axis=-1, keepdims=True) + EPS)
        unit = values * inv
        scaled = grad * gain
        return inv * (scaled - unit * jnp.mean(scaled * unit, axis=-1, keepdims=True)), jnp.sum(grad * unit, axis=0)

    def masks_of(row):
        pad = jnp.concatenate([jnp.full((CONV - 1,), -1, jnp.int32), row])
        ext = lax.dynamic_slice_in_dim(pad, context_pos * span, span + CONV - 1)
        own = ext[CONV - 1 :]
        cols = [(ext[CONV - 1 - k : CONV - 1 - k + span] == own).astype(F32) for k in range(1, CONV)]
        return jnp.stack(cols + [1.0 - cols[0]], axis=1)

    last_block = lax.rem(tensor_pos + 1, parts)
    tail_row = last_block * rows + rows - TILE

    saved = []
    for m, s in chains:
        x_rows = inputs[m, s].astype(F32)
        mask = masks_of(segments[m, s])
        wide_one = widen((unit_rows(x_rows) * norm_gain).astype(BF16))
        wide_cot = widen(cotangent[m, s])
        both_pre = matmul(wide_one, both_w)
        tail = lax.dynamic_slice(both_pre, (tail_row, width), (TILE, width)).astype(BF16)
        halo = step_by(tail, "context", 1)
        conv_low, pre, decays, prods, locals_, ends = forward_scan(
            pos, both_pre, halo, mask, params, gate_w, parts
        )
        state_in = carry_over(ends, 1)
        states = locals_ + prods * state_in
        mixed_low = (states * jax.nn.gelu(both_pre[:, :width])).astype(BF16)
        residual = x_rows + narrow(matmul(mixed_low, out_w).astype(BF16))
        wide_two = widen((unit_rows(residual) * mlp_gain).astype(BF16))
        pair_pre = matmul(wide_two, pair_w)
        gate_val, gate_slope = gelu_parts(pair_pre[:, :units])
        up_pre = pair_pre[:, units:]
        hidden_low = (gate_val * up_pre).astype(BF16)
        block_out = (residual + narrow(matmul(hidden_low, down_w).astype(BF16))).astype(BF16)
        hidden_grad = matmul_nt(wide_cot, down_w)
        pair_low = jnp.concatenate(
            [(hidden_grad * up_pre * gate_slope).astype(BF16), (hidden_grad * gate_val).astype(BF16)], axis=1
        )
        two_grad = narrow(matmul_nt(pair_low, pair_w).astype(BF16)).astype(BF16).astype(F32)
        norm_term, gain_two = norm_back(residual, two_grad, mlp_gain)
        resid_grad = cotangent[m, s].astype(F32) + norm_term
        wide_resid = widen(resid_grad.astype(BF16))
        mixed_grad = matmul_nt(wide_resid, out_w)
        branch_low, rev_prods, rev_grads, firsts = reverse_scan(pos, mixed_grad, both_pre, states, decays, parts)
        grad_in = carry_over(firsts, -1)
        gates_low, inner_grad, edge, sums = gates_back(
            pos, rev_prods, rev_grads, grad_in, states, state_in, decays, pre, conv_low, both_pre, halo, mask,
            params, gate_w, parts,
        )
        edge_in = step_by(edge, "context", -1)
        tail_grad = lax.dynamic_slice(inner_grad, (tail_row, 0), (TILE, width)) + edge_in
        inner_low = lax.dynamic_update_slice(inner_grad, tail_grad, (tail_row, 0)).astype(BF16)
        both_low = jnp.concatenate([branch_low, inner_low], axis=1)
        one_part = matmul_nt(both_low, both_w).astype(BF16)
        gain_one = jnp.sum(one_part.astype(F32) * wide_one.astype(F32), axis=0)
        one_grad = narrow(one_part).astype(BF16).astype(F32)
        norm_term_one, _ = norm_back(x_rows, one_grad, norm_gain)
        saved.append(
            dict(
                block_out=block_out, input_grad=resid_grad + norm_term_one, one=wide_one, both=both_low,
                mixed=mixed_low, resid=wide_resid, two=wide_two, pair=pair_low, hidden=hidden_low, cot=wide_cot,
                conv=conv_low, gates=gates_low, sums=sums, gain_one=gain_one, gain_two=gain_two,
            )
        )

    def joined(name):
        return jnp.concatenate([item[name] for item in saved], axis=0)

    def added(name):
        total = saved[0][name]
        for item in saved[1:]:
            total = total + item[name]
        return total

    def stacked(name):
        return jnp.stack([item[name] for item in saved]).reshape(micro, seqs, rows, model)

    def share(term, dim):
        return lax.psum_scatter(term.astype(BF16), owners, scatter_dimension=dim, tiled=True).astype(F32)

    down_grad = share(matmul_tn(joined("hidden"), joined("cot")), 1)
    pair_grad = share(matmul_tn(joined("two"), joined("pair")), 0)
    out_grad = share(matmul_tn(joined("mixed"), joined("resid")), 1)
    both_grad = share(matmul_tn(joined("one"), joined("both")), 0)
    gates_term = matmul_tn(joined("conv"), joined("gates"))
    gate_blocks = jnp.concatenate(
        [diagonal_blocks(gates_term[:, :width], blocks), diagonal_blocks(gates_term[:, width:], blocks)], axis=0
    )
    gate_blocks = sum_over(sum_over(gate_blocks.astype(BF16), "fsdp").astype(BF16), "context")
    sums = sum_over(sum_over(added("sums"), "fsdp"), "context")
    gains = jnp.stack([added("gain_one") / norm_gain, added("gain_two")])
    gains = sum_over(sum_over(sum_over(gains, "fsdp"), "context"), "tensor")
    return (
        stacked("block_out"),
        stacked("input_grad"),
        gains[0],
        both_grad[:, :width],
        both_grad[:, width:],
        sums[:CONV],
        sums[CONV],
        gate_blocks[:blocks],
        sums[CONV + 2],
        gate_blocks[blocks:],
        sums[CONV + 3],
        sums[CONV + 1] * (CPOW * jax.nn.sigmoid(-decay_param)),
        out_grad,
        gains[1],
        pair_grad[:, :units],
        pair_grad[:, units:],
        down_grad,
    )


def solution(mesh):
    tokens = P(None, "fsdp", ("context", "tensor"), None)
    by_rows = P(("fsdp", "context"), "tensor")
    by_cols = P("tensor", ("fsdp", "context"))
    channel = P("tensor")
    taps = P(None, "tensor")
    blocks = P("tensor", None, None)
    return jax.shard_map(
        per_device,
        mesh=mesh,
        in_specs=(
            tokens, P(None, "fsdp", None), P(), by_rows, by_rows, taps, channel, blocks, channel, blocks, channel,
            channel, by_cols, P(), by_rows, by_rows, by_cols, tokens,
        ),
        out_specs=(
            tokens, tokens, P(), by_rows, by_rows, taps, channel, blocks, channel, blocks, channel, channel,
            by_cols, P(), by_rows, by_rows, by_cols,
        ),
        check_vma=False,
    )
```

time: 2200 us -> 773 us (0.35); the launches traced: 2160 us -> 763 us
  waiting for transfers between devices: 967 us -> 325 us
  local copies, waits for them, and re-layouts: 614 us -> 49.1 us
  other arithmetic: 256 us -> 39.5 us
  starting transfers between devices: 40.2 us -> 168 us
  matrix products: 200 us -> 125 us
  blocking collectives: 68.4 us -> 0 us
  Pallas kernels: 0 us -> 40.6 us
    reduce_scatter x14 -> x4, waiting for transfers between devices: 590 us -> 18.8 us  [share(): lax.psum_scatter(term.astype(BF16), owners, scatter_dimension=dim, tiled=...]
    slice x240 -> x15, local copies, waits for them, and re-layouts: 391 us -> 9.24 us  [the longest x1 3.44 us: per_device(): pair_grad[:, units:]]
    all_gather x14 -> x4, waiting for transfers between devices: 359 us -> 0.46 us  [the longest x1 0.44 us: per_device(): lax.all_gather(jnp.concatenate([branch_weight, inner_weight], 1), owners,...]
    ppermute x16 -> x79, waiting for transfers between devices: 14.1 us -> 305 us  [the longest x63 291 us: shift(): lax.ppermute(value, axis, [(i, (i + by) % size) for i in range(size)])]
    pad x112 -> x0, local copies, waits for them, and re-layouts: 149 us -> none  [local_scan(): return lax.associative_scan(combine, (coeffs, offsets), axis=1)]
    ppermute x16 -> x79, starting transfers between devices: 37.4 us -> 168 us  [the longest x63 140 us: shift(): lax.ppermute(value, axis, [(i, (i + by) % size) for i in range(size)])]
    mul x62 -> x2, other arithmetic: 79.6 us -> 0.62 us  [the longest x1 0.61 us: per_device(): sums[CONV + 1] * (CPOW * jax.nn.sigmoid(-decay_param))]
    dot_general x48 -> x21, matrix products: 200 us -> 125 us  [the longest x8 43.3 us: matmul_nt(): lax.dot_general(left, right, (((1,), (1,)), ((), ())), preferred_element_...]
  transfers between devices with their start and end apart: 45 -> 87, of which waited for: 30 -> 36; matrix products, arithmetic and copies ran while one was open for 36% -> 25% of each run, Pallas kernels for 0% -> 5%
where the time goes in v1:
time: 773 us; the launch traced here: 763 us
  waiting for transfers between devices  325 us (42%)
  starting transfers between devices  168 us (22%)
  matrix products  125 us (16%)
  local copies, waits for them, and re-layouts  49.1 us (6%)
  Pallas kernels  40.6 us (5%)
  other arithmetic  39.5 us (5%)
  between operations  16.3 us (2%)
    ppermute x63, waiting for transfers between devices, shift(): lax.ppermute(value, axis, [(i, (i + by) % size) for i in range(size)])  291 us
    ppermute x63, starting transfers between devices, shift(): lax.ppermute(value, axis, [(i, (i + by) % size) for i in range(size)])  140 us
    dot_general x8, matrix products, matmul_nt(): lax.dot_general(left, right, (((1,), (1,)), ((), ())), preferred_element_...  43.3 us
    dot_general x8, matrix products, matmul(): return jnp.dot(left, right, preferred_element_type=F32)  41.5 us
    dot_general x5, matrix products, matmul_tn(): lax.dot_general(left, right, (((0,), (0,)), ((), ())), preferred_element_...  40 us
    unnamed x195, local copies, waits for them, and re-layouts  31.3 us
    ppermute x16, starting transfers between devices, step_by(): lax.ppermute(value, axis, [(i, i + by) for i in range(size) if 0 <= i + b...  28 us
    reduce_scatter x4, waiting for transfers between devices, share(): lax.psum_scatter(term.astype(BF16), owners, scatter_dimension=dim, tiled=...  18.8 us
  transfers between devices with their start and end apart: 87, of which 36 were waited for; matrix products, arithmetic and copies ran while one was open for 25% of the time, Pallas kernels for 5%

profile of v1, /device:TPU:0, one launch (start us, length us, event | category | flops | bytes accessed | tf_op | source)
XLA Modules:
  0.0 763.3 jit_solution(9683623279300713830)
XLA Ops:
  12.8 5.0 collective-permute-start.2
  20.5 8.4 %fusion.62.wg_ref = bf16[640,1280]{1,0:T(8,128)(2,1)} fusion(bf16[160,160]{1,0:T(8,128)(2,1)S(1)} %get-tuple-element.222, bf16[160,160]{1,0:T(8,128)(2,1)S(1)} %get-tuple-element.223, bf16[160,160]{1,0:T(8,128)(2,1)S(1)} %get-tuple-element.221, bf16[160,160]{1,0:T(8,128)(2,1)S(1)} %get-tuple-element.220, bf16[160,160]{1,0:T(8,128)(2,1)S(1)} %get-tuple-element.239, ...), kind=kLoop, calls=%fused_computation.95 | loop fusion | flops 40960000 | bytes 2048000 | tf_op jit(solution)/shard_map/concatenate | solution.py:393
  30.4 9.5 %collective-permute-done = bf16[80,2048]{1,0:T(8,128)(2,1)S(1)} collective-permute-done((bf16[80,2048]{1,0:T(8,128)(2,1)S(1)}, bf16[80,2048]{1,0:T(8,128)(2,1)S(1)}, u32[]{:S(2)}, u32[]{:S(2)}) %collective-permute-start) | collective-permute-done | bytes 327712 | tf_op jit(solution)/shard_map/ppermute | solution.py:22
  40.7 5.1 collective-permute-done.1
  48.3 3.6 collective-permute-start.17
  54.4 4.7 fusion.194.inner_ref.branch_ref.inner_prev_ref
  59.1 3.4 collective-permute-start.3
  62.5 17.8 %collective-permute-done.17 = bf16[80,2048]{1,0:T(8,128)(2,1)} collective-permute-done((bf16[80,2048]{1,0:T(8,128)(2,1)S(1)}, bf16[80,2048]{1,0:T(8,128)(2,1)}, u32[]{:S(2)}, u32[]{:S(2)}) %collective-permute-start.17) | collective-permute-done | bytes 327712 | tf_op jit(solution)/shard_map/ppermute | solution.py:22
  84.5 3.4 collective-permute-start.19
  88.5 7.0 shard_map.305
  102.3 7.0 shard_map.306
  117.3 3.2 convolution_convert_fusion.10
  120.8 3.9 collective-permute-start.7
  133.2 22.2 %collective-permute-done.8 = bf16[80,2048]{1,0:T(8,128)(2,1)S(1)} collective-permute-done((bf16[80,2048]{1,0:T(8,128)(2,1)S(1)}, bf16[80,2048]{1,0:T(8,128)(2,1)S(1)}, u32[]{:S(2)}, u32[]{:S(2)}) %collective-permute-start.8) | collective-permute-done | bytes 327712 | tf_op jit(solution)/shard_map/ppermute | solution.py:22
  155.4 17.0 %collective-permute-done.24 = bf16[80,2048]{1,0:T(8,128)(2,1)S(1)} collective-permute-done((bf16[80,2048]{1,0:T(8,128)(2,1)S(1)}, bf16[80,2048]{1,0:T(8,128)(2,1)S(1)}, u32[]{:S(2)}, u32[]{:S(2)}) %collective-permute-start.24) | collective-permute-done | bytes 327712 | tf_op jit(solution)/shard_map/ppermute | solution.py:22
  173.9 6.6 collective-permute-start.10
  185.0 3.8 collective-permute-done.10
  191.9 17.9 %collective-permute-done.12 = bf16[80,2048]{1,0:T(8,128)(2,1)S(1)} collective-permute-done((bf16[80,2048]{1,0:T(8,128)(2,1)S(1)}, bf16[80,2048]{1,0:T(8,128)(2,1)S(1)}, u32[]{:S(2)}, u32[]{:S(2)}) %collective-permute-start.12) | collective-permute-done | bytes 327712 | tf_op jit(solution)/shard_map/ppermute | solution.py:22
  209.8 4.3 collective-permute-start.50
  214.1 21.4 %collective-permute-done.11 = bf16[80,2048]{1,0:T(8,128)(2,1)S(1)} collective-permute-done((bf16[80,2048]{1,0:T(8,128)(2,1)S(1)}, bf16[80,2048]{1,0:T(8,128)(2,1)S(1)}, u32[]{:S(2)}, u32[]{:S(2)}) %collective-permute-start.11) | collective-permute-done | bytes 327712 | tf_op jit(solution)/shard_map/ppermute | solution.py:22
  236.2 11.1 %fusion.81 = f32[320,3072]{1,0:T(8,128)} fusion(bf16[2048,3072]{1,0:T(8,128)(2,1)} %all-gather.9.cloned.1.call-done, bf16[80,2048]{1,0:T(8,128)(2,1)} %copy-done.41, bf16[80,2048]{1,0:T(8,128)(2,1)} %copy-done.43, bf16[80,2048]{1,0:T(8,128)(2,1)} %copy-done.45, bf16[80,2048]{1,0:T(8,128)(2,1)} %copy-done.46), kind=kOutput, calls=%fused_computation.116 | convolution fusion | flops 4031774720 | bytes 17825792 | tf_op jit(solution)/shard_map/dot_general | solution.py:54
  247.4 8.6 %fusion.38 = (bf16[320,1536]{1,0:T(8,128)(2,1)S(1)}, bf16[320,1536]{1,0:T(8,128)(2,1)S(1)}, bf16[320,1536]{1,0:T(8,128)(2,1)}) fusion(f32[320,3072]{1,0:T(8,128)} %fusion.81, bf16[1536,2048]{1,0:T(8,128)(2,1)} %all-gather.11.cloned.1.call-done, bf16[80,2048]{1,0:T(8,128)(2,1)} %collective-permute-done.34, bf16[80,2048]{1,0:T(8,128)(2,1)} %collective-permute-done.33, ...), kind=kOutput, calls=%fused_computation.65 | convolution fusion | flops 2030305280 | bytes 14483456 | tf_op jit(solution)/shard_map/dot_general | solution.py:58
  257.2 7.6 convolution_convert_fusion.12
  264.9 12.8 %collective-permute-start.37 = (bf16[80,2048]{1,0:T(8,128)(2,1)S(1)}, bf16[80,2048]{1,0:T(8,128)(2,1)S(1)}, u32[]{:S(2)}, u32[]{:S(2)}) collective-permute-start(bf16[80,2048]{1,0:T(8,128)(2,1)S(1)} %get-tuple-element.190), channel_id=1, source_target_pairs={{0,1},{1,2},{2,3},{3,0},{4,5},{5,6},{6,7},{7,4},{8,9},{9,10},{10,1... | collective-permute-start | bytes 983048 | tf_op jit(solution)/shard_map/ppermute | solution.py:22
  282.9 10.3 %collective-permute-done.36 = bf16[80,2048]{1,0:T(8,128)(2,1)S(1)} collective-permute-done((bf16[80,2048]{1,0:T(8,128)(2,1)S(1)}, bf16[80,2048]{1,0:T(8,128)(2,1)S(1)}, u32[]{:S(2)}, u32[]{:S(2)}) %collective-permute-start.36) | collective-permute-done | bytes 327712 | tf_op jit(solution)/shard_map/ppermute | solution.py:22
  294.6 7.0 collective-permute-start.28
  305.2 4.6 collective-permute-done.28
  309.8 20.0 %collective-permute-start.48 = (bf16[80,2048]{1,0:T(8,128)(2,1)S(1)}, bf16[80,2048]{1,0:T(8,128)(2,1)S(1)}, u32[]{:S(2)}, u32[]{:S(2)}) collective-permute-start(bf16[80,2048]{1,0:T(8,128)(2,1)S(1)} %get-tuple-element.212), channel_id=1, source_target_pairs={{0,1},{1,2},{2,3},{3,0},{4,5},{5,6},{6,7},{7,4},{8,9},{9,10},{10,1... | collective-permute-start | bytes 983048 | tf_op jit(solution)/shard_map/ppermute | solution.py:22
  329.8 10.0 %collective-permute-done.27 = bf16[80,2048]{1,0:T(8,128)(2,1)S(1)} collective-permute-done((bf16[80,2048]{1,0:T(8,128)(2,1)S(1)}, bf16[80,2048]{1,0:T(8,128)(2,1)S(1)}, u32[]{:S(2)}, u32[]{:S(2)}) %collective-permute-start.27) | collective-permute-done | bytes 327712 | tf_op jit(solution)/shard_map/ppermute | solution.py:22
  339.9 7.5 fusion.89
  349.3 5.6 fusion.48
  356.2 7.5 convolution_convert_fusion.11
  370.4 8.5 %collective-permute-done.39 = bf16[80,2048]{1,0:T(8,128)(2,1)S(1)} collective-permute-done((bf16[80,2048]{1,0:T(8,128)(2,1)S(1)}, bf16[80,2048]{1,0:T(8,128)(2,1)S(1)}, u32[]{:S(2)}, u32[]{:S(2)}) %collective-permute-start.39) | collective-permute-done | bytes 327712 | tf_op jit(solution)/shard_map/ppermute | solution.py:22
  380.5 5.0 collective-permute-done.52
  388.5 4.5 collective-permute-start.54
  392.9 3.4 collective-permute-start.55
  396.3 8.1 %collective-permute-done.54 = bf16[80,2048]{1,0:T(8,128)(2,1)S(1)} collective-permute-done((bf16[80,2048]{1,0:T(8,128)(2,1)S(1)}, bf16[80,2048]{1,0:T(8,128)(2,1)S(1)}, u32[]{:S(2)}, u32[]{:S(2)}) %collective-permute-start.54) | collective-permute-done | bytes 327712 | tf_op jit(solution)/shard_map/ppermute | solution.py:22
  405.9 6.8 collective-permute-done.55
  415.7 5.5 convolution_convert_fusion.3
  424.9 4.3 fusion.105.mixed_ref
  429.1 4.9 shard_map.307
  439.7 4.7 collective-permute-done.42
  450.8 4.7 fusion.121.mixed_ref
  455.6 4.9 shard_map.309
  464.4 8.4 %shard_map.308 = (bf16[320,1280]{1,0:T(8,128)(2,1)}, f32[320,640]{1,0:T(8,128)}, f32[8,640]{1,0:T(8,128)}, f32[8,640]{1,0:T(8,128)}) custom-call(s32[1]{0:T(128)} %bitcast.1.pos_ref, f32[320,640]{1,0:T(8,128)} %get-tuple-element.53.prod_ref, f32[320,640]{1,0:T(8,128)} %get-tuple-element.54.grad_ref, f32[1,640]{1,0:T(1,128)} %fusion.203.in_ref, ...), custom_call_target="tpu_custom_call" | custom-call | flops 688128000 | bytes 9830400 | tf_op jit(solution)/shard_map/pallas_call | solution.py:335
  474.7 8.4 %shard_map.310 = (bf16[320,1280]{1,0:T(8,128)(2,1)}, f32[320,640]{1,0:T(8,128)}, f32[8,640]{1,0:T(8,128)}, f32[8,640]{1,0:T(8,128)}) custom-call(s32[1]{0:T(128)} %bitcast.1.pos_ref, f32[320,640]{1,0:T(8,128)} %get-tuple-element.62.prod_ref, f32[320,640]{1,0:T(8,128)} %get-tuple-element.63.grad_ref, f32[1,640]{1,0:T(1,128)} %fusion.199.in_ref, ...), custom_call_target="tpu_custom_call" | custom-call | flops 688128000 | bytes 9830400 | tf_op jit(solution)/shard_map/pallas_call | solution.py:335
  492.9 8.6 %convolution_convert_fusion.2 = bf16[2048,1280]{1,0:T(8,128)(2,1)} fusion(bf16[640,2048]{1,0:T(8,128)(2,1)} %constant_dynamic-update-slice_fusion, bf16[320,640]{1,0:T(8,128)(2,1)S(1)} %convert_element_type.370, bf16[320,640]{1,0:T(8,128)(2,1)} %get-tuple-element.61, bf16[320,640]{1,0:T(8,128)(2,1)S(1)} %convert_element_type.351, ...), kind=kOutput, calls=%fused_computation.2 | convolution fusion | flops 3364618240 | bytes 9502720 | tf_op jit(solution)/shard_map/dot_general | solution.py:62
  506.8 8.9 %convolution_convert_fusion.1 = bf16[1536,2048]{1,0:T(8,128)(2,1)} fusion(bf16[640,2048]{1,0:T(8,128)(2,1)} %constant_dynamic-update-slice_fusion.32, bf16[320,1536]{1,0:T(8,128)(2,1)} %get-tuple-element.174, bf16[320,1536]{1,0:T(8,128)(2,1)} %get-tuple-element.175), kind=kOutput, calls=%fused_computation.1 | convolution fusion | flops 4033609728 | bytes 10878976 | tf_op jit(solution)/shard_map/dot_general | solution.py:62
  521.3 15.5 %convolution_convert_fusion = bf16[2048,3072]{1,0:T(8,128)(2,1)} fusion(bf16[640,2048]{1,0:T(8,128)(2,1)} %constant_dynamic-update-slice_fusion.24, bf16[320,1536]{1,0:T(8,128)(2,1)} %copy-done.79, bf16[320,1536]{1,0:T(8,128)(2,1)} %copy-done.78, bf16[320,1536]{1,0:T(8,128)(2,1)} %copy-done.77, bf16[320,1536]{1,0:T(8,128)(2,1)} %copy-done.76), kind=kOutput, calls=%fused_computation | convolution fusion | flops 8075083776 | bytes 19136512 | tf_op jit(solution)/shard_map/dot_general | solution.py:62
  536.8 5.4 convolution_convert_fusion.6
  542.4 5.2 convolution_convert_fusion.5
  549.9 6.0 collective-permute-start.47
  558.9 4.1 collective-permute-start.74
  585.2 4.1 collective-permute-start.62
  592.0 9.9 %collective-permute-done.45 = bf16[80,2048]{1,0:T(8,128)(2,1)S(1)} collective-permute-done((bf16[80,2048]{1,0:T(8,128)(2,1)S(1)}, bf16[80,2048]{1,0:T(8,128)(2,1)S(1)}, u32[]{:S(2)}, u32[]{:S(2)}) %collective-permute-start.45) | collective-permute-done | bytes 327712 | tf_op jit(solution)/shard_map/ppermute | solution.py:22
  601.9 4.5 collective-permute-start.14
  607.9 34.9 %collective-permute-done.62 = bf16[80,2048]{1,0:T(8,128)(2,1)S(1)} collective-permute-done((bf16[80,2048]{1,0:T(8,128)(2,1)S(1)}, bf16[80,2048]{1,0:T(8,128)(2,1)S(1)}, u32[]{:S(2)}, u32[]{:S(2)}) %collective-permute-start.62) | collective-permute-done | bytes 327712 | tf_op jit(solution)/shard_map/ppermute | solution.py:22
  643.5 8.0 %collective-permute-start.13 = (bf16[80,2048]{1,0:T(8,128)(2,1)S(1)}, bf16[80,2048]{1,0:T(8,128)(2,1)S(1)}, u32[]{:S(2)}, u32[]{:S(2)}) collective-permute-start(bf16[80,2048]{1,0:T(8,128)(2,1)S(1)} %get-tuple-element.192), channel_id=1, source_target_pairs={{0,3},{1,0},{2,1},{3,2},{4,7},{5,4},{6,5},{7,6},{8,11},{9,8},{10,9... | collective-permute-start | bytes 983048 | tf_op jit(solution)/shard_map/ppermute | solution.py:22
  651.6 12.4 %collective-permute-done.30 = bf16[80,2048]{1,0:T(8,128)(2,1)S(1)} collective-permute-done((bf16[80,2048]{1,0:T(8,128)(2,1)S(1)}, bf16[80,2048]{1,0:T(8,128)(2,1)S(1)}, u32[]{:S(2)}, u32[]{:S(2)}) %collective-permute-start.30) | collective-permute-done | bytes 327712 | tf_op jit(solution)/shard_map/ppermute | solution.py:22
  665.9 8.4 %collective-permute-done.13 = bf16[80,2048]{1,0:T(8,128)(2,1)S(1)} collective-permute-done((bf16[80,2048]{1,0:T(8,128)(2,1)S(1)}, bf16[80,2048]{1,0:T(8,128)(2,1)S(1)}, u32[]{:S(2)}, u32[]{:S(2)}) %collective-permute-start.13) | collective-permute-done | bytes 327712 | tf_op jit(solution)/shard_map/ppermute | solution.py:22
  680.6 26.3 %collective-permute-done.78 = bf16[8,160,160]{2,1,0:T(8,128)(2,1)S(1)} collective-permute-done((bf16[8,160,160]{2,1,0:T(8,128)(2,1)S(1)}, bf16[8,160,160]{2,1,0:T(8,128)(2,1)S(1)}, u32[]{:S(2)}, u32[]{:S(2)}) %collective-permute-start.78) | collective-permute-done | bytes 409632 | tf_op jit(solution)/shard_map/ppermute | solution.py:22
  706.9 18.7 %collective-permute-done.76 = bf16[8,160,160]{2,1,0:T(8,128)(2,1)S(1)} collective-permute-done((bf16[8,160,160]{2,1,0:T(8,128)(2,1)S(1)}, bf16[8,160,160]{2,1,0:T(8,128)(2,1)S(1)}, u32[]{:S(2)}, u32[]{:S(2)}) %collective-permute-start.76) | collective-permute-done | bytes 409632 | tf_op jit(solution)/shard_map/ppermute | solution.py:22
  733.7 18.8 %reduce-scatter.9.cloned.1.call-done = bf16[256,3072]{1,0:T(8,128)(2,1)} async-done(((bf16[2048,3072]{1,0:T(8,128)(2,1)}), bf16[256,3072]{1,0:T(8,128)(2,1)}) %reduce-scatter.9.cloned.1.call-update) | async-done | bytes 1572880 | tf_op jit(solution)/shard_map/reduce_scatter | solution.py:484
  752.5 3.4 fusion.248
  (438 shorter events, 174.0 us)
Async XLA Ops:
  7.2 47.1 %all-gather.5.cloned.1.call-start = ((), (), s32[]{:S(2)}) async-start(), calls=%async_computation.4 | async-start | bytes 5898240 | tf_op jit(solution)/shard_map/all_gather | solution.py:389
  9.4 107.9 %all-gather.7.cloned.1.call-start = ((), (), s32[]{:S(2)}) async-start(), calls=%async_computation.5 | async-start | bytes 2949120 | tf_op jit(solution)/shard_map/all_gather | solution.py:390
  10.1 226.1 %all-gather.9.cloned.1.call-start = ((), (), s32[]{:S(2)}) async-start(), calls=%async_computation.6 | async-start | bytes 14155776 | tf_op jit(solution)/shard_map/all_gather | solution.py:391
  11.6 235.8 %all-gather.11.cloned.1.call-start = ((), (), s32[]{:S(2)}) async-start(), calls=%async_computation.7 | async-start | bytes 7077888 | tf_op jit(solution)/shard_map/all_gather | solution.py:392
  12.8 33.8 %collective-permute-start.2 = (bf16[80,2048]{1,0:T(8,128)(2,1)S(1)}, bf16[80,2048]{1,0:T(8,128)(2,1)S(1)}, u32[]{:S(2)}, u32[]{:S(2)}) collective-permute-start(bf16[80,2048]{1,0:T(8,128)(2,1)S(1)} %get-tuple-element.149), channel_id=1, source_target_pairs={{0,3},{1,0},{2,1},{3,2},{4,7},{5,4},{6,5},{7,6},{8,11},{9,8},{10,9... | collective-permute-start | bytes 983048 | tf_op jit(solution)/shard_map/ppermute | solution.py:22
  17.9 27.9 %collective-permute-start.1 = (bf16[80,2048]{1,0:T(8,128)(2,1)S(1)}, bf16[80,2048]{1,0:T(8,128)(2,1)S(1)}, u32[]{:S(2)}, u32[]{:S(2)}) collective-permute-start(bf16[80,2048]{1,0:T(8,128)(2,1)S(1)} %get-tuple-element.149), channel_id=1, source_target_pairs={{0,2},{1,3},{2,0},{3,1},{4,6},{5,7},{6,4},{7,5},{8,10},{9,11},{10,... | collective-permute-start | bytes 983048 | tf_op jit(solution)/shard_map/ppermute | solution.py:22
  17.9 22.0 %collective-permute-start = (bf16[80,2048]{1,0:T(8,128)(2,1)S(1)}, bf16[80,2048]{1,0:T(8,128)(2,1)S(1)}, u32[]{:S(2)}, u32[]{:S(2)}) collective-permute-start(bf16[80,2048]{1,0:T(8,128)(2,1)S(1)} %get-tuple-element.149), channel_id=1, source_target_pairs={{0,1},{1,2},{2,3},{3,0},{4,5},{5,6},{6,7},{7,4},{8,9},{9,10},{10,1... | collective-permute-start | bytes 983048 | tf_op jit(solution)/shard_map/ppermute | solution.py:22
  18.9 708.1 %reduce-scatter.7.cloned.1.call-start = ((), (), s32[]{:S(2)}) async-start(), calls=%async_computation.9 | async-start | bytes 2949120 | tf_op jit(solution)/shard_map/reduce_scatter | solution.py:484
  48.3 14.2 %collective-permute-start.18 = (bf16[80,2048]{1,0:T(8,128)(2,1)S(1)}, bf16[80,2048]{1,0:T(8,128)(2,1)}, u32[]{:S(2)}, u32[]{:S(2)}) collective-permute-start(bf16[80,2048]{1,0:T(8,128)(2,1)S(1)} %get-tuple-element.147), channel_id=1, source_target_pairs={{0,3},{1,0},{2,1},{3,2},{4,7},{5,4},{6,5},{7,6},{8,11},{9,8},{10,9... | collective-permute-start | bytes 983048 | tf_op jit(solution)/shard_map/ppermute | solution.py:22
  48.3 32.0 %collective-permute-start.17 = (bf16[80,2048]{1,0:T(8,128)(2,1)S(1)}, bf16[80,2048]{1,0:T(8,128)(2,1)}, u32[]{:S(2)}, u32[]{:S(2)}) collective-permute-start(bf16[80,2048]{1,0:T(8,128)(2,1)S(1)} %get-tuple-element.147), channel_id=1, source_target_pairs={{0,2},{1,3},{2,0},{3,1},{4,6},{5,7},{6,4},{7,5},{8,10},{9,11},{10,... | collective-permute-start | bytes 983048 | tf_op jit(solution)/shard_map/ppermute | solution.py:22
  51.9 28.4 %collective-permute-start.16 = (bf16[80,2048]{1,0:T(8,128)(2,1)S(1)}, bf16[80,2048]{1,0:T(8,128)(2,1)}, u32[]{:S(2)}, u32[]{:S(2)}) collective-permute-start(bf16[80,2048]{1,0:T(8,128)(2,1)S(1)} %get-tuple-element.147), channel_id=1, source_target_pairs={{0,1},{1,2},{2,3},{3,0},{4,5},{5,6},{6,7},{7,4},{8,9},{9,10},{10,1... | collective-permute-start | bytes 983048 | tf_op jit(solution)/shard_map/ppermute | solution.py:22
  59.1 28.8 %collective-permute-start.3 = (bf16[8,640]{1,0:T(8,128)(2,1)S(1)}, bf16[8,640]{1,0:T(8,128)(2,1)S(1)}, u32[]{:S(2)}, u32[]{:S(2)}) collective-permute-start(bf16[8,640]{1,0:T(8,128)(2,1)S(1)} %dynamic-slice_convert_fusion.1), channel_id=1, source_target_pairs={{0,4},{4,8},{8,12},{1,5},{5,9},{9,13},{2,6},{6,10},{10,14},{3,7},{... | collective-permute-start | bytes 30728 | tf_op jit(solution)/shard_map/ppermute | solution.py:27
  84.5 17.2 %collective-permute-start.19 = (bf16[8,640]{1,0:T(8,128)(2,1)S(1)}, bf16[8,640]{1,0:T(8,128)(2,1)S(1)}, u32[]{:S(2)}, u32[]{:S(2)}) collective-permute-start(bf16[8,640]{1,0:T(8,128)(2,1)S(1)} %dynamic-slice_convert_fusion), channel_id=1, source_target_pairs={{0,4},{4,8},{8,12},{1,5},{5,9},{9,13},{2,6},{6,10},{10,14},{3,7},{... | collective-permute-start | bytes 30728 | tf_op jit(solution)/shard_map/ppermute | solution.py:27
  95.5 16.4 %collective-permute-start.6 = (f32[2,640]{1,0:T(2,128)}, f32[2,640]{1,0:T(2,128)S(1)}, u32[]{:S(2)}, u32[]{:S(2)}) collective-permute-start(f32[2,640]{1,0:T(2,128)} %get-tuple-element.47), channel_id=1, source_target_pairs={{0,12},{1,13},{2,14},{3,15},{16,28},{17,29},{18,30},{19,31}} | collective-permute-start | bytes 15368 | tf_op jit(solution)/shard_map/ppermute | solution.py:27
  97.9 16.3 %collective-permute-start.5 = (f32[2,640]{1,0:T(2,128)}, f32[2,640]{1,0:T(2,128)S(1)}, u32[]{:S(2)}, u32[]{:S(2)}) collective-permute-start(f32[2,640]{1,0:T(2,128)} %get-tuple-element.47), channel_id=1, source_target_pairs={{0,8},{4,12},{1,9},{5,13},{2,10},{6,14},{3,11},{7,15},{16,24},{20,... | collective-permute-start | bytes 15368 | tf_op jit(solution)/shard_map/ppermute | solution.py:27
  99.9 14.3 %collective-permute-start.4 = (f32[2,640]{1,0:T(2,128)}, f32[2,640]{1,0:T(2,128)S(1)}, u32[]{:S(2)}, u32[]{:S(2)}) collective-permute-start(f32[2,640]{1,0:T(2,128)} %get-tuple-element.47), channel_id=1, source_target_pairs={{0,4},{4,8},{8,12},{1,5},{5,9},{9,13},{2,6},{6,10},{10,14},{3,7},{... | collective-permute-start | bytes 15368 | tf_op jit(solution)/shard_map/ppermute | solution.py:27
  110.6 14.1 %collective-permute-start.21 = (f32[2,640]{1,0:T(2,128)}, f32[2,640]{1,0:T(2,128)S(1)}, u32[]{:S(2)}, u32[]{:S(2)}) collective-permute-start(f32[2,640]{1,0:T(2,128)} %get-tuple-element.50), channel_id=1, source_target_pairs={{0,8},{4,12},{1,9},{5,13},{2,10},{6,14},{3,11},{7,15},{16,24},{20,... | collective-permute-start | bytes 15368 | tf_op jit(solution)/shard_map/ppermute | solution.py:27
  120.7 34.7 %collective-permute-start.8 = (bf16[80,2048]{1,0:T(8,128)(2,1)S(1)}, bf16[80,2048]{1,0:T(8,128)(2,1)S(1)}, u32[]{:S(2)}, u32[]{:S(2)}) collective-permute-start(bf16[80,2048]{1,0:T(8,128)(2,1)S(1)} %get-tuple-element.200), channel_id=1, source_target_pairs={{0,2},{1,3},{2,0},{3,1},{4,6},{5,7},{6,4},{7,5},{8,10},{9,11},{10,... | collective-permute-start | bytes 983048 | tf_op jit(solution)/shard_map/ppermute | solution.py:22
  120.8 34.6 %collective-permute-start.7 = (bf16[80,2048]{1,0:T(8,128)(2,1)S(1)}, bf16[80,2048]{1,0:T(8,128)(2,1)S(1)}, u32[]{:S(2)}, u32[]{:S(2)}) collective-permute-start(bf16[80,2048]{1,0:T(8,128)(2,1)S(1)} %get-tuple-element.198), channel_id=1, source_target_pairs={{0,3},{1,0},{2,1},{3,2},{4,7},{5,4},{6,5},{7,6},{8,11},{9,8},{10,9... | collective-permute-start | bytes 983048 | tf_op jit(solution)/shard_map/ppermute | solution.py:22
  127.9 27.5 %collective-permute-start.25 = (bf16[80,2048]{1,0:T(8,128)(2,1)S(1)}, bf16[80,2048]{1,0:T(8,128)(2,1)S(1)}, u32[]{:S(2)}, u32[]{:S(2)}) collective-permute-start(bf16[80,2048]{1,0:T(8,128)(2,1)S(1)} %get-tuple-element.202), channel_id=1, source_target_pairs={{0,1},{1,2},{2,3},{3,0},{4,5},{5,6},{6,7},{7,4},{8,9},{9,10},{10,1... | collective-permute-start | bytes 983048 | tf_op jit(solution)/shard_map/ppermute | solution.py:22
  128.6 43.8 %collective-permute-start.24 = (bf16[80,2048]{1,0:T(8,128)(2,1)S(1)}, bf16[80,2048]{1,0:T(8,128)(2,1)S(1)}, u32[]{:S(2)}, u32[]{:S(2)}) collective-permute-start(bf16[80,2048]{1,0:T(8,128)(2,1)S(1)} %get-tuple-element.203), channel_id=1, source_target_pairs={{0,2},{1,3},{2,0},{3,1},{4,6},{5,7},{6,4},{7,5},{8,10},{9,11},{10,... | collective-permute-start | bytes 983048 | tf_op jit(solution)/shard_map/ppermute | solution.py:22
  133.2 39.2 %collective-permute-start.23 = (bf16[80,2048]{1,0:T(8,128)(2,1)S(1)}, bf16[80,2048]{1,0:T(8,128)(2,1)S(1)}, u32[]{:S(2)}, u32[]{:S(2)}) collective-permute-start(bf16[80,2048]{1,0:T(8,128)(2,1)S(1)} %get-tuple-element.201), channel_id=1, source_target_pairs={{0,3},{1,0},{2,1},{3,2},{4,7},{5,4},{6,5},{7,6},{8,11},{9,8},{10,9... | collective-permute-start | bytes 983048 | tf_op jit(solution)/shard_map/ppermute | solution.py:22
  173.9 14.9 %collective-permute-start.10 = (bf16[80,2048]{1,0:T(8,128)(2,1)S(1)}, bf16[80,2048]{1,0:T(8,128)(2,1)S(1)}, u32[]{:S(2)}, u32[]{:S(2)}) collective-permute-start(bf16[80,2048]{1,0:T(8,128)(2,1)S(1)} %get-tuple-element.141), channel_id=1, source_target_pairs={{0,1},{1,2},{2,3},{3,0},{4,5},{5,6},{6,7},{7,4},{8,9},{9,10},{10,1... | collective-permute-start | bytes 983048 | tf_op jit(solution)/shard_map/ppermute | solution.py:22
  180.5 66.8 %collective-permute-start.34 = (bf16[80,2048]{1,0:T(8,128)(2,1)S(1)}, bf16[80,2048]{1,0:T(8,128)(2,1)}, u32[]{:S(2)}, u32[]{:S(2)}) collective-permute-start(bf16[80,2048]{1,0:T(8,128)(2,1)S(1)} %get-tuple-element.213), channel_id=1, source_target_pairs={{0,3},{1,0},{2,1},{3,2},{4,7},{5,4},{6,5},{7,6},{8,11},{9,8},{10,9... | collective-permute-start | bytes 983048 | tf_op jit(solution)/shard_map/ppermute | solution.py:22
  180.6 66.8 %collective-permute-start.33 = (bf16[80,2048]{1,0:T(8,128)(2,1)S(1)}, bf16[80,2048]{1,0:T(8,128)(2,1)}, u32[]{:S(2)}, u32[]{:S(2)}) collective-permute-start(bf16[80,2048]{1,0:T(8,128)(2,1)S(1)} %get-tuple-element.213), channel_id=1, source_target_pairs={{0,2},{1,3},{2,0},{3,1},{4,6},{5,7},{6,4},{7,5},{8,10},{9,11},{10,... | collective-permute-start | bytes 983048 | tf_op jit(solution)/shard_map/ppermute | solution.py:22
  182.0 27.7 %collective-permute-start.12 = (bf16[80,2048]{1,0:T(8,128)(2,1)S(1)}, bf16[80,2048]{1,0:T(8,128)(2,1)S(1)}, u32[]{:S(2)}, u32[]{:S(2)}) collective-permute-start(bf16[80,2048]{1,0:T(8,128)(2,1)S(1)} %get-tuple-element.141), channel_id=1, source_target_pairs={{0,3},{1,0},{2,1},{3,2},{4,7},{5,4},{6,5},{7,6},{8,11},{9,8},{10,9... | collective-permute-start | bytes 983048 | tf_op jit(solution)/shard_map/ppermute | solution.py:22
  185.0 50.5 %collective-permute-start.11 = (bf16[80,2048]{1,0:T(8,128)(2,1)S(1)}, bf16[80,2048]{1,0:T(8,128)(2,1)S(1)}, u32[]{:S(2)}, u32[]{:S(2)}) collective-permute-start(bf16[80,2048]{1,0:T(8,128)(2,1)S(1)} %get-tuple-element.141), channel_id=1, source_target_pairs={{0,2},{1,3},{2,0},{3,1},{4,6},{5,7},{6,4},{7,5},{8,10},{9,11},{10,... | collective-permute-start | bytes 983048 | tf_op jit(solution)/shard_map/ppermute | solution.py:22
  188.8 58.5 %collective-permute-start.32 = (bf16[80,2048]{1,0:T(8,128)(2,1)S(1)}, bf16[80,2048]{1,0:T(8,128)(2,1)}, u32[]{:S(2)}, u32[]{:S(2)}) collective-permute-start(bf16[80,2048]{1,0:T(8,128)(2,1)S(1)} %get-tuple-element.213), channel_id=1, source_target_pairs={{0,1},{1,2},{2,3},{3,0},{4,5},{5,6},{6,7},{7,4},{8,9},{9,10},{10,1... | collective-permute-start | bytes 983048 | tf_op jit(solution)/shard_map/ppermute | solution.py:22
  209.8 137.7 %collective-permute-start.50 = (bf16[80,2048]{1,0:T(8,128)(2,1)S(1)}, bf16[80,2048]{1,0:T(8,128)(2,1)}, u32[]{:S(2)}, u32[]{:S(2)}) collective-permute-start(bf16[80,2048]{1,0:T(8,128)(2,1)S(1)} %get-tuple-element.212), channel_id=1, source_target_pairs={{0,3},{1,0},{2,1},{3,2},{4,7},{5,4},{6,5},{7,6},{8,11},{9,8},{10,9... | collective-permute-start | bytes 983048 | tf_op jit(solution)/shard_map/ppermute | solution.py:22
  236.2 113.1 %collective-permute-start.49 = (bf16[80,2048]{1,0:T(8,128)(2,1)S(1)}, bf16[80,2048]{1,0:T(8,128)(2,1)}, u32[]{:S(2)}, u32[]{:S(2)}) collective-permute-start(bf16[80,2048]{1,0:T(8,128)(2,1)S(1)} %get-tuple-element.212), channel_id=1, source_target_pairs={{0,2},{1,3},{2,0},{3,1},{4,6},{5,7},{6,4},{7,5},{8,10},{9,11},{10,... | collective-permute-start | bytes 983048 | tf_op jit(solution)/shard_map/ppermute | solution.py:22
  264.9 18.0 %collective-permute-start.37 = (bf16[80,2048]{1,0:T(8,128)(2,1)S(1)}, bf16[80,2048]{1,0:T(8,128)(2,1)S(1)}, u32[]{:S(2)}, u32[]{:S(2)}) collective-permute-start(bf16[80,2048]{1,0:T(8,128)(2,1)S(1)} %get-tuple-element.190), channel_id=1, source_target_pairs={{0,1},{1,2},{2,3},{3,0},{4,5},{5,6},{6,7},{7,4},{8,9},{9,10},{10,1... | collective-permute-start | bytes 983048 | tf_op jit(solution)/shard_map/ppermute | solution.py:22
  277.7 15.4 %collective-permute-start.36 = (bf16[80,2048]{1,0:T(8,128)(2,1)S(1)}, bf16[80,2048]{1,0:T(8,128)(2,1)S(1)}, u32[]{:S(2)}, u32[]{:S(2)}) collective-permute-start(bf16[80,2048]{1,0:T(8,128)(2,1)S(1)} %get-tuple-element.191), channel_id=1, source_target_pairs={{0,2},{1,3},{2,0},{3,1},{4,6},{5,7},{6,4},{7,5},{8,10},{9,11},{10,... | collective-permute-start | bytes 983048 | tf_op jit(solution)/shard_map/ppermute | solution.py:22
  277.7 15.4 %collective-permute-start.35 = (bf16[80,2048]{1,0:T(8,128)(2,1)S(1)}, bf16[80,2048]{1,0:T(8,128)(2,1)S(1)}, u32[]{:S(2)}, u32[]{:S(2)}) collective-permute-start(bf16[80,2048]{1,0:T(8,128)(2,1)S(1)} %get-tuple-element.189), channel_id=1, source_target_pairs={{0,3},{1,0},{2,1},{3,2},{4,7},{5,4},{6,5},{7,6},{8,11},{9,8},{10,9... | collective-permute-start | bytes 983048 | tf_op jit(solution)/shard_map/ppermute | solution.py:22
  294.6 15.1 %collective-permute-start.28 = (bf16[80,2048]{1,0:T(8,128)(2,1)S(1)}, bf16[80,2048]{1,0:T(8,128)(2,1)S(1)}, u32[]{:S(2)}, u32[]{:S(2)}) collective-permute-start(bf16[80,2048]{1,0:T(8,128)(2,1)S(1)} %get-tuple-element.227), channel_id=1, source_target_pairs={{0,3},{1,0},{2,1},{3,2},{4,7},{5,4},{6,5},{7,6},{8,11},{9,8},{10,9... | collective-permute-start | bytes 983048 | tf_op jit(solution)/shard_map/ppermute | solution.py:22
  301.6 38.2 %collective-permute-start.27 = (bf16[80,2048]{1,0:T(8,128)(2,1)S(1)}, bf16[80,2048]{1,0:T(8,128)(2,1)S(1)}, u32[]{:S(2)}, u32[]{:S(2)}) collective-permute-start(bf16[80,2048]{1,0:T(8,128)(2,1)S(1)} %get-tuple-element.227), channel_id=1, source_target_pairs={{0,2},{1,3},{2,0},{3,1},{4,6},{5,7},{6,4},{7,5},{8,10},{9,11},{10,... | collective-permute-start | bytes 983048 | tf_op jit(solution)/shard_map/ppermute | solution.py:22
  301.6 38.2 %collective-permute-start.26 = (bf16[80,2048]{1,0:T(8,128)(2,1)S(1)}, bf16[80,2048]{1,0:T(8,128)(2,1)S(1)}, u32[]{:S(2)}, u32[]{:S(2)}) collective-permute-start(bf16[80,2048]{1,0:T(8,128)(2,1)S(1)} %get-tuple-element.227), channel_id=1, source_target_pairs={{0,1},{1,2},{2,3},{3,0},{4,5},{5,6},{6,7},{7,4},{8,9},{9,10},{10,1... | collective-permute-start | bytes 983048 | tf_op jit(solution)/shard_map/ppermute | solution.py:22
  309.8 39.5 %collective-permute-start.48 = (bf16[80,2048]{1,0:T(8,128)(2,1)S(1)}, bf16[80,2048]{1,0:T(8,128)(2,1)S(1)}, u32[]{:S(2)}, u32[]{:S(2)}) collective-permute-start(bf16[80,2048]{1,0:T(8,128)(2,1)S(1)} %get-tuple-element.212), channel_id=1, source_target_pairs={{0,1},{1,2},{2,3},{3,0},{4,5},{5,6},{6,7},{7,4},{8,9},{9,10},{10,1... | collective-permute-start | bytes 983048 | tf_op jit(solution)/shard_map/ppermute | solution.py:22
  339.8 39.9 %collective-permute-start.40 = (bf16[80,2048]{1,0:T(8,128)(2,1)S(1)}, bf16[80,2048]{1,0:T(8,128)(2,1)S(1)}, u32[]{:S(2)}, u32[]{:S(2)}) collective-permute-start(bf16[80,2048]{1,0:T(8,128)(2,1)S(1)} %get-tuple-element.145), channel_id=1, source_target_pairs={{0,3},{1,0},{2,1},{3,2},{4,7},{5,4},{6,5},{7,6},{8,11},{9,8},{10,9... | collective-permute-start | bytes 983048 | tf_op jit(solution)/shard_map/ppermute | solution.py:22
  339.8 39.1 %collective-permute-start.39 = (bf16[80,2048]{1,0:T(8,128)(2,1)S(1)}, bf16[80,2048]{1,0:T(8,128)(2,1)S(1)}, u32[]{:S(2)}, u32[]{:S(2)}) collective-permute-start(bf16[80,2048]{1,0:T(8,128)(2,1)S(1)} %get-tuple-element.145), channel_id=1, source_target_pairs={{0,2},{1,3},{2,0},{3,1},{4,6},{5,7},{6,4},{7,5},{8,10},{9,11},{10,... | collective-permute-start | bytes 983048 | tf_op jit(solution)/shard_map/ppermute | solution.py:22
  347.5 19.3 %collective-permute-start.38 = (bf16[80,2048]{1,0:T(8,128)(2,1)S(1)}, bf16[80,2048]{1,0:T(8,128)(2,1)S(1)}, u32[]{:S(2)}, u32[]{:S(2)}) collective-permute-start(bf16[80,2048]{1,0:T(8,128)(2,1)S(1)} %get-tuple-element.145), channel_id=1, source_target_pairs={{0,1},{1,2},{2,3},{3,0},{4,5},{5,6},{6,7},{7,4},{8,9},{9,10},{10,1... | collective-permute-start | bytes 983048 | tf_op jit(solution)/shard_map/ppermute | solution.py:22
  363.9 16.7 %collective-permute-start.53 = (bf16[80,2048]{1,0:T(8,128)(2,1)S(1)}, bf16[80,2048]{1,0:T(8,128)(2,1)S(1)}, u32[]{:S(2)}, u32[]{:S(2)}) collective-permute-start(bf16[80,2048]{1,0:T(8,128)(2,1)S(1)} %get-tuple-element.184), channel_id=1, source_target_pairs={{0,1},{1,2},{2,3},{3,0},{4,5},{5,6},{6,7},{7,4},{8,9},{9,10},{10,1... | collective-permute-start | bytes 983048 | tf_op jit(solution)/shard_map/ppermute | solution.py:22
  365.3 20.2 %collective-permute-start.52 = (bf16[80,2048]{1,0:T(8,128)(2,1)S(1)}, bf16[80,2048]{1,0:T(8,128)(2,1)S(1)}, u32[]{:S(2)}, u32[]{:S(2)}) collective-permute-start(bf16[80,2048]{1,0:T(8,128)(2,1)S(1)} %get-tuple-element.185), channel_id=1, source_target_pairs={{0,2},{1,3},{2,0},{3,1},{4,6},{5,7},{6,4},{7,5},{8,10},{9,11},{10,... | collective-permute-start | bytes 983048 | tf_op jit(solution)/shard_map/ppermute | solution.py:22
  366.8 20.2 %collective-permute-start.51 = (bf16[80,2048]{1,0:T(8,128)(2,1)S(1)}, bf16[80,2048]{1,0:T(8,128)(2,1)S(1)}, u32[]{:S(2)}, u32[]{:S(2)}) collective-permute-start(bf16[80,2048]{1,0:T(8,128)(2,1)S(1)} %get-tuple-element.183), channel_id=1, source_target_pairs={{0,3},{1,0},{2,1},{3,2},{4,7},{5,4},{6,5},{7,6},{8,11},{9,8},{10,9... | collective-permute-start | bytes 983048 | tf_op jit(solution)/shard_map/ppermute | solution.py:22
  388.5 16.0 %collective-permute-start.54 = (bf16[80,2048]{1,0:T(8,128)(2,1)S(1)}, bf16[80,2048]{1,0:T(8,128)(2,1)S(1)}, u32[]{:S(2)}, u32[]{:S(2)}) collective-permute-start(bf16[80,2048]{1,0:T(8,128)(2,1)S(1)} %get-tuple-element.143), channel_id=1, source_target_pairs={{0,1},{1,2},{2,3},{3,0},{4,5},{5,6},{6,7},{7,4},{8,9},{9,10},{10,1... | collective-permute-start | bytes 983048 | tf_op jit(solution)/shard_map/ppermute | solution.py:22
  392.9 19.8 %collective-permute-start.55 = (bf16[80,2048]{1,0:T(8,128)(2,1)S(1)}, bf16[80,2048]{1,0:T(8,128)(2,1)S(1)}, u32[]{:S(2)}, u32[]{:S(2)}) collective-permute-start(bf16[80,2048]{1,0:T(8,128)(2,1)S(1)} %get-tuple-element.143), channel_id=1, source_target_pairs={{0,2},{1,3},{2,0},{3,1},{4,6},{5,7},{6,4},{7,5},{8,10},{9,11},{10,... | collective-permute-start | bytes 983048 | tf_op jit(solution)/shard_map/ppermute | solution.py:22
  396.3 17.9 %collective-permute-start.56 = (bf16[80,2048]{1,0:T(8,128)(2,1)S(1)}, bf16[80,2048]{1,0:T(8,128)(2,1)S(1)}, u32[]{:S(2)}, u32[]{:S(2)}) collective-permute-start(bf16[80,2048]{1,0:T(8,128)(2,1)S(1)} %get-tuple-element.143), channel_id=1, source_target_pairs={{0,3},{1,0},{2,1},{3,2},{4,7},{5,4},{6,5},{7,6},{8,11},{9,8},{10,9... | collective-permute-start | bytes 983048 | tf_op jit(solution)/shard_map/ppermute | solution.py:22
  421.2 307.7 %reduce-scatter.5.cloned.1.call-start = ((), (), s32[]{:S(2)}) async-start(), calls=%async_computation.8 | async-start | bytes 5898240 | tf_op jit(solution)/shard_map/reduce_scatter | solution.py:484
  501.5 229.6 %reduce-scatter.11.cloned.1.call-start = ((), (), s32[]{:S(2)}) async-start(), calls=%async_computation.11 | async-start | bytes 7077888 | tf_op jit(solution)/shard_map/reduce_scatter | solution.py:484
  515.7 236.8 %reduce-scatter.9.cloned.1.call-start = ((), (), s32[]{:S(2)}) async-start(), calls=%async_computation.10 | async-start | bytes 14155776 | tf_op jit(solution)/shard_map/reduce_scatter | solution.py:484
  549.9 39.5 %collective-permute-start.47 = (bf16[80,2048]{1,0:T(8,128)(2,1)S(1)}, bf16[80,2048]{1,0:T(8,128)(2,1)S(1)}, u32[]{:S(2)}, u32[]{:S(2)}) collective-permute-start(bf16[80,2048]{1,0:T(8,128)(2,1)S(1)} %get-tuple-element.187), channel_id=1, source_target_pairs={{0,1},{1,2},{2,3},{3,0},{4,5},{5,6},{6,7},{7,4},{8,9},{9,10},{10,1... | collective-permute-start | bytes 983048 | tf_op jit(solution)/shard_map/ppermute | solution.py:22
  555.9 34.1 %collective-permute-start.46 = (bf16[80,2048]{1,0:T(8,128)(2,1)S(1)}, bf16[80,2048]{1,0:T(8,128)(2,1)S(1)}, u32[]{:S(2)}, u32[]{:S(2)}) collective-permute-start(bf16[80,2048]{1,0:T(8,128)(2,1)S(1)} %get-tuple-element.188), channel_id=1, source_target_pairs={{0,2},{1,3},{2,0},{3,1},{4,6},{5,7},{6,4},{7,5},{8,10},{9,11},{10,... | collective-permute-start | bytes 983048 | tf_op jit(solution)/shard_map/ppermute | solution.py:22
  582.6 19.3 %collective-permute-start.45 = (bf16[80,2048]{1,0:T(8,128)(2,1)S(1)}, bf16[80,2048]{1,0:T(8,128)(2,1)S(1)}, u32[]{:S(2)}, u32[]{:S(2)}) collective-permute-start(bf16[80,2048]{1,0:T(8,128)(2,1)S(1)} %get-tuple-element.186), channel_id=1, source_target_pairs={{0,3},{1,0},{2,1},{3,2},{4,7},{5,4},{6,5},{7,6},{8,11},{9,8},{10,9... | collective-permute-start | bytes 983048 | tf_op jit(solution)/shard_map/ppermute | solution.py:22
  584.5 21.9 %collective-permute-start.63 = (bf16[80,2048]{1,0:T(8,128)(2,1)S(1)}, bf16[80,2048]{1,0:T(8,128)(2,1)S(1)}, u32[]{:S(2)}, u32[]{:S(2)}) collective-permute-start(bf16[80,2048]{1,0:T(8,128)(2,1)S(1)} %get-tuple-element.181), channel_id=1, source_target_pairs={{0,1},{1,2},{2,3},{3,0},{4,5},{5,6},{6,7},{7,4},{8,9},{9,10},{10,1... | collective-permute-start | bytes 983048 | tf_op jit(solution)/shard_map/ppermute | solution.py:22
  585.2 57.6 %collective-permute-start.62 = (bf16[80,2048]{1,0:T(8,128)(2,1)S(1)}, bf16[80,2048]{1,0:T(8,128)(2,1)S(1)}, u32[]{:S(2)}, u32[]{:S(2)}) collective-permute-start(bf16[80,2048]{1,0:T(8,128)(2,1)S(1)} %get-tuple-element.182), channel_id=1, source_target_pairs={{0,2},{1,3},{2,0},{3,1},{4,6},{5,7},{6,4},{7,5},{8,10},{9,11},{10,... | collective-permute-start | bytes 983048 | tf_op jit(solution)/shard_map/ppermute | solution.py:22
  589.3 53.5 %collective-permute-start.61 = (bf16[80,2048]{1,0:T(8,128)(2,1)S(1)}, bf16[80,2048]{1,0:T(8,128)(2,1)S(1)}, u32[]{:S(2)}, u32[]{:S(2)}) collective-permute-start(bf16[80,2048]{1,0:T(8,128)(2,1)S(1)} %get-tuple-element.180), channel_id=1, source_target_pairs={{0,3},{1,0},{2,1},{3,2},{4,7},{5,4},{6,5},{7,6},{8,11},{9,8},{10,9... | collective-permute-start | bytes 983048 | tf_op jit(solution)/shard_map/ppermute | solution.py:22
  590.0 75.9 %collective-permute-start.15 = (bf16[80,2048]{1,0:T(8,128)(2,1)S(1)}, bf16[80,2048]{1,0:T(8,128)(2,1)S(1)}, u32[]{:S(2)}, u32[]{:S(2)}) collective-permute-start(bf16[80,2048]{1,0:T(8,128)(2,1)S(1)} %get-tuple-element.193), channel_id=1, source_target_pairs={{0,1},{1,2},{2,3},{3,0},{4,5},{5,6},{6,7},{7,4},{8,9},{9,10},{10,1... | collective-permute-start | bytes 983048 | tf_op jit(solution)/shard_map/ppermute | solution.py:22
  601.9 64.0 %collective-permute-start.14 = (bf16[80,2048]{1,0:T(8,128)(2,1)S(1)}, bf16[80,2048]{1,0:T(8,128)(2,1)S(1)}, u32[]{:S(2)}, u32[]{:S(2)}) collective-permute-start(bf16[80,2048]{1,0:T(8,128)(2,1)S(1)} %get-tuple-element.194), channel_id=1, source_target_pairs={{0,2},{1,3},{2,0},{3,1},{4,6},{5,7},{6,4},{7,5},{8,10},{9,11},{10,... | collective-permute-start | bytes 983048 | tf_op jit(solution)/shard_map/ppermute | solution.py:22
  606.4 37.1 %collective-permute-start.31 = (bf16[80,2048]{1,0:T(8,128)(2,1)S(1)}, bf16[80,2048]{1,0:T(8,128)(2,1)S(1)}, u32[]{:S(2)}, u32[]{:S(2)}) collective-permute-start(bf16[80,2048]{1,0:T(8,128)(2,1)S(1)} %get-tuple-element.196), channel_id=1, source_target_pairs={{0,1},{1,2},{2,3},{3,0},{4,5},{5,6},{6,7},{7,4},{8,9},{9,10},{10,1... | collective-permute-start | bytes 983048 | tf_op jit(solution)/shard_map/ppermute | solution.py:22
  642.8 21.1 %collective-permute-start.30 = (bf16[80,2048]{1,0:T(8,128)(2,1)S(1)}, bf16[80,2048]{1,0:T(8,128)(2,1)S(1)}, u32[]{:S(2)}, u32[]{:S(2)}) collective-permute-start(bf16[80,2048]{1,0:T(8,128)(2,1)S(1)} %get-tuple-element.197), channel_id=1, source_target_pairs={{0,2},{1,3},{2,0},{3,1},{4,6},{5,7},{6,4},{7,5},{8,10},{9,11},{10,... | collective-permute-start | bytes 983048 | tf_op jit(solution)/shard_map/ppermute | solution.py:22
  642.8 22.5 %collective-permute-start.29 = (bf16[80,2048]{1,0:T(8,128)(2,1)S(1)}, bf16[80,2048]{1,0:T(8,128)(2,1)S(1)}, u32[]{:S(2)}, u32[]{:S(2)}) collective-permute-start(bf16[80,2048]{1,0:T(8,128)(2,1)S(1)} %get-tuple-element.195), channel_id=1, source_target_pairs={{0,3},{1,0},{2,1},{3,2},{4,7},{5,4},{6,5},{7,6},{8,11},{9,8},{10,9... | collective-permute-start | bytes 983048 | tf_op jit(solution)/shard_map/ppermute | solution.py:22
  643.5 30.9 %collective-permute-start.13 = (bf16[80,2048]{1,0:T(8,128)(2,1)S(1)}, bf16[80,2048]{1,0:T(8,128)(2,1)S(1)}, u32[]{:S(2)}, u32[]{:S(2)}) collective-permute-start(bf16[80,2048]{1,0:T(8,128)(2,1)S(1)} %get-tuple-element.192), channel_id=1, source_target_pairs={{0,3},{1,0},{2,1},{3,2},{4,7},{5,4},{6,5},{7,6},{8,11},{9,8},{10,9... | collective-permute-start | bytes 983048 | tf_op jit(solution)/shard_map/ppermute | solution.py:22
  675.2 31.7 %collective-permute-start.78 = (bf16[8,160,160]{2,1,0:T(8,128)(2,1)S(1)}, bf16[8,160,160]{2,1,0:T(8,128)(2,1)S(1)}, u32[]{:S(2)}, u32[]{:S(2)}) collective-permute-start(bf16[8,160,160]{2,1,0:T(8,128)(2,1)S(1)} %add_convert_fusion), channel_id=1, source_target_pairs={{0,12},{4,0},{8,4},{12,8},{1,13},{5,1},{9,5},{13,9},{2,14},{6,2},{... | collective-permute-start | bytes 1228808 | tf_op jit(solution)/shard_map/ppermute | solution.py:22
  675.3 31.6 %collective-permute-start.77 = (bf16[8,160,160]{2,1,0:T(8,128)(2,1)S(1)}, bf16[8,160,160]{2,1,0:T(8,128)(2,1)S(1)}, u32[]{:S(2)}, u32[]{:S(2)}) collective-permute-start(bf16[8,160,160]{2,1,0:T(8,128)(2,1)S(1)} %add_convert_fusion), channel_id=1, source_target_pairs={{0,8},{4,12},{8,0},{12,4},{1,9},{5,13},{9,1},{13,5},{2,10},{6,14},... | collective-permute-start | bytes 1228808 | tf_op jit(solution)/shard_map/ppermute | solution.py:22
  676.5 49.0 %collective-permute-start.76 = (bf16[8,160,160]{2,1,0:T(8,128)(2,1)S(1)}, bf16[8,160,160]{2,1,0:T(8,128)(2,1)S(1)}, u32[]{:S(2)}, u32[]{:S(2)}) collective-permute-start(bf16[8,160,160]{2,1,0:T(8,128)(2,1)S(1)} %add_convert_fusion), channel_id=1, source_target_pairs={{0,4},{4,8},{8,12},{12,0},{1,5},{5,9},{9,13},{13,1},{2,6},{6,10},{... | collective-permute-start | bytes 1228808 | tf_op jit(solution)/shard_map/ppermute | solution.py:22
  (107 other events, 1416.3 us)
Sparse Core Ops, SparseCore 0:
  10.5 43.8 all-gather.4
  56.2 30.4 all-gather.6
  89.2 72.3 all-gather.8
  163.3 46.6 all-gather.10
  421.3 53.4 reduce-scatter.6
  501.6 61.4 reduce-scatter.4
  566.8 61.7 reduce-scatter.10
  632.1 120.3 reduce-scatter.8

commit v2 on v1

v2 whole, which is shorter than its diff:
```python
from functools import partial

import jax
import jax.numpy as jnp
from jax import lax
from jax.experimental import pallas as pl
from jax.experimental.pallas import tpu as pltpu
from jax.sharding import PartitionSpec as P

CONV = 4
CPOW = 8
EPS = 1e-06
TILE = 8
F32 = jnp.float32
BF16 = jnp.bfloat16
GELU_A = 0.7978845608028654
GELU_B = 0.044715
LONG = 10**4
RATE = 1e10


def shift(value, axis, by):
    size = lax.axis_size(axis)
    return lax.ppermute(value, axis, [(i, (i + by) % size) for i in range(size)])


def step_by(value, axis, by):
    size = lax.axis_size(axis)
    return lax.ppermute(value, axis, [(i, i + by) for i in range(size) if 0 <= i + by < size])


def sum_over(value, axis):
    size = lax.axis_size(axis)
    parts = [value] + [shift(value, axis, k) for k in range(1, size)]
    total = parts[0].astype(F32)
    for part in parts[1:]:
        total = total + part.astype(F32)
    return total


def gelu_parts(v):
    th = jnp.tanh(GELU_A * (v + GELU_B * (v * v * v)))
    half = 0.5 * (1.0 + th)
    slope = half + 0.5 * v * (1.0 - th * th) * (GELU_A * (1.0 + 3.0 * GELU_B * (v * v)))
    return v * half, slope


def neg_expm1(z):
    series = 1.0 + z * (1.0 / 10.0)
    for n in (9.0, 8.0, 7.0, 6.0, 5.0, 4.0, 3.0, 2.0):
        series = 1.0 + z * (1.0 / n) * series
    return jnp.where(z > -0.5, -z * series, 1.0 - jnp.exp(z))


def sigmoid(v):
    return 1.0 / (1.0 + jnp.exp(-v))


def tile_scan(coeffs, offsets, reverse):
    rows, width = coeffs.shape
    a = coeffs.reshape(rows // TILE, TILE, width)
    b = offsets.reshape(rows // TILE, TILE, width)
    place = lax.broadcasted_iota(jnp.int32, a.shape, 1)
    for s in (1, 2, 4):
        if reverse:
            inside, turn = place < TILE - s, TILE - s
        else:
            inside, turn = place >= s, s
        a_far = pltpu.roll(a, turn, 1)
        b_far = pltpu.roll(b, turn, 1)
        b = jnp.where(inside, b + a * b_far, b)
        a = jnp.where(inside, a * a_far, a)
    return a, b


def forward_kernel(
    inner_ref, halo_ref, mask_ref, par_ref, wg_ref,
    conv_ref, pre_ref, decay_ref, prod_ref, state_ref, last_ref, ext, run,
):
    rows = inner_ref.shape[0]
    step = pl.program_id(0)

    @pl.when(step == 0)
    def _():
        ext[0:TILE] = halo_ref[...].astype(F32)
        run[0:1] = jnp.ones_like(run[0:1])
        run[1:2] = jnp.zeros_like(run[1:2])

    inner = inner_ref[...].astype(BF16).astype(F32)
    ext[TILE : TILE + rows] = inner
    mask = mask_ref[...]
    conv = par_ref[CONV : CONV + 1] + par_ref[0:1] * inner
    for k in range(1, CONV):
        conv = conv + par_ref[k : k + 1] * ext[TILE - k : TILE - k + rows] * mask[:, k - 1 : k]
    ext[0:TILE] = inner[rows - TILE :]
    conv_low = conv.astype(BF16)
    conv_ref[...] = conv_low
    pre = jnp.dot(conv_low, wg_ref[...], preferred_element_type=F32)
    width = inner.shape[1]
    rate_pre = pre[:, :width] + par_ref[CONV + 2 : CONV + 3]
    input_pre = pre[:, width:] + par_ref[CONV + 3 : CONV + 4]
    pre_ref[:, :width] = rate_pre
    pre_ref[:, width:] = input_pre
    log_rate = par_ref[CONV + 1 : CONV + 2] * sigmoid(rate_pre)
    starts = mask[:, CONV - 1 : CONV] > 0.5
    decays = jnp.where(starts, 0.0, jnp.exp(log_rate))
    scale = jnp.where(starts, 1.0, jnp.sqrt(neg_expm1(2.0 * log_rate)))
    drives = scale * sigmoid(input_pre) * conv_low.astype(F32)
    decay_ref[...] = decays
    a, b = tile_scan(decays, drives, False)
    prod, state = run[0:1], run[1:2]
    for i in range(rows // TILE):
        prods = a[i] * prod
        states = b[i] + a[i] * state
        prod_ref[i * TILE : (i + 1) * TILE] = prods
        state_ref[i * TILE : (i + 1) * TILE] = states
        prod, state = prods[TILE - 1 :], states[TILE - 1 :]
    run[0:1] = prod
    run[1:2] = state
    last_ref[0:1] = prod
    last_ref[1:2] = state


def reverse_kernel(
    many, *refs
):
    blocks, refs = refs[: many + 1], refs[many + 1 :]
    (weight_ref, branch_ref, states_ref, decay_ref, wide_ref,
     low_ref, prod_ref, grad_ref, first_ref, mixed_all, ext, run) = refs
    rows = branch_ref.shape[0]
    step = pl.program_id(0)
    place = pl.num_programs(0) - 1 - step

    @pl.when(step == 0)
    def _():
        ext[rows : rows + TILE] = jnp.ones_like(ext[rows : rows + TILE])
        run[0:1] = jnp.ones_like(run[0:1])
        run[1:2] = jnp.zeros_like(run[1:2])
        assemble(blocks, wide_ref)
        mixed_all[...] = dot_nt(wide_ref[...], weight_ref[...])

    mixed = mixed_all[pl.ds(pl.multiple_of(place * rows, TILE), rows)]
    value, slope = gelu_parts(branch_ref[...])
    low_ref[...] = (mixed * states_ref[...] * slope).astype(BF16)
    decays = decay_ref[...]
    ext[0:rows] = decays
    following = ext[1 : rows + 1]
    ext[rows : rows + TILE] = decays[0:TILE]
    a, b = tile_scan(following, mixed * value, True)
    prod, grad = run[0:1], run[1:2]
    for i in reversed(range(rows // TILE)):
        prods = a[i] * prod
        grads = b[i] + a[i] * grad
        prod_ref[i * TILE : (i + 1) * TILE] = prods
        grad_ref[i * TILE : (i + 1) * TILE] = grads
        prod, grad = prods[0:1], grads[0:1]
    run[0:1] = prod
    run[1:2] = grad
    first_ref[0:1] = decays[0:1] * prod
    first_ref[1:2] = decays[0:1] * grad


def gates_kernel(
    prod_ref, grad_ref, in_ref, prev_ref, state_in_ref, states_ref, decay_ref, pre_ref, conv_ref,
    inner_ref, inner_prev_ref, halo_ref, mask_ref, par_ref, wg_ref,
    low_ref, inner_grad_ref, edge_ref, sums_ref, ext, later,
):
    rows, width = prod_ref.shape
    step = pl.program_id(0)
    at_start = step == pl.num_programs(0) - 1

    @pl.when(step == 0)
    def _():
        sums_ref[...] = jnp.zeros_like(sums_ref)
        later[...] = jnp.zeros_like(later)

    mask = mask_ref[...]
    starts = mask[:, CONV - 1 : CONV] > 0.5
    drive_grad = grad_ref[...] + prod_ref[...] * in_ref[...]
    ext[TILE : TILE + rows] = states_ref[...]
    ext[TILE - 1 : TILE] = jnp.where(at_start, state_in_ref[...], prev_ref[TILE - 1 : TILE])
    prev_states = ext[TILE - 1 : TILE - 1 + rows]
    rate = sigmoid(pre_ref[:, :width])
    gate = sigmoid(pre_ref[:, width:])
    conv = conv_ref[...].astype(F32)
    slope = par_ref[CONV + 1 : CONV + 2]
    log_rate = slope * rate
    decays = decay_ref[...]
    raw = jnp.sqrt(neg_expm1(2.0 * log_rate))
    scale = jnp.where(starts, 1.0, raw)
    scale_grad = drive_grad * gate * conv
    log_grad = jnp.where(
        starts, 0.0, drive_grad * prev_states * decays - scale_grad * (decays * decays) / raw
    )
    rate_low = (log_grad * slope * rate * (1.0 - rate)).astype(BF16)
    input_low = (drive_grad * scale * conv * gate * (1.0 - gate)).astype(BF16)
    low_ref[:, :width] = rate_low
    low_ref[:, width:] = input_low
    both = jnp.concatenate([rate_low, input_low], axis=1)
    conv_grad = drive_grad * scale * gate + lax.dot_general(
        both, wg_ref[...], (((1,), (1,)), ((), ())), preferred_element_type=F32
    )
    inner = inner_ref[...].astype(BF16).astype(F32)
    before = jnp.where(at_start, halo_ref[...].astype(F32), inner_prev_ref[...].astype(BF16).astype(F32))
    ext[0:TILE] = before
    ext[TILE : TILE + rows] = inner

    def total(values):
        return jnp.sum(values, axis=0, keepdims=True)

    sums_ref[0:1] += total(conv_grad * inner)
    sums_ref[CONV : CONV + 1] += total(conv_grad)
    sums_ref[CONV + 1 : CONV + 2] += total(log_grad * rate)
    sums_ref[CONV + 2 : CONV + 3] += total(rate_low.astype(F32))
    sums_ref[CONV + 3 : CONV + 4] += total(input_low.astype(F32))
    inner_grad = par_ref[0:1] * conv_grad
    heads = []
    for k in range(1, CONV):
        masked = conv_grad * mask[:, k - 1 : k]
        sums_ref[k : k + 1] += total(masked * ext[TILE - k : TILE - k + rows])
        heads.append(masked[0:TILE] * par_ref[k : k + 1])
    for k in range(1, CONV):
        masked = par_ref[k : k + 1] * (conv_grad * mask[:, k - 1 : k])
        ext[0:rows] = masked
        ext[rows : rows + TILE] = later[k - 1]
        inner_grad = inner_grad + ext[k : k + rows]
        later[k - 1] = heads[k - 1]
    inner_grad_ref[...] = inner_grad.astype(inner_grad_ref.dtype)

    @pl.when(at_start)
    def _():
        edge_ref[...] = jnp.zeros_like(edge_ref)
        for back in range(1, CONV):
            row = heads[back - 1][0:1]
            for k in range(back + 1, CONV):
                row = row + heads[k - 1][k - back : k - back + 1]
            edge_ref[TILE - back : TILE - back + 1] = row


def rows_spec(rows, width, parts, column=0, reverse=False):
    return pl.BlockSpec((rows, width), lambda step: (parts - 1 - step if reverse else step, column))


def before_spec(rows, width, parts, column=0):
    tiles = rows // TILE
    return pl.BlockSpec(
        (TILE, width), lambda step: (jnp.maximum(parts - 2 - step, 0) * tiles + tiles - 1, column)
    )


def whole_spec(shape):
    return pl.BlockSpec(shape, lambda step: (0,) * len(shape))


def dot_nt(left, right):
    return lax.dot_general(left, right, (((1,), (1,)), ((), ())), preferred_element_type=F32)


def dot_tn(left, right):
    return lax.dot_general(left, right, (((0,), (0,)), ((), ())), preferred_element_type=F32)


class Clock:
    def __init__(self):
        self.tick = jnp.zeros((TILE, 128), F32)

    def call(self, kernel, grid, operands, in_specs, out_specs, out_shape, scratch=(), after=(), cost=3.0):
        count, extra, outs = len(operands), len(after) + 1, len(out_shape)

        def body(*refs):
            given, refs = refs[:count], refs[count + extra :]
            kernel(*given, *refs[:outs], *refs[outs + 1 :])
            refs[outs][...] = jnp.zeros_like(refs[outs])

        whole = pl.BlockSpec((TILE, 128), lambda *step: (0, 0))
        *results, self.tick = pl.pallas_call(
            body,
            out_shape=list(out_shape) + [jax.ShapeDtypeStruct((TILE, 128), F32)],
            grid=grid,
            in_specs=list(in_specs) + [pl.BlockSpec(memory_space=pl.ANY)] * extra,
            out_specs=list(out_specs) + [whole],
            scratch_shapes=list(scratch),
            cost_estimate=pl.CostEstimate(flops=int(cost * RATE), bytes_accessed=int(cost * RATE), transcendentals=0),
        )(*operands, *after, self.tick)
        return results


def shape(dims, dtype):
    return jax.ShapeDtypeStruct(dims, dtype)


def held(array):
    dims = array.shape
    return pl.BlockSpec(dims, lambda *step: (0,) * len(dims), pipeline_mode=pl.Buffered(1))


def kept(dims):
    return pl.BlockSpec(dims, lambda *step: (0,) * len(dims))


def place_spec():
    return pl.BlockSpec(memory_space=pltpu.SMEM)


def spread(copies, apart):
    if not apart:
        return [lax.all_to_all(copies, "tensor", split_axis=0, concat_axis=0, tiled=True)]
    return [copies] + [shift(copies, "tensor", k) for k in range(1, lax.axis_size("tensor"))]


def gathered_sums(parts):
    if len(parts) == 1:
        return [lax.all_to_all(parts[0], "tensor", split_axis=0, concat_axis=0, tiled=True)]
    return [parts[0]] + [shift(parts[k], "tensor", k) for k in range(1, len(parts))]


def assemble(refs, wide_ref):
    place, blocks = refs[0], refs[1:]
    if len(blocks) == 1:
        wide_ref[...] = blocks[0][...]
        return
    rows = blocks[0].shape[0]
    for k, block in enumerate(blocks):
        owner = lax.rem(place[0] - k + len(blocks), len(blocks))
        wide_ref[pl.ds(pl.multiple_of(owner * rows, 2 * TILE), rows)] = block[...]


def deal(values, place, outs, work):
    if len(outs) == 1:
        outs[0][...] = values.astype(BF16)
        return
    work[...] = values
    rows = outs[0].shape[0]
    for k, out in enumerate(outs):
        owner = lax.rem(place[0] + k, len(outs))
        out[...] = work[pl.ds(pl.multiple_of(owner * rows, 2 * TILE), rows)].astype(BF16)


def added(refs, rows):
    if len(refs) == 1:
        count = refs[0].shape[0] // rows
        terms = [refs[0][k * rows : (k + 1) * rows].astype(F32) for k in range(count)]
    else:
        terms = [ref[...].astype(F32) for ref in refs]
    return sum(terms[1:], terms[0])


def repeat_to(ref, values, rows):
    for k in range(ref.shape[0] // rows):
        ref[k * rows : (k + 1) * rows] = values


def mean_of(values):
    return jnp.mean(values, axis=-1, keepdims=True)


def first_kernel(x_ref, gain_ref, out_ref):
    x = x_ref[...].astype(F32)
    repeat_to(out_ref, (x * lax.rsqrt(mean_of(x * x) + EPS) * gain_ref[...]).astype(BF16), x_ref.shape[0])


def first(clock, x, gain, copies):
    rows, model = x.shape
    return clock.call(
        first_kernel, (1,), [x, gain], [held(x), held(gain)],
        [kept((copies * rows, model))], [shape((copies * rows, model), BF16)],
        cost=0.2,
    )[0]


def copies_kernel(*refs):
    out_ref = refs[-1]
    rows = refs[0].shape[0]
    for k in range(out_ref.shape[0] // rows):
        out_ref[k * rows : (k + 1) * rows] = refs[k % (len(refs) - 1)][...]


def all_copies(clock, arrays, copies, after):
    rows, model = arrays[0].shape
    total = rows * len(arrays) * copies
    return clock.call(
        copies_kernel, (1,), arrays, [held(a) for a in arrays], [kept((total, model))],
        [shape((total, model), BF16)], after=after,
        cost=3.0,
    )[0]


def project_kernel(many, *refs):
    blocks, (weight_ref, wide_ref, out_ref, halo_ref) = refs[: many + 1], refs[many + 1 :]

    @pl.when(pl.program_id(0) == 0)
    def _():
        assemble(blocks, wide_ref)

    value = jnp.dot(wide_ref[...], weight_ref[...], preferred_element_type=F32)
    out_ref[...] = value

    @pl.when(pl.program_id(0) == pl.num_programs(0) - 1)
    def _():
        halo_ref[...] = value[value.shape[0] - TILE :].astype(BF16)


def project(clock, place, blocks, weight, after=()):
    model, cols = weight.shape
    rows = sum(block.shape[0] for block in blocks)
    width = cols // 2
    return clock.call(
        partial(project_kernel, len(blocks)), (2,), [place, *blocks, weight],
        [place_spec()] + [held(b) for b in blocks] + [pl.BlockSpec((model, width), lambda j: (0, j))],
        [kept((rows, model)), pl.BlockSpec((rows, width), lambda j: (0, j)), kept((TILE, width))],
        [shape((rows, model), BF16), shape((rows, cols), F32), shape((TILE, width), BF16)], after=after,
        cost=6.0,
    )


def mix_kernel(outs, place_ref, local_ref, prod_ref, in_ref, branch_ref, weight_ref, *refs):
    states_ref, mixed_ref = refs[:2]

    @pl.when(pl.program_id(0) == 0)
    def _():
        states = local_ref[...] + prod_ref[...] * in_ref[...]
        states_ref[...] = states
        mixed_ref[...] = (states * gelu_parts(branch_ref[...])[0]).astype(BF16)

    value = jnp.dot(mixed_ref[...], weight_ref[...], preferred_element_type=F32)
    deal(value, place_ref, refs[2 : 2 + outs], refs[-1])


def part_specs(rows, cols, tile, outs):
    return (
        [pl.BlockSpec((rows // outs, tile), lambda j: (0, j))] * outs,
        [shape((rows // outs, cols), BF16)] * outs,
        pltpu.VMEM((rows, tile), F32),
    )


def mix_out(clock, place, local, prods, state_in, both_pre, weight, outs, tile, after=()):
    rows, width = local.shape
    cols = weight.shape[1]
    part_spec, part_shape, work = part_specs(rows, cols, tile, outs)
    results = clock.call(
        partial(mix_kernel, outs), (cols // tile,), [place, local, prods, state_in, both_pre, weight],
        [place_spec(), held(local), held(prods), held(state_in),
         pl.BlockSpec((rows, width), lambda j: (0, 0), pipeline_mode=pl.Buffered(1)),
         pl.BlockSpec((width, tile), lambda j: (0, j))],
        [kept((rows, width)), kept((rows, width))] + part_spec,
        [shape((rows, width), F32), shape((rows, width), BF16)] + part_shape, [work], after,
        cost=5.7,
    )
    return results[0], results[1], results[2:]


def second_kernel(x_ref, gain_ref, *refs):
    terms, (resid_ref, out_ref) = refs[:-2], refs[-2:]
    rows = x_ref.shape[0]
    resid = x_ref[...].astype(F32) + added(terms, rows)
    resid_ref[...] = resid
    repeat_to(out_ref, (resid * lax.rsqrt(mean_of(resid * resid) + EPS) * gain_ref[...]).astype(BF16), rows)


def second(clock, x, gain, terms, copies):
    rows, model = x.shape
    return clock.call(
        second_kernel, (1,), [x, gain, *terms], [held(x), held(gain)] + [held(t) for t in terms],
        [kept((rows, model)), kept((copies * rows, model))],
        [shape((rows, model), F32), shape((copies * rows, model), BF16)],
        cost=3.0,
    )


def mlp_kernel(two_many, turn, turns, unit, outs, *refs):
    two_blocks, refs = refs[: two_many + 1], refs[two_many + 1 :]
    cot_all, gate_ref, up_ref, down_ref, two_ref, cot_ref, hidden_ref, pair_ref = refs[:8]
    parts, acc = refs[8 : 8 + outs], refs[-1]
    step = pl.program_id(0)

    @pl.when(step == 0)
    def _():
        assemble(two_blocks, two_ref)
        rows = unit
        for k in range(two_ref.shape[0] // rows):
            start = (k * turns + turn) * rows
            cot_ref[k * rows : (k + 1) * rows] = cot_all[start : start + rows]

    two = two_ref[...]
    gate_w, up_w = gate_ref[...], up_ref[...]
    gate_val, gate_slope = gelu_parts(jnp.dot(two, gate_w, preferred_element_type=F32))
    up_pre = jnp.dot(two, up_w, preferred_element_type=F32)
    hidden_ref[...] = (gate_val * up_pre).astype(BF16)
    hidden_grad = dot_nt(cot_ref[...], down_ref[...])
    gate_low = (hidden_grad * up_pre * gate_slope).astype(BF16)
    up_low = (hidden_grad * gate_val).astype(BF16)
    pair_ref[0] = gate_low
    pair_ref[1] = up_low
    term = dot_nt(gate_low, gate_w) + dot_nt(up_low, up_w)

    @pl.when(step == 0)
    def _():
        acc[...] = term

    @pl.when(step > 0)
    def _():
        acc[...] += term

    @pl.when(step == pl.num_programs(0) - 1)
    def _():
        rows = parts[0].shape[0]
        for k, out in enumerate(parts):
            start = 0 if outs == 1 else pl.multiple_of(lax.rem(two_blocks[0][0] + k, outs) * rows, 2 * TILE)
            out[...] = acc[pl.ds(start, rows)].astype(BF16)


def mlp(clock, place, two_blocks, cot_all, turn, turns, unit, pair_w, down_w, outs, tile, after=()):
    units, model = down_w.shape
    rows = sum(block.shape[0] for block in two_blocks)
    steps = units // tile
    results = clock.call(
        partial(mlp_kernel, len(two_blocks), turn, turns, unit, outs), (steps,),
        [place, *two_blocks, cot_all, pair_w, pair_w, down_w],
        [place_spec()] + [held(b) for b in two_blocks + [cot_all]]
        + [pl.BlockSpec((model, tile), lambda j: (0, j)), pl.BlockSpec((model, tile), lambda j: (0, steps + j)),
           pl.BlockSpec((tile, model), lambda j: (j, 0))],
        [kept((rows, model)), kept((rows, model)), pl.BlockSpec((rows, tile), lambda j: (0, j)),
         pl.BlockSpec((2, rows, tile), lambda j: (0, 0, j))] + [kept((rows // outs, model))] * outs,
        [shape((rows, model), BF16), shape((rows, model), BF16), shape((rows, units), BF16),
         shape((2, rows, units), BF16)] + [shape((rows // outs, model), BF16)] * outs,
        [pltpu.VMEM((rows, model), F32)], after,
        cost=27.0,
    )
    return *results[:4], results[4:]


def down_kernel(count, unit, *refs):
    right, out_ref = refs[count], refs[-1]
    for i in range(count):
        value = jnp.dot(refs[i][...], right[...], preferred_element_type=F32).astype(BF16)
        for k in range(value.shape[0] // unit):
            start = (k * count + i) * unit
            out_ref[start : start + unit] = value[k * unit : (k + 1) * unit]


def down_out(clock, lefts, right, unit, tile):
    depth, cols = right.shape
    count = len(lefts)
    total = count * lefts[0].shape[0]
    return clock.call(
        partial(down_kernel, count, unit), (cols // tile,), [*lefts, right],
        [held(a) for a in lefts] + [pl.BlockSpec((depth, tile), lambda j: (0, j))],
        [pl.BlockSpec((total, tile), lambda j: (0, j))], [shape((total, cols), BF16)],
        cost=0.01,
    )[0]


def norm_grad(values, grad, gain):
    inv = lax.rsqrt(mean_of(values * values) + EPS)
    unit = values * inv
    scaled = grad * gain
    return inv * (scaled - unit * mean_of(scaled * unit)), grad * unit


def third_kernel(resid_ref, cot_ref, gain_ref, *refs):
    terms, (grad_ref, low_ref, sum_ref) = refs[:-3], refs[-3:]
    rows = resid_ref.shape[0]
    grad = added(terms, rows).astype(BF16).astype(F32)
    term, product = norm_grad(resid_ref[...], grad, gain_ref[...])
    total = cot_ref[...].astype(F32) + term
    grad_ref[...] = total
    sum_ref[...] = jnp.sum(product, axis=0, keepdims=True)
    repeat_to(low_ref, total.astype(BF16), rows)


def third(clock, resid, cot, gain, terms, copies, cost):
    rows, model = resid.shape
    return clock.call(
        third_kernel, (1,), [resid, cot, gain, *terms], [held(resid), held(cot), held(gain)] + [held(t) for t in terms],
        [kept((rows, model)), kept((copies * rows, model)), kept((1, model))],
        [shape((rows, model), F32), shape((copies * rows, model), BF16), shape((1, model), F32)],
        cost=cost,
    )


def back_kernel(outs, place_ref, branch_ref, inner_ref, edge_ref, weight_ref, one_ref, *refs):
    both_ref, gain_ref = refs[:2]
    rows, width = branch_ref.shape

    @pl.when(pl.program_id(0) == 0)
    def _():
        both_ref[:, :width] = branch_ref[...]
        both_ref[: rows - 2 * TILE, width:] = inner_ref[: rows - 2 * TILE].astype(BF16)
        last = inner_ref[rows - 2 * TILE :]
        fixed = jnp.concatenate([last[:TILE], last[TILE:] + edge_ref[...]], axis=0)
        both_ref[rows - 2 * TILE :, width:] = fixed.astype(BF16)

    value = dot_nt(both_ref[...], weight_ref[...])
    gain_ref[...] = jnp.sum(value * one_ref[...].astype(F32), axis=0, keepdims=True)
    deal(value, place_ref, refs[2 : 2 + outs], refs[-1])


def back_one(clock, place, branch_low, inner_grad, edge_in, weight, wide_one, outs, tile):
    rows, width = branch_low.shape
    model = weight.shape[0]
    part_spec, part_shape, work = part_specs(rows, model, tile, outs)
    results = clock.call(
        partial(back_kernel, outs), (model // tile,), [place, branch_low, inner_grad, edge_in, weight, wide_one],
        [place_spec(), held(branch_low), held(inner_grad), held(edge_in),
         pl.BlockSpec((tile, 2 * width), lambda j: (j, 0)), pl.BlockSpec((rows, tile), lambda j: (0, j))],
        [kept((rows, 2 * width)), pl.BlockSpec((1, tile), lambda j: (0, j))] + part_spec,
        [shape((rows, 2 * width), BF16), shape((1, model), F32)] + part_shape, [work],
        cost=6.2,
    )
    return results[0], results[1], results[2:]


def last_kernel(x_ref, resid_ref, gain_ref, *refs):
    terms, out_ref = refs[:-1], refs[-1]
    grad = added(terms, x_ref.shape[0]).astype(BF16).astype(F32)
    out_ref[...] = resid_ref[...] + norm_grad(x_ref[...].astype(F32), grad, gain_ref[...])[0]


def last(clock, x, resid_grad, gain, terms):
    return clock.call(
        last_kernel, (1,), [x, resid_grad, gain, *terms],
        [held(x), held(resid_grad), held(gain)] + [held(t) for t in terms],
        [kept(resid_grad.shape)], [shape(resid_grad.shape, F32)], cost=LONG,
    )[0]


def out_kernel(count, *refs):
    terms, outs = refs[count], refs[count + 1 :]
    rows = refs[0].shape[0]
    for i in range(count):
        total = refs[i][...]
        for k in range(terms.shape[0] // (count * rows)):
            start = (k * count + i) * rows
            total = total + terms[start : start + rows].astype(F32)
        outs[i][...] = total.astype(BF16)


def block_results(clock, residuals, terms):
    count = len(residuals)
    dims = residuals[0].shape
    return clock.call(
        partial(out_kernel, count), (1,), [*residuals, terms], [held(r) for r in residuals] + [held(terms)],
        [kept(dims)] * count, [shape(dims, BF16)] * count,
        cost=3.0,
    )


def term_kernel(count, *refs):
    out_ref = refs[-1]
    total = None
    for i in range(count):
        right = refs[count + i]
        value = dot_tn(refs[i][...], right[0] if len(right.shape) == 3 else right[...])
        total = value if total is None else total + value
    out_ref[...] = total.astype(out_ref.dtype)


def weight_term(clock, lefts, rights, tile, cost, after=()):
    count = len(lefts)
    rows, depth = lefts[0].shape
    halves = rights[0].shape[0] if rights[0].ndim == 3 else 1
    cols = rights[0].shape[-1]
    if halves == 1:
        grid, left_at, out_at = (depth // tile,), (lambda j: (0, j)), (lambda j: (j, 0))
        right_spec = held(rights[0])
    else:
        grid, left_at, out_at = (halves, depth // tile), (lambda h, j: (0, j)), (lambda h, j: (j, h))
        right_spec = pl.BlockSpec((1, rows, cols), lambda h, j: (h, 0, 0))
    return clock.call(
        partial(term_kernel, count), grid, [*lefts, *rights],
        [pl.BlockSpec((rows, tile), left_at)] * count + [right_spec] * count,
        [pl.BlockSpec((tile, cols), out_at)], [shape((depth, halves * cols), BF16)], after=after,
        cost=cost,
    )[0]


def diagonal_kernel(count, cells, *refs):
    out_ref, work = refs[-2:]
    total = None
    for i in range(count):
        value = dot_tn(refs[i][...], refs[count + i][...])
        total = value if total is None else total + value
    work[...] = total
    cell = out_ref.shape[1]
    for i in range(cells):
        for h in range(2):
            col = (h * cells + i) * cell
            out_ref[h * cells + i] = work[i * cell : (i + 1) * cell, col : col + cell].astype(BF16)


def diagonal_terms(clock, lefts, rights, cells):
    count = len(lefts)
    width = lefts[0].shape[1]
    cell = width // cells
    return clock.call(
        partial(diagonal_kernel, count, cells), (1,), [*lefts, *rights],
        [held(a) for a in lefts] + [held(a) for a in rights],
        [kept((2 * cells, cell, cell))], [shape((2 * cells, cell, cell), BF16)],
        [pltpu.VMEM((width, 2 * width), F32)],
        cost=4.5,
    )[0]


def widen_kernel(width, in_ref, *outs):
    value = in_ref[...].astype(F32)
    for i, out in enumerate(outs):
        out[...] = value[:, i * width : (i + 1) * width]


def finish(clock, low, pieces):
    rows, cols = low.shape
    width = cols // pieces
    return clock.call(
        partial(widen_kernel, width), (1,), [low], [held(low)], [kept((rows, width))] * pieces,
        [shape((rows, width), F32)] * pieces, cost=LONG,
    )


def sum_kernel(*refs):
    refs[-1][...] = added(refs[:-1], refs[0].shape[0]).astype(refs[-1].dtype)


def sum_of(clock, arrays, dtype):
    dims = arrays[0].shape
    return clock.call(
        sum_kernel, (1,), arrays, [held(a) for a in arrays], [kept(dims)], [shape(dims, dtype)], cost=1.0,
    )[0]


def everyone(value, axis):
    return [value] + [shift(value, axis, k) for k in range(1, lax.axis_size(axis))]


def forward_scan(clock, both_pre, halo, mask, params, gate_w, parts):
    total, width = both_pre.shape[0], params.shape[1]
    rows = total // parts
    spec = partial(rows_spec, rows, width, parts)
    return clock.call(
        forward_kernel, (parts,), [both_pre, halo, mask, params, gate_w],
        [spec(column=1), held(halo), rows_spec(rows, mask.shape[1], parts), held(params), held(gate_w)],
        [spec(), rows_spec(rows, 2 * width, parts), spec(), spec(), spec(), kept((2, width))],
        [shape((total, width), BF16), shape((total, 2 * width), F32), shape((total, width), F32),
         shape((total, width), F32), shape((total, width), F32), shape((2, width), F32)],
        [pltpu.VMEM((rows + TILE, width), F32), pltpu.VMEM((TILE, width), F32)],
        cost=7.0,
    )


def reverse_scan(clock, place, blocks, out_w, both_pre, states, decays, parts, after=()):
    total, width = states.shape
    rows = total // parts
    model = out_w.shape[1]
    spec = rows_spec(rows, width, parts, reverse=True)
    return clock.call(
        partial(reverse_kernel, len(blocks)), (parts,), [place, *blocks, out_w, both_pre, states, decays],
        [place_spec()] + [held(b) for b in blocks] + [held(out_w), spec, spec, spec],
        [kept((total, model)), spec, spec, spec, kept((2, width))],
        [shape((total, model), BF16), shape((total, width), BF16), shape((total, width), F32),
         shape((total, width), F32), shape((2, width), F32)],
        [pltpu.VMEM((total, width), F32), pltpu.VMEM((rows + TILE, width), F32), pltpu.VMEM((TILE, width), F32)],
        after,
        cost=7.5,
    )


def gates_back(clock, prods, grads, grad_in, states, state_in, decays, pre, conv_low, both_pre, halo, mask,
               params, gate_w, parts):
    total, width = states.shape
    rows = total // parts
    spec = partial(rows_spec, rows, width, parts, reverse=True)
    return clock.call(
        gates_kernel, (parts,),
        [prods, grads, grad_in, states, state_in, states, decays, pre, conv_low, both_pre, both_pre, halo, mask,
         params, gate_w],
        [spec(), spec(), held(grad_in), before_spec(rows, width, parts), held(state_in),
         spec(), spec(), rows_spec(rows, 2 * width, parts, reverse=True), spec(), spec(column=1),
         before_spec(rows, width, parts, column=1), held(halo),
         rows_spec(rows, mask.shape[1], parts, reverse=True), held(params), held(gate_w)],
        [rows_spec(rows, 2 * width, parts, reverse=True), spec(), kept((TILE, width)), kept((TILE, width))],
        [shape((total, 2 * width), BF16), shape((total, width), F32), shape((TILE, width), F32),
         shape((TILE, width), F32)],
        [pltpu.VMEM((rows + TILE, width), F32), pltpu.VMEM((CONV - 1, TILE, width), F32)],
        cost=8.5,
    )


def carry_over(ends, direction):
    size = lax.axis_size("context")
    incoming = jnp.zeros_like(ends[1:2])
    parts = [step_by(ends, "context", direction * k) for k in range(1, size)]
    for part in reversed(parts):
        incoming = part[1:2] + part[0:1] * incoming
    return incoming


def carry_all(ends, direction):
    stacked = jnp.concatenate([e[:1] for e in ends] + [e[1:] for e in ends], axis=0)
    count = len(ends)
    incoming = jnp.zeros_like(stacked[:count])
    for part in reversed([step_by(stacked, "context", direction * k) for k in range(1, lax.axis_size("context"))]):
        incoming = part[count:] + part[:count] * incoming
    return [incoming[i : i + 1] for i in range(count)]


def block_diagonal(weight):
    count, rows, cols = weight.shape
    return jnp.concatenate(
        [jnp.pad(weight[i], ((0, 0), (i * cols, (count - 1 - i) * cols))) for i in range(count)], axis=0
    )


def per_device(
    inputs, segments, norm_gain, branch_weight, inner_weight, conv_weight, conv_bias, rate_weight, rate_bias,
    input_weight, input_bias, decay_param, out_weight, mlp_gain, gate_weight, up_weight, down_weight, cotangent,
):
    micro, seqs, rows, model = inputs.shape
    parts = lax.axis_size("tensor")
    span = rows * parts
    width = conv_bias.shape[0]
    blocks = rate_weight.shape[0]
    chains = [(m, s) for m in range(micro) for s in range(seqs)]
    context_pos = lax.axis_index("context")
    owners = ("fsdp", "context")

    both_w = lax.all_gather(jnp.concatenate([branch_weight, inner_weight], 1), owners, axis=0, tiled=True)
    out_w = lax.all_gather(out_weight, owners, axis=1, tiled=True)
    pair_w = lax.all_gather(jnp.concatenate([gate_weight, up_weight], 1), owners, axis=0, tiled=True)
    down_w = lax.all_gather(down_weight, owners, axis=1, tiled=True)
    gate_w = jnp.concatenate([block_diagonal(rate_weight), block_diagonal(input_weight)], axis=1)
    slope = -CPOW * jax.nn.softplus(-decay_param)
    params = jnp.concatenate(
        [conv_weight, conv_bias[None], slope[None], rate_bias[None], input_bias[None]], axis=0
    )

    def masks_of(row):
        pad = jnp.concatenate([jnp.full((CONV - 1,), -1, jnp.int32), row])
        ext = lax.dynamic_slice_in_dim(pad, context_pos * span, span + CONV - 1)
        own = ext[CONV - 1 :]
        cols = [(ext[CONV - 1 - k : CONV - 1 - k + span] == own).astype(F32) for k in range(1, CONV)]
        return jnp.stack(cols + [1.0 - cols[0]], axis=1)

    count = len(chains)
    turns = range(count)
    apart = [i % 2 == 1 for i in turns]
    copies = [1 if a else parts for a in apart]
    outs = [parts if a else 1 for a in apart]
    place = lax.axis_index("tensor").reshape(1).astype(jnp.int32)
    x_rows = [inputs[m, s] for m, s in chains]
    cot_rows = [cotangent[m, s] for m, s in chains]
    gain_one_row, gain_two_row = norm_gain[None], mlp_gain[None]
    mask = [masks_of(segments[m, s]) for m, s in chains]
    clock = Clock()

    def share(term, dim):
        return lax.psum_scatter(term, owners, scatter_dimension=dim, tiled=True)

    normed = [first(clock, x_rows[0], gain_one_row, copies[0])]
    cot_copies = all_copies(clock, cot_rows, parts, (gate_w, params, *mask))
    normed += [first(clock, x_rows[i], gain_one_row, copies[i]) for i in turns if i]
    one_blocks = [spread(normed[i], apart[i]) for i in turns]
    (cot_all,) = spread(cot_copies, False)
    projections = [project(clock, place, one_blocks[i], both_w) for i in turns]
    wide_one, both_pre, tails = map(list, zip(*projections))
    halo = [step_by(t, "context", 1) for t in tails]
    scans = [forward_scan(clock, both_pre[i], halo[i], mask[i], params, gate_w, parts) for i in turns]
    conv_low, pre, decays, prods, locals_, ends = map(list, zip(*scans))
    state_in = [carry_over(end, 1) for end in ends]
    mixes = [
        mix_out(clock, place, locals_[i], prods[i], state_in[i], both_pre[i], out_w, outs[i], 512,
                () if i else (cot_all,))
        for i in turns
    ]
    states, mixed_low, out_part = map(list, zip(*mixes))
    out_terms = [gathered_sums(p) for p in out_part]
    seconds = [second(clock, x_rows[i], gain_two_row, out_terms[i], copies[i]) for i in turns]
    residual = [t[0] for t in seconds]
    two_blocks = [spread(seconds[i][1], apart[i]) for i in turns]
    mlps = [
        mlp(clock, place, two_blocks[i], cot_all, i, count, rows, pair_w, down_w, outs[i], 256) for i in turns
    ]
    wide_two, wide_cot, hidden_low, pair_low, two_part = map(list, zip(*mlps))
    two_terms = [gathered_sums(p) for p in two_part]

    thirds = []
    for i in turns:
        thirds.append(third(clock, residual[i], cot_rows[i], gain_two_row, two_terms[i], copies[i], 0.01 if i else 3.4))
        if i == 0:
            pair_term = weight_term(clock, wide_two, pair_low, 256, 21.0)
    resid_grad, resid_low, gain_two = map(list, zip(*thirds))
    resid_blocks = [spread(resid_low[i], apart[i]) for i in turns]
    pair_grad = share(pair_term, 0)
    (down_terms,) = gathered_sums([down_out(clock, hidden_low, down_w, rows, 512)])
    down_term = weight_term(clock, hidden_low, wide_cot, 256, 0.01)
    down_grad = share(down_term, 1)

    reversed_ = [
        reverse_scan(clock, place, resid_blocks[i], out_w, both_pre[i], states[i], decays[i], parts) for i in turns
    ]
    wide_resid, branch_low, rev_prods, rev_grads, ends_back = map(list, zip(*reversed_))
    grad_in = carry_all(ends_back, -1)
    out_term = weight_term(clock, mixed_low, wide_resid, 128, 7.0)
    out_grad = share(out_term, 1)
    backs = []
    for i in turns:
        backs.append(gates_back(
            clock, rev_prods[i], rev_grads[i], grad_in[i], states[i], state_in[i], decays[i], pre[i], conv_low[i],
            both_pre[i], halo[i], mask[i], params, gate_w, parts,
        ))
    gates_low, inner_grad, edge, sums = map(list, zip(*backs))
    edge_in = [step_by(e, "context", -1) for e in edge]
    gate_blocks = diagonal_terms(clock, conv_low, gates_low, blocks)
    ones = []
    for i in turns:
        ones.append(back_one(
            clock, place, branch_low[i], inner_grad[i], edge_in[i], both_w, wide_one[i], outs[i], 512
        ))
        if i == 0:
            block_out = block_results(clock, residual, down_terms)
    both_low, gain_one, one_part = map(list, zip(*ones))
    one_terms = [gathered_sums(p) for p in one_part]
    both_term = weight_term(clock, wide_one, both_low, 256, 11.0)
    both_grad = share(both_term, 0)
    gate_blocks = sum_of(clock, everyone(gate_blocks, "fsdp"), BF16)
    gate_blocks = sum_of(clock, everyone(gate_blocks, "context"), F32)
    input_grad = [last(clock, x_rows[i], resid_grad[i], gain_one_row, one_terms[i]) for i in turns]
    gate_grad, up_grad = finish(clock, pair_grad, 2)
    (down_grad,) = finish(clock, down_grad, 1)
    (out_grad,) = finish(clock, out_grad, 1)
    branch_grad, inner_grad_w = finish(clock, both_grad, 2)

    def stacked(values):
        return jnp.stack(values).reshape(micro, seqs, rows, model)

    gains = jnp.concatenate([sum(gain_one) / gain_one_row, sum(gain_two)])
    small = jnp.concatenate([sum(sums).reshape(1, -1), gains.reshape(1, -1)], axis=1)
    small = sum_over(sum_over(small, "fsdp"), "context")
    sums = small[:, : TILE * width].reshape(TILE, width)
    gains = sum_over(small[:, TILE * width :], "tensor").reshape(2, model)
    return (
        stacked(block_out),
        stacked(input_grad),
        gains[0],
        branch_grad,
        inner_grad_w,
        sums[:CONV],
        sums[CONV],
        gate_blocks[:blocks],
        sums[CONV + 2],
        gate_blocks[blocks:],
        sums[CONV + 3],
        sums[CONV + 1] * (CPOW * jax.nn.sigmoid(-decay_param)),
        out_grad,
        gains[1],
        gate_grad,
        up_grad,
        down_grad,
    )


def solution(mesh):
    tokens = P(None, "fsdp", ("context", "tensor"), None)
    by_rows = P(("fsdp", "context"), "tensor")
    by_cols = P("tensor", ("fsdp", "context"))
    channel = P("tensor")
    taps = P(None, "tensor")
    blocks = P("tensor", None, None)
    return jax.shard_map(
        per_device,
        mesh=mesh,
        in_specs=(
            tokens, P(None, "fsdp", None), P(), by_rows, by_rows, taps, channel, blocks, channel, blocks, channel,
            channel, by_cols, P(), by_rows, by_rows, by_cols, tokens,
        ),
        out_specs=(
            tokens, tokens, P(), by_rows, by_rows, taps, channel, blocks, channel, blocks, channel, channel,
            by_cols, P(), by_rows, by_rows, by_cols,
        ),
        check_vma=False,
    )
```

time: 773 us -> 640 us (0.83)
  Pallas kernels: 40.6 us -> 246 us
  waiting for transfers between devices: 325 us -> 192 us
  matrix products: 125 us -> 0 us
  starting transfers between devices: 168 us -> 133 us
  local copies, waits for them, and re-layouts: 49.1 us -> 20.9 us
  other arithmetic: 39.5 us -> 20 us
    pallas_call x6 -> x36, Pallas kernels: 40.6 us -> 246 us  [call(): pl.pallas_call(body, out_shape=list(out_shape) + [jax.ShapeDtypeStruct((T...]
    ppermute x63 -> x29, waiting for transfers between devices: 291 us -> 89.2 us  [shift(): lax.ppermute(value, axis, [(i, (i + by) % size) for i in range(size)])]
    dot_general x21 -> x0, matrix products: 125 us -> none  [the longest x8 43.3 us: matmul_nt(): lax.dot_general(left, right, (((1,), (1,)), ((), ())), preferred_element_...]
    all_to_all x0 -> x8, waiting for transfers between devices: none -> 93 us  [the longest x4 57.4 us: spread(): lax.all_to_all(copies, 'tensor', split_axis=0, concat_axis=0, tiled=True)]
    ppermute x63 -> x29, starting transfers between devices: 140 us -> 72.4 us  [shift(): lax.ppermute(value, axis, [(i, (i + by) % size) for i in range(size)])]
    all_to_all x0 -> x8, starting transfers between devices: none -> 36.6 us  [the longest x4 18.6 us: spread(): lax.all_to_all(copies, 'tensor', split_axis=0, concat_axis=0, tiled=True)]
    unnamed x195 -> x105, local copies, waits for them, and re-layouts: 31.3 us -> 11.6 us
    ppermute x16 -> x13, waiting for transfers between devices: 13.3 us -> 0.03 us  [step_by(): lax.ppermute(value, axis, [(i, i + by) for i in range(size) if 0 <= i + b...]
  transfers between devices with their start and end apart: 87 -> 58, of which waited for: 36 -> 12; matrix products, arithmetic and copies ran while one was open for 25% -> 4% of each run, Pallas kernels for 5% -> 35%
where the time goes in v2:
time: 640 us; the launch traced here: 628 us
  Pallas kernels  246 us (38%)
  waiting for transfers between devices  192 us (30%)
  starting transfers between devices  133 us (21%)
  local copies, waits for them, and re-layouts  20.9 us (3%)
  other arithmetic  20 us (3%)
  between operations  15.5 us (2%)
    pallas_call x36, Pallas kernels, call(): pl.pallas_call(body, out_shape=list(out_shape) + [jax.ShapeDtypeStruct((T...  246 us
    ppermute x29, waiting for transfers between devices, shift(): lax.ppermute(value, axis, [(i, (i + by) % size) for i in range(size)])  89.2 us
    ppermute x29, starting transfers between devices, shift(): lax.ppermute(value, axis, [(i, (i + by) % size) for i in range(size)])  72.4 us
    all_to_all x4, waiting for transfers between devices, spread(): lax.all_to_all(copies, 'tensor', split_axis=0, concat_axis=0, tiled=True)  57.4 us
    all_to_all x4, waiting for transfers between devices, gathered_sums(): lax.all_to_all(parts[0], 'tensor', split_axis=0, concat_axis=0, tiled=True)  35.6 us
    ppermute x13, starting transfers between devices, step_by(): lax.ppermute(value, axis, [(i, i + by) for i in range(size) if 0 <= i + b...  23.9 us
    all_to_all x4, starting transfers between devices, spread(): lax.all_to_all(copies, 'tensor', split_axis=0, concat_axis=0, tiled=True)  18.6 us
    all_to_all x4, starting transfers between devices, gathered_sums(): lax.all_to_all(parts[0], 'tensor', split_axis=0, concat_axis=0, tiled=True)  18 us
  transfers between devices with their start and end apart: 58, of which 12 were waited for; matrix products, arithmetic and copies ran while one was open for 4% of the time, Pallas kernels for 35%

profile of v2, /device:TPU:0, one launch (start us, length us, event | category | flops | bytes accessed | tf_op | source)
XLA Modules:
  0.0 628.1 jit_solution(550564973510936752)
XLA Ops:
  14.6 6.5 %all-to-all-start = ((bf16[4,80,2048]{2,1,0:T(8,128)(2,1)}), bf16[4,80,2048]{2,1,0:T(8,128)(2,1)S(1)}, u32[]{:S(2)}, u32[]{:S(2)}) async-start(bf16[4,80,2048]{2,1,0:T(8,128)(2,1)} %bitcast.67), calls=%async_computation | async-start | bytes 2621440 | tf_op jit(solution)/shard_map/all_to_all | solution.py:307
  24.9 8.4 %fusion.24.refs_2_.refs_4_.refs_14_ = bf16[640,1280]{1,0:T(8,128)(2,1)} fusion(bf16[160,160]{1,0:T(8,128)(2,1)S(1)} %get-tuple-element.356, bf16[160,160]{1,0:T(8,128)(2,1)S(1)} %get-tuple-element.357, bf16[160,160]{1,0:T(8,128)(2,1)S(1)} %get-tuple-element.355, bf16[160,160]{1,0:T(8,128)(2,1)S(1)} %get-tuple-element.354, ...), kind=kLoop, calls=%fused_computation.32 | loop fusion | flops 40960000 | bytes 2048000 | tf_op jit(solution)/shard_map/concatenate | solution.py:830
  33.3 2.7 shard_map.306
  38.1 3.8 collective-permute-start.3
  44.5 23.1 %all-to-all-done = bf16[4,80,2048]{2,1,0:T(8,128)(2,1)S(1)} async-done(((bf16[4,80,2048]{2,1,0:T(8,128)(2,1)}), bf16[4,80,2048]{2,1,0:T(8,128)(2,1)S(1)}, u32[]{:S(2)}, u32[]{:S(2)}) %all-to-all-start) | async-done | bytes 1310752 | tf_op jit(solution)/shard_map/all_to_all | solution.py:307
  68.6 4.6 all-to-all-start.1
  73.2 6.0 shard_map.308
  79.2 3.4 collective-permute-start
  82.6 13.0 %collective-permute-done.2.refs_3_ = bf16[80,2048]{1,0:T(8,128)(2,1)S(1)} collective-permute-done((bf16[80,2048]{1,0:T(8,128)(2,1)}, bf16[80,2048]{1,0:T(8,128)(2,1)S(1)}, u32[]{:S(2)}, u32[]{:S(2)}) %collective-permute-start.2) | collective-permute-done | bytes 327712 | tf_op jit(solution)/shard_map/ppermute | solution.py:24
  96.4 6.1 shard_map.309
  102.5 3.4 collective-permute-start.7
  106.5 6.9 %shard_map.310 = (bf16[320,640]{1,0:T(8,128)(2,1)}, f32[320,1280]{1,0:T(8,128)}, f32[320,640]{1,0:T(8,128)}, f32[320,640]{1,0:T(8,128)}, f32[320,640]{1,0:T(8,128)}, /*index=5*/f32[2,640]{1,0:T(2,128)}, f32[8,128]{1,0:T(8,128)}) custom-call(f32[320,1280]{1,0:T(8,128)} %get-tuple-element.154.refs_0_.refs_4_.refs_3_.refs_9_.refs_10_, ...), custom_call_target="tpu_custom_call" | custom-call | flops 70000001024 | bytes 70000001024 | tf_op jit(solution)/shard_map/pallas_call | solution.py:276
  120.1 6.9 %shard_map.311 = (bf16[320,640]{1,0:T(8,128)(2,1)}, f32[320,1280]{1,0:T(8,128)}, f32[320,640]{1,0:T(8,128)}, f32[320,640]{1,0:T(8,128)}, f32[320,640]{1,0:T(8,128)}, /*index=5*/f32[2,640]{1,0:T(2,128)}, f32[8,128]{1,0:T(8,128)}) custom-call(f32[320,1280]{1,0:T(8,128)} %get-tuple-element.163.refs_0_.refs_4_.refs_6_.refs_9_.refs_10_, ...), custom_call_target="tpu_custom_call" | custom-call | flops 70000001024 | bytes 70000001024 | tf_op jit(solution)/shard_map/pallas_call | solution.py:276
  132.3 4.5 all-to-all-done.1
  136.8 5.7 shard_map.312
  142.5 3.6 all-to-all-start.2
  146.7 6.2 shard_map.313
  155.0 2.4 collective-permute-start.12
  158.8 33.2 %all-to-all-done.2 = bf16[4,80,2048]{2,1,0:T(8,128)(2,1)S(1)} async-done(((bf16[4,80,2048]{2,1,0:T(8,128)(2,1)}), bf16[4,80,2048]{2,1,0:T(8,128)(2,1)S(1)}, u32[]{:S(2)}, u32[]{:S(2)}) %all-to-all-start.2) | async-done | bytes 1310752 | tf_op jit(solution)/shard_map/all_to_all | solution.py:313
  193.0 3.0 shard_map.314
  196.1 3.9 all-to-all-start.3
  200.9 2.6 shard_map.315
  203.5 9.8 %collective-permute-start.16 = (bf16[80,2048]{1,0:T(8,128)(2,1)}, bf16[80,2048]{1,0:T(8,128)(2,1)}, u32[]{:S(2)}, u32[]{:S(2)}) collective-permute-start(bf16[80,2048]{1,0:T(8,128)(2,1)} %get-tuple-element.183.refs_1_), channel_id=1, source_target_pairs={{0,3},{1,0},{2,1},{3,2},{4,7},{5,4},{6,5},{7,6},{8,11},{9,8},{10,9... | collective-permute-start | bytes 983048 | tf_op jit(solution)/shard_map/ppermute | solution.py:24
  213.2 5.2 collective-permute-start.15
  218.4 29.8 %all-to-all-done.3 = bf16[4,80,2048]{2,1,0:T(8,128)(2,1)S(1)} async-done(((bf16[4,80,2048]{2,1,0:T(8,128)(2,1)}), bf16[4,80,2048]{2,1,0:T(8,128)(2,1)S(1)}, u32[]{:S(2)}, u32[]{:S(2)}) %all-to-all-start.3) | async-done | bytes 1310752 | tf_op jit(solution)/shard_map/all_to_all | solution.py:307
  249.2 27.2 %shard_map.316 = (bf16[320,2048]{1,0:T(8,128)(2,1)}, bf16[320,2048]{1,0:T(8,128)(2,1)}, bf16[320,1536]{1,0:T(8,128)(2,1)}, bf16[2,320,1536]{2,1,0:T(8,128)(2,1)}...) custom-call(s32[1]{0:T(128)} %bitcast.2.refs_0_, bf16[320,2048]{1,0:T(8,128)(2,1)} %bitcast.69, ...), custom_call_target="tpu_custom_call" | custom-call | flops 269999996928 | bytes 269999996928 | tf_op jit(solution)/shard_map/pallas_call | solution.py:276
  276.4 4.3 all-to-all-start.4
  280.8 27.3 %shard_map.317 = (bf16[320,2048]{1,0:T(8,128)(2,1)}, bf16[320,2048]{1,0:T(8,128)(2,1)}, bf16[320,1536]{1,0:T(8,128)(2,1)}, bf16[2,320,1536]{2,1,0:T(8,128)(2,1)}...) custom-call(s32[1]{0:T(128)} %bitcast.2.refs_0_, ...), custom_call_target="tpu_custom_call" | custom-call | flops 269999996928 | bytes 269999996928 | tf_op jit(solution)/shard_map/pallas_call | solution.py:276
  308.2 2.4 all-to-all-done.4
  310.6 3.6 shard_map.318
  314.1 21.5 %shard_map.319 = (bf16[2048,3072]{1,0:T(8,128)(2,1)}, f32[8,128]{1,0:T(8,128)}) custom-call(bf16[320,2048]{1,0:T(8,128)(2,1)} %get-tuple-element.190.refs_0_, bf16[320,2048]{1,0:T(8,128)(2,1)} %get-tuple-element.191.refs_1_, bf16[2,320,1536]{2,1,0:T(8,128)(2,1)} %get-tuple-element.192.refs_2_, bf16[2,320,1536]{2,1,0:T(8,128)(2,1)} %get-tuple-element.193.refs_3_, ...), custom_call_target="tpu_custom_call" | custom-call | flops 210000003072 | bytes 210000003072 | tf_op jit(solution)/shard_map/pallas_call | solution.py:276
  335.7 3.7 all-to-all-start.6
  341.4 2.4 collective-permute-start.18
  345.3 27.9 %collective-permute-done.17.refs_4_ = bf16[80,2048]{1,0:T(8,128)(2,1)S(1)} collective-permute-done((bf16[80,2048]{1,0:T(8,128)(2,1)S(1)}, bf16[80,2048]{1,0:T(8,128)(2,1)S(1)}, u32[]{:S(2)}, u32[]{:S(2)}) %collective-permute-start.17) | collective-permute-done | bytes 327712 | tf_op jit(solution)/shard_map/ppermute | solution.py:24
  373.2 19.1 %collective-permute-done.18.refs_5_ = bf16[80,2048]{1,0:T(8,128)(2,1)S(1)} collective-permute-done((bf16[80,2048]{1,0:T(8,128)(2,1)S(1)}, bf16[80,2048]{1,0:T(8,128)(2,1)S(1)}, u32[]{:S(2)}, u32[]{:S(2)}) %collective-permute-start.18) | collective-permute-done | bytes 327712 | tf_op jit(solution)/shard_map/ppermute | solution.py:24
  393.2 3.1 shard_map.320
  396.3 7.4 %collective-permute-start.22 = (bf16[80,2048]{1,0:T(8,128)(2,1)}, bf16[80,2048]{1,0:T(8,128)(2,1)S(1)}, u32[]{:S(2)}, u32[]{:S(2)}) collective-permute-start(bf16[80,2048]{1,0:T(8,128)(2,1)} %get-tuple-element.211.refs_1_), channel_id=1, source_target_pairs={{0,3},{1,0},{2,1},{3,2},{4,7},{5,4},{6,5},{7,6},{8,11},{9,8},{10,9... | collective-permute-start | bytes 983048 | tf_op jit(solution)/shard_map/ppermute | solution.py:24
  405.6 9.2 %shard_map.321 = (bf16[640,2048]{1,0:T(8,128)(2,1)}, f32[8,128]{1,0:T(8,128)}) custom-call(bf16[320,1536]{1,0:T(8,128)(2,1)} %get-tuple-element.182.refs_0_, bf16[320,1536]{1,0:T(8,128)(2,1)} %get-tuple-element.185.refs_1_, bf16[1536,2048]{1,0:T(8,128)(2,1)} %all-gather.11.cloned.1.call-done.refs_5_.refs_8_.refs_2_, f32[8,128]{1,0:T(8,128)} %get-tuple-element.198.refs_3_), custom_call_target="tpu_custom_call" | custom-call | flops 100000000 | bytes 100000000 | tf_op jit(solution)/shard_map/pallas_call | solution.py:276
  414.8 10.8 %shard_map.322 = (bf16[1536,2048]{1,0:T(8,128)(2,1)}, f32[8,128]{1,0:T(8,128)}) custom-call(bf16[320,1536]{1,0:T(8,128)(2,1)} %get-tuple-element.182.refs_0_, bf16[320,1536]{1,0:T(8,128)(2,1)} %get-tuple-element.185.refs_1_, bf16[320,2048]{1,0:T(8,128)(2,1)} %get-tuple-element.203.refs_2_, bf16[320,2048]{1,0:T(8,128)(2,1)} %get-tuple-element.204.refs_3_, ...), custom_call_target="tpu_custom_call" | custom-call | flops 100000000 | bytes 100000000 | tf_op jit(solution)/shard_map/pallas_call | solution.py:276
  426.7 5.2 all-to-all-start.5
  431.9 7.4 %shard_map.323 = (bf16[320,2048]{1,0:T(8,128)(2,1)}, bf16[320,640]{1,0:T(8,128)(2,1)}, f32[320,640]{1,0:T(8,128)}, f32[320,640]{1,0:T(8,128)}, f32[2,640]{1,0:T(2,128)}, /*index=5*/f32[8,128]{1,0:T(8,128)}) custom-call(s32[1]{0:T(128)} %bitcast.2.refs_0_, bf16[320,2048]{1,0:T(8,128)(2,1)} %bitcast.68, ...), custom_call_target="tpu_custom_call" | custom-call | flops 74999996416 | bytes 74999996416 | tf_op jit(solution)/shard_map/pallas_call | solution.py:276
  440.3 8.2 %shard_map.324 = (bf16[320,2048]{1,0:T(8,128)(2,1)}, bf16[320,640]{1,0:T(8,128)(2,1)}, f32[320,640]{1,0:T(8,128)}, f32[320,640]{1,0:T(8,128)}, f32[2,640]{1,0:T(2,128)}, /*index=5*/f32[8,128]{1,0:T(8,128)}) custom-call(s32[1]{0:T(128)} %bitcast.2.refs_0_, bf16[80,2048]{1,0:T(8,128)(2,1)} %get-tuple-element.211.refs_1_, bf16[80,2048]{1,0:T(8,128)(2,1)} %copy-done.37, ...), custom_call_target="tpu_custom_call" | custom-call | flops 74999996416 | bytes 74999996416 | tf_op jit(solution)/shard_map/pallas_call | solution.py:276
  453.3 7.8 %shard_map.325 = (bf16[640,2048]{1,0:T(8,128)(2,1)}, f32[8,128]{1,0:T(8,128)}) custom-call(bf16[320,640]{1,0:T(8,128)(2,1)} %get-tuple-element.218.refs_0_, bf16[320,640]{1,0:T(8,128)(2,1)} %get-tuple-element.219.refs_1_, bf16[320,2048]{1,0:T(8,128)(2,1)} %get-tuple-element.220.refs_2_, bf16[320,2048]{1,0:T(8,128)(2,1)} %get-tuple-element.221.refs_3_, ...), custom_call_target="tpu_custom_call" | custom-call | flops 70000001024 | bytes 70000001024 | tf_op jit(solution)/shard_map/pallas_call | solution.py:276
  461.7 8.6 %shard_map.326 = (bf16[320,1280]{1,0:T(8,128)(2,1)}, f32[320,640]{1,0:T(8,128)}, f32[8,640]{1,0:T(8,128)}, f32[8,640]{1,0:T(8,128)}, f32[8,128]{1,0:T(8,128)}) custom-call(f32[320,640]{1,0:T(8,128)} %get-tuple-element.208.refs_0_, f32[320,640]{1,0:T(8,128)} %get-tuple-element.209.refs_1_, f32[1,640]{1,0:T(1,128)} %get-tuple-element.361.refs_2_, ...), custom_call_target="tpu_custom_call" | custom-call | flops 85000003584 | bytes 85000003584 | tf_op jit(solution)/shard_map/pallas_call | solution.py:276
  470.3 8.7 %shard_map.327 = (bf16[320,1280]{1,0:T(8,128)(2,1)}, f32[320,640]{1,0:T(8,128)}, f32[8,640]{1,0:T(8,128)}, f32[8,640]{1,0:T(8,128)}, f32[8,128]{1,0:T(8,128)}) custom-call(f32[320,640]{1,0:T(8,128)} %get-tuple-element.229.refs_0_, f32[320,640]{1,0:T(8,128)} %get-tuple-element.230.refs_1_, f32[1,640]{1,0:T(1,128)} %get-tuple-element.360.refs_2_, ...), custom_call_target="tpu_custom_call" | custom-call | flops 85000003584 | bytes 85000003584 | tf_op jit(solution)/shard_map/pallas_call | solution.py:276
  483.0 4.4 shard_map.328
  488.0 6.2 shard_map.329
  494.2 5.0 all-to-all-start.7
  499.1 3.2 shard_map.330
  503.0 6.6 %shard_map.331 = (bf16[320,1280]{1,0:T(8,128)(2,1)}, f32[1,2048]{1,0:T(1,128)}, bf16[80,2048]{1,0:T(8,128)(2,1)}, bf16[80,2048]{1,0:T(8,128)(2,1)}, bf16[80,2048...) custom-call(s32[1]{0:T(128)} %bitcast.2.refs_0_, bf16[320,640]{1,0:T(8,128)(2,1)} %get-tuple-element.244.refs_1_, ...), custom_call_target="tpu_custom_call" | custom-call | flops 62000001024 | bytes 62000001024 | tf_op jit(solution)/shard_map/pallas_call | solution.py:276
  510.8 10.7 %shard_map.332 = (bf16[2048,1280]{1,0:T(8,128)(2,1)}, f32[8,128]{1,0:T(8,128)}) custom-call(bf16[320,2048]{1,0:T(8,128)(2,1)} %get-tuple-element.226.refs_5_.refs_0_, bf16[320,2048]{1,0:T(8,128)(2,1)} %get-tuple-element.242.refs_5_.refs_1_, bf16[320,1280]{1,0:T(8,128)(2,1)} %get-tuple-element.243.refs_2_, bf16[320,1280]{1,0:T(8,128)(2,1)} %get-tuple-element.248.refs_3_, ...), custom_call_target="tpu_custom_call" | custom-call | flops 109999996928 | bytes 109999996928 | tf_op jit(solution)/shard_map/pallas_call | solution.py:276
  521.5 2.3 shard_map.333
  523.9 6.3 %collective-permute-start.31 = (bf16[8,160,160]{2,1,0:T(8,128)(2,1)}, bf16[8,160,160]{2,1,0:T(8,128)(2,1)S(1)}, u32[]{:S(2)}, u32[]{:S(2)}) collective-permute-start(bf16[8,160,160]{2,1,0:T(8,128)(2,1)} %get-tuple-element.251.refs_0_), channel_id=1, source_target_pairs={{0,12},{4,0},{8,4},{12,8},{1,13},{5,1},{9,5},{13,9},{2,14},{6,2},{... | collective-permute-start | bytes 1228808 | tf_op jit(solution)/shard_map/ppermute | solution.py:24
  535.5 14.0 %collective-permute-done.38 = f32[1,9216]{1,0:T(1,128)S(1)} collective-permute-done((f32[1,9216]{1,0:T(1,128)S(1)}, f32[1,9216]{1,0:T(1,128)S(1)}, u32[]{:S(2)}, u32[]{:S(2)}) %collective-permute-start.38) | collective-permute-done | bytes 36896 | tf_op jit(solution)/shard_map/ppermute | solution.py:24
  549.5 2.5 collective-permute-done.37
  552.8 3.0 collective-permute-start.40
  559.1 12.6 %collective-permute-start.29 = (bf16[8,160,160]{2,1,0:T(8,128)(2,1)S(1)}, bf16[8,160,160]{2,1,0:T(8,128)(2,1)S(1)}, u32[]{:S(2)}, u32[]{:S(2)}) collective-permute-start(bf16[8,160,160]{2,1,0:T(8,128)(2,1)S(1)} %copy-done.31), channel_id=1, source_target_pairs={{0,4},{4,8},{8,12},{12,0},{1,5},{5,9},{9,13},{13,1},{2,6},{6,10},{... | collective-permute-start | bytes 1228808 | tf_op jit(solution)/shard_map/ppermute | solution.py:24
  576.6 12.5 %collective-permute-done.29.refs_1_ = bf16[8,160,160]{2,1,0:T(8,128)(2,1)S(1)} collective-permute-done((bf16[8,160,160]{2,1,0:T(8,128)(2,1)S(1)}, bf16[8,160,160]{2,1,0:T(8,128)(2,1)S(1)}, u32[]{:S(2)}, u32[]{:S(2)}) %collective-permute-start.29) | collective-permute-done | bytes 409632 | tf_op jit(solution)/shard_map/ppermute | solution.py:24
  590.0 3.0 shard_map.334
  593.0 3.1 shard_map.335
  597.3 3.0 shard_map.336
  602.6 3.2 shard_map.337
  605.8 2.4 shard_map.338
  610.0 8.6 %reduce-scatter.5.cloned.1.call-done.refs_0_ = bf16[256,1280]{1,0:T(8,128)(2,1)} async-done(((bf16[2048,1280]{1,0:T(8,128)(2,1)}), bf16[256,1280]{1,0:T(8,128)(2,1)}) %reduce-scatter.5.cloned.1.call-update) | async-done | bytes 655376 | tf_op jit(solution)/shard_map/reduce_scatter | solution.py:856
  (256 shorter events, 79.5 us)
Async XLA Ops:
  7.2 66.0 %all-gather.5.cloned.1.call-start = ((), (), s32[]{:S(2)}) async-start(), calls=%async_computation.12 | async-start | bytes 5898240 | tf_op jit(solution)/shard_map/all_gather | solution.py:826
  9.3 127.6 %all-gather.7.cloned.1.call-start = ((), (), s32[]{:S(2)}) async-start(), calls=%async_computation.13 | async-start | bytes 2949120 | tf_op jit(solution)/shard_map/all_gather | solution.py:827
  10.0 208.4 %all-gather.11.cloned.1.call-start = ((), (), s32[]{:S(2)}) async-start(), calls=%async_computation.15 | async-start | bytes 7077888 | tf_op jit(solution)/shard_map/all_gather | solution.py:829
  14.6 52.9 %all-to-all-start = ((bf16[4,80,2048]{2,1,0:T(8,128)(2,1)}), bf16[4,80,2048]{2,1,0:T(8,128)(2,1)S(1)}, u32[]{:S(2)}, u32[]{:S(2)}) async-start(bf16[4,80,2048]{2,1,0:T(8,128)(2,1)} %bitcast.67), calls=%async_computation | async-start | bytes 2621440 | tf_op jit(solution)/shard_map/all_to_all | solution.py:307
  21.1 227.1 %all-gather.9.cloned.1.call-start = ((), (), s32[]{:S(2)}) async-start(), calls=%async_computation.14 | async-start | bytes 14155776 | tf_op jit(solution)/shard_map/all_gather | solution.py:828
  38.1 44.5 %collective-permute-start.3 = (bf16[80,2048]{1,0:T(8,128)(2,1)}, bf16[80,2048]{1,0:T(8,128)(2,1)S(1)}, u32[]{:S(2)}, u32[]{:S(2)}) collective-permute-start(bf16[80,2048]{1,0:T(8,128)(2,1)} %get-tuple-element.156.refs_1_), channel_id=1, source_target_pairs={{0,3},{1,0},{2,1},{3,2},{4,7},{5,4},{6,5},{7,6},{8,11},{9,8},{10,9... | collective-permute-start | bytes 983048 | tf_op jit(solution)/shard_map/ppermute | solution.py:24
  41.9 53.7 %collective-permute-start.2 = (bf16[80,2048]{1,0:T(8,128)(2,1)}, bf16[80,2048]{1,0:T(8,128)(2,1)S(1)}, u32[]{:S(2)}, u32[]{:S(2)}) collective-permute-start(bf16[80,2048]{1,0:T(8,128)(2,1)} %get-tuple-element.156.refs_1_), channel_id=1, source_target_pairs={{0,2},{1,3},{2,0},{3,1},{4,6},{5,7},{6,4},{7,5},{8,10},{9,11},{10,... | collective-permute-start | bytes 983048 | tf_op jit(solution)/shard_map/ppermute | solution.py:24
  41.9 53.7 %collective-permute-start.1 = (bf16[80,2048]{1,0:T(8,128)(2,1)}, bf16[80,2048]{1,0:T(8,128)(2,1)}, u32[]{:S(2)}, u32[]{:S(2)}) collective-permute-start(bf16[80,2048]{1,0:T(8,128)(2,1)} %get-tuple-element.156.refs_1_), channel_id=1, source_target_pairs={{0,1},{1,2},{2,3},{3,0},{4,5},{5,6},{6,7},{7,4},{8,9},{9,10},{10,1... | collective-permute-start | bytes 983048 | tf_op jit(solution)/shard_map/ppermute | solution.py:24
  68.6 68.2 %all-to-all-start.1 = ((bf16[4,160,2048]{2,1,0:T(8,128)(2,1)}), bf16[4,160,2048]{2,1,0:T(8,128)(2,1)}, u32[]{:S(2)}, u32[]{:S(2)}) async-start(bf16[4,160,2048]{2,1,0:T(8,128)(2,1)} %bitcast.17), calls=%async_computation.1 | async-start | bytes 5242880 | tf_op jit(solution)/shard_map/all_to_all | solution.py:307
  79.2 26.7 %collective-permute-start = (bf16[8,640]{1,0:T(8,128)(2,1)}, bf16[8,640]{1,0:T(8,128)(2,1)S(1)}, u32[]{:S(2)}, u32[]{:S(2)}) collective-permute-start(bf16[8,640]{1,0:T(8,128)(2,1)} %get-tuple-element.155), channel_id=1, source_target_pairs={{0,4},{4,8},{8,12},{1,5},{5,9},{9,13},{2,6},{6,10},{10,14},{3,7},{... | collective-permute-start | bytes 30728 | tf_op jit(solution)/shard_map/ppermute | solution.py:29
  102.5 17.0 %collective-permute-start.7 = (bf16[8,640]{1,0:T(8,128)(2,1)}, bf16[8,640]{1,0:T(8,128)(2,1)S(1)}, u32[]{:S(2)}, u32[]{:S(2)}) collective-permute-start(bf16[8,640]{1,0:T(8,128)(2,1)} %get-tuple-element.164), channel_id=1, source_target_pairs={{0,4},{4,8},{8,12},{1,5},{5,9},{9,13},{2,6},{6,10},{10,14},{3,7},{... | collective-permute-start | bytes 30728 | tf_op jit(solution)/shard_map/ppermute | solution.py:29
  113.4 16.2 %collective-permute-start.6 = (f32[2,640]{1,0:T(2,128)}, f32[2,640]{1,0:T(2,128)S(1)}, u32[]{:S(2)}, u32[]{:S(2)}) collective-permute-start(f32[2,640]{1,0:T(2,128)} %get-tuple-element.161), channel_id=1, source_target_pairs={{0,12},{1,13},{2,14},{3,15},{16,28},{17,29},{18,30},{19,31}} | collective-permute-start | bytes 15368 | tf_op jit(solution)/shard_map/ppermute | solution.py:29
  115.7 16.0 %collective-permute-start.5 = (f32[2,640]{1,0:T(2,128)}, f32[2,640]{1,0:T(2,128)S(1)}, u32[]{:S(2)}, u32[]{:S(2)}) collective-permute-start(f32[2,640]{1,0:T(2,128)} %get-tuple-element.161), channel_id=1, source_target_pairs={{0,8},{4,12},{1,9},{5,13},{2,10},{6,14},{3,11},{7,15},{16,24},{20,... | collective-permute-start | bytes 15368 | tf_op jit(solution)/shard_map/ppermute | solution.py:29
  117.5 14.2 %collective-permute-start.4 = (f32[2,640]{1,0:T(2,128)}, f32[2,640]{1,0:T(2,128)S(1)}, u32[]{:S(2)}, u32[]{:S(2)}) collective-permute-start(f32[2,640]{1,0:T(2,128)} %get-tuple-element.161), channel_id=1, source_target_pairs={{0,4},{4,8},{8,12},{1,5},{5,9},{9,13},{2,6},{6,10},{10,14},{3,7},{... | collective-permute-start | bytes 15368 | tf_op jit(solution)/shard_map/ppermute | solution.py:29
  127.0 19.1 %collective-permute-start.10 = (f32[2,640]{1,0:T(2,128)}, f32[2,640]{1,0:T(2,128)S(1)}, u32[]{:S(2)}, u32[]{:S(2)}) collective-permute-start(f32[2,640]{1,0:T(2,128)} %get-tuple-element.170), channel_id=1, source_target_pairs={{0,12},{1,13},{2,14},{3,15},{16,28},{17,29},{18,30},{19,31}} | collective-permute-start | bytes 15368 | tf_op jit(solution)/shard_map/ppermute | solution.py:29
  128.3 17.8 %collective-permute-start.9 = (f32[2,640]{1,0:T(2,128)}, f32[2,640]{1,0:T(2,128)S(1)}, u32[]{:S(2)}, u32[]{:S(2)}) collective-permute-start(f32[2,640]{1,0:T(2,128)} %get-tuple-element.170), channel_id=1, source_target_pairs={{0,8},{4,12},{1,9},{5,13},{2,10},{6,14},{3,11},{7,15},{16,24},{20,... | collective-permute-start | bytes 15368 | tf_op jit(solution)/shard_map/ppermute | solution.py:29
  129.6 16.5 %collective-permute-start.8 = (f32[2,640]{1,0:T(2,128)}, f32[2,640]{1,0:T(2,128)S(1)}, u32[]{:S(2)}, u32[]{:S(2)}) collective-permute-start(f32[2,640]{1,0:T(2,128)} %get-tuple-element.170), channel_id=1, source_target_pairs={{0,4},{4,8},{8,12},{1,5},{5,9},{9,13},{2,6},{6,10},{10,14},{3,7},{... | collective-permute-start | bytes 15368 | tf_op jit(solution)/shard_map/ppermute | solution.py:29
  142.5 49.5 %all-to-all-start.2 = ((bf16[4,80,2048]{2,1,0:T(8,128)(2,1)}), bf16[4,80,2048]{2,1,0:T(8,128)(2,1)S(1)}, u32[]{:S(2)}, u32[]{:S(2)}) async-start(bf16[4,80,2048]{2,1,0:T(8,128)(2,1)} %bitcast.71), calls=%async_computation.2 | async-start | bytes 2621440 | tf_op jit(solution)/shard_map/all_to_all | solution.py:313
  152.9 47.0 %collective-permute-start.11 = (bf16[80,2048]{1,0:T(8,128)(2,1)}, bf16[80,2048]{1,0:T(8,128)(2,1)S(1)}, u32[]{:S(2)}, u32[]{:S(2)}) collective-permute-start(bf16[80,2048]{1,0:T(8,128)(2,1)} %get-tuple-element.175), channel_id=1, source_target_pairs={{0,1},{1,2},{2,3},{3,0},{4,5},{5,6},{6,7},{7,4},{8,9},{9,10},{10,1... | collective-permute-start | bytes 983048 | tf_op jit(solution)/shard_map/ppermute | solution.py:24
  155.0 45.0 %collective-permute-start.12 = (bf16[80,2048]{1,0:T(8,128)(2,1)}, bf16[80,2048]{1,0:T(8,128)(2,1)S(1)}, u32[]{:S(2)}, u32[]{:S(2)}) collective-permute-start(bf16[80,2048]{1,0:T(8,128)(2,1)} %get-tuple-element.176), channel_id=1, source_target_pairs={{0,2},{1,3},{2,0},{3,1},{4,6},{5,7},{6,4},{7,5},{8,10},{9,11},{10,... | collective-permute-start | bytes 983048 | tf_op jit(solution)/shard_map/ppermute | solution.py:24
  157.3 42.6 %collective-permute-start.13 = (bf16[80,2048]{1,0:T(8,128)(2,1)}, bf16[80,2048]{1,0:T(8,128)(2,1)S(1)}, u32[]{:S(2)}, u32[]{:S(2)}) collective-permute-start(bf16[80,2048]{1,0:T(8,128)(2,1)} %get-tuple-element.177), channel_id=1, source_target_pairs={{0,3},{1,0},{2,1},{3,2},{4,7},{5,4},{6,5},{7,6},{8,11},{9,8},{10,9... | collective-permute-start | bytes 983048 | tf_op jit(solution)/shard_map/ppermute | solution.py:24
  196.1 52.1 %all-to-all-start.3 = ((bf16[4,80,2048]{2,1,0:T(8,128)(2,1)}), bf16[4,80,2048]{2,1,0:T(8,128)(2,1)S(1)}, u32[]{:S(2)}, u32[]{:S(2)}) async-start(bf16[4,80,2048]{2,1,0:T(8,128)(2,1)} %bitcast.72), calls=%async_computation.3 | async-start | bytes 2621440 | tf_op jit(solution)/shard_map/all_to_all | solution.py:307
  203.5 77.3 %collective-permute-start.16 = (bf16[80,2048]{1,0:T(8,128)(2,1)}, bf16[80,2048]{1,0:T(8,128)(2,1)}, u32[]{:S(2)}, u32[]{:S(2)}) collective-permute-start(bf16[80,2048]{1,0:T(8,128)(2,1)} %get-tuple-element.183.refs_1_), channel_id=1, source_target_pairs={{0,3},{1,0},{2,1},{3,2},{4,7},{5,4},{6,5},{7,6},{8,11},{9,8},{10,9... | collective-permute-start | bytes 983048 | tf_op jit(solution)/shard_map/ppermute | solution.py:24
  213.2 67.6 %collective-permute-start.15 = (bf16[80,2048]{1,0:T(8,128)(2,1)}, bf16[80,2048]{1,0:T(8,128)(2,1)}, u32[]{:S(2)}, u32[]{:S(2)}) collective-permute-start(bf16[80,2048]{1,0:T(8,128)(2,1)} %get-tuple-element.183.refs_1_), channel_id=1, source_target_pairs={{0,2},{1,3},{2,0},{3,1},{4,6},{5,7},{6,4},{7,5},{8,10},{9,11},{10,... | collective-permute-start | bytes 983048 | tf_op jit(solution)/shard_map/ppermute | solution.py:24
  218.4 62.4 %collective-permute-start.14 = (bf16[80,2048]{1,0:T(8,128)(2,1)}, bf16[80,2048]{1,0:T(8,128)(2,1)}, u32[]{:S(2)}, u32[]{:S(2)}) collective-permute-start(bf16[80,2048]{1,0:T(8,128)(2,1)} %get-tuple-element.183.refs_1_), channel_id=1, source_target_pairs={{0,1},{1,2},{2,3},{3,0},{4,5},{5,6},{6,7},{7,4},{8,9},{9,10},{10,1... | collective-permute-start | bytes 983048 | tf_op jit(solution)/shard_map/ppermute | solution.py:24
  276.4 34.1 %all-to-all-start.4 = ((bf16[4,80,2048]{2,1,0:T(8,128)(2,1)}), bf16[4,80,2048]{2,1,0:T(8,128)(2,1)}, u32[]{:S(2)}, u32[]{:S(2)}) async-start(bf16[4,80,2048]{2,1,0:T(8,128)(2,1)} %bitcast.73), calls=%async_computation.4 | async-start | bytes 2621440 | tf_op jit(solution)/shard_map/all_to_all | solution.py:313
  280.7 321.9 %reduce-scatter.11.cloned.1.call-start = ((), (), s32[]{:S(2)}) async-start(), calls=%async_computation.19 | async-start | bytes 14155776 | tf_op jit(solution)/shard_map/reduce_scatter | solution.py:856
  335.7 90.0 %all-to-all-start.6 = ((bf16[4,80,2048]{2,1,0:T(8,128)(2,1)}), bf16[4,80,2048]{2,1,0:T(8,128)(2,1)S(1)}, u32[]{:S(2)}, u32[]{:S(2)}) async-start(bf16[4,80,2048]{2,1,0:T(8,128)(2,1)} %bitcast.27), calls=%async_computation.6 | async-start | bytes 2621440 | tf_op jit(solution)/shard_map/all_to_all | solution.py:307
  339.4 64.9 %copy-start.24 = (f32[1,2048]{1,0:T(1,128)S(1)}, f32[1,2048]{1,0:T(1,128)}, u32[]{:S(2)}) copy-start(f32[1,2048]{1,0:T(1,128)} %get-tuple-element.266) | copy-start | bytes 24580
  339.4 266.4 %reduce-scatter.9.cloned.1.call-start = ((), (), s32[]{:S(2)}) async-start(), calls=%async_computation.18 | async-start | bytes 7077888 | tf_op jit(solution)/shard_map/reduce_scatter | solution.py:856
  339.5 33.7 %collective-permute-start.17 = (bf16[80,2048]{1,0:T(8,128)(2,1)S(1)}, bf16[80,2048]{1,0:T(8,128)(2,1)S(1)}, u32[]{:S(2)}, u32[]{:S(2)}) collective-permute-start(bf16[80,2048]{1,0:T(8,128)(2,1)S(1)} %copy-done.41), channel_id=1, source_target_pairs={{0,1},{1,2},{2,3},{3,0},{4,5},{5,6},{6,7},{7,4},{8,9},{9,10},{10,1... | collective-permute-start | bytes 983048 | tf_op jit(solution)/shard_map/ppermute | solution.py:24
  341.4 50.9 %collective-permute-start.18 = (bf16[80,2048]{1,0:T(8,128)(2,1)S(1)}, bf16[80,2048]{1,0:T(8,128)(2,1)S(1)}, u32[]{:S(2)}, u32[]{:S(2)}) collective-permute-start(bf16[80,2048]{1,0:T(8,128)(2,1)S(1)} %copy-done.39), channel_id=1, source_target_pairs={{0,2},{1,3},{2,0},{3,1},{4,6},{5,7},{6,4},{7,5},{8,10},{9,11},{10,... | collective-permute-start | bytes 983048 | tf_op jit(solution)/shard_map/ppermute | solution.py:24
  343.8 48.5 %collective-permute-start.19 = (bf16[80,2048]{1,0:T(8,128)(2,1)S(1)}, bf16[80,2048]{1,0:T(8,128)(2,1)S(1)}, u32[]{:S(2)}, u32[]{:S(2)}) collective-permute-start(bf16[80,2048]{1,0:T(8,128)(2,1)S(1)} %copy-done.38), channel_id=1, source_target_pairs={{0,3},{1,0},{2,1},{3,2},{4,7},{5,4},{6,5},{7,6},{8,11},{9,8},{10,9... | collective-permute-start | bytes 983048 | tf_op jit(solution)/shard_map/ppermute | solution.py:24
  373.2 19.2 %copy-start.14 = (bf16[80,2048]{1,0:T(8,128)(2,1)}, bf16[80,2048]{1,0:T(8,128)(2,1)S(1)}, u32[]{:S(2)}) copy-start(bf16[80,2048]{1,0:T(8,128)(2,1)S(1)} %collective-permute-done.17.refs_4_) | copy-start | bytes 983044
  396.3 43.0 %collective-permute-start.22 = (bf16[80,2048]{1,0:T(8,128)(2,1)}, bf16[80,2048]{1,0:T(8,128)(2,1)S(1)}, u32[]{:S(2)}, u32[]{:S(2)}) collective-permute-start(bf16[80,2048]{1,0:T(8,128)(2,1)} %get-tuple-element.211.refs_1_), channel_id=1, source_target_pairs={{0,3},{1,0},{2,1},{3,2},{4,7},{5,4},{6,5},{7,6},{8,11},{9,8},{10,9... | collective-permute-start | bytes 983048 | tf_op jit(solution)/shard_map/ppermute | solution.py:24
  403.7 35.6 %collective-permute-start.21 = (bf16[80,2048]{1,0:T(8,128)(2,1)}, bf16[80,2048]{1,0:T(8,128)(2,1)S(1)}, u32[]{:S(2)}, u32[]{:S(2)}) collective-permute-start(bf16[80,2048]{1,0:T(8,128)(2,1)} %get-tuple-element.211.refs_1_), channel_id=1, source_target_pairs={{0,2},{1,3},{2,0},{3,1},{4,6},{5,7},{6,4},{7,5},{8,10},{9,11},{10,... | collective-permute-start | bytes 983048 | tf_op jit(solution)/shard_map/ppermute | solution.py:24
  404.2 35.2 %collective-permute-start.20 = (bf16[80,2048]{1,0:T(8,128)(2,1)}, bf16[80,2048]{1,0:T(8,128)(2,1)S(1)}, u32[]{:S(2)}, u32[]{:S(2)}) collective-permute-start(bf16[80,2048]{1,0:T(8,128)(2,1)} %get-tuple-element.211.refs_1_), channel_id=1, source_target_pairs={{0,1},{1,2},{2,3},{3,0},{4,5},{5,6},{6,7},{7,4},{8,9},{9,10},{10,1... | collective-permute-start | bytes 983048 | tf_op jit(solution)/shard_map/ppermute | solution.py:24
  426.7 67.4 %all-to-all-start.5 = ((bf16[4,160,2048]{2,1,0:T(8,128)(2,1)}), bf16[4,160,2048]{2,1,0:T(8,128)(2,1)}, u32[]{:S(2)}, u32[]{:S(2)}) async-start(bf16[4,160,2048]{2,1,0:T(8,128)(2,1)} %bitcast.25), calls=%async_computation.5 | async-start | bytes 5242880 | tf_op jit(solution)/shard_map/all_to_all | solution.py:313
  431.9 176.3 %reduce-scatter.7.cloned.1.call-start = ((), (), s32[]{:S(2)}) async-start(), calls=%async_computation.17 | async-start | bytes 2949120 | tf_op jit(solution)/shard_map/reduce_scatter | solution.py:856
  449.4 11.7 %collective-permute-start.25 = (f32[4,640]{1,0:T(4,128)S(1)}, f32[4,640]{1,0:T(4,128)S(1)}, u32[]{:S(2)}, u32[]{:S(2)}) collective-permute-start(f32[4,640]{1,0:T(4,128)S(1)} %pad_maximum_fusion.2), channel_id=1, source_target_pairs={{12,0},{13,1},{14,2},{15,3},{28,16},{29,17},{30,18},{31,19}} | collective-permute-start | bytes 30728 | tf_op jit(solution)/shard_map/ppermute | solution.py:29
  450.7 10.4 %collective-permute-start.24 = (f32[4,640]{1,0:T(4,128)S(1)}, f32[4,640]{1,0:T(4,128)S(1)}, u32[]{:S(2)}, u32[]{:S(2)}) collective-permute-start(f32[4,640]{1,0:T(4,128)S(1)} %pad_maximum_fusion.2), channel_id=1, source_target_pairs={{8,0},{12,4},{9,1},{13,5},{10,2},{14,6},{11,3},{15,7},{24,16},{28,... | collective-permute-start | bytes 30728 | tf_op jit(solution)/shard_map/ppermute | solution.py:29
  452.0 9.1 %collective-permute-start.23 = (f32[4,640]{1,0:T(4,128)S(1)}, f32[4,640]{1,0:T(4,128)S(1)}, u32[]{:S(2)}, u32[]{:S(2)}) collective-permute-start(f32[4,640]{1,0:T(4,128)S(1)} %pad_maximum_fusion.2), channel_id=1, source_target_pairs={{4,0},{8,4},{12,8},{5,1},{9,5},{13,9},{6,2},{10,6},{14,10},{7,3},{... | collective-permute-start | bytes 30728 | tf_op jit(solution)/shard_map/ppermute | solution.py:29
  480.4 7.0 %collective-permute-start.26 = (f32[8,640]{1,0:T(8,128)S(1)}, f32[8,640]{1,0:T(8,128)S(1)}, u32[]{:S(2)}, u32[]{:S(2)}) collective-permute-start(f32[8,640]{1,0:T(8,128)S(1)} %copy-done.47), channel_id=1, source_target_pairs={{4,0},{8,4},{12,8},{5,1},{9,5},{13,9},{6,2},{10,6},{14,10},{7,3},{... | collective-permute-start | bytes 61448 | tf_op jit(solution)/shard_map/ppermute | solution.py:29
  481.7 20.7 %collective-permute-start.28 = (f32[8,640]{1,0:T(8,128)}, f32[8,640]{1,0:T(8,128)S(1)}, u32[]{:S(2)}, u32[]{:S(2)}) collective-permute-start(f32[8,640]{1,0:T(8,128)} %get-tuple-element.246), channel_id=1, source_target_pairs={{4,0},{8,4},{12,8},{5,1},{9,5},{13,9},{6,2},{10,6},{14,10},{7,3},{... | collective-permute-start | bytes 61448 | tf_op jit(solution)/shard_map/ppermute | solution.py:29
  487.4 34.1 %collective-permute-start.27 = (bf16[8,160,160]{2,1,0:T(8,128)(2,1)}, bf16[8,160,160]{2,1,0:T(8,128)(2,1)}, u32[]{:S(2)}, u32[]{:S(2)}) collective-permute-start(bf16[8,160,160]{2,1,0:T(8,128)(2,1)} %get-tuple-element.241.refs_0_), channel_id=1, source_target_pairs={{0,16},{16,0},{1,17},{17,1},{2,18},{18,2},{3,19},{19,3},{4,20},{20... | collective-permute-start | bytes 1228808 | tf_op jit(solution)/shard_map/ppermute | solution.py:24
  494.2 98.8 %all-to-all-start.7 = ((bf16[4,80,2048]{2,1,0:T(8,128)(2,1)}), bf16[4,80,2048]{2,1,0:T(8,128)(2,1)}, u32[]{:S(2)}, u32[]{:S(2)}) async-start(bf16[4,80,2048]{2,1,0:T(8,128)(2,1)} %bitcast.65), calls=%async_computation.7 | async-start | bytes 2621440 | tf_op jit(solution)/shard_map/all_to_all | solution.py:313
  499.1 119.5 %reduce-scatter.5.cloned.1.call-start = ((), (), s32[]{:S(2)}) async-start(), calls=%async_computation.16 | async-start | bytes 5898240 | tf_op jit(solution)/shard_map/reduce_scatter | solution.py:856
  510.5 19.7 %collective-permute-start.35 = (f32[1,9216]{1,0:T(1,128)S(1)}, f32[1,9216]{1,0:T(1,128)S(1)}, u32[]{:S(2)}, u32[]{:S(2)}) collective-permute-start(f32[1,9216]{1,0:T(1,128)S(1)} %constant_dynamic-update-slice_fusion), channel_id=1, source_target_pairs={{0,16},{16,0},{1,17},{17,1},{2,18},{18,2},{3,19},{19,3},{4,20},{20... | collective-permute-start | bytes 110600 | tf_op jit(solution)/shard_map/ppermute | solution.py:24
  521.5 13.0 %copy-start.12 = (bf16[80,2048]{1,0:T(8,128)(2,1)S(1)}, bf16[80,2048]{1,0:T(8,128)(2,1)}, u32[]{:S(2)}) copy-start(bf16[80,2048]{1,0:T(8,128)(2,1)} %get-tuple-element.237) | copy-start | bytes 983044
  521.5 13.0 %copy-start.13 = (bf16[80,2048]{1,0:T(8,128)(2,1)S(1)}, bf16[80,2048]{1,0:T(8,128)(2,1)}, u32[]{:S(2)}) copy-start(bf16[80,2048]{1,0:T(8,128)(2,1)} %get-tuple-element.238) | copy-start | bytes 983044
  523.9 52.2 %collective-permute-start.31 = (bf16[8,160,160]{2,1,0:T(8,128)(2,1)}, bf16[8,160,160]{2,1,0:T(8,128)(2,1)S(1)}, u32[]{:S(2)}, u32[]{:S(2)}) collective-permute-start(bf16[8,160,160]{2,1,0:T(8,128)(2,1)} %get-tuple-element.251.refs_0_), channel_id=1, source_target_pairs={{0,12},{4,0},{8,4},{12,8},{1,13},{5,1},{9,5},{13,9},{2,14},{6,2},{... | collective-permute-start | bytes 1228808 | tf_op jit(solution)/shard_map/ppermute | solution.py:24
  530.2 46.4 %collective-permute-start.30 = (bf16[8,160,160]{2,1,0:T(8,128)(2,1)}, bf16[8,160,160]{2,1,0:T(8,128)(2,1)S(1)}, u32[]{:S(2)}, u32[]{:S(2)}) collective-permute-start(bf16[8,160,160]{2,1,0:T(8,128)(2,1)} %get-tuple-element.251.refs_0_), channel_id=1, source_target_pairs={{0,8},{4,12},{8,0},{12,4},{1,9},{5,13},{9,1},{13,5},{2,10},{6,14},... | collective-permute-start | bytes 1228808 | tf_op jit(solution)/shard_map/ppermute | solution.py:24
  530.2 19.3 %collective-permute-start.38 = (f32[1,9216]{1,0:T(1,128)S(1)}, f32[1,9216]{1,0:T(1,128)S(1)}, u32[]{:S(2)}, u32[]{:S(2)}) collective-permute-start(f32[1,9216]{1,0:T(1,128)S(1)} %add.110), channel_id=1, source_target_pairs={{0,12},{4,0},{8,4},{12,8},{1,13},{5,1},{9,5},{13,9},{2,14},{6,2},{... | collective-permute-start | bytes 110600 | tf_op jit(solution)/shard_map/ppermute | solution.py:24
  530.3 21.8 %collective-permute-start.37 = (f32[1,9216]{1,0:T(1,128)S(1)}, f32[1,9216]{1,0:T(1,128)S(1)}, u32[]{:S(2)}, u32[]{:S(2)}) collective-permute-start(f32[1,9216]{1,0:T(1,128)S(1)} %add.110), channel_id=1, source_target_pairs={{0,8},{4,12},{8,0},{12,4},{1,9},{5,13},{9,1},{13,5},{2,10},{6,14},... | collective-permute-start | bytes 110600 | tf_op jit(solution)/shard_map/ppermute | solution.py:24
  532.4 19.7 %collective-permute-start.36 = (f32[1,9216]{1,0:T(1,128)S(1)}, f32[1,9216]{1,0:T(1,128)S(1)}, u32[]{:S(2)}, u32[]{:S(2)}) collective-permute-start(f32[1,9216]{1,0:T(1,128)S(1)} %add.110), channel_id=1, source_target_pairs={{0,4},{4,8},{8,12},{12,0},{1,5},{5,9},{9,13},{13,1},{2,6},{6,10},{... | collective-permute-start | bytes 110600 | tf_op jit(solution)/shard_map/ppermute | solution.py:24
  535.5 22.3 %copy-start.21 = (f32[640]{0:T(1024)S(1)}, f32[640]{0:T(1024)}, u32[]{:S(2)}) copy-start(f32[640]{0:T(1024)} %param.29) | copy-start | bytes 7684
  535.5 23.6 %copy-start.31 = (bf16[8,160,160]{2,1,0:T(8,128)(2,1)S(1)}, bf16[8,160,160]{2,1,0:T(8,128)(2,1)}, u32[]{:S(2)}) copy-start(bf16[8,160,160]{2,1,0:T(8,128)(2,1)} %get-tuple-element.251.refs_0_) | copy-start | bytes 1228804
  552.8 6.3 %collective-permute-start.40 = (f32[1,4096]{1,0:T(1,128)S(1)}, f32[1,4096]{1,0:T(1,128)S(1)}, u32[]{:S(2)}, u32[]{:S(2)}) collective-permute-start(f32[1,4096]{1,0:T(1,128)S(1)} %slice.260), channel_id=1, source_target_pairs={{0,2},{1,3},{2,0},{3,1},{4,6},{5,7},{6,4},{7,5},{8,10},{9,11},{10,... | collective-permute-start | bytes 49160 | tf_op jit(solution)/shard_map/ppermute | solution.py:24
  555.8 15.9 %collective-permute-start.41 = (f32[1,4096]{1,0:T(1,128)S(1)}, f32[1,4096]{1,0:T(1,128)S(1)}, u32[]{:S(2)}, u32[]{:S(2)}) collective-permute-start(f32[1,4096]{1,0:T(1,128)S(1)} %slice.260), channel_id=1, source_target_pairs={{0,3},{1,0},{2,1},{3,2},{4,7},{5,4},{6,5},{7,6},{8,11},{9,8},{10,9... | collective-permute-start | bytes 49160 | tf_op jit(solution)/shard_map/ppermute | solution.py:24
  557.2 15.9 %collective-permute-start.39 = (f32[1,4096]{1,0:T(1,128)S(1)}, f32[1,4096]{1,0:T(1,128)S(1)}, u32[]{:S(2)}, u32[]{:S(2)}) collective-permute-start(f32[1,4096]{1,0:T(1,128)S(1)} %slice.260), channel_id=1, source_target_pairs={{0,1},{1,2},{2,3},{3,0},{4,5},{5,6},{6,7},{7,4},{8,9},{9,10},{10,1... | collective-permute-start | bytes 49160 | tf_op jit(solution)/shard_map/ppermute | solution.py:24
  559.1 30.1 %collective-permute-start.29 = (bf16[8,160,160]{2,1,0:T(8,128)(2,1)S(1)}, bf16[8,160,160]{2,1,0:T(8,128)(2,1)S(1)}, u32[]{:S(2)}, u32[]{:S(2)}) collective-permute-start(bf16[8,160,160]{2,1,0:T(8,128)(2,1)S(1)} %copy-done.31), channel_id=1, source_target_pairs={{0,4},{4,8},{8,12},{12,0},{1,5},{5,9},{9,13},{13,1},{2,6},{6,10},{... | collective-permute-start | bytes 1228808 | tf_op jit(solution)/shard_map/ppermute | solution.py:24
  571.6 25.7 %collective-permute-start.32 = (bf16[80,2048]{1,0:T(8,128)(2,1)}, bf16[80,2048]{1,0:T(8,128)(2,1)}, u32[]{:S(2)}, u32[]{:S(2)}) collective-permute-start(bf16[80,2048]{1,0:T(8,128)(2,1)} %get-tuple-element.257), channel_id=1, source_target_pairs={{0,1},{1,2},{2,3},{3,0},{4,5},{5,6},{6,7},{7,4},{8,9},{9,10},{10,1... | collective-permute-start | bytes 983048 | tf_op jit(solution)/shard_map/ppermute | solution.py:24
  573.1 24.2 %collective-permute-start.33 = (bf16[80,2048]{1,0:T(8,128)(2,1)}, bf16[80,2048]{1,0:T(8,128)(2,1)}, u32[]{:S(2)}, u32[]{:S(2)}) collective-permute-start(bf16[80,2048]{1,0:T(8,128)(2,1)} %get-tuple-element.258), channel_id=1, source_target_pairs={{0,2},{1,3},{2,0},{3,1},{4,6},{5,7},{6,4},{7,5},{8,10},{9,11},{10,... | collective-permute-start | bytes 983048 | tf_op jit(solution)/shard_map/ppermute | solution.py:24
  576.1 21.2 %collective-permute-start.34 = (bf16[80,2048]{1,0:T(8,128)(2,1)}, bf16[80,2048]{1,0:T(8,128)(2,1)}, u32[]{:S(2)}, u32[]{:S(2)}) collective-permute-start(bf16[80,2048]{1,0:T(8,128)(2,1)} %get-tuple-element.259), channel_id=1, source_target_pairs={{0,3},{1,0},{2,1},{3,2},{4,7},{5,4},{6,5},{7,6},{8,11},{9,8},{10,9... | collective-permute-start | bytes 983048 | tf_op jit(solution)/shard_map/ppermute | solution.py:24
  (45 other events, 220.3 us)
Sparse Core Ops, SparseCore 0:
  10.5 43.8 all-gather.4
  56.2 30.4 all-gather.6
  88.6 46.8 all-gather.10
  137.8 72.2 all-gather.8
  335.8 91.4 reduce-scatter.10
  430.6 62.4 reduce-scatter.8
  496.7 47.4 reduce-scatter.6
  548.0 70.6 reduce-scatter.4

commit v3 on v2

--- a/solution.py
+++ b/solution.py
@@ -16,7 +16,7 @@
 GELU_A = 0.7978845608028654
 GELU_B = 0.044715
 LONG = 10**4
-RATE = 1e10
+RATE = 3e9
 
 
 def shift(value, axis, by):
@@ -137,7 +137,7 @@
         run[0:1] = jnp.ones_like(run[0:1])
         run[1:2] = jnp.zeros_like(run[1:2])
         assemble(blocks, wide_ref)
-        mixed_all[...] = dot_nt(wide_ref[...], weight_ref[...])
+        mixed_all[...] = jnp.dot(wide_ref[...], weight_ref[...], preferred_element_type=F32)
 
     mixed = mixed_all[pl.ds(pl.multiple_of(place * rows, TILE), rows)]
     value, slope = gelu_parts(branch_ref[...])
@@ -260,11 +260,19 @@
     return lax.dot_general(left, right, (((0,), (0,)), ((), ())), preferred_element_type=F32)
 
 
+COSTS = (
+    0.2, 3, 0.2, 6, 6, 7, 7, 5.7, 5.7, 3, 3, 27, 27, 3.4, 21, 60, 0.01, 0.01, 7.5, 7.5, 6, 7, 8, 40.0, 40.0, 0.01, 0.01, 0.01, 0.01, 0.01, 0.01, 0.01, 0.01, 0.01, 3, 10000.0, 1, 3,
+)
+
+
 class Clock:
     def __init__(self):
         self.tick = jnp.zeros((TILE, 128), F32)
+        self.calls = 0
 
     def call(self, kernel, grid, operands, in_specs, out_specs, out_shape, scratch=(), after=(), cost=3.0):
+        cost = COSTS[self.calls] if self.calls < len(COSTS) else cost
+        self.calls += 1
         count, extra, outs = len(operands), len(after) + 1, len(out_shape)
 
         def body(*refs):
@@ -400,8 +408,8 @@
         halo_ref[...] = value[value.shape[0] - TILE :].astype(BF16)
 
 
-def project(clock, place, blocks, weight, after=()):
-    model, cols = weight.shape
+def project(clock, place, blocks, weight, cols, after=()):
+    model = weight.shape[0]
     rows = sum(block.shape[0] for block in blocks)
     width = cols // 2
     return clock.call(
@@ -422,7 +430,7 @@
         states_ref[...] = states
         mixed_ref[...] = (states * gelu_parts(branch_ref[...])[0]).astype(BF16)
 
-    value = jnp.dot(mixed_ref[...], weight_ref[...], preferred_element_type=F32)
+    value = dot_nt(mixed_ref[...], weight_ref[...])
     deal(value, place_ref, refs[2 : 2 + outs], refs[-1])
 
 
@@ -436,13 +444,13 @@
 
 def mix_out(clock, place, local, prods, state_in, both_pre, weight, outs, tile, after=()):
     rows, width = local.shape
-    cols = weight.shape[1]
+    cols = weight.shape[0]
     part_spec, part_shape, work = part_specs(rows, cols, tile, outs)
     results = clock.call(
         partial(mix_kernel, outs), (cols // tile,), [place, local, prods, state_in, both_pre, weight],
         [place_spec(), held(local), held(prods), held(state_in),
          pl.BlockSpec((rows, width), lambda j: (0, 0), pipeline_mode=pl.Buffered(1)),
-         pl.BlockSpec((width, tile), lambda j: (0, j))],
+         pl.BlockSpec((tile, width), lambda j: (j, 2))],
         [kept((rows, width)), kept((rows, width))] + part_spec,
         [shape((rows, width), F32), shape((rows, width), BF16)] + part_shape, [work], after,
         cost=5.7,
@@ -458,12 +466,13 @@
     repeat_to(out_ref, (resid * lax.rsqrt(mean_of(resid * resid) + EPS) * gain_ref[...]).astype(BF16), rows)
 
 
-def second(clock, x, gain, terms, copies):
+def second(clock, x, gain, terms, copies, after=()):
     rows, model = x.shape
     return clock.call(
         second_kernel, (1,), [x, gain, *terms], [held(x), held(gain)] + [held(t) for t in terms],
         [kept((rows, model)), kept((copies * rows, model))],
         [shape((rows, model), F32), shape((copies * rows, model), BF16)],
+        after=after,
         cost=3.0,
     )
 
@@ -487,7 +496,7 @@
     gate_val, gate_slope = gelu_parts(jnp.dot(two, gate_w, preferred_element_type=F32))
     up_pre = jnp.dot(two, up_w, preferred_element_type=F32)
     hidden_ref[...] = (gate_val * up_pre).astype(BF16)
-    hidden_grad = dot_nt(cot_ref[...], down_ref[...])
+    hidden_grad = jnp.dot(cot_ref[...], down_ref[...], preferred_element_type=F32)
     gate_low = (hidden_grad * up_pre * gate_slope).astype(BF16)
     up_low = (hidden_grad * gate_val).astype(BF16)
     pair_ref[0] = gate_low
@@ -510,16 +519,16 @@
             out[...] = acc[pl.ds(start, rows)].astype(BF16)
 
 
-def mlp(clock, place, two_blocks, cot_all, turn, turns, unit, pair_w, down_w, outs, tile, after=()):
-    units, model = down_w.shape
+def mlp(clock, place, two_blocks, cot_all, turn, turns, unit, weight, outs, tile, after=()):
+    model, units = weight.shape[0], weight.shape[1] // 3
     rows = sum(block.shape[0] for block in two_blocks)
     steps = units // tile
     results = clock.call(
         partial(mlp_kernel, len(two_blocks), turn, turns, unit, outs), (steps,),
-        [place, *two_blocks, cot_all, pair_w, pair_w, down_w],
+        [place, *two_blocks, cot_all, weight, weight, weight],
         [place_spec()] + [held(b) for b in two_blocks + [cot_all]]
         + [pl.BlockSpec((model, tile), lambda j: (0, j)), pl.BlockSpec((model, tile), lambda j: (0, steps + j)),
-           pl.BlockSpec((tile, model), lambda j: (j, 0))],
+           pl.BlockSpec((model, tile), lambda j: (0, 2 * steps + j))],
         [kept((rows, model)), kept((rows, model)), pl.BlockSpec((rows, tile), lambda j: (0, j)),
          pl.BlockSpec((2, rows, tile), lambda j: (0, 0, j))] + [kept((rows // outs, model))] * outs,
         [shape((rows, model), BF16), shape((rows, model), BF16), shape((rows, units), BF16),
@@ -533,19 +542,19 @@
 def down_kernel(count, unit, *refs):
     right, out_ref = refs[count], refs[-1]
     for i in range(count):
-        value = jnp.dot(refs[i][...], right[...], preferred_element_type=F32).astype(BF16)
+        value = dot_nt(refs[i][...], right[...]).astype(BF16)
         for k in range(value.shape[0] // unit):
             start = (k * count + i) * unit
             out_ref[start : start + unit] = value[k * unit : (k + 1) * unit]
 
 
 def down_out(clock, lefts, right, unit, tile):
-    depth, cols = right.shape
+    cols, depth = right.shape[0], lefts[0].shape[1]
     count = len(lefts)
     total = count * lefts[0].shape[0]
     return clock.call(
         partial(down_kernel, count, unit), (cols // tile,), [*lefts, right],
-        [held(a) for a in lefts] + [pl.BlockSpec((depth, tile), lambda j: (0, j))],
+        [held(a) for a in lefts] + [pl.BlockSpec((tile, depth), lambda j: (j, 2))],
         [pl.BlockSpec((total, tile), lambda j: (0, j))], [shape((total, cols), BF16)],
         cost=0.01,
     )[0]
@@ -580,7 +589,8 @@
 
 
 def back_kernel(outs, place_ref, branch_ref, inner_ref, edge_ref, weight_ref, one_ref, *refs):
-    both_ref, gain_ref = refs[:2]
+    low_ref, gain_ref = refs[:2]
+    both_ref, work = refs[-2:]
     rows, width = branch_ref.shape
 
     @pl.when(pl.program_id(0) == 0)
@@ -590,10 +600,11 @@
         last = inner_ref[rows - 2 * TILE :]
         fixed = jnp.concatenate([last[:TILE], last[TILE:] + edge_ref[...]], axis=0)
         both_ref[rows - 2 * TILE :, width:] = fixed.astype(BF16)
+        low_ref[...] = both_ref[:, width:]
 
     value = dot_nt(both_ref[...], weight_ref[...])
     gain_ref[...] = jnp.sum(value * one_ref[...].astype(F32), axis=0, keepdims=True)
-    deal(value, place_ref, refs[2 : 2 + outs], refs[-1])
+    deal(value, place_ref, refs[2 : 2 + outs], work)
 
 
 def back_one(clock, place, branch_low, inner_grad, edge_in, weight, wide_one, outs, tile):
@@ -604,8 +615,9 @@
         partial(back_kernel, outs), (model // tile,), [place, branch_low, inner_grad, edge_in, weight, wide_one],
         [place_spec(), held(branch_low), held(inner_grad), held(edge_in),
          pl.BlockSpec((tile, 2 * width), lambda j: (j, 0)), pl.BlockSpec((rows, tile), lambda j: (0, j))],
-        [kept((rows, 2 * width)), pl.BlockSpec((1, tile), lambda j: (0, j))] + part_spec,
-        [shape((rows, 2 * width), BF16), shape((1, model), F32)] + part_shape, [work],
+        [kept((rows, width)), pl.BlockSpec((1, tile), lambda j: (0, j))] + part_spec,
+        [shape((rows, width), BF16), shape((1, model), F32)] + part_shape,
+        [pltpu.VMEM((rows, 2 * width), BF16), work],
         cost=6.2,
     )
     return results[0], results[1], results[2:]
@@ -617,11 +629,11 @@
     out_ref[...] = resid_ref[...] + norm_grad(x_ref[...].astype(F32), grad, gain_ref[...])[0]
 
 
-def last(clock, x, resid_grad, gain, terms):
+def last(clock, x, resid_grad, gain, terms, cost):
     return clock.call(
         last_kernel, (1,), [x, resid_grad, gain, *terms],
         [held(x), held(resid_grad), held(gain)] + [held(t) for t in terms],
-        [kept(resid_grad.shape)], [shape(resid_grad.shape, F32)], cost=LONG,
+        [kept(resid_grad.shape)], [shape(resid_grad.shape, F32)], cost=cost,
     )[0]
 
 
@@ -646,14 +658,15 @@
     )
 
 
+def stack_rows(refs):
+    return jnp.concatenate(refs, axis=0) if len(refs) > 1 else refs[0]
+
+
 def term_kernel(count, *refs):
-    out_ref = refs[-1]
-    total = None
-    for i in range(count):
-        right = refs[count + i]
-        value = dot_tn(refs[i][...], right[0] if len(right.shape) == 3 else right[...])
-        total = value if total is None else total + value
-    out_ref[...] = total.astype(out_ref.dtype)
+    halved = len(refs[count].shape) == 3
+    left = stack_rows([refs[i][...] for i in range(count)])
+    right = stack_rows([refs[count + i][0] if halved else refs[count + i][...] for i in range(count)])
+    refs[-1][...] = dot_tn(left, right).astype(refs[-1].dtype)
 
 
 def weight_term(clock, lefts, rights, tile, cost, after=()):
@@ -702,18 +715,74 @@
     )[0]
 
 
-def widen_kernel(width, in_ref, *outs):
-    value = in_ref[...].astype(F32)
-    for i, out in enumerate(outs):
-        out[...] = value[:, i * width : (i + 1) * width]
-
-
-def finish(clock, low, pieces):
-    rows, cols = low.shape
-    width = cols // pieces
-    return clock.call(
-        partial(widen_kernel, width), (1,), [low], [held(low)], [kept((rows, width))] * pieces,
-        [shape((rows, width), F32)] * pieces, cost=LONG,
+def split_term_kernel(count, groups, unit, place_ref, *refs):
+    k, c = pl.program_id(0), pl.program_id(1)
+    owner = lax.rem(place_ref[0] + k, groups) * pl.num_programs(1) + c
+    start = pl.multiple_of(owner * unit, unit)
+    left = stack_rows([refs[i][:, pl.ds(start, unit)] for i in range(count)])
+    total = dot_tn(left, stack_rows([refs[count + i][...] for i in range(count)])).astype(BF16)
+    for g in range(groups):
+        @pl.when(k == g)
+        def _(g=g):
+            refs[2 * count + g][...] = total
+
+
+def split_term(clock, place, lefts, rights, groups, steps, cost, after=()):
+    count = len(lefts)
+    depth = lefts[0].shape[1]
+    cols = rights[0].size // rights[0].shape[-2]
+    unit = depth // (groups * steps)
+
+    def spec(g):
+        return pl.BlockSpec(
+            (unit, cols), lambda k, c: (jnp.where(k < g, 0, jnp.where(k > g, steps - 1, c)), 0)
+        )
+
+    parts = clock.call(
+        partial(split_term_kernel, count, groups, unit), (groups, steps), [place, *lefts, *rights],
+        [place_spec()] + [held(a) for a in lefts] + [held(a) for a in rights],
+        [spec(g) for g in range(groups)], [shape((unit * steps, cols), BF16)] * groups, after=after, cost=cost,
+    )
+    return [parts[0]] + [shift(parts[k], "fsdp", k) for k in range(1, groups)]
+
+
+def member_kernel(groups, *refs):
+    out_ref = refs[-1]
+    col = 0
+    for i in range(0, len(refs) - 1, groups):
+        total = added(refs[i : i + groups], refs[i].shape[0])
+        out_ref[:, col : col + total.shape[1]] = total.astype(BF16)
+        col += total.shape[1]
+
+
+def member_sums(clock, terms, cost=8.0):
+    flat = [t for some in terms for t in some]
+    rows, cols = flat[0].shape[0], sum(some[0].shape[1] for some in terms)
+    tile = rows // 4
+    added_up = clock.call(
+        partial(member_kernel, len(terms[0])), (4,), flat,
+        [pl.BlockSpec((tile, t.shape[1]), lambda j: (j, 0)) for t in flat],
+        [pl.BlockSpec((tile, cols), lambda j: (j, 0))], [shape((rows, cols), BF16)], cost=cost,
+    )[0]
+    return lax.psum_scatter(added_up, "context", scatter_dimension=0, tiled=True)
+
+
+def turned_kernel(cuts, in_ref, *outs):
+    total = in_ref[...].astype(F32)
+    col = 0
+    for out, turned in zip(outs, cuts):
+        step = out.shape[0] if turned else out.shape[1]
+        piece = total[:, col : col + step]
+        out[...] = piece.T if turned else piece
+        col += step
+
+
+def turned_pieces(clock, low, cuts):
+    rows = low.shape[0]
+    dims = [(cols, rows) if turned else (rows, cols) for cols, turned in cuts]
+    return clock.call(
+        partial(turned_kernel, [turned for _, turned in cuts]), (1,), [low], [held(low)], [kept(d) for d in dims],
+        [shape(d, F32) for d in dims], cost=3.0,
     )
 
 
@@ -750,11 +819,11 @@
 def reverse_scan(clock, place, blocks, out_w, both_pre, states, decays, parts, after=()):
     total, width = states.shape
     rows = total // parts
-    model = out_w.shape[1]
+    model = out_w.shape[0]
     spec = rows_spec(rows, width, parts, reverse=True)
     return clock.call(
         partial(reverse_kernel, len(blocks)), (parts,), [place, *blocks, out_w, both_pre, states, decays],
-        [place_spec()] + [held(b) for b in blocks] + [held(out_w), spec, spec, spec],
+        [place_spec()] + [held(b) for b in blocks] + [pl.BlockSpec((model, width), lambda step: (0, 2), pipeline_mode=pl.Buffered(1)), spec, spec, spec],
         [kept((total, model)), spec, spec, spec, kept((2, width))],
         [shape((total, model), BF16), shape((total, width), BF16), shape((total, width), F32),
          shape((total, width), F32), shape((2, width), F32)],
@@ -819,14 +888,17 @@
     span = rows * parts
     width = conv_bias.shape[0]
     blocks = rate_weight.shape[0]
+    units = gate_weight.shape[1]
     chains = [(m, s) for m in range(micro) for s in range(seqs)]
     context_pos = lax.axis_index("context")
     owners = ("fsdp", "context")
 
-    both_w = lax.all_gather(jnp.concatenate([branch_weight, inner_weight], 1), owners, axis=0, tiled=True)
-    out_w = lax.all_gather(out_weight, owners, axis=1, tiled=True)
-    pair_w = lax.all_gather(jnp.concatenate([gate_weight, up_weight], 1), owners, axis=0, tiled=True)
-    down_w = lax.all_gather(down_weight, owners, axis=1, tiled=True)
+    first_w = lax.all_gather(
+        jnp.concatenate([branch_weight, inner_weight, out_weight.T], 1), owners, axis=0, tiled=True
+    )
+    second_w = lax.all_gather(
+        jnp.concatenate([gate_weight, up_weight, down_weight.T], 1), owners, axis=0, tiled=True
+    )
     gate_w = jnp.concatenate([block_diagonal(rate_weight), block_diagonal(input_weight)], axis=1)
     slope = -CPOW * jax.nn.softplus(-decay_param)
     params = jnp.concatenate(
@@ -852,97 +924,120 @@
     mask = [masks_of(segments[m, s]) for m, s in chains]
     clock = Clock()
 
-    def share(term, dim):
-        return lax.psum_scatter(term, owners, scatter_dimension=dim, tiled=True)
-
+    groups, members = lax.axis_size("fsdp"), lax.axis_size("context")
+    group_place = lax.axis_index("fsdp").reshape(1).astype(jnp.int32)
     normed = [first(clock, x_rows[0], gain_one_row, copies[0])]
     cot_copies = all_copies(clock, cot_rows, parts, (gate_w, params, *mask))
     normed += [first(clock, x_rows[i], gain_one_row, copies[i]) for i in turns if i]
     one_blocks = [spread(normed[i], apart[i]) for i in turns]
     (cot_all,) = spread(cot_copies, False)
-    projections = [project(clock, place, one_blocks[i], both_w) for i in turns]
+    projections, halo, scans, mixes, ends_in = [], [], [], [], []
+
+    def start_chain(i):
+        projections.append(project(clock, place, one_blocks[i], first_w, 2 * width))
+        halo.append(step_by(projections[i][2], "context", 1))
+
+    def scan_chain(i):
+        scans.append(forward_scan(clock, projections[i][1], halo[i], mask[i], params, gate_w, parts))
+        ends_in.append(carry_over(scans[i][5], 1))
+
+    def mix_chain(i):
+        mixes.append(mix_out(
+            clock, place, scans[i][4], scans[i][3], ends_in[i], projections[i][1], first_w, outs[i], 512,
+            () if i else (cot_all,),
+        ))
+
+    for step in (start_chain, scan_chain, mix_chain):
+        for i in turns:
+            step(i)
     wide_one, both_pre, tails = map(list, zip(*projections))
-    halo = [step_by(t, "context", 1) for t in tails]
-    scans = [forward_scan(clock, both_pre[i], halo[i], mask[i], params, gate_w, parts) for i in turns]
     conv_low, pre, decays, prods, locals_, ends = map(list, zip(*scans))
-    state_in = [carry_over(end, 1) for end in ends]
-    mixes = [
-        mix_out(clock, place, locals_[i], prods[i], state_in[i], both_pre[i], out_w, outs[i], 512,
-                () if i else (cot_all,))
-        for i in turns
-    ]
+    state_in = ends_in
     states, mixed_low, out_part = map(list, zip(*mixes))
     out_terms = [gathered_sums(p) for p in out_part]
-    seconds = [second(clock, x_rows[i], gain_two_row, out_terms[i], copies[i]) for i in turns]
-    residual = [t[0] for t in seconds]
-    two_blocks = [spread(seconds[i][1], apart[i]) for i in turns]
+    residual, two_blocks = [], []
+    for i in turns:
+        res, low = second(clock, x_rows[i], gain_two_row, out_terms[i], copies[i], two_blocks[-1] if i else out_terms[-1])
+        residual.append(res)
+        two_blocks.append(spread(low, apart[i]))
     mlps = [
-        mlp(clock, place, two_blocks[i], cot_all, i, count, rows, pair_w, down_w, outs[i], 256) for i in turns
+        mlp(clock, place, two_blocks[i], cot_all, i, count, rows, second_w, outs[i], 256) for i in turns
     ]
     wide_two, wide_cot, hidden_low, pair_low, two_part = map(list, zip(*mlps))
     two_terms = [gathered_sums(p) for p in two_part]
 
     thirds = []
     for i in turns:
-        thirds.append(third(clock, residual[i], cot_rows[i], gain_two_row, two_terms[i], copies[i], 0.01 if i else 3.4))
+        thirds.append(third(
+            clock, residual[i], cot_rows[i], gain_two_row, two_terms[i], copies[i], 60.0 if i else 3.4
+        ))
         if i == 0:
-            pair_term = weight_term(clock, wide_two, pair_low, 256, 21.0)
+            pair_grad = lax.psum_scatter(
+                weight_term(clock, wide_two, pair_low, 512, 21.0), owners, scatter_dimension=0, tiled=True
+            )
     resid_grad, resid_low, gain_two = map(list, zip(*thirds))
     resid_blocks = [spread(resid_low[i], apart[i]) for i in turns]
-    pair_grad = share(pair_term, 0)
-    (down_terms,) = gathered_sums([down_out(clock, hidden_low, down_w, rows, 512)])
-    down_term = weight_term(clock, hidden_low, wide_cot, 256, 0.01)
-    down_grad = share(down_term, 1)
+    down_split = split_term(clock, group_place, wide_cot, hidden_low, groups, 2, 0.01)
+    (down_terms,) = gathered_sums([down_out(clock, hidden_low, second_w, rows, 512)])
 
     reversed_ = [
-        reverse_scan(clock, place, resid_blocks[i], out_w, both_pre[i], states[i], decays[i], parts) for i in turns
+        reverse_scan(clock, place, resid_blocks[i], first_w, both_pre[i], states[i], decays[i], parts) for i in turns
     ]
     wide_resid, branch_low, rev_prods, rev_grads, ends_back = map(list, zip(*reversed_))
     grad_in = carry_all(ends_back, -1)
-    out_term = weight_term(clock, mixed_low, wide_resid, 128, 7.0)
-    out_grad = share(out_term, 1)
-    backs = []
-    for i in turns:
-        backs.append(gates_back(
+    branch_split = split_term(clock, group_place, wide_one, branch_low, groups, 1, 6.0)
+    out_split = split_term(clock, group_place, wide_resid, mixed_low, groups, 1, 7.0)
+    early = member_sums(clock, [down_split, branch_split], 8.0)
+    backs = [
+        gates_back(
             clock, rev_prods[i], rev_grads[i], grad_in[i], states[i], state_in[i], decays[i], pre[i], conv_low[i],
             both_pre[i], halo[i], mask[i], params, gate_w, parts,
-        ))
+        )
+        for i in turns
+    ]
     gates_low, inner_grad, edge, sums = map(list, zip(*backs))
-    edge_in = [step_by(e, "context", -1) for e in edge]
+    gate_grad, up_grad = turned_pieces(clock, pair_grad, [(units, False), (units, False)])
+    edges = step_by(jnp.concatenate(edge, axis=0), "context", -1)
+    edge_in = [edges[i * TILE : (i + 1) * TILE] for i in turns]
     gate_blocks = diagonal_terms(clock, conv_low, gates_low, blocks)
     ones = []
     for i in turns:
         ones.append(back_one(
-            clock, place, branch_low[i], inner_grad[i], edge_in[i], both_w, wide_one[i], outs[i], 512
+            clock, place, branch_low[i], inner_grad[i], edge_in[i], first_w, wide_one[i], 1 if i else parts, 512
         ))
         if i == 0:
             block_out = block_results(clock, residual, down_terms)
-    both_low, gain_one, one_part = map(list, zip(*ones))
+    inner_low, gain_one, one_part = map(list, zip(*ones))
     one_terms = [gathered_sums(p) for p in one_part]
-    both_term = weight_term(clock, wide_one, both_low, 256, 11.0)
-    both_grad = share(both_term, 0)
-    gate_blocks = sum_of(clock, everyone(gate_blocks, "fsdp"), BF16)
-    gate_blocks = sum_of(clock, everyone(gate_blocks, "context"), F32)
-    input_grad = [last(clock, x_rows[i], resid_grad[i], gain_one_row, one_terms[i]) for i in turns]
-    gate_grad, up_grad = finish(clock, pair_grad, 2)
-    (down_grad,) = finish(clock, down_grad, 1)
-    (out_grad,) = finish(clock, out_grad, 1)
-    branch_grad, inner_grad_w = finish(clock, both_grad, 2)
+    inner_split = split_term(clock, group_place, wide_one, inner_low, groups, 1, 8.0)
+    gains = sum_over(jnp.concatenate([sum(gain_one) / gain_one_row, sum(gain_two)]), "tensor")
+    small = jnp.concatenate([sum(sums).reshape(-1), gains.reshape(-1)]).astype(BF16)
+    cells, side = gate_blocks.shape[0], gate_blocks.shape[2]
+    extra = -(-small.size // (cells * side * 2 * TILE)) * 2 * TILE
+    small = jnp.pad(small, (0, cells * extra * side - small.size)).reshape(cells, extra, side)
+    packed_all = everyone(jnp.concatenate([gate_blocks, small], axis=1), "fsdp")
+    late = member_sums(clock, [out_split, inner_split], 3.0)
+    packed = sum_of(clock, packed_all, BF16)
+    packed_all = everyone(packed, "context")
+    input_grad = [last(clock, x_rows[i], resid_grad[i], gain_one_row, one_terms[i], 3.0) for i in turns[:-1]]
+    down_grad, branch_grad = turned_pieces(clock, early, [(units, True), (width, False)])
+    input_grad.append(last(clock, x_rows[-1], resid_grad[-1], gain_one_row, one_terms[-1], LONG))
+    packed = sum_of(clock, packed_all, F32)
+    gate_blocks = packed[:, :side]
+    small = packed[:, side:].reshape(-1)
+    sums = small[: TILE * width].reshape(TILE, width)
+    gains = small[TILE * width : TILE * width + 2 * model].reshape(2, model)
+    out_grad, inner_weight_grad = turned_pieces(clock, late, [(width, True), (width, False)])
 
     def stacked(values):
         return jnp.stack(values).reshape(micro, seqs, rows, model)
 
-    gains = jnp.concatenate([sum(gain_one) / gain_one_row, sum(gain_two)])
-    small = jnp.concatenate([sum(sums).reshape(1, -1), gains.reshape(1, -1)], axis=1)
-    small = sum_over(sum_over(small, "fsdp"), "context")
-    sums = small[:, : TILE * width].reshape(TILE, width)
-    gains = sum_over(small[:, TILE * width :], "tensor").reshape(2, model)
     return (
         stacked(block_out),
         stacked(input_grad),
         gains[0],
         branch_grad,
-        inner_grad_w,
+        inner_weight_grad,
         sums[:CONV],
         sums[CONV],
         gate_blocks[:blocks],

time: 640 us -> 616 us (0.963)
  waiting for transfers between devices: 192 us -> 149 us
  local copies, waits for them, and re-layouts: 20.9 us -> 41 us
    all_to_all x4, waiting for transfers between devices: 35.6 us -> 0.01 us  [gathered_sums(): lax.all_to_all(parts[0], 'tensor', split_axis=0, concat_axis=0, tiled=True)]
    reduce_scatter x4 -> x3, waiting for transfers between devices: 8.65 us -> 0.01 us  [the longest x2 0.01 us: member_sums(): lax.psum_scatter(added_up, 'context', scatter_dimension=0, tiled=True)]
    ppermute x29, starting transfers between devices: 72.4 us -> 65.1 us  [shift(): lax.ppermute(value, axis, [(i, (i + by) % size) for i in range(size)])]
    ppermute x0 -> x4, local copies, waits for them, and re-layouts: none -> 7.03 us  [shift(): lax.ppermute(value, axis, [(i, (i + by) % size) for i in range(size)])]
    unnamed x105 -> x100, local copies, waits for them, and re-layouts: 11.6 us -> 17.8 us
    pallas_call x36 -> x38, Pallas kernels: 246 us -> 251 us  [call(): pl.pallas_call(body, out_shape=list(out_shape) + [jax.ShapeDtypeStruct((T...]
    ppermute x13 -> x12, starting transfers between devices: 23.9 us -> 22.6 us  [step_by(): lax.ppermute(value, axis, [(i, i + by) for i in range(size) if 0 <= i + b...]
  transfers between devices with their start and end apart: 58 -> 54, of which waited for: 12 -> 11; matrix products, arithmetic and copies ran while one was open for 4% -> 7% of each run, Pallas kernels for 35% -> 41%
where the time goes in v3:
time: 616 us; the launch traced here: 605 us
  Pallas kernels  251 us (41%)
  waiting for transfers between devices  149 us (24%)
  starting transfers between devices  128 us (21%)
  local copies, waits for them, and re-layouts  41 us (7%)
  other arithmetic  20.4 us (3%)
  between operations  15 us (2%)
    pallas_call x38, Pallas kernels, call(): pl.pallas_call(body, out_shape=list(out_shape) + [jax.ShapeDtypeStruct((T...  251 us
    ppermute x29, waiting for transfers between devices, shift(): lax.ppermute(value, axis, [(i, (i + by) % size) for i in range(size)])  84.6 us
    ppermute x29, starting transfers between devices, shift(): lax.ppermute(value, axis, [(i, (i + by) % size) for i in range(size)])  65.1 us
    all_to_all x4, waiting for transfers between devices, spread(): lax.all_to_all(copies, 'tensor', split_axis=0, concat_axis=0, tiled=True)  58.4 us
    all_to_all x4, starting transfers between devices, spread(): lax.all_to_all(copies, 'tensor', split_axis=0, concat_axis=0, tiled=True)  23.2 us
    ppermute x12, starting transfers between devices, step_by(): lax.ppermute(value, axis, [(i, i + by) for i in range(size) if 0 <= i + b...  22.6 us
    unnamed x100, local copies, waits for them, and re-layouts  17.8 us
    all_to_all x4, starting transfers between devices, gathered_sums(): lax.all_to_all(parts[0], 'tensor', split_axis=0, concat_axis=0, tiled=True)  17.4 us
  transfers between devices with their start and end apart: 54, of which 11 were waited for; matrix products, arithmetic and copies ran while one was open for 7% of the time, Pallas kernels for 41%

profile of v3, /device:TPU:0, one launch (start us, length us, event | category | flops | bytes accessed | tf_op | source)
XLA Modules:
  0.0 604.7 jit_solution(13253137697643859781)
XLA Ops:
  18.4 6.5 %all-to-all-start = ((bf16[4,80,2048]{2,1,0:T(8,128)(2,1)}), bf16[4,80,2048]{2,1,0:T(8,128)(2,1)S(1)}, u32[]{:S(2)}, u32[]{:S(2)}) async-start(bf16[4,80,2048]{2,1,0:T(8,128)(2,1)} %bitcast.70), calls=%async_computation | async-start | bytes 2621440 | tf_op jit(solution)/shard_map/all_to_all | solution.py:315
  25.4 8.5 %fusion.24.refs_2_.refs_4_.refs_14_ = bf16[640,1280]{1,0:T(8,128)(2,1)} fusion(bf16[160,160]{1,0:T(8,128)(2,1)S(1)} %get-tuple-element.374, bf16[160,160]{1,0:T(8,128)(2,1)S(1)} %get-tuple-element.375, bf16[160,160]{1,0:T(8,128)(2,1)S(1)} %get-tuple-element.373, bf16[160,160]{1,0:T(8,128)(2,1)S(1)} %get-tuple-element.372, ...), kind=kLoop, calls=%fused_computation.33 | loop fusion | flops 40960000 | bytes 2048000 | tf_op jit(solution)/shard_map/concatenate | solution.py:902
  37.2 2.8 shard_map.306
  41.9 3.8 collective-permute-start.3
  46.8 24.5 %all-to-all-done = bf16[4,80,2048]{2,1,0:T(8,128)(2,1)S(1)} async-done(((bf16[4,80,2048]{2,1,0:T(8,128)(2,1)}), bf16[4,80,2048]{2,1,0:T(8,128)(2,1)S(1)}, u32[]{:S(2)}, u32[]{:S(2)}) %all-to-all-start) | async-done | bytes 1310752 | tf_op jit(solution)/shard_map/all_to_all | solution.py:315
  72.4 3.8 all-to-all-start.1
  76.2 6.4 %shard_map.308 = (bf16[320,2048]{1,0:T(8,128)(2,1)}, f32[320,1280]{1,0:T(8,128)}, bf16[8,640]{1,0:T(8,128)(2,1)}, f32[8,128]{1,0:T(8,128)}) custom-call(s32[1]{0:T(128)} %bitcast.2.refs_0_, bf16[320,2048]{1,0:T(8,128)(2,1)} %bitcast.69, bf16[2048,1920]{1,0:T(8,128)(2,1)} %all-gather.3.cloned.1.call-done.refs_2_.refs_5_.refs_4_, ...), custom_call_target="tpu_custom_call" | custom-call | flops 17999998976 | bytes 17999998976 | tf_op jit(solution)/shard_map/pallas_call | solution.py:284
  82.7 3.5 collective-permute-start
  86.2 13.3 %collective-permute-done.2.refs_3_ = bf16[80,2048]{1,0:T(8,128)(2,1)S(1)} collective-permute-done((bf16[80,2048]{1,0:T(8,128)(2,1)}, bf16[80,2048]{1,0:T(8,128)(2,1)S(1)}, u32[]{:S(2)}, u32[]{:S(2)}) %collective-permute-start.2) | collective-permute-done | bytes 327712 | tf_op jit(solution)/shard_map/ppermute | solution.py:24
  100.2 6.0 shard_map.309
  106.2 3.4 collective-permute-start.7
  110.2 7.5 %shard_map.310 = (bf16[320,640]{1,0:T(8,128)(2,1)}, f32[320,1280]{1,0:T(8,128)}, f32[320,640]{1,0:T(8,128)}, f32[320,640]{1,0:T(8,128)}, f32[320,640]{1,0:T(8,128)}, /*index=5*/f32[2,640]{1,0:T(2,128)}, f32[8,128]{1,0:T(8,128)}) custom-call(f32[320,1280]{1,0:T(8,128)} %get-tuple-element.163.refs_0_.refs_4_.refs_3_.refs_9_.refs_10_, ...), custom_call_target="tpu_custom_call" | custom-call | flops 20999999488 | bytes 20999999488 | tf_op jit(solution)/shard_map/pallas_call | solution.py:284
  123.7 7.0 %shard_map.311 = (bf16[320,640]{1,0:T(8,128)(2,1)}, f32[320,1280]{1,0:T(8,128)}, f32[320,640]{1,0:T(8,128)}, f32[320,640]{1,0:T(8,128)}, f32[320,640]{1,0:T(8,128)}, /*index=5*/f32[2,640]{1,0:T(2,128)}, f32[8,128]{1,0:T(8,128)}) custom-call(f32[320,1280]{1,0:T(8,128)} %get-tuple-element.172.refs_0_.refs_4_.refs_6_.refs_9_.refs_10_, ...), custom_call_target="tpu_custom_call" | custom-call | flops 20999999488 | bytes 20999999488 | tf_op jit(solution)/shard_map/pallas_call | solution.py:284
  136.2 4.3 all-to-all-done.1
  142.1 5.8 shard_map.312
  147.8 3.5 all-to-all-start.2
  152.0 5.9 shard_map.313
  159.8 2.4 collective-permute-start.12
  163.8 21.4 %collective-permute-done.11.refs_4_.refs_3_ = bf16[80,2048]{1,0:T(8,128)(2,1)S(1)} collective-permute-done((bf16[80,2048]{1,0:T(8,128)(2,1)}, bf16[80,2048]{1,0:T(8,128)(2,1)S(1)}, u32[]{:S(2)}, u32[]{:S(2)}) %collective-permute-start.11) | collective-permute-done | bytes 327712 | tf_op jit(solution)/shard_map/ppermute | solution.py:24
  185.2 19.1 %collective-permute-done.12.refs_5_.refs_4_ = bf16[80,2048]{1,0:T(8,128)(2,1)S(1)} collective-permute-done((bf16[80,2048]{1,0:T(8,128)(2,1)}, bf16[80,2048]{1,0:T(8,128)(2,1)S(1)}, u32[]{:S(2)}, u32[]{:S(2)}) %collective-permute-start.12) | collective-permute-done | bytes 327712 | tf_op jit(solution)/shard_map/ppermute | solution.py:24
  205.5 3.0 shard_map.314
  208.5 8.7 %all-to-all-start.3 = ((bf16[4,80,2048]{2,1,0:T(8,128)(2,1)}), bf16[4,80,2048]{2,1,0:T(8,128)(2,1)S(1)}, u32[]{:S(2)}, u32[]{:S(2)}) async-start(bf16[4,80,2048]{2,1,0:T(8,128)(2,1)} %bitcast.78), calls=%async_computation.3 | async-start | bytes 2621440 | tf_op jit(solution)/shard_map/all_to_all | solution.py:315
  217.2 29.6 %all-to-all-done.3 = bf16[4,80,2048]{2,1,0:T(8,128)(2,1)S(1)} async-done(((bf16[4,80,2048]{2,1,0:T(8,128)(2,1)}), bf16[4,80,2048]{2,1,0:T(8,128)(2,1)S(1)}, u32[]{:S(2)}, u32[]{:S(2)}) %all-to-all-start.3) | async-done | bytes 1310752 | tf_op jit(solution)/shard_map/all_to_all | solution.py:315
  247.9 2.6 shard_map.315
  253.3 27.3 %shard_map.316 = (bf16[320,2048]{1,0:T(8,128)(2,1)}, bf16[320,2048]{1,0:T(8,128)(2,1)}, bf16[320,1536]{1,0:T(8,128)(2,1)}, bf16[2,320,1536]{2,1,0:T(8,128)(2,1)}...) custom-call(s32[1]{0:T(128)} %bitcast.2.refs_0_, bf16[320,2048]{1,0:T(8,128)(2,1)} %bitcast.76, bf16[640,2048]{1,0:T(8,128)(2,1)} %bitcast.63, ...), custom_call_target="tpu_custom_call" | custom-call | flops 80999997440 | bytes 80999997440 | tf_op jit(solution)/shard_map/pallas_call | solution.py:284
  280.6 4.5 all-to-all-start.4
  286.0 27.4 %shard_map.317 = (bf16[320,2048]{1,0:T(8,128)(2,1)}, bf16[320,2048]{1,0:T(8,128)(2,1)}, bf16[320,1536]{1,0:T(8,128)(2,1)}, bf16[2,320,1536]{2,1,0:T(8,128)(2,1)}...) custom-call(s32[1]{0:T(128)} %bitcast.2.refs_0_, ...), custom_call_target="tpu_custom_call" | custom-call | flops 80999997440 | bytes 80999997440 | tf_op jit(solution)/shard_map/pallas_call | solution.py:284
  315.5 2.4 collective-permute-start.18
  320.4 3.5 shard_map.318
  323.9 4.3 all-to-all-start.6
  328.3 15.5 %shard_map.319 = (bf16[2048,3072]{1,0:T(8,128)(2,1)}, f32[8,128]{1,0:T(8,128)}) custom-call(bf16[320,2048]{1,0:T(8,128)(2,1)} %get-tuple-element.201.refs_0_, bf16[320,2048]{1,0:T(8,128)(2,1)} %get-tuple-element.202.refs_1_, bf16[2,320,1536]{2,1,0:T(8,128)(2,1)} %get-tuple-element.203.refs_2_, bf16[2,320,1536]{2,1,0:T(8,128)(2,1)} %get-tuple-element.204.refs_3_, ...), custom_call_target="tpu_custom_call" | custom-call | flops 62999998464 | bytes 62999998464 | tf_op jit(solution)/shard_map/pallas_call | solution.py:284
  344.8 3.1 shard_map.320
  348.0 25.6 %collective-permute-start.22 = (bf16[80,2048]{1,0:T(8,128)(2,1)}, bf16[80,2048]{1,0:T(8,128)(2,1)S(1)}, u32[]{:S(2)}, u32[]{:S(2)}) collective-permute-start(bf16[80,2048]{1,0:T(8,128)(2,1)} %get-tuple-element.220.refs_1_), channel_id=1, source_target_pairs={{0,3},{1,0},{2,1},{3,2},{4,7},{5,4},{6,5},{7,6},{8,11},{9,8},{10,9... | collective-permute-start | bytes 983048 | tf_op jit(solution)/shard_map/ppermute | solution.py:24
  374.4 10.6 %shard_map.321 = (bf16[1024,1536]{1,0:T(8,128)(2,1)}, bf16[1024,1536]{1,0:T(8,128)(2,1)}, f32[8,128]{1,0:T(8,128)}) custom-call(s32[1]{0:T(128)} %bitcast.25.refs_0_, bf16[320,2048]{1,0:T(8,128)(2,1)} %get-tuple-element.195.refs_1_, bf16[320,2048]{1,0:T(8,128)(2,1)} %get-tuple-element.196.refs_2_, bf16[320,1536]{1,0:T(8,128)(2,1)} %get-tuple-element.191.refs_3_.refs_0_, ...), custom_call_target="tpu_custom_call" | custom-call | flops 30000000 | bytes 30000000 | tf_op jit(solution)/shard_map/pallas_call | solution.py:284
  385.6 8.9 %shard_map.322 = (bf16[640,2048]{1,0:T(8,128)(2,1)}, f32[8,128]{1,0:T(8,128)}) custom-call(bf16[320,1536]{1,0:T(8,128)(2,1)} %get-tuple-element.191.refs_3_.refs_0_, bf16[320,1536]{1,0:T(8,128)(2,1)} %get-tuple-element.194.refs_4_.refs_1_, bf16[2048,4608]{1,0:T(8,128)(2,1)} %all-gather.5.cloned.1.call-done.refs_3_.refs_4_.refs_5_.refs_6_.refs_7_.refs_8_.refs_2_, ...), custom_call_target="tpu_custom_call" | custom-call | flops 30000000 | bytes 30000000 | tf_op jit(solution)/shard_map/pallas_call | solution.py:284
  394.5 4.7 all-to-all-start.5
  399.2 7.4 %shard_map.323 = (bf16[320,2048]{1,0:T(8,128)(2,1)}, bf16[320,640]{1,0:T(8,128)(2,1)}, f32[320,640]{1,0:T(8,128)}, f32[320,640]{1,0:T(8,128)}, f32[2,640]{1,0:T(2,128)}, /*index=5*/f32[8,128]{1,0:T(8,128)}) custom-call(s32[1]{0:T(128)} %bitcast.2.refs_0_, bf16[320,2048]{1,0:T(8,128)(2,1)} %bitcast.31.refs_1_, ...), custom_call_target="tpu_custom_call" | custom-call | flops 22499999744 | bytes 22499999744 | tf_op jit(solution)/shard_map/pallas_call | solution.py:284
  408.1 7.4 %shard_map.324 = (bf16[320,2048]{1,0:T(8,128)(2,1)}, bf16[320,640]{1,0:T(8,128)(2,1)}, f32[320,640]{1,0:T(8,128)}, f32[320,640]{1,0:T(8,128)}, f32[2,640]{1,0:T(2,128)}, /*index=5*/f32[8,128]{1,0:T(8,128)}) custom-call(s32[1]{0:T(128)} %bitcast.2.refs_0_, bf16[80,2048]{1,0:T(8,128)(2,1)} %get-tuple-element.220.refs_1_, ...), custom_call_target="tpu_custom_call" | custom-call | flops 22499999744 | bytes 22499999744 | tf_op jit(solution)/shard_map/pallas_call | solution.py:284
  420.3 6.5 %shard_map.325 = (bf16[1024,640]{1,0:T(8,128)(2,1)}, bf16[1024,640]{1,0:T(8,128)(2,1)}, f32[8,128]{1,0:T(8,128)}) custom-call(s32[1]{0:T(128)} %bitcast.25.refs_0_, bf16[320,2048]{1,0:T(8,128)(2,1)} %get-tuple-element.229.refs_1_.refs_5_, bf16[320,2048]{1,0:T(8,128)(2,1)} %get-tuple-element.230.refs_2_.refs_5_, ...), custom_call_target="tpu_custom_call" | custom-call | flops 17999998976 | bytes 17999998976 | tf_op jit(solution)/shard_map/pallas_call | solution.py:284
  426.9 6.5 %shard_map.326 = (bf16[1024,640]{1,0:T(8,128)(2,1)}, bf16[1024,640]{1,0:T(8,128)(2,1)}, f32[8,128]{1,0:T(8,128)}) custom-call(s32[1]{0:T(128)} %bitcast.25.refs_0_, bf16[320,2048]{1,0:T(8,128)(2,1)} %get-tuple-element.235.refs_1_, bf16[320,2048]{1,0:T(8,128)(2,1)} %get-tuple-element.236.refs_2_, bf16[320,640]{1,0:T(8,128)(2,1)} %get-tuple-element.237.refs_3_, ...), custom_call_target="tpu_custom_call" | custom-call | flops 20999999488 | bytes 20999999488 | tf_op jit(solution)/shard_map/pallas_call | solution.py:284
  436.1 6.2 %shard_map.327 = (bf16[1024,2176]{1,0:T(8,128)(2,1)}, f32[8,128]{1,0:T(8,128)}) custom-call(bf16[1024,1536]{1,0:T(8,128)(2,1)} %get-tuple-element.227.refs_0_, bf16[1024,1536]{1,0:T(8,128)(2,1)} %copy-done.33, bf16[1024,640]{1,0:T(8,128)(2,1)} %get-tuple-element.233.refs_2_, bf16[1024,640]{1,0:T(8,128)(2,1)} %collective-permute-done.27.refs_3_, ...), custom_call_target="tpu_custom_call" | custom-call | flops 24000000000 | bytes 24000000000 | tf_op jit(solution)/shard_map/pallas_call | solution.py:284
  442.3 8.5 %shard_map.328 = (bf16[320,1280]{1,0:T(8,128)(2,1)}, f32[320,640]{1,0:T(8,128)}, f32[8,640]{1,0:T(8,128)}, f32[8,640]{1,0:T(8,128)}, f32[8,128]{1,0:T(8,128)}) custom-call(f32[320,640]{1,0:T(8,128)} %get-tuple-element.217.refs_0_, f32[320,640]{1,0:T(8,128)} %get-tuple-element.218.refs_1_, f32[1,640]{1,0:T(1,128)} %get-tuple-element.381.refs_2_, ...), custom_call_target="tpu_custom_call" | custom-call | flops 120000004096 | bytes 120000004096 | tf_op jit(solution)/shard_map/pallas_call | solution.py:284
  450.8 8.8 %shard_map.329 = (bf16[320,1280]{1,0:T(8,128)(2,1)}, f32[320,640]{1,0:T(8,128)}, f32[8,640]{1,0:T(8,128)}, f32[8,640]{1,0:T(8,128)}, f32[8,128]{1,0:T(8,128)}) custom-call(f32[320,640]{1,0:T(8,128)} %get-tuple-element.244.refs_0_, f32[320,640]{1,0:T(8,128)} %get-tuple-element.245.refs_1_, f32[1,640]{1,0:T(1,128)} %get-tuple-element.380.refs_2_, ...), custom_call_target="tpu_custom_call" | custom-call | flops 120000004096 | bytes 120000004096 | tf_op jit(solution)/shard_map/pallas_call | solution.py:284
  462.7 5.8 collective-permute-done.28
  469.1 3.2 shard_map.330
  472.3 4.4 shard_map.331
  476.8 6.4 %shard_map.332 = (bf16[320,640]{1,0:T(8,128)(2,1)}, f32[1,2048]{1,0:T(1,128)}, bf16[80,2048]{1,0:T(8,128)(2,1)}, bf16[80,2048]{1,0:T(8,128)(2,1)}, bf16[80,2048]...) custom-call(s32[1]{0:T(128)} %bitcast.2.refs_0_, bf16[320,640]{1,0:T(8,128)(2,1)} %get-tuple-element.216.refs_3_.refs_1_, ...), custom_call_target="tpu_custom_call" | custom-call | flops 30000000 | bytes 30000000 | tf_op jit(solution)/shard_map/pallas_call | solution.py:284
  483.2 3.3 shard_map.333
  486.5 6.3 %shard_map.334 = (bf16[320,640]{1,0:T(8,128)(2,1)}, f32[1,2048]{1,0:T(1,128)}, bf16[320,2048]{1,0:T(8,128)(2,1)}, f32[8,128]{1,0:T(8,128)}) custom-call(s32[1]{0:T(128)} %bitcast.2.refs_0_, bf16[320,640]{1,0:T(8,128)(2,1)} %get-tuple-element.231.refs_4_.refs_1_, f32[320,640]{1,0:T(8,128)} %get-tuple-element.268.refs_2_, ...), custom_call_target="tpu_custom_call" | custom-call | flops 30000000 | bytes 30000000 | tf_op jit(solution)/shard_map/pallas_call | solution.py:284
  493.6 2.8 collective-permute-start.33
  498.5 4.5 all-to-all-start.7
  503.0 6.5 %shard_map.335 = (bf16[1024,640]{1,0:T(8,128)(2,1)}, bf16[1024,640]{1,0:T(8,128)(2,1)}, f32[8,128]{1,0:T(8,128)}) custom-call(s32[1]{0:T(128)} %bitcast.25.refs_0_, bf16[320,2048]{1,0:T(8,128)(2,1)} %get-tuple-element.229.refs_1_.refs_5_, bf16[320,2048]{1,0:T(8,128)(2,1)} %get-tuple-element.230.refs_2_.refs_5_, bf16[320,640]{1,0:T(8,128)(2,1)} %get-tuple-element.275.refs_3_, ...), custom_call_target="tpu_custom_call" | custom-call | flops 30000000 | bytes 30000000 | tf_op jit(solution)/shard_map/pallas_call | solution.py:284
  513.5 2.4 collective-permute-start.30
  523.0 4.7 shard_map.336
  527.7 2.4 shard_map.337
  533.4 2.5 collective-permute-start.39
  536.9 2.8 collective-permute-start.38
  539.7 16.3 %collective-permute-done.30.refs_5_ = bf16[80,2048]{1,0:T(8,128)(2,1)} collective-permute-done((bf16[80,2048]{1,0:T(8,128)(2,1)}, bf16[80,2048]{1,0:T(8,128)(2,1)}, u32[]{:S(2)}, u32[]{:S(2)}) %collective-permute-start.30) | collective-permute-done | bytes 327712 | tf_op jit(solution)/shard_map/ppermute | solution.py:24
  556.0 3.0 shard_map.338
  559.0 2.9 shard_map.339
  563.2 5.3 collective-permute-done.39
  569.6 8.2 %collective-permute-done.38 = bf16[8,176,160]{1,2,0:T(8,128)(2,1)} collective-permute-done((bf16[8,176,160]{1,2,0:T(8,128)(2,1)S(1)}, bf16[8,176,160]{1,2,0:T(8,128)(2,1)}, u32[]{:S(2)}, u32[]{:S(2)}) %collective-permute-start.38) | collective-permute-done | bytes 450592 | tf_op jit(solution)/shard_map/ppermute | solution.py:24
  581.2 3.3 shard_map.340
  584.5 3.3 shard_map.341
  (254 shorter events, 97.0 us)
Async XLA Ops:
  7.2 69.0 %all-gather.3.cloned.1.call-start = ((), (), s32[]{:S(2)}) async-start(), calls=%async_computation.11 | async-start | bytes 8847360 | tf_op jit(solution)/shard_map/all_gather | solution.py:896
  10.6 242.6 %all-gather.5.cloned.1.call-start = ((), (), s32[]{:S(2)}) async-start(), calls=%async_computation.12 | async-start | bytes 21233664 | tf_op jit(solution)/shard_map/all_gather | solution.py:899
  18.4 52.9 %all-to-all-start = ((bf16[4,80,2048]{2,1,0:T(8,128)(2,1)}), bf16[4,80,2048]{2,1,0:T(8,128)(2,1)S(1)}, u32[]{:S(2)}, u32[]{:S(2)}) async-start(bf16[4,80,2048]{2,1,0:T(8,128)(2,1)} %bitcast.70), calls=%async_computation | async-start | bytes 2621440 | tf_op jit(solution)/shard_map/all_to_all | solution.py:315
  25.4 10.3 %copy-start.25 = (f32[4,640]{1,0:T(4,128)S(1)}, f32[4,640]{1,0:T(4,128)}, u32[]{:S(2)}) copy-start(f32[4,640]{1,0:T(4,128)} %param.23) | copy-start | bytes 30724
  25.4 10.9 %copy-start.15 = (bf16[2,1,80,2048]{3,2,1,0:T(8,128)(2,1)S(1)}, bf16[2,1,80,2048]{3,2,1,0:T(8,128)(2,1)}, u32[]{:S(2)}) copy-start(bf16[2,1,80,2048]{3,2,1,0:T(8,128)(2,1)} %param.35) | copy-start | bytes 1966084
  41.9 44.3 %collective-permute-start.3 = (bf16[80,2048]{1,0:T(8,128)(2,1)}, bf16[80,2048]{1,0:T(8,128)(2,1)S(1)}, u32[]{:S(2)}, u32[]{:S(2)}) collective-permute-start(bf16[80,2048]{1,0:T(8,128)(2,1)} %get-tuple-element.165.refs_1_), channel_id=1, source_target_pairs={{0,3},{1,0},{2,1},{3,2},{4,7},{5,4},{6,5},{7,6},{8,11},{9,8},{10,9... | collective-permute-start | bytes 983048 | tf_op jit(solution)/shard_map/ppermute | solution.py:24
  45.7 53.8 %collective-permute-start.2 = (bf16[80,2048]{1,0:T(8,128)(2,1)}, bf16[80,2048]{1,0:T(8,128)(2,1)S(1)}, u32[]{:S(2)}, u32[]{:S(2)}) collective-permute-start(bf16[80,2048]{1,0:T(8,128)(2,1)} %get-tuple-element.165.refs_1_), channel_id=1, source_target_pairs={{0,2},{1,3},{2,0},{3,1},{4,6},{5,7},{6,4},{7,5},{8,10},{9,11},{10,... | collective-permute-start | bytes 983048 | tf_op jit(solution)/shard_map/ppermute | solution.py:24
  45.7 53.8 %collective-permute-start.1 = (bf16[80,2048]{1,0:T(8,128)(2,1)}, bf16[80,2048]{1,0:T(8,128)(2,1)}, u32[]{:S(2)}, u32[]{:S(2)}) collective-permute-start(bf16[80,2048]{1,0:T(8,128)(2,1)} %get-tuple-element.165.refs_1_), channel_id=1, source_target_pairs={{0,1},{1,2},{2,3},{3,0},{4,5},{5,6},{6,7},{7,4},{8,9},{9,10},{10,1... | collective-permute-start | bytes 983048 | tf_op jit(solution)/shard_map/ppermute | solution.py:24
  72.4 68.1 %all-to-all-start.1 = ((bf16[4,160,2048]{2,1,0:T(8,128)(2,1)}), bf16[4,160,2048]{2,1,0:T(8,128)(2,1)S(1)}, u32[]{:S(2)}, u32[]{:S(2)}) async-start(bf16[4,160,2048]{2,1,0:T(8,128)(2,1)} %bitcast.66), calls=%async_computation.1 | async-start | bytes 5242880 | tf_op jit(solution)/shard_map/all_to_all | solution.py:315
  82.7 26.9 %collective-permute-start = (bf16[8,640]{1,0:T(8,128)(2,1)}, bf16[8,640]{1,0:T(8,128)(2,1)S(1)}, u32[]{:S(2)}, u32[]{:S(2)}) collective-permute-start(bf16[8,640]{1,0:T(8,128)(2,1)} %get-tuple-element.164), channel_id=1, source_target_pairs={{0,4},{4,8},{8,12},{1,5},{5,9},{9,13},{2,6},{6,10},{10,14},{3,7},{... | collective-permute-start | bytes 30728 | tf_op jit(solution)/shard_map/ppermute | solution.py:29
  86.2 13.3 %copy-start.38 = (bf16[80,2048]{1,0:T(8,128)(2,1)}, bf16[80,2048]{1,0:T(8,128)(2,1)S(1)}, u32[]{:S(2)}) copy-start(bf16[80,2048]{1,0:T(8,128)(2,1)S(1)} %collective-permute-done.3.refs_4_) | copy-start | bytes 983044
  106.2 17.0 %collective-permute-start.7 = (bf16[8,640]{1,0:T(8,128)(2,1)}, bf16[8,640]{1,0:T(8,128)(2,1)S(1)}, u32[]{:S(2)}, u32[]{:S(2)}) collective-permute-start(bf16[8,640]{1,0:T(8,128)(2,1)} %get-tuple-element.173), channel_id=1, source_target_pairs={{0,4},{4,8},{8,12},{1,5},{5,9},{9,13},{2,6},{6,10},{10,14},{3,7},{... | collective-permute-start | bytes 30728 | tf_op jit(solution)/shard_map/ppermute | solution.py:29
  117.7 15.6 %collective-permute-start.6 = (f32[2,640]{1,0:T(2,128)}, f32[2,640]{1,0:T(2,128)S(1)}, u32[]{:S(2)}, u32[]{:S(2)}) collective-permute-start(f32[2,640]{1,0:T(2,128)} %get-tuple-element.170), channel_id=1, source_target_pairs={{0,12},{1,13},{2,14},{3,15},{16,28},{17,29},{18,30},{19,31}} | collective-permute-start | bytes 15368 | tf_op jit(solution)/shard_map/ppermute | solution.py:29
  119.4 16.3 %collective-permute-start.5 = (f32[2,640]{1,0:T(2,128)}, f32[2,640]{1,0:T(2,128)S(1)}, u32[]{:S(2)}, u32[]{:S(2)}) collective-permute-start(f32[2,640]{1,0:T(2,128)} %get-tuple-element.170), channel_id=1, source_target_pairs={{0,8},{4,12},{1,9},{5,13},{2,10},{6,14},{3,11},{7,15},{16,24},{20,... | collective-permute-start | bytes 15368 | tf_op jit(solution)/shard_map/ppermute | solution.py:29
  121.4 14.2 %collective-permute-start.4 = (f32[2,640]{1,0:T(2,128)}, f32[2,640]{1,0:T(2,128)S(1)}, u32[]{:S(2)}, u32[]{:S(2)}) collective-permute-start(f32[2,640]{1,0:T(2,128)} %get-tuple-element.170), channel_id=1, source_target_pairs={{0,4},{4,8},{8,12},{1,5},{5,9},{9,13},{2,6},{6,10},{10,14},{3,7},{... | collective-permute-start | bytes 15368 | tf_op jit(solution)/shard_map/ppermute | solution.py:29
  130.7 20.7 %collective-permute-start.10 = (f32[2,640]{1,0:T(2,128)}, f32[2,640]{1,0:T(2,128)S(1)}, u32[]{:S(2)}, u32[]{:S(2)}) collective-permute-start(f32[2,640]{1,0:T(2,128)} %get-tuple-element.179), channel_id=1, source_target_pairs={{0,12},{1,13},{2,14},{3,15},{16,28},{17,29},{18,30},{19,31}} | collective-permute-start | bytes 15368 | tf_op jit(solution)/shard_map/ppermute | solution.py:29
  132.0 19.4 %collective-permute-start.9 = (f32[2,640]{1,0:T(2,128)}, f32[2,640]{1,0:T(2,128)S(1)}, u32[]{:S(2)}, u32[]{:S(2)}) collective-permute-start(f32[2,640]{1,0:T(2,128)} %get-tuple-element.179), channel_id=1, source_target_pairs={{0,8},{4,12},{1,9},{5,13},{2,10},{6,14},{3,11},{7,15},{16,24},{20,... | collective-permute-start | bytes 15368 | tf_op jit(solution)/shard_map/ppermute | solution.py:29
  133.3 18.1 %collective-permute-start.8 = (f32[2,640]{1,0:T(2,128)}, f32[2,640]{1,0:T(2,128)S(1)}, u32[]{:S(2)}, u32[]{:S(2)}) collective-permute-start(f32[2,640]{1,0:T(2,128)} %get-tuple-element.179), channel_id=1, source_target_pairs={{0,4},{4,8},{8,12},{1,5},{5,9},{9,13},{2,6},{6,10},{10,14},{3,7},{... | collective-permute-start | bytes 15368 | tf_op jit(solution)/shard_map/ppermute | solution.py:29
  147.8 56.4 %all-to-all-start.2 = ((bf16[4,80,2048]{2,1,0:T(8,128)(2,1)}), bf16[4,80,2048]{2,1,0:T(8,128)(2,1)S(1)}, u32[]{:S(2)}, u32[]{:S(2)}) async-start(bf16[4,80,2048]{2,1,0:T(8,128)(2,1)} %bitcast.73), calls=%async_computation.2 | async-start | bytes 2621440 | tf_op jit(solution)/shard_map/all_to_all | solution.py:321
  158.0 27.2 %collective-permute-start.11 = (bf16[80,2048]{1,0:T(8,128)(2,1)}, bf16[80,2048]{1,0:T(8,128)(2,1)S(1)}, u32[]{:S(2)}, u32[]{:S(2)}) collective-permute-start(bf16[80,2048]{1,0:T(8,128)(2,1)} %get-tuple-element.182), channel_id=1, source_target_pairs={{0,1},{1,2},{2,3},{3,0},{4,5},{5,6},{6,7},{7,4},{8,9},{9,10},{10,1... | collective-permute-start | bytes 983048 | tf_op jit(solution)/shard_map/ppermute | solution.py:24
  159.8 44.5 %collective-permute-start.12 = (bf16[80,2048]{1,0:T(8,128)(2,1)}, bf16[80,2048]{1,0:T(8,128)(2,1)S(1)}, u32[]{:S(2)}, u32[]{:S(2)}) collective-permute-start(bf16[80,2048]{1,0:T(8,128)(2,1)} %get-tuple-element.183), channel_id=1, source_target_pairs={{0,2},{1,3},{2,0},{3,1},{4,6},{5,7},{6,4},{7,5},{8,10},{9,11},{10,... | collective-permute-start | bytes 983048 | tf_op jit(solution)/shard_map/ppermute | solution.py:24
  162.2 42.1 %collective-permute-start.13 = (bf16[80,2048]{1,0:T(8,128)(2,1)}, bf16[80,2048]{1,0:T(8,128)(2,1)S(1)}, u32[]{:S(2)}, u32[]{:S(2)}) collective-permute-start(bf16[80,2048]{1,0:T(8,128)(2,1)} %get-tuple-element.184), channel_id=1, source_target_pairs={{0,3},{1,0},{2,1},{3,2},{4,7},{5,4},{6,5},{7,6},{8,11},{9,8},{10,9... | collective-permute-start | bytes 983048 | tf_op jit(solution)/shard_map/ppermute | solution.py:24
  185.2 19.1 %copy-start.39 = (bf16[80,2048]{1,0:T(8,128)(2,1)}, bf16[80,2048]{1,0:T(8,128)(2,1)S(1)}, u32[]{:S(2)}) copy-start(bf16[80,2048]{1,0:T(8,128)(2,1)S(1)} %collective-permute-done.11.refs_4_.refs_3_) | copy-start | bytes 983044
  208.5 38.3 %all-to-all-start.3 = ((bf16[4,80,2048]{2,1,0:T(8,128)(2,1)}), bf16[4,80,2048]{2,1,0:T(8,128)(2,1)S(1)}, u32[]{:S(2)}, u32[]{:S(2)}) async-start(bf16[4,80,2048]{2,1,0:T(8,128)(2,1)} %bitcast.78), calls=%async_computation.3 | async-start | bytes 2621440 | tf_op jit(solution)/shard_map/all_to_all | solution.py:315
  250.5 34.6 %collective-permute-start.16 = (bf16[80,2048]{1,0:T(8,128)(2,1)}, bf16[80,2048]{1,0:T(8,128)(2,1)S(1)}, u32[]{:S(2)}, u32[]{:S(2)}) collective-permute-start(bf16[80,2048]{1,0:T(8,128)(2,1)} %get-tuple-element.192.refs_1_), channel_id=1, source_target_pairs={{0,3},{1,0},{2,1},{3,2},{4,7},{5,4},{6,5},{7,6},{8,11},{9,8},{10,9... | collective-permute-start | bytes 983048 | tf_op jit(solution)/shard_map/ppermute | solution.py:24
  252.7 32.4 %collective-permute-start.15 = (bf16[80,2048]{1,0:T(8,128)(2,1)}, bf16[80,2048]{1,0:T(8,128)(2,1)S(1)}, u32[]{:S(2)}, u32[]{:S(2)}) collective-permute-start(bf16[80,2048]{1,0:T(8,128)(2,1)} %get-tuple-element.192.refs_1_), channel_id=1, source_target_pairs={{0,2},{1,3},{2,0},{3,1},{4,6},{5,7},{6,4},{7,5},{8,10},{9,11},{10,... | collective-permute-start | bytes 983048 | tf_op jit(solution)/shard_map/ppermute | solution.py:24
  252.7 32.4 %collective-permute-start.14 = (bf16[80,2048]{1,0:T(8,128)(2,1)}, bf16[80,2048]{1,0:T(8,128)(2,1)S(1)}, u32[]{:S(2)}, u32[]{:S(2)}) collective-permute-start(bf16[80,2048]{1,0:T(8,128)(2,1)} %get-tuple-element.192.refs_1_), channel_id=1, source_target_pairs={{0,1},{1,2},{2,3},{3,0},{4,5},{5,6},{6,7},{7,4},{8,9},{9,10},{10,1... | collective-permute-start | bytes 983048 | tf_op jit(solution)/shard_map/ppermute | solution.py:24
  280.6 38.8 %all-to-all-start.4 = ((bf16[4,80,2048]{2,1,0:T(8,128)(2,1)}), bf16[4,80,2048]{2,1,0:T(8,128)(2,1)S(1)}, u32[]{:S(2)}, u32[]{:S(2)}) async-start(bf16[4,80,2048]{2,1,0:T(8,128)(2,1)} %bitcast.77), calls=%async_computation.4 | async-start | bytes 2621440 | tf_op jit(solution)/shard_map/all_to_all | solution.py:321
  313.4 30.4 %collective-permute-start.17 = (bf16[80,2048]{1,0:T(8,128)(2,1)}, bf16[80,2048]{1,0:T(8,128)(2,1)S(1)}, u32[]{:S(2)}, u32[]{:S(2)}) collective-permute-start(bf16[80,2048]{1,0:T(8,128)(2,1)} %get-tuple-element.198), channel_id=1, source_target_pairs={{0,1},{1,2},{2,3},{3,0},{4,5},{5,6},{6,7},{7,4},{8,9},{9,10},{10,1... | collective-permute-start | bytes 983048 | tf_op jit(solution)/shard_map/ppermute | solution.py:24
  315.5 28.4 %collective-permute-start.18 = (bf16[80,2048]{1,0:T(8,128)(2,1)}, bf16[80,2048]{1,0:T(8,128)(2,1)S(1)}, u32[]{:S(2)}, u32[]{:S(2)}) collective-permute-start(bf16[80,2048]{1,0:T(8,128)(2,1)} %get-tuple-element.199), channel_id=1, source_target_pairs={{0,2},{1,3},{2,0},{3,1},{4,6},{5,7},{6,4},{7,5},{8,10},{9,11},{10,... | collective-permute-start | bytes 983048 | tf_op jit(solution)/shard_map/ppermute | solution.py:24
  317.9 26.1 %collective-permute-start.19 = (bf16[80,2048]{1,0:T(8,128)(2,1)}, bf16[80,2048]{1,0:T(8,128)(2,1)S(1)}, u32[]{:S(2)}, u32[]{:S(2)}) collective-permute-start(bf16[80,2048]{1,0:T(8,128)(2,1)} %get-tuple-element.200), channel_id=1, source_target_pairs={{0,3},{1,0},{2,1},{3,2},{4,7},{5,4},{6,5},{7,6},{8,11},{9,8},{10,9... | collective-permute-start | bytes 983048 | tf_op jit(solution)/shard_map/ppermute | solution.py:24
  323.9 70.6 %all-to-all-start.6 = ((bf16[4,80,2048]{2,1,0:T(8,128)(2,1)}), bf16[4,80,2048]{2,1,0:T(8,128)(2,1)}, u32[]{:S(2)}, u32[]{:S(2)}) async-start(bf16[4,80,2048]{2,1,0:T(8,128)(2,1)} %bitcast.71), calls=%async_computation.6 | async-start | bytes 2621440 | tf_op jit(solution)/shard_map/all_to_all | solution.py:315
  328.2 140.9 %reduce-scatter.4.cloned.1.call-start = ((), (), s32[]{:S(2)}) async-start(), calls=%async_computation.13 | async-start | bytes 14155776 | tf_op jit(solution)/shard_map/reduce_scatter | solution.py:975
  348.0 59.5 %collective-permute-start.22 = (bf16[80,2048]{1,0:T(8,128)(2,1)}, bf16[80,2048]{1,0:T(8,128)(2,1)S(1)}, u32[]{:S(2)}, u32[]{:S(2)}) collective-permute-start(bf16[80,2048]{1,0:T(8,128)(2,1)} %get-tuple-element.220.refs_1_), channel_id=1, source_target_pairs={{0,3},{1,0},{2,1},{3,2},{4,7},{5,4},{6,5},{7,6},{8,11},{9,8},{10,9... | collective-permute-start | bytes 983048 | tf_op jit(solution)/shard_map/ppermute | solution.py:24
  373.6 33.8 %collective-permute-start.21 = (bf16[80,2048]{1,0:T(8,128)(2,1)}, bf16[80,2048]{1,0:T(8,128)(2,1)}, u32[]{:S(2)}, u32[]{:S(2)}) collective-permute-start(bf16[80,2048]{1,0:T(8,128)(2,1)} %get-tuple-element.220.refs_1_), channel_id=1, source_target_pairs={{0,2},{1,3},{2,0},{3,1},{4,6},{5,7},{6,4},{7,5},{8,10},{9,11},{10,... | collective-permute-start | bytes 983048 | tf_op jit(solution)/shard_map/ppermute | solution.py:24
  373.6 33.8 %collective-permute-start.20 = (bf16[80,2048]{1,0:T(8,128)(2,1)}, bf16[80,2048]{1,0:T(8,128)(2,1)}, u32[]{:S(2)}, u32[]{:S(2)}) collective-permute-start(bf16[80,2048]{1,0:T(8,128)(2,1)} %get-tuple-element.220.refs_1_), channel_id=1, source_target_pairs={{0,1},{1,2},{2,3},{3,0},{4,5},{5,6},{6,7},{7,4},{8,9},{9,10},{10,1... | collective-permute-start | bytes 983048 | tf_op jit(solution)/shard_map/ppermute | solution.py:24
  374.4 10.6 %copy-start.27 = (f32[1,2048]{1,0:T(1,128)S(1)}, f32[1,2048]{1,0:T(1,128)}, u32[]{:S(2)}) copy-start(f32[1,2048]{1,0:T(1,128)} %get-tuple-element.271) | copy-start | bytes 24580
  374.4 10.6 %copy-start.28 = (f32[1,2048]{1,0:T(1,128)S(1)}, f32[1,2048]{1,0:T(1,128)}, u32[]{:S(2)}) copy-start(f32[1,2048]{1,0:T(1,128)} %get-tuple-element.272) | copy-start | bytes 24580
  385.0 49.4 %collective-permute-start.26 = (bf16[1024,1536]{1,0:T(8,128)(2,1)}, bf16[1024,1536]{1,0:T(8,128)(2,1)S(1)}, u32[]{:S(2)}, u32[]{:S(2)}) collective-permute-start(bf16[1024,1536]{1,0:T(8,128)(2,1)} %get-tuple-element.228), channel_id=1, source_target_pairs={{0,16},{16,0},{1,17},{17,1},{2,18},{18,2},{3,19},{19,3},{4,20},{20... | collective-permute-start | bytes 9437192 | tf_op jit(solution)/shard_map/ppermute | solution.py:24
  394.5 88.7 %all-to-all-start.5 = ((bf16[4,160,2048]{2,1,0:T(8,128)(2,1)}), bf16[4,160,2048]{2,1,0:T(8,128)(2,1)}, u32[]{:S(2)}, u32[]{:S(2)}) async-start(bf16[4,160,2048]{2,1,0:T(8,128)(2,1)} %bitcast.65), calls=%async_computation.5 | async-start | bytes 5242880 | tf_op jit(solution)/shard_map/all_to_all | solution.py:321
  399.2 159.8 %reduce-scatter.6.cloned.1.call-start = ((), (), s32[]{:S(2)}) async-start(), calls=%async_computation.14 | async-start | bytes 5570560 | tf_op jit(solution)/shard_map/reduce_scatter | solution.py:767
  416.4 17.0 %collective-permute-start.25 = (f32[4,640]{1,0:T(4,128)S(1)}, f32[4,640]{1,0:T(4,128)S(1)}, u32[]{:S(2)}, u32[]{:S(2)}) collective-permute-start(f32[4,640]{1,0:T(4,128)S(1)} %pad_maximum_fusion.4), channel_id=1, source_target_pairs={{12,0},{13,1},{14,2},{15,3},{28,16},{29,17},{30,18},{31,19}} | collective-permute-start | bytes 30728 | tf_op jit(solution)/shard_map/ppermute | solution.py:29
  417.7 16.2 %collective-permute-start.24 = (f32[4,640]{1,0:T(4,128)S(1)}, f32[4,640]{1,0:T(4,128)S(1)}, u32[]{:S(2)}, u32[]{:S(2)}) collective-permute-start(f32[4,640]{1,0:T(4,128)S(1)} %pad_maximum_fusion.4), channel_id=1, source_target_pairs={{8,0},{12,4},{9,1},{13,5},{10,2},{14,6},{11,3},{15,7},{24,16},{28,... | collective-permute-start | bytes 30728 | tf_op jit(solution)/shard_map/ppermute | solution.py:29
  419.0 14.9 %collective-permute-start.23 = (f32[4,640]{1,0:T(4,128)S(1)}, f32[4,640]{1,0:T(4,128)S(1)}, u32[]{:S(2)}, u32[]{:S(2)}) collective-permute-start(f32[4,640]{1,0:T(4,128)S(1)} %pad_maximum_fusion.4), channel_id=1, source_target_pairs={{4,0},{8,4},{12,8},{5,1},{9,5},{13,9},{6,2},{10,6},{14,10},{7,3},{... | collective-permute-start | bytes 30728 | tf_op jit(solution)/shard_map/ppermute | solution.py:29
  426.8 7.7 %collective-permute-start.27 = (bf16[1024,640]{1,0:T(8,128)(2,1)}, bf16[1024,640]{1,0:T(8,128)(2,1)}, u32[]{:S(2)}, u32[]{:S(2)}) collective-permute-start(bf16[1024,640]{1,0:T(8,128)(2,1)} %get-tuple-element.234), channel_id=1, source_target_pairs={{0,16},{16,0},{1,17},{17,1},{2,18},{18,2},{3,19},{19,3},{4,20},{20... | collective-permute-start | bytes 3932168 | tf_op jit(solution)/shard_map/ppermute | solution.py:24
  433.4 88.6 %collective-permute-start.36 = (bf16[1024,640]{1,0:T(8,128)(2,1)}, bf16[1024,640]{1,0:T(8,128)(2,1)}, u32[]{:S(2)}, u32[]{:S(2)}) collective-permute-start(bf16[1024,640]{1,0:T(8,128)(2,1)} %get-tuple-element.274), channel_id=1, source_target_pairs={{0,16},{16,0},{1,17},{17,1},{2,18},{18,2},{3,19},{19,3},{4,20},{20... | collective-permute-start | bytes 3932168 | tf_op jit(solution)/shard_map/ppermute | solution.py:24
  450.8 8.8 %copy-start.22 = (f32[8,640]{1,0:T(8,128)S(1)}, f32[8,640]{1,0:T(8,128)}, u32[]{:S(2)}) copy-start(f32[8,640]{1,0:T(8,128)} %get-tuple-element.243) | copy-start | bytes 61444
  450.8 11.1 %copy-start.21 = (f32[8,640]{1,0:T(8,128)S(1)}, f32[8,640]{1,0:T(8,128)}, u32[]{:S(2)}) copy-start(f32[8,640]{1,0:T(8,128)} %get-tuple-element.265) | copy-start | bytes 61444
  460.4 8.1 %collective-permute-start.28 = (f32[16,640]{1,0:T(8,128)S(1)}, f32[16,640]{1,0:T(8,128)S(1)}, u32[]{:S(2)}, u32[]{:S(2)}) collective-permute-start(f32[16,640]{1,0:T(8,128)S(1)} %pad_maximum_fusion.2), channel_id=1, source_target_pairs={{4,0},{8,4},{12,8},{5,1},{9,5},{13,9},{6,2},{10,6},{14,10},{7,3},{... | collective-permute-start | bytes 122888 | tf_op jit(solution)/shard_map/ppermute | solution.py:29
  492.8 10.2 %copy-start.16 = (bf16[8,160,160]{2,1,0:T(8,128)(2,1)S(1)}, bf16[8,160,160]{2,1,0:T(8,128)(2,1)}, u32[]{:S(2)}) copy-start(bf16[8,160,160]{2,1,0:T(8,128)(2,1)} %get-tuple-element.264) | copy-start | bytes 1228804
  493.6 15.9 %collective-permute-start.33 = (f32[2,2048]{1,0:T(2,128)S(1)}, f32[2,2048]{1,0:T(2,128)S(1)}, u32[]{:S(2)}, u32[]{:S(2)}) collective-permute-start(f32[2,2048]{1,0:T(2,128)S(1)} %pad_maximum_fusion.3), channel_id=1, source_target_pairs={{0,2},{1,3},{2,0},{3,1},{4,6},{5,7},{6,4},{7,5},{8,10},{9,11},{10,... | collective-permute-start | bytes 49160 | tf_op jit(solution)/shard_map/ppermute | solution.py:24
  496.4 13.1 %collective-permute-start.34 = (f32[2,2048]{1,0:T(2,128)S(1)}, f32[2,2048]{1,0:T(2,128)S(1)}, u32[]{:S(2)}, u32[]{:S(2)}) collective-permute-start(f32[2,2048]{1,0:T(2,128)S(1)} %pad_maximum_fusion.3), channel_id=1, source_target_pairs={{0,3},{1,0},{2,1},{3,2},{4,7},{5,4},{6,5},{7,6},{8,11},{9,8},{10,9... | collective-permute-start | bytes 49160 | tf_op jit(solution)/shard_map/ppermute | solution.py:24
  497.9 11.7 %collective-permute-start.32 = (f32[2,2048]{1,0:T(2,128)S(1)}, f32[2,2048]{1,0:T(2,128)S(1)}, u32[]{:S(2)}, u32[]{:S(2)}) collective-permute-start(f32[2,2048]{1,0:T(2,128)S(1)} %pad_maximum_fusion.3), channel_id=1, source_target_pairs={{0,1},{1,2},{2,3},{3,0},{4,5},{5,6},{6,7},{7,4},{8,9},{9,10},{10,1... | collective-permute-start | bytes 49160 | tf_op jit(solution)/shard_map/ppermute | solution.py:24
  498.5 81.7 %all-to-all-start.7 = ((bf16[4,80,2048]{2,1,0:T(8,128)(2,1)}), bf16[4,80,2048]{2,1,0:T(8,128)(2,1)S(1)}, u32[]{:S(2)}, u32[]{:S(2)}) async-start(bf16[4,80,2048]{2,1,0:T(8,128)(2,1)} %bitcast.67), calls=%async_computation.8 | async-start | bytes 2621440 | tf_op jit(solution)/shard_map/all_to_all | solution.py:321
  503.0 92.4 %reduce-scatter.8.cloned.1.call-start = ((), (), s32[]{:S(2)}) async-start(), calls=%async_computation.15 | async-start | bytes 3276800 | tf_op jit(solution)/shard_map/reduce_scatter | solution.py:767
  509.5 12.4 %collective-permute-start.37 = (bf16[1024,640]{1,0:T(8,128)(2,1)}, bf16[1024,640]{1,0:T(8,128)(2,1)S(1)}, u32[]{:S(2)}, u32[]{:S(2)}) collective-permute-start(bf16[1024,640]{1,0:T(8,128)(2,1)} %get-tuple-element.279), channel_id=1, source_target_pairs={{0,16},{16,0},{1,17},{17,1},{2,18},{18,2},{3,19},{19,3},{4,20},{20... | collective-permute-start | bytes 3932168 | tf_op jit(solution)/shard_map/ppermute | solution.py:24
  509.8 12.2 %copy-start = (bf16[8,176,160]{2,1,0:T(8,128)(2,1)}, bf16[8,176,160]{2,1,0:T(8,128)(2,1)S(1)}, u32[]{:S(2)}) copy-start(bf16[8,176,160]{2,1,0:T(8,128)(2,1)S(1)} %constant_dynamic-update-slice_fusion.refs_0_) | copy-start | bytes 1351684
  511.0 4.9 collective-permute-start.35
  511.5 25.5 %collective-permute-start.29 = (bf16[80,2048]{1,0:T(8,128)(2,1)}, bf16[80,2048]{1,0:T(8,128)(2,1)}, u32[]{:S(2)}, u32[]{:S(2)}) collective-permute-start(bf16[80,2048]{1,0:T(8,128)(2,1)} %get-tuple-element.261), channel_id=1, source_target_pairs={{0,1},{1,2},{2,3},{3,0},{4,5},{5,6},{6,7},{7,4},{8,9},{9,10},{10,1... | collective-permute-start | bytes 983048 | tf_op jit(solution)/shard_map/ppermute | solution.py:24
  513.5 42.5 %collective-permute-start.30 = (bf16[80,2048]{1,0:T(8,128)(2,1)}, bf16[80,2048]{1,0:T(8,128)(2,1)}, u32[]{:S(2)}, u32[]{:S(2)}) collective-permute-start(bf16[80,2048]{1,0:T(8,128)(2,1)} %get-tuple-element.262), channel_id=1, source_target_pairs={{0,2},{1,3},{2,0},{3,1},{4,6},{5,7},{6,4},{7,5},{8,10},{9,11},{10,... | collective-permute-start | bytes 983048 | tf_op jit(solution)/shard_map/ppermute | solution.py:24
  515.8 40.2 %collective-permute-start.31 = (bf16[80,2048]{1,0:T(8,128)(2,1)}, bf16[80,2048]{1,0:T(8,128)(2,1)}, u32[]{:S(2)}, u32[]{:S(2)}) collective-permute-start(bf16[80,2048]{1,0:T(8,128)(2,1)} %get-tuple-element.263), channel_id=1, source_target_pairs={{0,3},{1,0},{2,1},{3,2},{4,7},{5,4},{6,5},{7,6},{8,11},{9,8},{10,9... | collective-permute-start | bytes 983048 | tf_op jit(solution)/shard_map/ppermute | solution.py:24
  531.6 30.4 %collective-permute-start.40 = (bf16[8,176,160]{1,2,0:T(8,128)(2,1)S(1)}, bf16[8,176,160]{1,2,0:T(8,128)(2,1)S(1)}, u32[]{:S(2)}, u32[]{:S(2)}) collective-permute-start(bf16[8,176,160]{1,2,0:T(8,128)(2,1)S(1)} %copy.61), channel_id=1, source_target_pairs={{0,12},{4,0},{8,4},{12,8},{1,13},{5,1},{9,5},{13,9},{2,14},{6,2},{... | collective-permute-start | bytes 1351688 | tf_op jit(solution)/shard_map/ppermute | solution.py:24
  533.4 35.1 %collective-permute-start.39 = (bf16[8,176,160]{1,2,0:T(8,128)(2,1)S(1)}, bf16[8,176,160]{1,2,0:T(8,128)(2,1)S(1)}, u32[]{:S(2)}, u32[]{:S(2)}) collective-permute-start(bf16[8,176,160]{1,2,0:T(8,128)(2,1)S(1)} %copy.61), channel_id=1, source_target_pairs={{0,8},{4,12},{8,0},{12,4},{1,9},{5,13},{9,1},{13,5},{2,10},{6,14},... | collective-permute-start | bytes 1351688 | tf_op jit(solution)/shard_map/ppermute | solution.py:24
  536.9 40.9 %collective-permute-start.38 = (bf16[8,176,160]{1,2,0:T(8,128)(2,1)S(1)}, bf16[8,176,160]{1,2,0:T(8,128)(2,1)}, u32[]{:S(2)}, u32[]{:S(2)}) collective-permute-start(bf16[8,176,160]{1,2,0:T(8,128)(2,1)S(1)} %copy.61), channel_id=1, source_target_pairs={{0,4},{4,8},{8,12},{12,0},{1,5},{5,9},{9,13},{13,1},{2,6},{6,10},{... | collective-permute-start | bytes 1351688 | tf_op jit(solution)/shard_map/ppermute | solution.py:24
  (38 other events, 120.5 us)
Sparse Core Ops, SparseCore 0:
  10.7 54.8 all-gather.2
  67.6 98.8 all-gather.4
  344.0 94.1 reduce-scatter.3
  442.5 59.5 reduce-scatter.5
  536.0 56.8 reduce-scatter.7

commit v4 on v3

--- a/solution.py
+++ b/solution.py
@@ -261,7 +261,7 @@
 
 
 COSTS = (
-    0.2, 3, 0.2, 6, 6, 7, 7, 5.7, 5.7, 3, 3, 27, 27, 3.4, 21, 60, 0.01, 0.01, 7.5, 7.5, 6, 7, 8, 40.0, 40.0, 0.01, 0.01, 0.01, 0.01, 0.01, 0.01, 0.01, 0.01, 0.01, 3, 10000.0, 1, 3,
+    0.2, 3, 0.2, 6, 0.01, 6, 5.7, 7, 5.7, 3, 3, 27, 27, 3.4, 21, 60, 0.01, 0.01, 7.5, 7.5, 6, 7, 8, 40, 40, 0.01, 0.01, 0.01, 0.01, 0.01, 0.01, 0.01, 0.01, 0.01, 3, 10000.0, 1, 3,
 )
 
 
@@ -927,10 +927,14 @@
     groups, members = lax.axis_size("fsdp"), lax.axis_size("context")
     group_place = lax.axis_index("fsdp").reshape(1).astype(jnp.int32)
     normed = [first(clock, x_rows[0], gain_one_row, copies[0])]
-    cot_copies = all_copies(clock, cot_rows, parts, (gate_w, params, *mask))
+    cot_copies = all_copies(clock, cot_rows[:1], parts, (gate_w, params, *mask))
     normed += [first(clock, x_rows[i], gain_one_row, copies[i]) for i in turns if i]
     one_blocks = [spread(normed[i], apart[i]) for i in turns]
-    (cot_all,) = spread(cot_copies, False)
+    cots = spread(cot_copies, False)
+    later = cot_rows[1:]
+    if later:
+        second_w, later = lax.optimization_barrier((second_w, later))
+        cots += [lax.all_gather(rows_in, "tensor", axis=0, tiled=True) for rows_in in later]
     projections, halo, scans, mixes, ends_in = [], [], [], [], []
 
     def start_chain(i):
@@ -944,12 +948,17 @@
     def mix_chain(i):
         mixes.append(mix_out(
             clock, place, scans[i][4], scans[i][3], ends_in[i], projections[i][1], first_w, outs[i], 512,
-            () if i else (cot_all,),
+            () if i else tuple(cots[:1]),
         ))
 
-    for step in (start_chain, scan_chain, mix_chain):
-        for i in turns:
-            step(i)
+    start_chain(0)
+    scan_chain(0)
+    for i in turns:
+        if i + 1 < count:
+            start_chain(i + 1)
+        mix_chain(i)
+        if i + 1 < count:
+            scan_chain(i + 1)
     wide_one, both_pre, tails = map(list, zip(*projections))
     conv_low, pre, decays, prods, locals_, ends = map(list, zip(*scans))
     state_in = ends_in
@@ -957,11 +966,11 @@
     out_terms = [gathered_sums(p) for p in out_part]
     residual, two_blocks = [], []
     for i in turns:
-        res, low = second(clock, x_rows[i], gain_two_row, out_terms[i], copies[i], two_blocks[-1] if i else out_terms[-1])
+        res, low = second(clock, x_rows[i], gain_two_row, out_terms[i], copies[i])
         residual.append(res)
         two_blocks.append(spread(low, apart[i]))
     mlps = [
-        mlp(clock, place, two_blocks[i], cot_all, i, count, rows, second_w, outs[i], 256) for i in turns
+        mlp(clock, place, two_blocks[i], cots[i], 0, 1, rows, second_w, outs[i], 256) for i in turns
     ]
     wide_two, wide_cot, hidden_low, pair_low, two_part = map(list, zip(*mlps))
     two_terms = [gathered_sums(p) for p in two_part]

time: 616 us -> 628 us (1.019)
  waiting for transfers between devices: 149 us -> 175 us
  starting transfers between devices: 128 us -> 118 us
    ppermute x29, waiting for transfers between devices: 84.6 us -> 124 us  [shift(): lax.ppermute(value, axis, [(i, (i + by) % size) for i in range(size)])]
    all_to_all x4, waiting for transfers between devices: 58.4 us -> 33.1 us  [spread(): lax.all_to_all(copies, 'tensor', split_axis=0, concat_axis=0, tiled=True)]
    ppermute x29, starting transfers between devices: 65.1 us -> 54.3 us  [shift(): lax.ppermute(value, axis, [(i, (i + by) % size) for i in range(size)])]
    all_to_all x4, waiting for transfers between devices: 0.01 us -> 7.47 us  [gathered_sums(): lax.all_to_all(parts[0], 'tensor', split_axis=0, concat_axis=0, tiled=True)]
    unnamed x100 -> x106, local copies, waits for them, and re-layouts: 17.8 us -> 15.4 us
  transfers between devices with their start and end apart: 54 -> 55, of which waited for: 11 -> 15; matrix products, arithmetic and copies ran while one was open for 7% -> 7% of each run, Pallas kernels for 41% -> 40%
where the time goes in v4:
time: 628 us; the launch traced here: 617 us
  Pallas kernels  249 us (40%)
  waiting for transfers between devices  175 us (28%)
  starting transfers between devices  118 us (19%)
  local copies, waits for them, and re-layouts  38.5 us (6%)
  other arithmetic  20.4 us (3%)
  between operations  15.4 us (2%)
    pallas_call x38, Pallas kernels, call(): pl.pallas_call(body, out_shape=list(out_shape) + [jax.ShapeDtypeStruct((T...  249 us
    ppermute x29, waiting for transfers between devices, shift(): lax.ppermute(value, axis, [(i, (i + by) % size) for i in range(size)])  124 us
    ppermute x29, starting transfers between devices, shift(): lax.ppermute(value, axis, [(i, (i + by) % size) for i in range(size)])  54.3 us
    all_to_all x4, waiting for transfers between devices, spread(): lax.all_to_all(copies, 'tensor', split_axis=0, concat_axis=0, tiled=True)  33.1 us
    ppermute x12, starting transfers between devices, step_by(): lax.ppermute(value, axis, [(i, i + by) for i in range(size) if 0 <= i + b...  26.8 us
    all_to_all x4, starting transfers between devices, gathered_sums(): lax.all_to_all(parts[0], 'tensor', split_axis=0, concat_axis=0, tiled=True)  18.7 us
    all_to_all x4, starting transfers between devices, spread(): lax.all_to_all(copies, 'tensor', split_axis=0, concat_axis=0, tiled=True)  18 us
    unnamed x106, local copies, waits for them, and re-layouts  15.4 us
  transfers between devices with their start and end apart: 55, of which 15 were waited for; matrix products, arithmetic and copies ran while one was open for 7% of the time, Pallas kernels for 40%

profile of v4, /device:TPU:0, one launch (start us, length us, event | category | flops | bytes accessed | tf_op | source)
XLA Modules:
  0.0 616.6 jit_solution(4687519014904247257)
XLA Ops:
  18.4 6.5 %all-to-all-start = ((bf16[4,80,2048]{2,1,0:T(8,128)(2,1)}), bf16[4,80,2048]{2,1,0:T(8,128)(2,1)S(1)}, u32[]{:S(2)}, u32[]{:S(2)}) async-start(bf16[4,80,2048]{2,1,0:T(8,128)(2,1)} %bitcast.68), calls=%async_computation | async-start | bytes 2621440 | tf_op jit(solution)/shard_map/all_to_all | solution.py:315
  25.4 8.4 %fusion.24.refs_1_.refs_4_.refs_14_ = bf16[640,1280]{1,0:T(8,128)(2,1)} fusion(bf16[160,160]{1,0:T(8,128)(2,1)S(1)} %get-tuple-element.378, bf16[160,160]{1,0:T(8,128)(2,1)S(1)} %get-tuple-element.379, bf16[160,160]{1,0:T(8,128)(2,1)S(1)} %get-tuple-element.377, bf16[160,160]{1,0:T(8,128)(2,1)S(1)} %get-tuple-element.376, ...), kind=kLoop, calls=%fused_computation.33 | loop fusion | flops 40960000 | bytes 2048000 | tf_op jit(solution)/shard_map/concatenate | solution.py:902
  41.1 3.8 collective-permute-start.6
  46.0 25.3 %all-to-all-done = bf16[4,80,2048]{2,1,0:T(8,128)(2,1)S(1)} async-done(((bf16[4,80,2048]{2,1,0:T(8,128)(2,1)}), bf16[4,80,2048]{2,1,0:T(8,128)(2,1)S(1)}, u32[]{:S(2)}, u32[]{:S(2)}) %all-to-all-start) | async-done | bytes 1310752 | tf_op jit(solution)/shard_map/all_to_all | solution.py:315
  71.3 3.6 all-to-all-start.1
  75.0 6.7 %shard_map.308 = (bf16[320,2048]{1,0:T(8,128)(2,1)}, f32[320,1280]{1,0:T(8,128)}, bf16[8,640]{1,0:T(8,128)(2,1)}, f32[8,128]{1,0:T(8,128)}) custom-call(s32[1]{0:T(128)} %bitcast.2.refs_0_, bf16[320,2048]{1,0:T(8,128)(2,1)} %bitcast.67, bf16[2048,1920]{1,0:T(8,128)(2,1)} %all-gather.4.cloned.1.call-done.refs_2_.refs_5_.refs_4_, ...), custom_call_target="tpu_custom_call" | custom-call | flops 17999998976 | bytes 17999998976 | tf_op jit(solution)/shard_map/pallas_call | solution.py:284
  81.7 3.4 collective-permute-start
  87.3 6.9 %shard_map.309 = (bf16[320,640]{1,0:T(8,128)(2,1)}, f32[320,1280]{1,0:T(8,128)}, f32[320,640]{1,0:T(8,128)}, f32[320,640]{1,0:T(8,128)}, f32[320,640]{1,0:T(8,128)}, /*index=5*/f32[2,640]{1,0:T(2,128)}, f32[8,128]{1,0:T(8,128)}) custom-call(f32[320,1280]{1,0:T(8,128)} %get-tuple-element.165.refs_0_.refs_4_.refs_3_.refs_9_.refs_10_, ...), custom_call_target="tpu_custom_call" | custom-call | flops 30000000 | bytes 30000000 | tf_op jit(solution)/shard_map/pallas_call | solution.py:284
  94.2 5.3 collective-permute-start.3
  100.9 2.5 collective-permute-start.1
  104.1 5.9 shard_map.310
  113.6 6.0 shard_map.311
  119.6 5.0 all-to-all-start.2
  125.1 6.9 %shard_map.312 = (bf16[320,640]{1,0:T(8,128)(2,1)}, f32[320,1280]{1,0:T(8,128)}, f32[320,640]{1,0:T(8,128)}, f32[320,640]{1,0:T(8,128)}, f32[320,640]{1,0:T(8,128)}, /*index=5*/f32[2,640]{1,0:T(2,128)}, f32[8,128]{1,0:T(8,128)}) custom-call(f32[320,1280]{1,0:T(8,128)} %get-tuple-element.176.refs_0_.refs_4_.refs_6_.refs_9_.refs_10_, ...), custom_call_target="tpu_custom_call" | custom-call | flops 20999999488 | bytes 20999999488 | tf_op jit(solution)/shard_map/pallas_call | solution.py:284
  132.1 3.2 collective-permute-start.10
  141.2 5.8 shard_map.313
  147.0 7.5 %all-to-all-done.2 = bf16[4,80,2048]{2,1,0:T(8,128)(2,1)S(1)} async-done(((bf16[4,80,2048]{2,1,0:T(8,128)(2,1)}), bf16[4,80,2048]{2,1,0:T(8,128)(2,1)S(1)}, u32[]{:S(2)}, u32[]{:S(2)}) %all-to-all-start.2) | async-done | bytes 1310752 | tf_op jit(solution)/shard_map/all_to_all | solution.py:321
  155.6 3.0 shard_map.314
  158.6 3.7 all-to-all-start.3
  168.3 27.8 %collective-permute-done.11.refs_3_ = bf16[80,2048]{1,0:T(8,128)(2,1)S(1)} collective-permute-done((bf16[80,2048]{1,0:T(8,128)(2,1)S(1)}, bf16[80,2048]{1,0:T(8,128)(2,1)S(1)}, u32[]{:S(2)}, u32[]{:S(2)}) %collective-permute-start.11) | collective-permute-done | bytes 327712 | tf_op jit(solution)/shard_map/ppermute | solution.py:24
  196.0 19.1 %collective-permute-done.12.refs_4_ = bf16[80,2048]{1,0:T(8,128)(2,1)S(1)} collective-permute-done((bf16[80,2048]{1,0:T(8,128)(2,1)S(1)}, bf16[80,2048]{1,0:T(8,128)(2,1)S(1)}, u32[]{:S(2)}, u32[]{:S(2)}) %collective-permute-start.12) | collective-permute-done | bytes 327712 | tf_op jit(solution)/shard_map/ppermute | solution.py:24
  216.0 2.6 shard_map.315
  218.6 7.4 %collective-permute-start.16 = (bf16[80,2048]{1,0:T(8,128)(2,1)}, bf16[80,2048]{1,0:T(8,128)(2,1)S(1)}, u32[]{:S(2)}, u32[]{:S(2)}) collective-permute-start(bf16[80,2048]{1,0:T(8,128)(2,1)} %get-tuple-element.195.refs_1_), channel_id=1, source_target_pairs={{0,3},{1,0},{2,1},{3,2},{4,7},{5,4},{6,5},{7,6},{8,11},{9,8},{10,9... | collective-permute-start | bytes 983048 | tf_op jit(solution)/shard_map/ppermute | solution.py:24
  227.7 26.9 %shard_map.316 = (bf16[320,2048]{1,0:T(8,128)(2,1)}, bf16[320,2048]{1,0:T(8,128)(2,1)}, bf16[320,1536]{1,0:T(8,128)(2,1)}, bf16[2,320,1536]{2,1,0:T(8,128)(2,1)}...) custom-call(s32[1]{0:T(128)} %bitcast.2.refs_0_, bf16[320,2048]{1,0:T(8,128)(2,1)} %bitcast.71, bf16[320,2048]{1,0:T(8,128)(2,1)} %bitcast.64, ...), custom_call_target="tpu_custom_call" | custom-call | flops 80999997440 | bytes 80999997440 | tf_op jit(solution)/shard_map/pallas_call | solution.py:284
  254.6 5.0 all-to-all-start.4
  259.6 31.2 %collective-permute-done.15.refs_3_ = bf16[80,2048]{1,0:T(8,128)(2,1)S(1)} collective-permute-done((bf16[80,2048]{1,0:T(8,128)(2,1)}, bf16[80,2048]{1,0:T(8,128)(2,1)S(1)}, u32[]{:S(2)}, u32[]{:S(2)}) %collective-permute-start.15) | collective-permute-done | bytes 327712 | tf_op jit(solution)/shard_map/ppermute | solution.py:24
  292.6 26.9 %shard_map.317 = (bf16[320,2048]{1,0:T(8,128)(2,1)}, bf16[320,2048]{1,0:T(8,128)(2,1)}, bf16[320,1536]{1,0:T(8,128)(2,1)}, bf16[2,320,1536]{2,1,0:T(8,128)(2,1)}...) custom-call(s32[1]{0:T(128)} %bitcast.2.refs_0_, ...), custom_call_target="tpu_custom_call" | custom-call | flops 80999997440 | bytes 80999997440 | tf_op jit(solution)/shard_map/pallas_call | solution.py:284
  319.7 3.7 collective-permute-start.19
  324.5 3.5 shard_map.318
  328.1 4.3 all-to-all-start.6
  332.4 15.5 %shard_map.319 = (bf16[2048,3072]{1,0:T(8,128)(2,1)}, f32[8,128]{1,0:T(8,128)}) custom-call(bf16[320,2048]{1,0:T(8,128)(2,1)} %get-tuple-element.205.refs_0_, bf16[320,2048]{1,0:T(8,128)(2,1)} %get-tuple-element.206.refs_1_, bf16[2,320,1536]{2,1,0:T(8,128)(2,1)} %get-tuple-element.207.refs_2_, bf16[2,320,1536]{2,1,0:T(8,128)(2,1)} %get-tuple-element.208.refs_3_, ...), custom_call_target="tpu_custom_call" | custom-call | flops 62999998464 | bytes 62999998464 | tf_op jit(solution)/shard_map/pallas_call | solution.py:284
  348.9 3.2 shard_map.320
  352.1 3.7 collective-permute-start.22
  355.8 11.1 %collective-permute-start.21 = (bf16[80,2048]{1,0:T(8,128)(2,1)}, bf16[80,2048]{1,0:T(8,128)(2,1)}, u32[]{:S(2)}, u32[]{:S(2)}) collective-permute-start(bf16[80,2048]{1,0:T(8,128)(2,1)} %get-tuple-element.224.refs_1_), channel_id=1, source_target_pairs={{0,2},{1,3},{2,0},{3,1},{4,6},{5,7},{6,4},{7,5},{8,10},{9,11},{10,... | collective-permute-start | bytes 983048 | tf_op jit(solution)/shard_map/ppermute | solution.py:24
  367.1 10.8 %shard_map.321 = (bf16[1024,1536]{1,0:T(8,128)(2,1)}, bf16[1024,1536]{1,0:T(8,128)(2,1)}, f32[8,128]{1,0:T(8,128)}) custom-call(s32[1]{0:T(128)} %bitcast.25.refs_0_, bf16[320,2048]{1,0:T(8,128)(2,1)} %get-tuple-element.199.refs_1_, bf16[320,2048]{1,0:T(8,128)(2,1)} %get-tuple-element.200.refs_2_, bf16[320,1536]{1,0:T(8,128)(2,1)} %get-tuple-element.194.refs_3_.refs_0_, ...), custom_call_target="tpu_custom_call" | custom-call | flops 30000000 | bytes 30000000 | tf_op jit(solution)/shard_map/pallas_call | solution.py:284
  378.5 8.5 %shard_map.322 = (bf16[640,2048]{1,0:T(8,128)(2,1)}, f32[8,128]{1,0:T(8,128)}) custom-call(bf16[320,1536]{1,0:T(8,128)(2,1)} %get-tuple-element.194.refs_3_.refs_0_, bf16[320,1536]{1,0:T(8,128)(2,1)} %get-tuple-element.198.refs_4_.refs_1_, bf16[2048,4608]{1,0:T(8,128)(2,1)} %all-gather.6.cloned.1.call-done.refs_3_.refs_4_.refs_5_.refs_6_.refs_7_.refs_8_.refs_2_, ...), custom_call_target="tpu_custom_call" | custom-call | flops 30000000 | bytes 30000000 | tf_op jit(solution)/shard_map/pallas_call | solution.py:284
  387.0 7.8 %all-to-all-done.6 = bf16[4,80,2048]{2,1,0:T(8,128)(2,1)} async-done(((bf16[4,80,2048]{2,1,0:T(8,128)(2,1)}), bf16[4,80,2048]{2,1,0:T(8,128)(2,1)}, u32[]{:S(2)}, u32[]{:S(2)}) %all-to-all-start.6) | async-done | bytes 1310752 | tf_op jit(solution)/shard_map/all_to_all | solution.py:315
  394.8 4.6 all-to-all-start.5
  399.4 7.4 %shard_map.323 = (bf16[320,2048]{1,0:T(8,128)(2,1)}, bf16[320,640]{1,0:T(8,128)(2,1)}, f32[320,640]{1,0:T(8,128)}, f32[320,640]{1,0:T(8,128)}, f32[2,640]{1,0:T(2,128)}, /*index=5*/f32[8,128]{1,0:T(8,128)}) custom-call(s32[1]{0:T(128)} %bitcast.2.refs_0_, bf16[320,2048]{1,0:T(8,128)(2,1)} %bitcast.31.refs_1_, ...), custom_call_target="tpu_custom_call" | custom-call | flops 22499999744 | bytes 22499999744 | tf_op jit(solution)/shard_map/pallas_call | solution.py:284
  407.6 15.3 %collective-permute-done.21.refs_3_ = bf16[80,2048]{1,0:T(8,128)(2,1)} collective-permute-done((bf16[80,2048]{1,0:T(8,128)(2,1)}, bf16[80,2048]{1,0:T(8,128)(2,1)}, u32[]{:S(2)}, u32[]{:S(2)}) %collective-permute-start.21) | collective-permute-done | bytes 327712 | tf_op jit(solution)/shard_map/ppermute | solution.py:24
  422.9 7.4 %shard_map.324 = (bf16[320,2048]{1,0:T(8,128)(2,1)}, bf16[320,640]{1,0:T(8,128)(2,1)}, f32[320,640]{1,0:T(8,128)}, f32[320,640]{1,0:T(8,128)}, f32[2,640]{1,0:T(2,128)}, /*index=5*/f32[8,128]{1,0:T(8,128)}) custom-call(s32[1]{0:T(128)} %bitcast.2.refs_0_, bf16[80,2048]{1,0:T(8,128)(2,1)} %get-tuple-element.224.refs_1_, ...), custom_call_target="tpu_custom_call" | custom-call | flops 22499999744 | bytes 22499999744 | tf_op jit(solution)/shard_map/pallas_call | solution.py:284
  435.0 6.5 %shard_map.325 = (bf16[1024,640]{1,0:T(8,128)(2,1)}, bf16[1024,640]{1,0:T(8,128)(2,1)}, f32[8,128]{1,0:T(8,128)}) custom-call(s32[1]{0:T(128)} %bitcast.25.refs_0_, bf16[320,2048]{1,0:T(8,128)(2,1)} %get-tuple-element.233.refs_1_.refs_5_, bf16[320,2048]{1,0:T(8,128)(2,1)} %get-tuple-element.234.refs_2_.refs_5_, ...), custom_call_target="tpu_custom_call" | custom-call | flops 17999998976 | bytes 17999998976 | tf_op jit(solution)/shard_map/pallas_call | solution.py:284
  441.5 6.5 %shard_map.326 = (bf16[1024,640]{1,0:T(8,128)(2,1)}, bf16[1024,640]{1,0:T(8,128)(2,1)}, f32[8,128]{1,0:T(8,128)}) custom-call(s32[1]{0:T(128)} %bitcast.25.refs_0_, bf16[320,2048]{1,0:T(8,128)(2,1)} %get-tuple-element.239.refs_1_, bf16[320,2048]{1,0:T(8,128)(2,1)} %get-tuple-element.240.refs_2_, bf16[320,640]{1,0:T(8,128)(2,1)} %get-tuple-element.241.refs_3_, ...), custom_call_target="tpu_custom_call" | custom-call | flops 20999999488 | bytes 20999999488 | tf_op jit(solution)/shard_map/pallas_call | solution.py:284
  450.9 6.2 %shard_map.327 = (bf16[1024,2176]{1,0:T(8,128)(2,1)}, f32[8,128]{1,0:T(8,128)}) custom-call(bf16[1024,1536]{1,0:T(8,128)(2,1)} %get-tuple-element.231.refs_0_, bf16[1024,1536]{1,0:T(8,128)(2,1)} %copy-done.34, bf16[1024,640]{1,0:T(8,128)(2,1)} %get-tuple-element.237.refs_2_, bf16[1024,640]{1,0:T(8,128)(2,1)} %collective-permute-done.27.refs_3_, ...), custom_call_target="tpu_custom_call" | custom-call | flops 24000000000 | bytes 24000000000 | tf_op jit(solution)/shard_map/pallas_call | solution.py:284
  457.1 8.5 %shard_map.328 = (bf16[320,1280]{1,0:T(8,128)(2,1)}, f32[320,640]{1,0:T(8,128)}, f32[8,640]{1,0:T(8,128)}, f32[8,640]{1,0:T(8,128)}, f32[8,128]{1,0:T(8,128)}) custom-call(f32[320,640]{1,0:T(8,128)} %get-tuple-element.221.refs_0_, f32[320,640]{1,0:T(8,128)} %get-tuple-element.222.refs_1_, f32[1,640]{1,0:T(1,128)} %get-tuple-element.385.refs_2_, ...), custom_call_target="tpu_custom_call" | custom-call | flops 120000004096 | bytes 120000004096 | tf_op jit(solution)/shard_map/pallas_call | solution.py:284
  465.5 8.6 %shard_map.329 = (bf16[320,1280]{1,0:T(8,128)(2,1)}, f32[320,640]{1,0:T(8,128)}, f32[8,640]{1,0:T(8,128)}, f32[8,640]{1,0:T(8,128)}, f32[8,128]{1,0:T(8,128)}) custom-call(f32[320,640]{1,0:T(8,128)} %get-tuple-element.248.refs_0_, f32[320,640]{1,0:T(8,128)} %get-tuple-element.249.refs_1_, f32[1,640]{1,0:T(1,128)} %get-tuple-element.384.refs_2_, ...), custom_call_target="tpu_custom_call" | custom-call | flops 120000004096 | bytes 120000004096 | tf_op jit(solution)/shard_map/pallas_call | solution.py:284
  477.2 5.3 collective-permute-done.28
  483.2 3.2 shard_map.330
  486.4 4.5 shard_map.331
  490.9 6.3 %shard_map.332 = (bf16[320,640]{1,0:T(8,128)(2,1)}, f32[1,2048]{1,0:T(1,128)}, bf16[80,2048]{1,0:T(8,128)(2,1)}, bf16[80,2048]{1,0:T(8,128)(2,1)}, bf16[80,2048]...) custom-call(s32[1]{0:T(128)} %bitcast.2.refs_0_, bf16[320,640]{1,0:T(8,128)(2,1)} %get-tuple-element.220.refs_3_.refs_1_, ...), custom_call_target="tpu_custom_call" | custom-call | flops 30000000 | bytes 30000000 | tf_op jit(solution)/shard_map/pallas_call | solution.py:284
  497.2 3.8 shard_map.333
  501.1 6.2 %shard_map.334 = (bf16[320,640]{1,0:T(8,128)(2,1)}, f32[1,2048]{1,0:T(1,128)}, bf16[320,2048]{1,0:T(8,128)(2,1)}, f32[8,128]{1,0:T(8,128)}) custom-call(s32[1]{0:T(128)} %bitcast.2.refs_0_, bf16[320,640]{1,0:T(8,128)(2,1)} %get-tuple-element.235.refs_4_.refs_1_, f32[320,640]{1,0:T(8,128)} %get-tuple-element.272.refs_2_, ...), custom_call_target="tpu_custom_call" | custom-call | flops 30000000 | bytes 30000000 | tf_op jit(solution)/shard_map/pallas_call | solution.py:284
  510.2 4.1 all-to-all-start.7
  514.4 6.5 %shard_map.335 = (bf16[1024,640]{1,0:T(8,128)(2,1)}, bf16[1024,640]{1,0:T(8,128)(2,1)}, f32[8,128]{1,0:T(8,128)}) custom-call(s32[1]{0:T(128)} %bitcast.25.refs_0_, bf16[320,2048]{1,0:T(8,128)(2,1)} %get-tuple-element.233.refs_1_.refs_5_, bf16[320,2048]{1,0:T(8,128)(2,1)} %get-tuple-element.234.refs_2_.refs_5_, bf16[320,640]{1,0:T(8,128)(2,1)} %get-tuple-element.279.refs_3_, ...), custom_call_target="tpu_custom_call" | custom-call | flops 30000000 | bytes 30000000 | tf_op jit(solution)/shard_map/pallas_call | solution.py:284
  534.4 4.7 shard_map.336
  544.8 2.5 collective-permute-start.39
  548.3 2.9 collective-permute-start.38
  551.2 15.5 %collective-permute-done.30.refs_5_ = bf16[80,2048]{1,0:T(8,128)(2,1)} collective-permute-done((bf16[80,2048]{1,0:T(8,128)(2,1)}, bf16[80,2048]{1,0:T(8,128)(2,1)}, u32[]{:S(2)}, u32[]{:S(2)}) %collective-permute-start.30) | collective-permute-done | bytes 327712 | tf_op jit(solution)/shard_map/ppermute | solution.py:24
  566.7 3.1 shard_map.338
  569.8 2.9 shard_map.339
  573.9 5.9 collective-permute-done.39
  581.1 8.3 %collective-permute-done.38 = bf16[8,176,160]{1,2,0:T(8,128)(2,1)} collective-permute-done((bf16[8,176,160]{1,2,0:T(8,128)(2,1)S(1)}, bf16[8,176,160]{1,2,0:T(8,128)(2,1)}, u32[]{:S(2)}, u32[]{:S(2)}) %collective-permute-start.38) | collective-permute-done | bytes 450592 | tf_op jit(solution)/shard_map/ppermute | solution.py:24
  592.7 3.4 shard_map.340
  596.2 3.3 shard_map.341
  (263 shorter events, 99.2 us)
Async XLA Ops:
  7.2 67.8 %all-gather.4.cloned.1.call-start = ((), (), s32[]{:S(2)}) async-start(), calls=%async_computation.11 | async-start | bytes 8847360 | tf_op jit(solution)/shard_map/all_gather | solution.py:896
  10.6 216.0 %all-gather.6.cloned.1.call-start = ((), (), s32[]{:S(2)}) async-start(), calls=%async_computation.12 | async-start | bytes 21233664 | tf_op jit(solution)/shard_map/all_gather | solution.py:899
  18.4 52.9 %all-to-all-start = ((bf16[4,80,2048]{2,1,0:T(8,128)(2,1)}), bf16[4,80,2048]{2,1,0:T(8,128)(2,1)S(1)}, u32[]{:S(2)}, u32[]{:S(2)}) async-start(bf16[4,80,2048]{2,1,0:T(8,128)(2,1)} %bitcast.68), calls=%async_computation | async-start | bytes 2621440 | tf_op jit(solution)/shard_map/all_to_all | solution.py:315
  25.3 10.3 %copy-start.26 = (f32[4,640]{1,0:T(4,128)S(1)}, f32[4,640]{1,0:T(4,128)}, u32[]{:S(2)}) copy-start(f32[4,640]{1,0:T(4,128)} %param.23) | copy-start | bytes 30724
  25.3 10.9 %copy-start.15 = (bf16[2,1,80,2048]{3,2,1,0:T(8,128)(2,1)S(1)}, bf16[2,1,80,2048]{3,2,1,0:T(8,128)(2,1)}, u32[]{:S(2)}) copy-start(bf16[2,1,80,2048]{3,2,1,0:T(8,128)(2,1)} %param.35) | copy-start | bytes 1966084
  41.1 59.8 %collective-permute-start.6 = (bf16[80,2048]{1,0:T(8,128)(2,1)}, bf16[80,2048]{1,0:T(8,128)(2,1)S(1)}, u32[]{:S(2)}, u32[]{:S(2)}) collective-permute-start(bf16[80,2048]{1,0:T(8,128)(2,1)} %get-tuple-element.172.refs_1_), channel_id=1, source_target_pairs={{0,3},{1,0},{2,1},{3,2},{4,7},{5,4},{6,5},{7,6},{8,11},{9,8},{10,9... | collective-permute-start | bytes 983048 | tf_op jit(solution)/shard_map/ppermute | solution.py:24
  44.9 58.4 %collective-permute-start.5 = (bf16[80,2048]{1,0:T(8,128)(2,1)}, bf16[80,2048]{1,0:T(8,128)(2,1)S(1)}, u32[]{:S(2)}, u32[]{:S(2)}) collective-permute-start(bf16[80,2048]{1,0:T(8,128)(2,1)} %get-tuple-element.172.refs_1_), channel_id=1, source_target_pairs={{0,2},{1,3},{2,0},{3,1},{4,6},{5,7},{6,4},{7,5},{8,10},{9,11},{10,... | collective-permute-start | bytes 983048 | tf_op jit(solution)/shard_map/ppermute | solution.py:24
  44.9 58.5 %collective-permute-start.4 = (bf16[80,2048]{1,0:T(8,128)(2,1)}, bf16[80,2048]{1,0:T(8,128)(2,1)}, u32[]{:S(2)}, u32[]{:S(2)}) collective-permute-start(bf16[80,2048]{1,0:T(8,128)(2,1)} %get-tuple-element.172.refs_1_), channel_id=1, source_target_pairs={{0,1},{1,2},{2,3},{3,0},{4,5},{5,6},{6,7},{7,4},{8,9},{9,10},{10,1... | collective-permute-start | bytes 983048 | tf_op jit(solution)/shard_map/ppermute | solution.py:24
  71.3 41.2 %all-to-all-start.1 = ((bf16[4,80,2048]{2,1,0:T(8,128)(2,1)}), bf16[4,80,2048]{2,1,0:T(8,128)(2,1)S(1)}, u32[]{:S(2)}, u32[]{:S(2)}) async-start(bf16[4,80,2048]{2,1,0:T(8,128)(2,1)} %bitcast.69), calls=%async_computation.1 | async-start | bytes 2621440 | tf_op jit(solution)/shard_map/all_to_all | solution.py:315
  81.7 5.0 collective-permute-start
  94.2 17.7 %collective-permute-start.3 = (f32[2,640]{1,0:T(2,128)}, f32[2,640]{1,0:T(2,128)S(1)}, u32[]{:S(2)}, u32[]{:S(2)}) collective-permute-start(f32[2,640]{1,0:T(2,128)} %get-tuple-element.170), channel_id=1, source_target_pairs={{0,12},{1,13},{2,14},{3,15},{16,28},{17,29},{18,30},{19,31}} | collective-permute-start | bytes 15368 | tf_op jit(solution)/shard_map/ppermute | solution.py:29
  99.6 12.4 %collective-permute-start.2 = (f32[2,640]{1,0:T(2,128)}, f32[2,640]{1,0:T(2,128)S(1)}, u32[]{:S(2)}, u32[]{:S(2)}) collective-permute-start(f32[2,640]{1,0:T(2,128)} %get-tuple-element.170), channel_id=1, source_target_pairs={{0,8},{4,12},{1,9},{5,13},{2,10},{6,14},{3,11},{7,15},{16,24},{20,... | collective-permute-start | bytes 15368 | tf_op jit(solution)/shard_map/ppermute | solution.py:29
  100.9 11.1 %collective-permute-start.1 = (f32[2,640]{1,0:T(2,128)}, f32[2,640]{1,0:T(2,128)S(1)}, u32[]{:S(2)}, u32[]{:S(2)}) collective-permute-start(f32[2,640]{1,0:T(2,128)} %get-tuple-element.170), channel_id=1, source_target_pairs={{0,4},{4,8},{8,12},{1,5},{5,9},{9,13},{2,6},{6,10},{10,14},{3,7},{... | collective-permute-start | bytes 15368 | tf_op jit(solution)/shard_map/ppermute | solution.py:29
  110.0 14.6 %collective-permute-start.7 = (bf16[8,640]{1,0:T(8,128)(2,1)}, bf16[8,640]{1,0:T(8,128)(2,1)S(1)}, u32[]{:S(2)}, u32[]{:S(2)}) collective-permute-start(bf16[8,640]{1,0:T(8,128)(2,1)} %get-tuple-element.177), channel_id=1, source_target_pairs={{0,4},{4,8},{8,12},{1,5},{5,9},{9,13},{2,6},{6,10},{10,14},{3,7},{... | collective-permute-start | bytes 30728 | tf_op jit(solution)/shard_map/ppermute | solution.py:29
  119.6 34.9 %all-to-all-start.2 = ((bf16[4,80,2048]{2,1,0:T(8,128)(2,1)}), bf16[4,80,2048]{2,1,0:T(8,128)(2,1)S(1)}, u32[]{:S(2)}, u32[]{:S(2)}) async-start(bf16[4,80,2048]{2,1,0:T(8,128)(2,1)} %bitcast.74), calls=%async_computation.2 | async-start | bytes 2621440 | tf_op jit(solution)/shard_map/all_to_all | solution.py:321
  132.1 7.0 %collective-permute-start.10 = (f32[2,640]{1,0:T(2,128)}, f32[2,640]{1,0:T(2,128)S(1)}, u32[]{:S(2)}, u32[]{:S(2)}) collective-permute-start(f32[2,640]{1,0:T(2,128)} %get-tuple-element.181), channel_id=1, source_target_pairs={{0,12},{1,13},{2,14},{3,15},{16,28},{17,29},{18,30},{19,31}} | collective-permute-start | bytes 15368 | tf_op jit(solution)/shard_map/ppermute | solution.py:29
  135.3 3.8 collective-permute-start.9
  136.6 4.0 collective-permute-start.8
  158.6 68.1 %all-to-all-start.3 = ((bf16[4,80,2048]{2,1,0:T(8,128)(2,1)}), bf16[4,80,2048]{2,1,0:T(8,128)(2,1)S(1)}, u32[]{:S(2)}, u32[]{:S(2)}) async-start(bf16[4,80,2048]{2,1,0:T(8,128)(2,1)} %bitcast.72), calls=%async_computation.3 | async-start | bytes 2621440 | tf_op jit(solution)/shard_map/all_to_all | solution.py:315
  162.2 130.4 %all-gather.8.cloned.1.call-start = ((), (), s32[]{:S(2)}) async-start(), calls=%async_computation.13 | async-start | bytes 1638400 | tf_op jit(solution)/shard_map/all_gather | solution.py:937
  162.3 33.7 %collective-permute-start.11 = (bf16[80,2048]{1,0:T(8,128)(2,1)S(1)}, bf16[80,2048]{1,0:T(8,128)(2,1)S(1)}, u32[]{:S(2)}, u32[]{:S(2)}) collective-permute-start(bf16[80,2048]{1,0:T(8,128)(2,1)S(1)} %copy-done.46), channel_id=1, source_target_pairs={{0,1},{1,2},{2,3},{3,0},{4,5},{5,6},{6,7},{7,4},{8,9},{9,10},{10,1... | collective-permute-start | bytes 983048 | tf_op jit(solution)/shard_map/ppermute | solution.py:24
  164.2 50.9 %collective-permute-start.12 = (bf16[80,2048]{1,0:T(8,128)(2,1)S(1)}, bf16[80,2048]{1,0:T(8,128)(2,1)S(1)}, u32[]{:S(2)}, u32[]{:S(2)}) collective-permute-start(bf16[80,2048]{1,0:T(8,128)(2,1)S(1)} %copy-done.45), channel_id=1, source_target_pairs={{0,2},{1,3},{2,0},{3,1},{4,6},{5,7},{6,4},{7,5},{8,10},{9,11},{10,... | collective-permute-start | bytes 983048 | tf_op jit(solution)/shard_map/ppermute | solution.py:24
  166.6 48.6 %collective-permute-start.13 = (bf16[80,2048]{1,0:T(8,128)(2,1)S(1)}, bf16[80,2048]{1,0:T(8,128)(2,1)S(1)}, u32[]{:S(2)}, u32[]{:S(2)}) collective-permute-start(bf16[80,2048]{1,0:T(8,128)(2,1)S(1)} %copy-done.44), channel_id=1, source_target_pairs={{0,3},{1,0},{2,1},{3,2},{4,7},{5,4},{6,5},{7,6},{8,11},{9,8},{10,9... | collective-permute-start | bytes 983048 | tf_op jit(solution)/shard_map/ppermute | solution.py:24
  196.0 19.2 %copy-start.47 = (bf16[80,2048]{1,0:T(8,128)(2,1)}, bf16[80,2048]{1,0:T(8,128)(2,1)S(1)}, u32[]{:S(2)}) copy-start(bf16[80,2048]{1,0:T(8,128)(2,1)S(1)} %collective-permute-done.11.refs_3_) | copy-start | bytes 983044
  218.6 40.9 %collective-permute-start.16 = (bf16[80,2048]{1,0:T(8,128)(2,1)}, bf16[80,2048]{1,0:T(8,128)(2,1)S(1)}, u32[]{:S(2)}, u32[]{:S(2)}) collective-permute-start(bf16[80,2048]{1,0:T(8,128)(2,1)} %get-tuple-element.195.refs_1_), channel_id=1, source_target_pairs={{0,3},{1,0},{2,1},{3,2},{4,7},{5,4},{6,5},{7,6},{8,11},{9,8},{10,9... | collective-permute-start | bytes 983048 | tf_op jit(solution)/shard_map/ppermute | solution.py:24
  226.1 64.7 %collective-permute-start.15 = (bf16[80,2048]{1,0:T(8,128)(2,1)}, bf16[80,2048]{1,0:T(8,128)(2,1)S(1)}, u32[]{:S(2)}, u32[]{:S(2)}) collective-permute-start(bf16[80,2048]{1,0:T(8,128)(2,1)} %get-tuple-element.195.refs_1_), channel_id=1, source_target_pairs={{0,2},{1,3},{2,0},{3,1},{4,6},{5,7},{6,4},{7,5},{8,10},{9,11},{10,... | collective-permute-start | bytes 983048 | tf_op jit(solution)/shard_map/ppermute | solution.py:24
  226.5 64.3 %collective-permute-start.14 = (bf16[80,2048]{1,0:T(8,128)(2,1)}, bf16[80,2048]{1,0:T(8,128)(2,1)S(1)}, u32[]{:S(2)}, u32[]{:S(2)}) collective-permute-start(bf16[80,2048]{1,0:T(8,128)(2,1)} %get-tuple-element.195.refs_1_), channel_id=1, source_target_pairs={{0,1},{1,2},{2,3},{3,0},{4,5},{5,6},{6,7},{7,4},{8,9},{9,10},{10,1... | collective-permute-start | bytes 983048 | tf_op jit(solution)/shard_map/ppermute | solution.py:24
  254.6 68.9 %all-to-all-start.4 = ((bf16[4,80,2048]{2,1,0:T(8,128)(2,1)}), bf16[4,80,2048]{2,1,0:T(8,128)(2,1)S(1)}, u32[]{:S(2)}, u32[]{:S(2)}) async-start(bf16[4,80,2048]{2,1,0:T(8,128)(2,1)} %bitcast.76), calls=%async_computation.4 | async-start | bytes 2621440 | tf_op jit(solution)/shard_map/all_to_all | solution.py:321
  259.6 33.1 %copy-start.39 = (bf16[80,2048]{1,0:T(8,128)(2,1)}, bf16[80,2048]{1,0:T(8,128)(2,1)S(1)}, u32[]{:S(2)}) copy-start(bf16[80,2048]{1,0:T(8,128)(2,1)S(1)} %collective-permute-done.16.refs_4_) | copy-start | bytes 983044
  319.6 28.4 %collective-permute-start.17 = (bf16[80,2048]{1,0:T(8,128)(2,1)}, bf16[80,2048]{1,0:T(8,128)(2,1)S(1)}, u32[]{:S(2)}, u32[]{:S(2)}) collective-permute-start(bf16[80,2048]{1,0:T(8,128)(2,1)} %get-tuple-element.202), channel_id=1, source_target_pairs={{0,1},{1,2},{2,3},{3,0},{4,5},{5,6},{6,7},{7,4},{8,9},{9,10},{10,1... | collective-permute-start | bytes 983048 | tf_op jit(solution)/shard_map/ppermute | solution.py:24
  319.6 28.4 %collective-permute-start.18 = (bf16[80,2048]{1,0:T(8,128)(2,1)}, bf16[80,2048]{1,0:T(8,128)(2,1)S(1)}, u32[]{:S(2)}, u32[]{:S(2)}) collective-permute-start(bf16[80,2048]{1,0:T(8,128)(2,1)} %get-tuple-element.203), channel_id=1, source_target_pairs={{0,2},{1,3},{2,0},{3,1},{4,6},{5,7},{6,4},{7,5},{8,10},{9,11},{10,... | collective-permute-start | bytes 983048 | tf_op jit(solution)/shard_map/ppermute | solution.py:24
  319.7 28.3 %collective-permute-start.19 = (bf16[80,2048]{1,0:T(8,128)(2,1)}, bf16[80,2048]{1,0:T(8,128)(2,1)S(1)}, u32[]{:S(2)}, u32[]{:S(2)}) collective-permute-start(bf16[80,2048]{1,0:T(8,128)(2,1)} %get-tuple-element.204), channel_id=1, source_target_pairs={{0,3},{1,0},{2,1},{3,2},{4,7},{5,4},{6,5},{7,6},{8,11},{9,8},{10,9... | collective-permute-start | bytes 983048 | tf_op jit(solution)/shard_map/ppermute | solution.py:24
  328.1 66.7 %all-to-all-start.6 = ((bf16[4,80,2048]{2,1,0:T(8,128)(2,1)}), bf16[4,80,2048]{2,1,0:T(8,128)(2,1)}, u32[]{:S(2)}, u32[]{:S(2)}) async-start(bf16[4,80,2048]{2,1,0:T(8,128)(2,1)} %bitcast.70), calls=%async_computation.6 | async-start | bytes 2621440 | tf_op jit(solution)/shard_map/all_to_all | solution.py:315
  332.4 150.8 %reduce-scatter.4.cloned.1.call-start = ((), (), s32[]{:S(2)}) async-start(), calls=%async_computation.14 | async-start | bytes 14155776 | tf_op jit(solution)/shard_map/reduce_scatter | solution.py:984
  352.1 55.5 %collective-permute-start.22 = (bf16[80,2048]{1,0:T(8,128)(2,1)}, bf16[80,2048]{1,0:T(8,128)(2,1)S(1)}, u32[]{:S(2)}, u32[]{:S(2)}) collective-permute-start(bf16[80,2048]{1,0:T(8,128)(2,1)} %get-tuple-element.224.refs_1_), channel_id=1, source_target_pairs={{0,3},{1,0},{2,1},{3,2},{4,7},{5,4},{6,5},{7,6},{8,11},{9,8},{10,9... | collective-permute-start | bytes 983048 | tf_op jit(solution)/shard_map/ppermute | solution.py:24
  355.8 67.1 %collective-permute-start.21 = (bf16[80,2048]{1,0:T(8,128)(2,1)}, bf16[80,2048]{1,0:T(8,128)(2,1)}, u32[]{:S(2)}, u32[]{:S(2)}) collective-permute-start(bf16[80,2048]{1,0:T(8,128)(2,1)} %get-tuple-element.224.refs_1_), channel_id=1, source_target_pairs={{0,2},{1,3},{2,0},{3,1},{4,6},{5,7},{6,4},{7,5},{8,10},{9,11},{10,... | collective-permute-start | bytes 983048 | tf_op jit(solution)/shard_map/ppermute | solution.py:24
  366.9 56.0 %collective-permute-start.20 = (bf16[80,2048]{1,0:T(8,128)(2,1)}, bf16[80,2048]{1,0:T(8,128)(2,1)}, u32[]{:S(2)}, u32[]{:S(2)}) collective-permute-start(bf16[80,2048]{1,0:T(8,128)(2,1)} %get-tuple-element.224.refs_1_), channel_id=1, source_target_pairs={{0,1},{1,2},{2,3},{3,0},{4,5},{5,6},{6,7},{7,4},{8,9},{9,10},{10,1... | collective-permute-start | bytes 983048 | tf_op jit(solution)/shard_map/ppermute | solution.py:24
  367.1 10.8 %copy-start.28 = (f32[1,2048]{1,0:T(1,128)S(1)}, f32[1,2048]{1,0:T(1,128)}, u32[]{:S(2)}) copy-start(f32[1,2048]{1,0:T(1,128)} %get-tuple-element.275) | copy-start | bytes 24580
  367.1 10.8 %copy-start.29 = (f32[1,2048]{1,0:T(1,128)S(1)}, f32[1,2048]{1,0:T(1,128)}, u32[]{:S(2)}) copy-start(f32[1,2048]{1,0:T(1,128)} %get-tuple-element.276) | copy-start | bytes 24580
  377.9 71.3 %collective-permute-start.26 = (bf16[1024,1536]{1,0:T(8,128)(2,1)}, bf16[1024,1536]{1,0:T(8,128)(2,1)S(1)}, u32[]{:S(2)}, u32[]{:S(2)}) collective-permute-start(bf16[1024,1536]{1,0:T(8,128)(2,1)} %get-tuple-element.232), channel_id=1, source_target_pairs={{0,16},{16,0},{1,17},{17,1},{2,18},{18,2},{3,19},{19,3},{4,20},{20... | collective-permute-start | bytes 9437192 | tf_op jit(solution)/shard_map/ppermute | solution.py:24
  394.8 102.5 %all-to-all-start.5 = ((bf16[4,160,2048]{2,1,0:T(8,128)(2,1)}), bf16[4,160,2048]{2,1,0:T(8,128)(2,1)}, u32[]{:S(2)}, u32[]{:S(2)}) async-start(bf16[4,160,2048]{2,1,0:T(8,128)(2,1)} %bitcast.62), calls=%async_computation.5 | async-start | bytes 5242880 | tf_op jit(solution)/shard_map/all_to_all | solution.py:321
  399.3 170.5 %reduce-scatter.6.cloned.1.call-start = ((), (), s32[]{:S(2)}) async-start(), calls=%async_computation.15 | async-start | bytes 5570560 | tf_op jit(solution)/shard_map/reduce_scatter | solution.py:767
  407.6 15.3 %copy-start.37 = (bf16[80,2048]{1,0:T(8,128)(2,1)}, bf16[80,2048]{1,0:T(8,128)(2,1)S(1)}, u32[]{:S(2)}) copy-start(bf16[80,2048]{1,0:T(8,128)(2,1)S(1)} %collective-permute-done.22.refs_4_) | copy-start | bytes 983044
  431.1 16.9 %collective-permute-start.25 = (f32[4,640]{1,0:T(4,128)S(1)}, f32[4,640]{1,0:T(4,128)S(1)}, u32[]{:S(2)}, u32[]{:S(2)}) collective-permute-start(f32[4,640]{1,0:T(4,128)S(1)} %pad_maximum_fusion.4), channel_id=1, source_target_pairs={{12,0},{13,1},{14,2},{15,3},{28,16},{29,17},{30,18},{31,19}} | collective-permute-start | bytes 30728 | tf_op jit(solution)/shard_map/ppermute | solution.py:29
  432.4 16.1 %collective-permute-start.24 = (f32[4,640]{1,0:T(4,128)S(1)}, f32[4,640]{1,0:T(4,128)S(1)}, u32[]{:S(2)}, u32[]{:S(2)}) collective-permute-start(f32[4,640]{1,0:T(4,128)S(1)} %pad_maximum_fusion.4), channel_id=1, source_target_pairs={{8,0},{12,4},{9,1},{13,5},{10,2},{14,6},{11,3},{15,7},{24,16},{28,... | collective-permute-start | bytes 30728 | tf_op jit(solution)/shard_map/ppermute | solution.py:29
  433.7 14.8 %collective-permute-start.23 = (f32[4,640]{1,0:T(4,128)S(1)}, f32[4,640]{1,0:T(4,128)S(1)}, u32[]{:S(2)}, u32[]{:S(2)}) collective-permute-start(f32[4,640]{1,0:T(4,128)S(1)} %pad_maximum_fusion.4), channel_id=1, source_target_pairs={{4,0},{8,4},{12,8},{5,1},{9,5},{13,9},{6,2},{10,6},{14,10},{7,3},{... | collective-permute-start | bytes 30728 | tf_op jit(solution)/shard_map/ppermute | solution.py:29
  441.5 7.6 %collective-permute-start.27 = (bf16[1024,640]{1,0:T(8,128)(2,1)}, bf16[1024,640]{1,0:T(8,128)(2,1)}, u32[]{:S(2)}, u32[]{:S(2)}) collective-permute-start(bf16[1024,640]{1,0:T(8,128)(2,1)} %get-tuple-element.238), channel_id=1, source_target_pairs={{0,16},{16,0},{1,17},{17,1},{2,18},{18,2},{3,19},{19,3},{4,20},{20... | collective-permute-start | bytes 3932168 | tf_op jit(solution)/shard_map/ppermute | solution.py:24
  448.1 85.2 %collective-permute-start.36 = (bf16[1024,640]{1,0:T(8,128)(2,1)}, bf16[1024,640]{1,0:T(8,128)(2,1)}, u32[]{:S(2)}, u32[]{:S(2)}) collective-permute-start(bf16[1024,640]{1,0:T(8,128)(2,1)} %get-tuple-element.278), channel_id=1, source_target_pairs={{0,16},{16,0},{1,17},{17,1},{2,18},{18,2},{3,19},{19,3},{4,20},{20... | collective-permute-start | bytes 3932168 | tf_op jit(solution)/shard_map/ppermute | solution.py:24
  465.5 10.9 %copy-start.21 = (f32[8,640]{1,0:T(8,128)S(1)}, f32[8,640]{1,0:T(8,128)}, u32[]{:S(2)}) copy-start(f32[8,640]{1,0:T(8,128)} %get-tuple-element.269) | copy-start | bytes 61444
  474.9 7.7 %collective-permute-start.28 = (f32[16,640]{1,0:T(8,128)S(1)}, f32[16,640]{1,0:T(8,128)S(1)}, u32[]{:S(2)}, u32[]{:S(2)}) collective-permute-start(f32[16,640]{1,0:T(8,128)S(1)} %pad_maximum_fusion.2), channel_id=1, source_target_pairs={{4,0},{8,4},{12,8},{5,1},{9,5},{13,9},{6,2},{10,6},{14,10},{7,3},{... | collective-permute-start | bytes 122888 | tf_op jit(solution)/shard_map/ppermute | solution.py:29
  508.1 12.8 %collective-permute-start.33 = (f32[2,2048]{1,0:T(2,128)S(1)}, f32[2,2048]{1,0:T(2,128)S(1)}, u32[]{:S(2)}, u32[]{:S(2)}) collective-permute-start(f32[2,2048]{1,0:T(2,128)S(1)} %pad_maximum_fusion.3), channel_id=1, source_target_pairs={{0,2},{1,3},{2,0},{3,1},{4,6},{5,7},{6,4},{7,5},{8,10},{9,11},{10,... | collective-permute-start | bytes 49160 | tf_op jit(solution)/shard_map/ppermute | solution.py:24
  508.2 12.8 %collective-permute-start.34 = (f32[2,2048]{1,0:T(2,128)S(1)}, f32[2,2048]{1,0:T(2,128)S(1)}, u32[]{:S(2)}, u32[]{:S(2)}) collective-permute-start(f32[2,2048]{1,0:T(2,128)S(1)} %pad_maximum_fusion.3), channel_id=1, source_target_pairs={{0,3},{1,0},{2,1},{3,2},{4,7},{5,4},{6,5},{7,6},{8,11},{9,8},{10,9... | collective-permute-start | bytes 49160 | tf_op jit(solution)/shard_map/ppermute | solution.py:24
  508.2 12.7 %collective-permute-start.32 = (f32[2,2048]{1,0:T(2,128)S(1)}, f32[2,2048]{1,0:T(2,128)S(1)}, u32[]{:S(2)}, u32[]{:S(2)}) collective-permute-start(f32[2,2048]{1,0:T(2,128)S(1)} %pad_maximum_fusion.3), channel_id=1, source_target_pairs={{0,1},{1,2},{2,3},{3,0},{4,5},{5,6},{6,7},{7,4},{8,9},{9,10},{10,1... | collective-permute-start | bytes 49160 | tf_op jit(solution)/shard_map/ppermute | solution.py:24
  510.2 81.5 %all-to-all-start.7 = ((bf16[4,80,2048]{2,1,0:T(8,128)(2,1)}), bf16[4,80,2048]{2,1,0:T(8,128)(2,1)S(1)}, u32[]{:S(2)}, u32[]{:S(2)}) async-start(bf16[4,80,2048]{2,1,0:T(8,128)(2,1)} %bitcast.65), calls=%async_computation.8 | async-start | bytes 2621440 | tf_op jit(solution)/shard_map/all_to_all | solution.py:321
  514.4 92.7 %reduce-scatter.8.cloned.1.call-start = ((), (), s32[]{:S(2)}) async-start(), calls=%async_computation.16 | async-start | bytes 3276800 | tf_op jit(solution)/shard_map/reduce_scatter | solution.py:767
  520.9 12.4 %collective-permute-start.37 = (bf16[1024,640]{1,0:T(8,128)(2,1)}, bf16[1024,640]{1,0:T(8,128)(2,1)S(1)}, u32[]{:S(2)}, u32[]{:S(2)}) collective-permute-start(bf16[1024,640]{1,0:T(8,128)(2,1)} %get-tuple-element.283), channel_id=1, source_target_pairs={{0,16},{16,0},{1,17},{17,1},{2,18},{18,2},{3,19},{19,3},{4,20},{20... | collective-permute-start | bytes 3932168 | tf_op jit(solution)/shard_map/ppermute | solution.py:24
  521.1 12.2 %copy-start = (bf16[8,176,160]{2,1,0:T(8,128)(2,1)}, bf16[8,176,160]{2,1,0:T(8,128)(2,1)S(1)}, u32[]{:S(2)}) copy-start(bf16[8,176,160]{2,1,0:T(8,128)(2,1)S(1)} %constant_dynamic-update-slice_fusion.refs_0_) | copy-start | bytes 1351684
  522.3 4.9 collective-permute-start.35
  522.8 25.5 %collective-permute-start.29 = (bf16[80,2048]{1,0:T(8,128)(2,1)}, bf16[80,2048]{1,0:T(8,128)(2,1)}, u32[]{:S(2)}, u32[]{:S(2)}) collective-permute-start(bf16[80,2048]{1,0:T(8,128)(2,1)} %get-tuple-element.265), channel_id=1, source_target_pairs={{0,1},{1,2},{2,3},{3,0},{4,5},{5,6},{6,7},{7,4},{8,9},{9,10},{10,1... | collective-permute-start | bytes 983048 | tf_op jit(solution)/shard_map/ppermute | solution.py:24
  524.8 41.9 %collective-permute-start.30 = (bf16[80,2048]{1,0:T(8,128)(2,1)}, bf16[80,2048]{1,0:T(8,128)(2,1)}, u32[]{:S(2)}, u32[]{:S(2)}) collective-permute-start(bf16[80,2048]{1,0:T(8,128)(2,1)} %get-tuple-element.266), channel_id=1, source_target_pairs={{0,2},{1,3},{2,0},{3,1},{4,6},{5,7},{6,4},{7,5},{8,10},{9,11},{10,... | collective-permute-start | bytes 983048 | tf_op jit(solution)/shard_map/ppermute | solution.py:24
  527.2 39.5 %collective-permute-start.31 = (bf16[80,2048]{1,0:T(8,128)(2,1)}, bf16[80,2048]{1,0:T(8,128)(2,1)}, u32[]{:S(2)}, u32[]{:S(2)}) collective-permute-start(bf16[80,2048]{1,0:T(8,128)(2,1)} %get-tuple-element.267), channel_id=1, source_target_pairs={{0,3},{1,0},{2,1},{3,2},{4,7},{5,4},{6,5},{7,6},{8,11},{9,8},{10,9... | collective-permute-start | bytes 983048 | tf_op jit(solution)/shard_map/ppermute | solution.py:24
  542.9 29.8 %collective-permute-start.40 = (bf16[8,176,160]{1,2,0:T(8,128)(2,1)S(1)}, bf16[8,176,160]{1,2,0:T(8,128)(2,1)S(1)}, u32[]{:S(2)}, u32[]{:S(2)}) collective-permute-start(bf16[8,176,160]{1,2,0:T(8,128)(2,1)S(1)} %copy.61), channel_id=1, source_target_pairs={{0,12},{4,0},{8,4},{12,8},{1,13},{5,1},{9,5},{13,9},{2,14},{6,2},{... | collective-permute-start | bytes 1351688 | tf_op jit(solution)/shard_map/ppermute | solution.py:24
  544.8 35.1 %collective-permute-start.39 = (bf16[8,176,160]{1,2,0:T(8,128)(2,1)S(1)}, bf16[8,176,160]{1,2,0:T(8,128)(2,1)S(1)}, u32[]{:S(2)}, u32[]{:S(2)}) collective-permute-start(bf16[8,176,160]{1,2,0:T(8,128)(2,1)S(1)} %copy.61), channel_id=1, source_target_pairs={{0,8},{4,12},{8,0},{12,4},{1,9},{5,13},{9,1},{13,5},{2,10},{6,14},... | collective-permute-start | bytes 1351688 | tf_op jit(solution)/shard_map/ppermute | solution.py:24
  548.3 41.1 %collective-permute-start.38 = (bf16[8,176,160]{1,2,0:T(8,128)(2,1)S(1)}, bf16[8,176,160]{1,2,0:T(8,128)(2,1)}, u32[]{:S(2)}, u32[]{:S(2)}) collective-permute-start(bf16[8,176,160]{1,2,0:T(8,128)(2,1)S(1)} %copy.61), channel_id=1, source_target_pairs={{0,4},{4,8},{8,12},{12,0},{1,5},{5,9},{9,13},{13,1},{2,6},{6,10},{... | collective-permute-start | bytes 1351688 | tf_op jit(solution)/shard_map/ppermute | solution.py:24
  (42 other events, 158.2 us)
Sparse Core Ops, SparseCore 0:
  10.7 54.8 all-gather.3
  67.5 98.9 all-gather.5
  226.8 65.8 all-gather.7
  348.1 94.0 reduce-scatter.3
  457.2 56.2 reduce-scatter.5
  547.4 56.8 reduce-scatter.7

commit v5 on v4

--- a/solution.py
+++ b/solution.py
@@ -261,7 +261,7 @@
 
 
 COSTS = (
-    0.2, 3, 0.2, 6, 0.01, 6, 5.7, 7, 5.7, 3, 3, 27, 27, 3.4, 21, 60, 0.01, 0.01, 7.5, 7.5, 6, 7, 8, 40, 40, 0.01, 0.01, 0.01, 0.01, 0.01, 0.01, 0.01, 0.01, 0.01, 3, 10000.0, 1, 3,
+    0.2, 3, 0.2, 6, 0.01, 6, 5.7, 7, 5.7, 3, 3, 3, 27, 3.4, 21, 60, 0.01, 0.01, 7.5, 7.5, 6, 7, 8, 40, 40, 0.01, 0.01, 0.01, 0.01, 0.01, 0.01, 0.01, 0.01, 0.01, 3, 10000.0, 1, 3,
 )
 
 
@@ -966,7 +966,7 @@
     out_terms = [gathered_sums(p) for p in out_part]
     residual, two_blocks = [], []
     for i in turns:
-        res, low = second(clock, x_rows[i], gain_two_row, out_terms[i], copies[i])
+        res, low = second(clock, x_rows[i], gain_two_row, out_terms[i], copies[i], () if i else (second_w,))
         residual.append(res)
         two_blocks.append(spread(low, apart[i]))
     mlps = [

time: 628 us -> 627 us (level)
  waiting for transfers between devices: 175 us -> 153 us
  starting transfers between devices: 118 us -> 139 us
    ppermute x29, waiting for transfers between devices: 124 us -> 99.3 us  [shift(): lax.ppermute(value, axis, [(i, (i + by) % size) for i in range(size)])]
    all_gather x1, waiting for transfers between devices: 0.01 us -> 19.5 us  [per_device(): lax.all_gather(jnp.concatenate([gate_weight, up_weight, down_weight.T], 1...]
    ppermute x29, starting transfers between devices: 54.3 us -> 73.1 us  [shift(): lax.ppermute(value, axis, [(i, (i + by) % size) for i in range(size)])]
    all_to_all x4, waiting for transfers between devices: 33.1 us -> 25.3 us  [spread(): lax.all_to_all(copies, 'tensor', split_axis=0, concat_axis=0, tiled=True)]
    all_to_all x4, waiting for transfers between devices: 7.47 us -> 0.01 us  [gathered_sums(): lax.all_to_all(parts[0], 'tensor', split_axis=0, concat_axis=0, tiled=True)]
  transfers between devices with their start and end apart: 55 -> 55, of which waited for: 15 -> 11; matrix products, arithmetic and copies ran while one was open for 7% -> 7% of each run, Pallas kernels for 40% -> 40%
where the time goes in v5:
time: 627 us; the launch traced here: 616 us
  Pallas kernels  249 us (40%)
  waiting for transfers between devices  153 us (24%)
  starting transfers between devices  139 us (22%)
  local copies, waits for them, and re-layouts  40 us (6%)
  other arithmetic  20.4 us (3%)
  between operations  15.4 us (2%)
    pallas_call x38, Pallas kernels, call(): pl.pallas_call(body, out_shape=list(out_shape) + [jax.ShapeDtypeStruct((T...  249 us
    ppermute x29, waiting for transfers between devices, shift(): lax.ppermute(value, axis, [(i, (i + by) % size) for i in range(size)])  99.3 us
    ppermute x29, starting transfers between devices, shift(): lax.ppermute(value, axis, [(i, (i + by) % size) for i in range(size)])  73.1 us
    ppermute x12, starting transfers between devices, step_by(): lax.ppermute(value, axis, [(i, i + by) for i in range(size) if 0 <= i + b...  26.8 us
    all_to_all x4, waiting for transfers between devices, spread(): lax.all_to_all(copies, 'tensor', split_axis=0, concat_axis=0, tiled=True)  25.3 us
    all_to_all x4, starting transfers between devices, gathered_sums(): lax.all_to_all(parts[0], 'tensor', split_axis=0, concat_axis=0, tiled=True)  19.6 us
    all_gather x1, waiting for transfers between devices, per_device(): lax.all_gather(jnp.concatenate([gate_weight, up_weight, down_weight.T], 1...  19.5 us
    all_to_all x4, starting transfers between devices, spread(): lax.all_to_all(copies, 'tensor', split_axis=0, concat_axis=0, tiled=True)  19.1 us
  transfers between devices with their start and end apart: 55, of which 11 were waited for; matrix products, arithmetic and copies ran while one was open for 7% of the time, Pallas kernels for 40%

profile of v5, /device:TPU:0, one launch (start us, length us, event | category | flops | bytes accessed | tf_op | source)
XLA Modules:
  0.0 615.9 jit_solution(15868646468704943845)
XLA Ops:
  18.4 6.5 %all-to-all-start = ((bf16[4,80,2048]{2,1,0:T(8,128)(2,1)}), bf16[4,80,2048]{2,1,0:T(8,128)(2,1)S(1)}, u32[]{:S(2)}, u32[]{:S(2)}) async-start(bf16[4,80,2048]{2,1,0:T(8,128)(2,1)} %bitcast.69), calls=%async_computation | async-start | bytes 2621440 | tf_op jit(solution)/shard_map/all_to_all | solution.py:315
  25.4 8.4 %fusion.24.refs_1_.refs_4_.refs_14_ = bf16[640,1280]{1,0:T(8,128)(2,1)} fusion(bf16[160,160]{1,0:T(8,128)(2,1)S(1)} %get-tuple-element.378, bf16[160,160]{1,0:T(8,128)(2,1)S(1)} %get-tuple-element.379, bf16[160,160]{1,0:T(8,128)(2,1)S(1)} %get-tuple-element.377, bf16[160,160]{1,0:T(8,128)(2,1)S(1)} %get-tuple-element.376, ...), kind=kLoop, calls=%fused_computation.33 | loop fusion | flops 40960000 | bytes 2048000 | tf_op jit(solution)/shard_map/concatenate | solution.py:902
  41.1 3.8 collective-permute-start.6
  46.0 25.3 %all-to-all-done = bf16[4,80,2048]{2,1,0:T(8,128)(2,1)S(1)} async-done(((bf16[4,80,2048]{2,1,0:T(8,128)(2,1)}), bf16[4,80,2048]{2,1,0:T(8,128)(2,1)S(1)}, u32[]{:S(2)}, u32[]{:S(2)}) %all-to-all-start) | async-done | bytes 1310752 | tf_op jit(solution)/shard_map/all_to_all | solution.py:315
  71.3 3.6 all-to-all-start.1
  75.0 6.7 %shard_map.308 = (bf16[320,2048]{1,0:T(8,128)(2,1)}, f32[320,1280]{1,0:T(8,128)}, bf16[8,640]{1,0:T(8,128)(2,1)}, f32[8,128]{1,0:T(8,128)}) custom-call(s32[1]{0:T(128)} %bitcast.2.refs_0_, bf16[320,2048]{1,0:T(8,128)(2,1)} %bitcast.68, bf16[2048,1920]{1,0:T(8,128)(2,1)} %all-gather.4.cloned.1.call-done.refs_2_.refs_5_.refs_4_, ...), custom_call_target="tpu_custom_call" | custom-call | flops 17999998976 | bytes 17999998976 | tf_op jit(solution)/shard_map/pallas_call | solution.py:284
  81.7 3.4 collective-permute-start
  87.3 6.9 %shard_map.309 = (bf16[320,640]{1,0:T(8,128)(2,1)}, f32[320,1280]{1,0:T(8,128)}, f32[320,640]{1,0:T(8,128)}, f32[320,640]{1,0:T(8,128)}, f32[320,640]{1,0:T(8,128)}, /*index=5*/f32[2,640]{1,0:T(2,128)}, f32[8,128]{1,0:T(8,128)}) custom-call(f32[320,1280]{1,0:T(8,128)} %get-tuple-element.165.refs_0_.refs_4_.refs_3_.refs_9_.refs_10_, ...), custom_call_target="tpu_custom_call" | custom-call | flops 30000000 | bytes 30000000 | tf_op jit(solution)/shard_map/pallas_call | solution.py:284
  94.2 5.3 collective-permute-start.3
  100.9 2.5 collective-permute-start.1
  104.1 5.9 shard_map.310
  113.6 6.0 shard_map.311
  119.6 5.0 all-to-all-start.2
  125.1 6.9 %shard_map.312 = (bf16[320,640]{1,0:T(8,128)(2,1)}, f32[320,1280]{1,0:T(8,128)}, f32[320,640]{1,0:T(8,128)}, f32[320,640]{1,0:T(8,128)}, f32[320,640]{1,0:T(8,128)}, /*index=5*/f32[2,640]{1,0:T(2,128)}, f32[8,128]{1,0:T(8,128)}) custom-call(f32[320,1280]{1,0:T(8,128)} %get-tuple-element.177.refs_0_.refs_4_.refs_6_.refs_9_.refs_10_, ...), custom_call_target="tpu_custom_call" | custom-call | flops 20999999488 | bytes 20999999488 | tf_op jit(solution)/shard_map/pallas_call | solution.py:284
  132.1 3.2 collective-permute-start.10
  136.6 2.5 collective-permute-start.8
  141.2 5.8 shard_map.313
  147.0 19.5 %all-gather.6.cloned.1.call-done.refs_3_.refs_4_.refs_5_.refs_6_.refs_7_.refs_8_.refs_2_ = bf16[2048,4608]{1,0:T(8,128)(2,1)} async-done(((bf16[256,4608]{1,0:T(8,128)(2,1)}), bf16[2048,4608]{1,0:T(8,128)(2,1)}) %all-gather.6.cloned.1.call-update) | async-done | bytes 18874384 | tf_op jit(solution)/shard_map/all_gather | solution.py:899
  167.5 3.0 shard_map.314
  170.6 4.7 all-to-all-start.3
  177.3 2.4 collective-permute-start.12
  181.4 45.3 %collective-permute-done.11.refs_3_ = bf16[80,2048]{1,0:T(8,128)(2,1)S(1)} collective-permute-done((bf16[80,2048]{1,0:T(8,128)(2,1)S(1)}, bf16[80,2048]{1,0:T(8,128)(2,1)S(1)}, u32[]{:S(2)}, u32[]{:S(2)}) %collective-permute-start.11) | collective-permute-done | bytes 327712 | tf_op jit(solution)/shard_map/ppermute | solution.py:24
  226.7 23.4 %collective-permute-done.12.refs_4_ = bf16[80,2048]{1,0:T(8,128)(2,1)S(1)} collective-permute-done((bf16[80,2048]{1,0:T(8,128)(2,1)S(1)}, bf16[80,2048]{1,0:T(8,128)(2,1)S(1)}, u32[]{:S(2)}, u32[]{:S(2)}) %collective-permute-start.12) | collective-permute-done | bytes 327712 | tf_op jit(solution)/shard_map/ppermute | solution.py:24
  251.0 2.6 shard_map.315
  253.6 7.5 %collective-permute-start.16 = (bf16[80,2048]{1,0:T(8,128)(2,1)}, bf16[80,2048]{1,0:T(8,128)(2,1)S(1)}, u32[]{:S(2)}, u32[]{:S(2)}) collective-permute-start(bf16[80,2048]{1,0:T(8,128)(2,1)} %get-tuple-element.195.refs_1_), channel_id=1, source_target_pairs={{0,3},{1,0},{2,1},{3,2},{4,7},{5,4},{6,5},{7,6},{8,11},{9,8},{10,9... | collective-permute-start | bytes 983048 | tf_op jit(solution)/shard_map/ppermute | solution.py:24
  262.8 26.9 %shard_map.316 = (bf16[320,2048]{1,0:T(8,128)(2,1)}, bf16[320,2048]{1,0:T(8,128)(2,1)}, bf16[320,1536]{1,0:T(8,128)(2,1)}, bf16[2,320,1536]{2,1,0:T(8,128)(2,1)}...) custom-call(s32[1]{0:T(128)} %bitcast.2.refs_0_, bf16[320,2048]{1,0:T(8,128)(2,1)} %bitcast.63, bf16[320,2048]{1,0:T(8,128)(2,1)} %bitcast.62, ...), custom_call_target="tpu_custom_call" | custom-call | flops 8999999488 | bytes 8999999488 | tf_op jit(solution)/shard_map/pallas_call | solution.py:284
  289.6 5.0 all-to-all-start.4
  295.6 26.9 %shard_map.317 = (bf16[320,2048]{1,0:T(8,128)(2,1)}, bf16[320,2048]{1,0:T(8,128)(2,1)}, bf16[320,1536]{1,0:T(8,128)(2,1)}, bf16[2,320,1536]{2,1,0:T(8,128)(2,1)}...) custom-call(s32[1]{0:T(128)} %bitcast.2.refs_0_, ...), custom_call_target="tpu_custom_call" | custom-call | flops 80999997440 | bytes 80999997440 | tf_op jit(solution)/shard_map/pallas_call | solution.py:284
  324.6 2.4 collective-permute-start.18
  329.5 3.5 shard_map.318
  333.0 4.3 all-to-all-start.6
  337.4 15.5 %shard_map.319 = (bf16[2048,3072]{1,0:T(8,128)(2,1)}, f32[8,128]{1,0:T(8,128)}) custom-call(bf16[320,2048]{1,0:T(8,128)(2,1)} %get-tuple-element.205.refs_0_, bf16[320,2048]{1,0:T(8,128)(2,1)} %get-tuple-element.206.refs_1_, bf16[2,320,1536]{2,1,0:T(8,128)(2,1)} %get-tuple-element.207.refs_2_, bf16[2,320,1536]{2,1,0:T(8,128)(2,1)} %get-tuple-element.208.refs_3_, ...), custom_call_target="tpu_custom_call" | custom-call | flops 62999998464 | bytes 62999998464 | tf_op jit(solution)/shard_map/pallas_call | solution.py:284
  353.9 3.2 shard_map.320
  357.0 26.3 %collective-permute-start.22 = (bf16[80,2048]{1,0:T(8,128)(2,1)}, bf16[80,2048]{1,0:T(8,128)(2,1)S(1)}, u32[]{:S(2)}, u32[]{:S(2)}) collective-permute-start(bf16[80,2048]{1,0:T(8,128)(2,1)} %get-tuple-element.224.refs_1_), channel_id=1, source_target_pairs={{0,3},{1,0},{2,1},{3,2},{4,7},{5,4},{6,5},{7,6},{8,11},{9,8},{10,9... | collective-permute-start | bytes 983048 | tf_op jit(solution)/shard_map/ppermute | solution.py:24
  384.1 10.5 %shard_map.321 = (bf16[1024,1536]{1,0:T(8,128)(2,1)}, bf16[1024,1536]{1,0:T(8,128)(2,1)}, f32[8,128]{1,0:T(8,128)}) custom-call(s32[1]{0:T(128)} %bitcast.25.refs_0_, bf16[320,2048]{1,0:T(8,128)(2,1)} %get-tuple-element.199.refs_1_, bf16[320,2048]{1,0:T(8,128)(2,1)} %get-tuple-element.200.refs_2_, bf16[320,1536]{1,0:T(8,128)(2,1)} %get-tuple-element.194.refs_3_.refs_0_, ...), custom_call_target="tpu_custom_call" | custom-call | flops 30000000 | bytes 30000000 | tf_op jit(solution)/shard_map/pallas_call | solution.py:284
  395.3 8.4 %shard_map.322 = (bf16[640,2048]{1,0:T(8,128)(2,1)}, f32[8,128]{1,0:T(8,128)}) custom-call(bf16[320,1536]{1,0:T(8,128)(2,1)} %get-tuple-element.194.refs_3_.refs_0_, bf16[320,1536]{1,0:T(8,128)(2,1)} %get-tuple-element.198.refs_4_.refs_1_, bf16[2048,4608]{1,0:T(8,128)(2,1)} %all-gather.6.cloned.1.call-done.refs_3_.refs_4_.refs_5_.refs_6_.refs_7_.refs_8_.refs_2_, ...), custom_call_target="tpu_custom_call" | custom-call | flops 30000000 | bytes 30000000 | tf_op jit(solution)/shard_map/pallas_call | solution.py:284
  403.7 4.6 all-to-all-start.5
  408.3 7.4 %shard_map.323 = (bf16[320,2048]{1,0:T(8,128)(2,1)}, bf16[320,640]{1,0:T(8,128)(2,1)}, f32[320,640]{1,0:T(8,128)}, f32[320,640]{1,0:T(8,128)}, f32[2,640]{1,0:T(2,128)}, /*index=5*/f32[8,128]{1,0:T(8,128)}) custom-call(s32[1]{0:T(128)} %bitcast.2.refs_0_, bf16[320,2048]{1,0:T(8,128)(2,1)} %bitcast.31.refs_1_, ...), custom_call_target="tpu_custom_call" | custom-call | flops 22499999744 | bytes 22499999744 | tf_op jit(solution)/shard_map/pallas_call | solution.py:284
  417.2 7.4 %shard_map.324 = (bf16[320,2048]{1,0:T(8,128)(2,1)}, bf16[320,640]{1,0:T(8,128)(2,1)}, f32[320,640]{1,0:T(8,128)}, f32[320,640]{1,0:T(8,128)}, f32[2,640]{1,0:T(2,128)}, /*index=5*/f32[8,128]{1,0:T(8,128)}) custom-call(s32[1]{0:T(128)} %bitcast.2.refs_0_, bf16[80,2048]{1,0:T(8,128)(2,1)} %get-tuple-element.224.refs_1_, ...), custom_call_target="tpu_custom_call" | custom-call | flops 22499999744 | bytes 22499999744 | tf_op jit(solution)/shard_map/pallas_call | solution.py:284
  429.3 6.5 %shard_map.325 = (bf16[1024,640]{1,0:T(8,128)(2,1)}, bf16[1024,640]{1,0:T(8,128)(2,1)}, f32[8,128]{1,0:T(8,128)}) custom-call(s32[1]{0:T(128)} %bitcast.25.refs_0_, bf16[320,2048]{1,0:T(8,128)(2,1)} %get-tuple-element.233.refs_1_.refs_5_, bf16[320,2048]{1,0:T(8,128)(2,1)} %get-tuple-element.234.refs_2_.refs_5_, ...), custom_call_target="tpu_custom_call" | custom-call | flops 17999998976 | bytes 17999998976 | tf_op jit(solution)/shard_map/pallas_call | solution.py:284
  436.3 6.6 %shard_map.326 = (bf16[1024,640]{1,0:T(8,128)(2,1)}, bf16[1024,640]{1,0:T(8,128)(2,1)}, f32[8,128]{1,0:T(8,128)}) custom-call(s32[1]{0:T(128)} %bitcast.25.refs_0_, bf16[320,2048]{1,0:T(8,128)(2,1)} %get-tuple-element.239.refs_1_, bf16[320,2048]{1,0:T(8,128)(2,1)} %get-tuple-element.240.refs_2_, bf16[320,640]{1,0:T(8,128)(2,1)} %get-tuple-element.241.refs_3_, ...), custom_call_target="tpu_custom_call" | custom-call | flops 20999999488 | bytes 20999999488 | tf_op jit(solution)/shard_map/pallas_call | solution.py:284
  445.3 6.3 %shard_map.327 = (bf16[1024,2176]{1,0:T(8,128)(2,1)}, f32[8,128]{1,0:T(8,128)}) custom-call(bf16[1024,1536]{1,0:T(8,128)(2,1)} %get-tuple-element.231.refs_0_, bf16[1024,1536]{1,0:T(8,128)(2,1)} %copy-done.34, bf16[1024,640]{1,0:T(8,128)(2,1)} %get-tuple-element.237.refs_2_, bf16[1024,640]{1,0:T(8,128)(2,1)} %collective-permute-done.27.refs_3_, ...), custom_call_target="tpu_custom_call" | custom-call | flops 24000000000 | bytes 24000000000 | tf_op jit(solution)/shard_map/pallas_call | solution.py:284
  451.6 8.5 %shard_map.328 = (bf16[320,1280]{1,0:T(8,128)(2,1)}, f32[320,640]{1,0:T(8,128)}, f32[8,640]{1,0:T(8,128)}, f32[8,640]{1,0:T(8,128)}, f32[8,128]{1,0:T(8,128)}) custom-call(f32[320,640]{1,0:T(8,128)} %get-tuple-element.221.refs_0_, f32[320,640]{1,0:T(8,128)} %get-tuple-element.222.refs_1_, f32[1,640]{1,0:T(1,128)} %get-tuple-element.385.refs_2_, ...), custom_call_target="tpu_custom_call" | custom-call | flops 120000004096 | bytes 120000004096 | tf_op jit(solution)/shard_map/pallas_call | solution.py:284
  460.1 9.1 %shard_map.329 = (bf16[320,1280]{1,0:T(8,128)(2,1)}, f32[320,640]{1,0:T(8,128)}, f32[8,640]{1,0:T(8,128)}, f32[8,640]{1,0:T(8,128)}, f32[8,128]{1,0:T(8,128)}) custom-call(f32[320,640]{1,0:T(8,128)} %get-tuple-element.248.refs_0_, f32[320,640]{1,0:T(8,128)} %get-tuple-element.249.refs_1_, f32[1,640]{1,0:T(1,128)} %get-tuple-element.384.refs_2_, ...), custom_call_target="tpu_custom_call" | custom-call | flops 120000004096 | bytes 120000004096 | tf_op jit(solution)/shard_map/pallas_call | solution.py:284
  472.3 5.2 collective-permute-done.28
  478.1 3.2 shard_map.330
  481.3 4.4 shard_map.331
  485.8 6.4 %shard_map.332 = (bf16[320,640]{1,0:T(8,128)(2,1)}, f32[1,2048]{1,0:T(1,128)}, bf16[80,2048]{1,0:T(8,128)(2,1)}, bf16[80,2048]{1,0:T(8,128)(2,1)}, bf16[80,2048]...) custom-call(s32[1]{0:T(128)} %bitcast.2.refs_0_, bf16[320,640]{1,0:T(8,128)(2,1)} %get-tuple-element.220.refs_3_.refs_1_, ...), custom_call_target="tpu_custom_call" | custom-call | flops 30000000 | bytes 30000000 | tf_op jit(solution)/shard_map/pallas_call | solution.py:284
  492.2 3.2 shard_map.333
  495.4 6.3 %shard_map.334 = (bf16[320,640]{1,0:T(8,128)(2,1)}, f32[1,2048]{1,0:T(1,128)}, bf16[320,2048]{1,0:T(8,128)(2,1)}, f32[8,128]{1,0:T(8,128)}) custom-call(s32[1]{0:T(128)} %bitcast.2.refs_0_, bf16[320,640]{1,0:T(8,128)(2,1)} %get-tuple-element.235.refs_4_.refs_1_, f32[320,640]{1,0:T(8,128)} %get-tuple-element.272.refs_2_, ...), custom_call_target="tpu_custom_call" | custom-call | flops 30000000 | bytes 30000000 | tf_op jit(solution)/shard_map/pallas_call | solution.py:284
  502.5 2.8 collective-permute-start.33
  507.5 5.1 all-to-all-start.7
  512.7 6.5 %shard_map.335 = (bf16[1024,640]{1,0:T(8,128)(2,1)}, bf16[1024,640]{1,0:T(8,128)(2,1)}, f32[8,128]{1,0:T(8,128)}) custom-call(s32[1]{0:T(128)} %bitcast.25.refs_0_, bf16[320,2048]{1,0:T(8,128)(2,1)} %get-tuple-element.233.refs_1_.refs_5_, bf16[320,2048]{1,0:T(8,128)(2,1)} %get-tuple-element.234.refs_2_.refs_5_, bf16[320,640]{1,0:T(8,128)(2,1)} %get-tuple-element.279.refs_3_, ...), custom_call_target="tpu_custom_call" | custom-call | flops 30000000 | bytes 30000000 | tf_op jit(solution)/shard_map/pallas_call | solution.py:284
  523.1 2.4 collective-permute-start.30
  532.7 4.7 shard_map.336
  542.9 3.4 collective-permute-start.39
  546.6 3.6 collective-permute-start.38
  550.2 15.4 %collective-permute-done.30.refs_5_ = bf16[80,2048]{1,0:T(8,128)(2,1)} collective-permute-done((bf16[80,2048]{1,0:T(8,128)(2,1)}, bf16[80,2048]{1,0:T(8,128)(2,1)}, u32[]{:S(2)}, u32[]{:S(2)}) %collective-permute-start.30) | collective-permute-done | bytes 327712 | tf_op jit(solution)/shard_map/ppermute | solution.py:24
  565.6 3.0 shard_map.338
  568.6 2.9 shard_map.339
  572.7 6.1 collective-permute-done.39
  580.0 8.7 %collective-permute-done.38 = bf16[8,176,160]{1,2,0:T(8,128)(2,1)} collective-permute-done((bf16[8,176,160]{1,2,0:T(8,128)(2,1)S(1)}, bf16[8,176,160]{1,2,0:T(8,128)(2,1)}, u32[]{:S(2)}, u32[]{:S(2)}) %collective-permute-start.38) | collective-permute-done | bytes 450592 | tf_op jit(solution)/shard_map/ppermute | solution.py:24
  592.1 3.4 shard_map.340
  595.5 3.3 shard_map.341
  (263 shorter events, 95.1 us)
Async XLA Ops:
  7.2 67.8 %all-gather.4.cloned.1.call-start = ((), (), s32[]{:S(2)}) async-start(), calls=%async_computation.11 | async-start | bytes 8847360 | tf_op jit(solution)/shard_map/all_gather | solution.py:896
  10.6 155.9 %all-gather.6.cloned.1.call-start = ((), (), s32[]{:S(2)}) async-start(), calls=%async_computation.12 | async-start | bytes 21233664 | tf_op jit(solution)/shard_map/all_gather | solution.py:899
  18.4 52.9 %all-to-all-start = ((bf16[4,80,2048]{2,1,0:T(8,128)(2,1)}), bf16[4,80,2048]{2,1,0:T(8,128)(2,1)S(1)}, u32[]{:S(2)}, u32[]{:S(2)}) async-start(bf16[4,80,2048]{2,1,0:T(8,128)(2,1)} %bitcast.69), calls=%async_computation | async-start | bytes 2621440 | tf_op jit(solution)/shard_map/all_to_all | solution.py:315
  25.3 10.3 %copy-start.26 = (f32[4,640]{1,0:T(4,128)S(1)}, f32[4,640]{1,0:T(4,128)}, u32[]{:S(2)}) copy-start(f32[4,640]{1,0:T(4,128)} %param.23) | copy-start | bytes 30724
  25.3 10.9 %copy-start.15 = (bf16[2,1,80,2048]{3,2,1,0:T(8,128)(2,1)S(1)}, bf16[2,1,80,2048]{3,2,1,0:T(8,128)(2,1)}, u32[]{:S(2)}) copy-start(bf16[2,1,80,2048]{3,2,1,0:T(8,128)(2,1)} %param.35) | copy-start | bytes 1966084
  41.1 59.8 %collective-permute-start.6 = (bf16[80,2048]{1,0:T(8,128)(2,1)}, bf16[80,2048]{1,0:T(8,128)(2,1)S(1)}, u32[]{:S(2)}, u32[]{:S(2)}) collective-permute-start(bf16[80,2048]{1,0:T(8,128)(2,1)} %get-tuple-element.172.refs_1_), channel_id=1, source_target_pairs={{0,3},{1,0},{2,1},{3,2},{4,7},{5,4},{6,5},{7,6},{8,11},{9,8},{10,9... | collective-permute-start | bytes 983048 | tf_op jit(solution)/shard_map/ppermute | solution.py:24
  44.9 58.4 %collective-permute-start.5 = (bf16[80,2048]{1,0:T(8,128)(2,1)}, bf16[80,2048]{1,0:T(8,128)(2,1)S(1)}, u32[]{:S(2)}, u32[]{:S(2)}) collective-permute-start(bf16[80,2048]{1,0:T(8,128)(2,1)} %get-tuple-element.172.refs_1_), channel_id=1, source_target_pairs={{0,2},{1,3},{2,0},{3,1},{4,6},{5,7},{6,4},{7,5},{8,10},{9,11},{10,... | collective-permute-start | bytes 983048 | tf_op jit(solution)/shard_map/ppermute | solution.py:24
  44.9 58.5 %collective-permute-start.4 = (bf16[80,2048]{1,0:T(8,128)(2,1)}, bf16[80,2048]{1,0:T(8,128)(2,1)}, u32[]{:S(2)}, u32[]{:S(2)}) collective-permute-start(bf16[80,2048]{1,0:T(8,128)(2,1)} %get-tuple-element.172.refs_1_), channel_id=1, source_target_pairs={{0,1},{1,2},{2,3},{3,0},{4,5},{5,6},{6,7},{7,4},{8,9},{9,10},{10,1... | collective-permute-start | bytes 983048 | tf_op jit(solution)/shard_map/ppermute | solution.py:24
  71.3 41.2 %all-to-all-start.1 = ((bf16[4,80,2048]{2,1,0:T(8,128)(2,1)}), bf16[4,80,2048]{2,1,0:T(8,128)(2,1)S(1)}, u32[]{:S(2)}, u32[]{:S(2)}) async-start(bf16[4,80,2048]{2,1,0:T(8,128)(2,1)} %bitcast.70), calls=%async_computation.1 | async-start | bytes 2621440 | tf_op jit(solution)/shard_map/all_to_all | solution.py:315
  81.7 5.0 collective-permute-start
  94.2 17.7 %collective-permute-start.3 = (f32[2,640]{1,0:T(2,128)}, f32[2,640]{1,0:T(2,128)S(1)}, u32[]{:S(2)}, u32[]{:S(2)}) collective-permute-start(f32[2,640]{1,0:T(2,128)} %get-tuple-element.170), channel_id=1, source_target_pairs={{0,12},{1,13},{2,14},{3,15},{16,28},{17,29},{18,30},{19,31}} | collective-permute-start | bytes 15368 | tf_op jit(solution)/shard_map/ppermute | solution.py:29
  99.6 12.4 %collective-permute-start.2 = (f32[2,640]{1,0:T(2,128)}, f32[2,640]{1,0:T(2,128)S(1)}, u32[]{:S(2)}, u32[]{:S(2)}) collective-permute-start(f32[2,640]{1,0:T(2,128)} %get-tuple-element.170), channel_id=1, source_target_pairs={{0,8},{4,12},{1,9},{5,13},{2,10},{6,14},{3,11},{7,15},{16,24},{20,... | collective-permute-start | bytes 15368 | tf_op jit(solution)/shard_map/ppermute | solution.py:29
  100.9 11.1 %collective-permute-start.1 = (f32[2,640]{1,0:T(2,128)}, f32[2,640]{1,0:T(2,128)S(1)}, u32[]{:S(2)}, u32[]{:S(2)}) collective-permute-start(f32[2,640]{1,0:T(2,128)} %get-tuple-element.170), channel_id=1, source_target_pairs={{0,4},{4,8},{8,12},{1,5},{5,9},{9,13},{2,6},{6,10},{10,14},{3,7},{... | collective-permute-start | bytes 15368 | tf_op jit(solution)/shard_map/ppermute | solution.py:29
  110.0 14.6 %collective-permute-start.7 = (bf16[8,640]{1,0:T(8,128)(2,1)}, bf16[8,640]{1,0:T(8,128)(2,1)S(1)}, u32[]{:S(2)}, u32[]{:S(2)}) collective-permute-start(bf16[8,640]{1,0:T(8,128)(2,1)} %get-tuple-element.178), channel_id=1, source_target_pairs={{0,4},{4,8},{8,12},{1,5},{5,9},{9,13},{2,6},{6,10},{10,14},{3,7},{... | collective-permute-start | bytes 30728 | tf_op jit(solution)/shard_map/ppermute | solution.py:29
  119.6 46.9 %all-to-all-start.2 = ((bf16[4,80,2048]{2,1,0:T(8,128)(2,1)}), bf16[4,80,2048]{2,1,0:T(8,128)(2,1)S(1)}, u32[]{:S(2)}, u32[]{:S(2)}) async-start(bf16[4,80,2048]{2,1,0:T(8,128)(2,1)} %bitcast.74), calls=%async_computation.2 | async-start | bytes 2621440 | tf_op jit(solution)/shard_map/all_to_all | solution.py:321
  132.1 7.0 %collective-permute-start.10 = (f32[2,640]{1,0:T(2,128)}, f32[2,640]{1,0:T(2,128)S(1)}, u32[]{:S(2)}, u32[]{:S(2)}) collective-permute-start(f32[2,640]{1,0:T(2,128)} %get-tuple-element.182), channel_id=1, source_target_pairs={{0,12},{1,13},{2,14},{3,15},{16,28},{17,29},{18,30},{19,31}} | collective-permute-start | bytes 15368 | tf_op jit(solution)/shard_map/ppermute | solution.py:29
  135.3 3.8 collective-permute-start.9
  136.6 4.0 collective-permute-start.8
  170.6 91.2 %all-to-all-start.3 = ((bf16[4,80,2048]{2,1,0:T(8,128)(2,1)}), bf16[4,80,2048]{2,1,0:T(8,128)(2,1)S(1)}, u32[]{:S(2)}, u32[]{:S(2)}) async-start(bf16[4,80,2048]{2,1,0:T(8,128)(2,1)} %bitcast.73), calls=%async_computation.3 | async-start | bytes 2621440 | tf_op jit(solution)/shard_map/all_to_all | solution.py:315
  175.3 119.4 %all-gather.8.cloned.1.call-start = ((), (), s32[]{:S(2)}) async-start(), calls=%async_computation.13 | async-start | bytes 1638400 | tf_op jit(solution)/shard_map/all_gather | solution.py:937
  175.3 51.4 %collective-permute-start.11 = (bf16[80,2048]{1,0:T(8,128)(2,1)S(1)}, bf16[80,2048]{1,0:T(8,128)(2,1)S(1)}, u32[]{:S(2)}, u32[]{:S(2)}) collective-permute-start(bf16[80,2048]{1,0:T(8,128)(2,1)S(1)} %copy-done.42), channel_id=1, source_target_pairs={{0,1},{1,2},{2,3},{3,0},{4,5},{5,6},{6,7},{7,4},{8,9},{9,10},{10,1... | collective-permute-start | bytes 983048 | tf_op jit(solution)/shard_map/ppermute | solution.py:24
  177.3 72.8 %collective-permute-start.12 = (bf16[80,2048]{1,0:T(8,128)(2,1)S(1)}, bf16[80,2048]{1,0:T(8,128)(2,1)S(1)}, u32[]{:S(2)}, u32[]{:S(2)}) collective-permute-start(bf16[80,2048]{1,0:T(8,128)(2,1)S(1)} %copy-done.40), channel_id=1, source_target_pairs={{0,2},{1,3},{2,0},{3,1},{4,6},{5,7},{6,4},{7,5},{8,10},{9,11},{10,... | collective-permute-start | bytes 983048 | tf_op jit(solution)/shard_map/ppermute | solution.py:24
  179.7 70.5 %collective-permute-start.13 = (bf16[80,2048]{1,0:T(8,128)(2,1)S(1)}, bf16[80,2048]{1,0:T(8,128)(2,1)S(1)}, u32[]{:S(2)}, u32[]{:S(2)}) collective-permute-start(bf16[80,2048]{1,0:T(8,128)(2,1)S(1)} %copy-done.38), channel_id=1, source_target_pairs={{0,3},{1,0},{2,1},{3,2},{4,7},{5,4},{6,5},{7,6},{8,11},{9,8},{10,9... | collective-permute-start | bytes 983048 | tf_op jit(solution)/shard_map/ppermute | solution.py:24
  226.7 23.5 %copy-start.47 = (bf16[80,2048]{1,0:T(8,128)(2,1)}, bf16[80,2048]{1,0:T(8,128)(2,1)S(1)}, u32[]{:S(2)}) copy-start(bf16[80,2048]{1,0:T(8,128)(2,1)S(1)} %collective-permute-done.11.refs_3_) | copy-start | bytes 983044
  253.6 41.0 %collective-permute-start.16 = (bf16[80,2048]{1,0:T(8,128)(2,1)}, bf16[80,2048]{1,0:T(8,128)(2,1)S(1)}, u32[]{:S(2)}, u32[]{:S(2)}) collective-permute-start(bf16[80,2048]{1,0:T(8,128)(2,1)} %get-tuple-element.195.refs_1_), channel_id=1, source_target_pairs={{0,3},{1,0},{2,1},{3,2},{4,7},{5,4},{6,5},{7,6},{8,11},{9,8},{10,9... | collective-permute-start | bytes 983048 | tf_op jit(solution)/shard_map/ppermute | solution.py:24
  261.1 33.5 %collective-permute-start.15 = (bf16[80,2048]{1,0:T(8,128)(2,1)}, bf16[80,2048]{1,0:T(8,128)(2,1)S(1)}, u32[]{:S(2)}, u32[]{:S(2)}) collective-permute-start(bf16[80,2048]{1,0:T(8,128)(2,1)} %get-tuple-element.195.refs_1_), channel_id=1, source_target_pairs={{0,2},{1,3},{2,0},{3,1},{4,6},{5,7},{6,4},{7,5},{8,10},{9,11},{10,... | collective-permute-start | bytes 983048 | tf_op jit(solution)/shard_map/ppermute | solution.py:24
  261.6 33.0 %collective-permute-start.14 = (bf16[80,2048]{1,0:T(8,128)(2,1)}, bf16[80,2048]{1,0:T(8,128)(2,1)S(1)}, u32[]{:S(2)}, u32[]{:S(2)}) collective-permute-start(bf16[80,2048]{1,0:T(8,128)(2,1)} %get-tuple-element.195.refs_1_), channel_id=1, source_target_pairs={{0,1},{1,2},{2,3},{3,0},{4,5},{5,6},{6,7},{7,4},{8,9},{9,10},{10,1... | collective-permute-start | bytes 983048 | tf_op jit(solution)/shard_map/ppermute | solution.py:24
  289.6 38.8 %all-to-all-start.4 = ((bf16[4,80,2048]{2,1,0:T(8,128)(2,1)}), bf16[4,80,2048]{2,1,0:T(8,128)(2,1)S(1)}, u32[]{:S(2)}, u32[]{:S(2)}) async-start(bf16[4,80,2048]{2,1,0:T(8,128)(2,1)} %bitcast.76), calls=%async_computation.4 | async-start | bytes 2621440 | tf_op jit(solution)/shard_map/all_to_all | solution.py:321
  322.5 30.4 %collective-permute-start.17 = (bf16[80,2048]{1,0:T(8,128)(2,1)}, bf16[80,2048]{1,0:T(8,128)(2,1)S(1)}, u32[]{:S(2)}, u32[]{:S(2)}) collective-permute-start(bf16[80,2048]{1,0:T(8,128)(2,1)} %get-tuple-element.202), channel_id=1, source_target_pairs={{0,1},{1,2},{2,3},{3,0},{4,5},{5,6},{6,7},{7,4},{8,9},{9,10},{10,1... | collective-permute-start | bytes 983048 | tf_op jit(solution)/shard_map/ppermute | solution.py:24
  324.6 28.4 %collective-permute-start.18 = (bf16[80,2048]{1,0:T(8,128)(2,1)}, bf16[80,2048]{1,0:T(8,128)(2,1)S(1)}, u32[]{:S(2)}, u32[]{:S(2)}) collective-permute-start(bf16[80,2048]{1,0:T(8,128)(2,1)} %get-tuple-element.203), channel_id=1, source_target_pairs={{0,2},{1,3},{2,0},{3,1},{4,6},{5,7},{6,4},{7,5},{8,10},{9,11},{10,... | collective-permute-start | bytes 983048 | tf_op jit(solution)/shard_map/ppermute | solution.py:24
  326.9 26.0 %collective-permute-start.19 = (bf16[80,2048]{1,0:T(8,128)(2,1)}, bf16[80,2048]{1,0:T(8,128)(2,1)S(1)}, u32[]{:S(2)}, u32[]{:S(2)}) collective-permute-start(bf16[80,2048]{1,0:T(8,128)(2,1)} %get-tuple-element.204), channel_id=1, source_target_pairs={{0,3},{1,0},{2,1},{3,2},{4,7},{5,4},{6,5},{7,6},{8,11},{9,8},{10,9... | collective-permute-start | bytes 983048 | tf_op jit(solution)/shard_map/ppermute | solution.py:24
  333.0 70.7 %all-to-all-start.6 = ((bf16[4,80,2048]{2,1,0:T(8,128)(2,1)}), bf16[4,80,2048]{2,1,0:T(8,128)(2,1)}, u32[]{:S(2)}, u32[]{:S(2)}) async-start(bf16[4,80,2048]{2,1,0:T(8,128)(2,1)} %bitcast.71), calls=%async_computation.6 | async-start | bytes 2621440 | tf_op jit(solution)/shard_map/all_to_all | solution.py:315
  337.3 140.8 %reduce-scatter.4.cloned.1.call-start = ((), (), s32[]{:S(2)}) async-start(), calls=%async_computation.14 | async-start | bytes 14155776 | tf_op jit(solution)/shard_map/reduce_scatter | solution.py:984
  357.0 59.4 %collective-permute-start.22 = (bf16[80,2048]{1,0:T(8,128)(2,1)}, bf16[80,2048]{1,0:T(8,128)(2,1)S(1)}, u32[]{:S(2)}, u32[]{:S(2)}) collective-permute-start(bf16[80,2048]{1,0:T(8,128)(2,1)} %get-tuple-element.224.refs_1_), channel_id=1, source_target_pairs={{0,3},{1,0},{2,1},{3,2},{4,7},{5,4},{6,5},{7,6},{8,11},{9,8},{10,9... | collective-permute-start | bytes 983048 | tf_op jit(solution)/shard_map/ppermute | solution.py:24
  383.3 33.1 %collective-permute-start.21 = (bf16[80,2048]{1,0:T(8,128)(2,1)}, bf16[80,2048]{1,0:T(8,128)(2,1)}, u32[]{:S(2)}, u32[]{:S(2)}) collective-permute-start(bf16[80,2048]{1,0:T(8,128)(2,1)} %get-tuple-element.224.refs_1_), channel_id=1, source_target_pairs={{0,2},{1,3},{2,0},{3,1},{4,6},{5,7},{6,4},{7,5},{8,10},{9,11},{10,... | collective-permute-start | bytes 983048 | tf_op jit(solution)/shard_map/ppermute | solution.py:24
  383.3 33.2 %collective-permute-start.20 = (bf16[80,2048]{1,0:T(8,128)(2,1)}, bf16[80,2048]{1,0:T(8,128)(2,1)}, u32[]{:S(2)}, u32[]{:S(2)}) collective-permute-start(bf16[80,2048]{1,0:T(8,128)(2,1)} %get-tuple-element.224.refs_1_), channel_id=1, source_target_pairs={{0,1},{1,2},{2,3},{3,0},{4,5},{5,6},{6,7},{7,4},{8,9},{9,10},{10,1... | collective-permute-start | bytes 983048 | tf_op jit(solution)/shard_map/ppermute | solution.py:24
  384.1 10.5 %copy-start.28 = (f32[1,2048]{1,0:T(1,128)S(1)}, f32[1,2048]{1,0:T(1,128)}, u32[]{:S(2)}) copy-start(f32[1,2048]{1,0:T(1,128)} %get-tuple-element.275) | copy-start | bytes 24580
  384.1 10.5 %copy-start.29 = (f32[1,2048]{1,0:T(1,128)S(1)}, f32[1,2048]{1,0:T(1,128)}, u32[]{:S(2)}) copy-start(f32[1,2048]{1,0:T(1,128)} %get-tuple-element.276) | copy-start | bytes 24580
  394.6 49.0 %collective-permute-start.26 = (bf16[1024,1536]{1,0:T(8,128)(2,1)}, bf16[1024,1536]{1,0:T(8,128)(2,1)S(1)}, u32[]{:S(2)}, u32[]{:S(2)}) collective-permute-start(bf16[1024,1536]{1,0:T(8,128)(2,1)} %get-tuple-element.232), channel_id=1, source_target_pairs={{0,16},{16,0},{1,17},{17,1},{2,18},{18,2},{3,19},{19,3},{4,20},{20... | collective-permute-start | bytes 9437192 | tf_op jit(solution)/shard_map/ppermute | solution.py:24
  403.7 88.5 %all-to-all-start.5 = ((bf16[4,160,2048]{2,1,0:T(8,128)(2,1)}), bf16[4,160,2048]{2,1,0:T(8,128)(2,1)}, u32[]{:S(2)}, u32[]{:S(2)}) async-start(bf16[4,160,2048]{2,1,0:T(8,128)(2,1)} %bitcast.65), calls=%async_computation.5 | async-start | bytes 5242880 | tf_op jit(solution)/shard_map/all_to_all | solution.py:321
  408.2 160.3 %reduce-scatter.6.cloned.1.call-start = ((), (), s32[]{:S(2)}) async-start(), calls=%async_computation.15 | async-start | bytes 5570560 | tf_op jit(solution)/shard_map/reduce_scatter | solution.py:767
  425.4 17.5 %collective-permute-start.25 = (f32[4,640]{1,0:T(4,128)S(1)}, f32[4,640]{1,0:T(4,128)S(1)}, u32[]{:S(2)}, u32[]{:S(2)}) collective-permute-start(f32[4,640]{1,0:T(4,128)S(1)} %pad_maximum_fusion.4), channel_id=1, source_target_pairs={{12,0},{13,1},{14,2},{15,3},{28,16},{29,17},{30,18},{31,19}} | collective-permute-start | bytes 30728 | tf_op jit(solution)/shard_map/ppermute | solution.py:29
  426.7 16.3 %collective-permute-start.24 = (f32[4,640]{1,0:T(4,128)S(1)}, f32[4,640]{1,0:T(4,128)S(1)}, u32[]{:S(2)}, u32[]{:S(2)}) collective-permute-start(f32[4,640]{1,0:T(4,128)S(1)} %pad_maximum_fusion.4), channel_id=1, source_target_pairs={{8,0},{12,4},{9,1},{13,5},{10,2},{14,6},{11,3},{15,7},{24,16},{28,... | collective-permute-start | bytes 30728 | tf_op jit(solution)/shard_map/ppermute | solution.py:29
  428.0 15.0 %collective-permute-start.23 = (f32[4,640]{1,0:T(4,128)S(1)}, f32[4,640]{1,0:T(4,128)S(1)}, u32[]{:S(2)}, u32[]{:S(2)}) collective-permute-start(f32[4,640]{1,0:T(4,128)S(1)} %pad_maximum_fusion.4), channel_id=1, source_target_pairs={{4,0},{8,4},{12,8},{5,1},{9,5},{13,9},{6,2},{10,6},{14,10},{7,3},{... | collective-permute-start | bytes 30728 | tf_op jit(solution)/shard_map/ppermute | solution.py:29
  435.8 7.8 %collective-permute-start.27 = (bf16[1024,640]{1,0:T(8,128)(2,1)}, bf16[1024,640]{1,0:T(8,128)(2,1)}, u32[]{:S(2)}, u32[]{:S(2)}) collective-permute-start(bf16[1024,640]{1,0:T(8,128)(2,1)} %get-tuple-element.238), channel_id=1, source_target_pairs={{0,16},{16,0},{1,17},{17,1},{2,18},{18,2},{3,19},{19,3},{4,20},{20... | collective-permute-start | bytes 3932168 | tf_op jit(solution)/shard_map/ppermute | solution.py:24
  442.9 88.7 %collective-permute-start.36 = (bf16[1024,640]{1,0:T(8,128)(2,1)}, bf16[1024,640]{1,0:T(8,128)(2,1)}, u32[]{:S(2)}, u32[]{:S(2)}) collective-permute-start(bf16[1024,640]{1,0:T(8,128)(2,1)} %get-tuple-element.278), channel_id=1, source_target_pairs={{0,16},{16,0},{1,17},{17,1},{2,18},{18,2},{3,19},{19,3},{4,20},{20... | collective-permute-start | bytes 3932168 | tf_op jit(solution)/shard_map/ppermute | solution.py:24
  460.1 9.2 %copy-start.22 = (f32[8,640]{1,0:T(8,128)S(1)}, f32[8,640]{1,0:T(8,128)}, u32[]{:S(2)}) copy-start(f32[8,640]{1,0:T(8,128)} %get-tuple-element.247) | copy-start | bytes 61444
  460.1 11.4 %copy-start.21 = (f32[8,640]{1,0:T(8,128)S(1)}, f32[8,640]{1,0:T(8,128)}, u32[]{:S(2)}) copy-start(f32[8,640]{1,0:T(8,128)} %get-tuple-element.269) | copy-start | bytes 61444
  470.0 7.5 %collective-permute-start.28 = (f32[16,640]{1,0:T(8,128)S(1)}, f32[16,640]{1,0:T(8,128)S(1)}, u32[]{:S(2)}, u32[]{:S(2)}) collective-permute-start(f32[16,640]{1,0:T(8,128)S(1)} %pad_maximum_fusion.2), channel_id=1, source_target_pairs={{4,0},{8,4},{12,8},{5,1},{9,5},{13,9},{6,2},{10,6},{14,10},{7,3},{... | collective-permute-start | bytes 122888 | tf_op jit(solution)/shard_map/ppermute | solution.py:29
  501.7 10.9 %copy-start.16 = (bf16[8,160,160]{2,1,0:T(8,128)(2,1)S(1)}, bf16[8,160,160]{2,1,0:T(8,128)(2,1)}, u32[]{:S(2)}) copy-start(bf16[8,160,160]{2,1,0:T(8,128)(2,1)} %get-tuple-element.268) | copy-start | bytes 1228804
  502.5 16.6 %collective-permute-start.33 = (f32[2,2048]{1,0:T(2,128)S(1)}, f32[2,2048]{1,0:T(2,128)S(1)}, u32[]{:S(2)}, u32[]{:S(2)}) collective-permute-start(f32[2,2048]{1,0:T(2,128)S(1)} %pad_maximum_fusion.3), channel_id=1, source_target_pairs={{0,2},{1,3},{2,0},{3,1},{4,6},{5,7},{6,4},{7,5},{8,10},{9,11},{10,... | collective-permute-start | bytes 49160 | tf_op jit(solution)/shard_map/ppermute | solution.py:24
  505.4 13.8 %collective-permute-start.34 = (f32[2,2048]{1,0:T(2,128)S(1)}, f32[2,2048]{1,0:T(2,128)S(1)}, u32[]{:S(2)}, u32[]{:S(2)}) collective-permute-start(f32[2,2048]{1,0:T(2,128)S(1)} %pad_maximum_fusion.3), channel_id=1, source_target_pairs={{0,3},{1,0},{2,1},{3,2},{4,7},{5,4},{6,5},{7,6},{8,11},{9,8},{10,9... | collective-permute-start | bytes 49160 | tf_op jit(solution)/shard_map/ppermute | solution.py:24
  507.5 11.7 %collective-permute-start.32 = (f32[2,2048]{1,0:T(2,128)S(1)}, f32[2,2048]{1,0:T(2,128)S(1)}, u32[]{:S(2)}, u32[]{:S(2)}) collective-permute-start(f32[2,2048]{1,0:T(2,128)S(1)} %pad_maximum_fusion.3), channel_id=1, source_target_pairs={{0,1},{1,2},{2,3},{3,0},{4,5},{5,6},{6,7},{7,4},{8,9},{9,10},{10,1... | collective-permute-start | bytes 49160 | tf_op jit(solution)/shard_map/ppermute | solution.py:24
  507.5 83.5 %all-to-all-start.7 = ((bf16[4,80,2048]{2,1,0:T(8,128)(2,1)}), bf16[4,80,2048]{2,1,0:T(8,128)(2,1)S(1)}, u32[]{:S(2)}, u32[]{:S(2)}) async-start(bf16[4,80,2048]{2,1,0:T(8,128)(2,1)} %bitcast.66), calls=%async_computation.8 | async-start | bytes 2621440 | tf_op jit(solution)/shard_map/all_to_all | solution.py:321
  512.6 93.7 %reduce-scatter.8.cloned.1.call-start = ((), (), s32[]{:S(2)}) async-start(), calls=%async_computation.16 | async-start | bytes 3276800 | tf_op jit(solution)/shard_map/reduce_scatter | solution.py:767
  519.2 12.4 %collective-permute-start.37 = (bf16[1024,640]{1,0:T(8,128)(2,1)}, bf16[1024,640]{1,0:T(8,128)(2,1)S(1)}, u32[]{:S(2)}, u32[]{:S(2)}) collective-permute-start(bf16[1024,640]{1,0:T(8,128)(2,1)} %get-tuple-element.283), channel_id=1, source_target_pairs={{0,16},{16,0},{1,17},{17,1},{2,18},{18,2},{3,19},{19,3},{4,20},{20... | collective-permute-start | bytes 3932168 | tf_op jit(solution)/shard_map/ppermute | solution.py:24
  519.4 12.2 %copy-start = (bf16[8,176,160]{2,1,0:T(8,128)(2,1)}, bf16[8,176,160]{2,1,0:T(8,128)(2,1)S(1)}, u32[]{:S(2)}) copy-start(bf16[8,176,160]{2,1,0:T(8,128)(2,1)S(1)} %constant_dynamic-update-slice_fusion.refs_0_) | copy-start | bytes 1351684
  520.6 4.9 collective-permute-start.35
  521.1 25.5 %collective-permute-start.29 = (bf16[80,2048]{1,0:T(8,128)(2,1)}, bf16[80,2048]{1,0:T(8,128)(2,1)}, u32[]{:S(2)}, u32[]{:S(2)}) collective-permute-start(bf16[80,2048]{1,0:T(8,128)(2,1)} %get-tuple-element.265), channel_id=1, source_target_pairs={{0,1},{1,2},{2,3},{3,0},{4,5},{5,6},{6,7},{7,4},{8,9},{9,10},{10,1... | collective-permute-start | bytes 983048 | tf_op jit(solution)/shard_map/ppermute | solution.py:24
  523.1 42.4 %collective-permute-start.30 = (bf16[80,2048]{1,0:T(8,128)(2,1)}, bf16[80,2048]{1,0:T(8,128)(2,1)}, u32[]{:S(2)}, u32[]{:S(2)}) collective-permute-start(bf16[80,2048]{1,0:T(8,128)(2,1)} %get-tuple-element.266), channel_id=1, source_target_pairs={{0,2},{1,3},{2,0},{3,1},{4,6},{5,7},{6,4},{7,5},{8,10},{9,11},{10,... | collective-permute-start | bytes 983048 | tf_op jit(solution)/shard_map/ppermute | solution.py:24
  525.5 40.1 %collective-permute-start.31 = (bf16[80,2048]{1,0:T(8,128)(2,1)}, bf16[80,2048]{1,0:T(8,128)(2,1)}, u32[]{:S(2)}, u32[]{:S(2)}) collective-permute-start(bf16[80,2048]{1,0:T(8,128)(2,1)} %get-tuple-element.267), channel_id=1, source_target_pairs={{0,3},{1,0},{2,1},{3,2},{4,7},{5,4},{6,5},{7,6},{8,11},{9,8},{10,9... | collective-permute-start | bytes 983048 | tf_op jit(solution)/shard_map/ppermute | solution.py:24
  541.2 30.3 %collective-permute-start.40 = (bf16[8,176,160]{1,2,0:T(8,128)(2,1)S(1)}, bf16[8,176,160]{1,2,0:T(8,128)(2,1)S(1)}, u32[]{:S(2)}, u32[]{:S(2)}) collective-permute-start(bf16[8,176,160]{1,2,0:T(8,128)(2,1)S(1)} %copy.61), channel_id=1, source_target_pairs={{0,12},{4,0},{8,4},{12,8},{1,13},{5,1},{9,5},{13,9},{2,14},{6,2},{... | collective-permute-start | bytes 1351688 | tf_op jit(solution)/shard_map/ppermute | solution.py:24
  542.9 36.0 %collective-permute-start.39 = (bf16[8,176,160]{1,2,0:T(8,128)(2,1)S(1)}, bf16[8,176,160]{1,2,0:T(8,128)(2,1)S(1)}, u32[]{:S(2)}, u32[]{:S(2)}) collective-permute-start(bf16[8,176,160]{1,2,0:T(8,128)(2,1)S(1)} %copy.61), channel_id=1, source_target_pairs={{0,8},{4,12},{8,0},{12,4},{1,9},{5,13},{9,1},{13,5},{2,10},{6,14},... | collective-permute-start | bytes 1351688 | tf_op jit(solution)/shard_map/ppermute | solution.py:24
  546.6 42.2 %collective-permute-start.38 = (bf16[8,176,160]{1,2,0:T(8,128)(2,1)S(1)}, bf16[8,176,160]{1,2,0:T(8,128)(2,1)}, u32[]{:S(2)}, u32[]{:S(2)}) collective-permute-start(bf16[8,176,160]{1,2,0:T(8,128)(2,1)S(1)} %copy.61), channel_id=1, source_target_pairs={{0,4},{4,8},{8,12},{12,0},{1,5},{5,9},{9,13},{13,1},{2,6},{6,10},{... | collective-permute-start | bytes 1351688 | tf_op jit(solution)/shard_map/ppermute | solution.py:24
  (42 other events, 145.6 us)
Sparse Core Ops, SparseCore 0:
  10.7 54.8 all-gather.3
  67.5 98.9 all-gather.5
  181.5 61.9 all-gather.7
  353.0 93.2 reduce-scatter.3
  451.8 59.2 reduce-scatter.5
  546.4 56.8 reduce-scatter.7
